TPU v7x, 256 devices: a whole 4x4x8 slice. The times are simulated.
256 devices in a mesh: gx: 16 (over y, z_lo), gy: 16 (over z_hi, x, core).
Axes of the slice: x: 4, y: 4, z: 8 (z_hi: 2, z_lo: 4; z = z_hi * 4 + z_lo), core: 2. Of those that a mesh axis runs over, the one named last changes fastest.
Arguments:
- object_field: float32 [2, 8192, 8192], P(None, 'gy', 'gx'), may hold values from -6 to 6
- probe_field: float32 [2, 256, 256], replicated, may hold values from -5 to 5
- measured: float32 [16, 16, 4, 256, 256], P('gy', 'gx'), may hold values from 0 to 2.5
- offsets: int32 [16, 16, 4, 2], P('gy', 'gx'), may hold values from 0 to 512
- counts: int32 [16, 16], P('gy', 'gx'), may hold values from 1 to 4
Outputs:
- updated_object: float32 [2, 8192, 8192], P(None, 'gy', 'gx')
Inputs may be any that keep to these rules, and one draw needn't show every extreme that they name: `offsets`: A window lies within its tile and the 128 cells around it. Windows 0 to counts - 1 of a tile are live, the others unused.
All inputs are finite; a program needn't handle non-finite values.
Results may differ from a plain program's by a relative error of at most 0.0055.
Values sent between devices are 32-bit elements; how exact they have to be, the bound alone decides.
No kernel may reach another device: no remote copies, remote signals or barrier semaphores. Data moves between devices by JAX's collectives and lax.ppermute only.
A program may use at most 128 MiB of HBM per device.

v0:
```python
import functools
import math

import jax
import jax.numpy as jnp
from jax import lax
from jax.experimental import pallas as pl
from jax.experimental.pallas import tpu as pltpu
from jax.sharding import PartitionSpec as P


ITERS = 2
step_size = 0.25
amplitude_floor = 0.5

MIB = 1 << 20

GX_ODD, GY_ODD, EDGE, RELAY, LIVE, OFFS = 0, 1, 2, 3, 4, 5


def pairs(count, first):
    ups = [(i, i + 1) for i in range(first, count - 1, 2)]
    return ups + [(b, a) for a, b in ups]


def swap_rows(direct, detour, even_cells):
    count = lax.axis_size("gy")
    low = count // 2 - 1
    far = [(low, low + 1), (low + 1, low)]
    near = [p for p in pairs(count, 1) if p not in far]
    first = lax.ppermute(detour, "gy", near + [(low, 0), (low + 1, count - 1)])
    straight = lax.ppermute(direct, "gy", near + far)
    even = lax.ppermute(even_cells, "gy", pairs(count, 0))
    second = lax.ppermute(first, "gy", [(0, low + 1), (count - 1, low)])
    return straight, first, second, even


def swap_columns(odd_cells, even_cells):
    count = lax.axis_size("gx")
    from_odd = lax.ppermute(odd_cells, "gx", pairs(count, 1))
    from_even = lax.ppermute(even_cells, "gx", pairs(count, 0))
    return from_odd, from_even


CUT = 128


def pack(real, imag, direct, detour):
    wide = real.shape[1]
    direct[:, :wide] = real
    direct[:, wide:] = imag[:, :CUT]
    detour[...] = imag[:, CUT:]


def unpack(meta, direct, detour, relayed, line):
    wide = line.shape[2]
    own = meta[RELAY] == 0
    line[0] = direct[:, :wide]
    line[1, :, :CUT] = direct[:, wide:]
    line[1, :, CUT:] = jnp.where(own, detour[...], jnp.zeros_like(detour)) + relayed[...]


def dot(a, b):
    return jnp.dot(a, b, preferred_element_type=jnp.float32)


def table_blocks(shift, half, side):
    rows = lax.broadcasted_iota(jnp.int32, (half, half), 0)
    cols = lax.broadcasted_iota(jnp.int32, (half, half), 1)
    scale = 2.0 * math.pi / side
    norm = 1.0 / math.sqrt(side)

    def entries(freq, cell):
        phase = (freq * (cell - shift + side)) & (side - 1)
        angle = phase.astype(jnp.float32) * scale
        return jnp.cos(angle) * norm, jnp.sin(angle) * norm

    out = []
    for odd in (0, 1):
        c, s = entries(2 * rows + odd, cols)
        ct, st = entries(2 * cols + odd, rows)
        out.append((c, s, ct, st))
    return out


def prepare_kernel(side, windows, meta, probe, measured, probes, tables, amps):
    half = side // 2
    bf = jnp.bfloat16
    rows = lax.broadcasted_iota(jnp.int32, (side, side), 0)
    cols = lax.broadcasted_iota(jnp.int32, (side, side), 1)
    place = jnp.where(cols < half, 2 * cols, 2 * (cols - half) + 1)
    picks = (rows == place).astype(jnp.float32).astype(bf)
    place_t = jnp.where(rows < half, 2 * rows, 2 * (rows - half) + 1)
    picks_t = (cols == place_t).astype(jnp.float32).astype(bf)

    def parts(x):
        high = x.astype(bf)
        rest = x - high.astype(jnp.float32)
        mid = rest.astype(bf)
        low = (rest - mid.astype(jnp.float32)).astype(bf)
        return high, mid, low

    def body(w, _):
        row = meta[OFFS + 2 * w] & (side - 1)
        col = meta[OFFS + 2 * w + 1] & (side - 1)
        for part in (0, 1):
            turned = pltpu.roll(probe[part], row, 0)
            probes[w, part] = pltpu.roll(turned, col, 1)
        for axis, shift in ((0, row), (1, col)):
            for odd, (c, s, ct, st) in enumerate(table_blocks(shift, half, side)):
                at = 4 * axis + 2 * odd
                tables[w, at, :half, :half] = c.astype(bf)
                tables[w, at, :half, half:] = s.astype(bf)
                tables[w, at, half:, :half] = (-s).astype(bf)
                tables[w, at, half:, half:] = c.astype(bf)
                tables[w, at + 1, :half, :half] = ct.astype(bf)
                tables[w, at + 1, :half, half:] = (-st).astype(bf)
                tables[w, at + 1, half:, :half] = st.astype(bf)
                tables[w, at + 1, half:, half:] = ct.astype(bf)
        a = [dot(x, picks) for x in parts(measured[w])]
        b = [dot(picks_t, x) for x in parts(a[0] + (a[1] + a[2]))]
        amps[w] = b[0] + (b[1] + b[2])
        return 0

    lax.fori_loop(0, windows, body, 0)


def gradient_kernel(
    side,
    windows,
    meta,
    centre,
    halo_direct,
    halo_detour,
    halo_relayed,
    halo_even,
    probes,
    tables,
    amps,
    grad,
    rim_direct,
    rim_detour,
    rim_even,
    band_odd,
    band_even,
    field,
    total,
    mixed,
    line,
):
    half = side // 2
    tile, wide = centre.shape[1:]
    bf = jnp.bfloat16
    odd_row = meta[GY_ODD]
    bottom = half + tile
    at_odd = pl.multiple_of(odd_row * bottom, half)
    at_even = pl.multiple_of((1 - odd_row) * bottom, half)
    field[:, pl.ds(half, tile), :] = centre[...]
    unpack(meta, halo_direct, halo_detour, halo_relayed, line)
    field[:, pl.ds(at_odd, half), :] = line[...]
    field[:, pl.ds(at_even, half), :] = halo_even[...]
    total[...] = jnp.zeros_like(total)
    chunk = 32
    zero = jnp.float32(0)

    for w in range(windows):
        a, b = meta[OFFS + 2 * w], meta[OFFS + 2 * w + 1]
        live = w < meta[LIVE]
        hi_a, hi_b = (a >= side).astype(jnp.int32), (b >= side).astype(jnp.int32)
        row0, col0 = pl.multiple_of(hi_a * side, side), pl.multiple_of(hi_b * side, side)
        row_in, col_in = a - row0, b - col0
        near = lax.broadcasted_iota(jnp.int32, (chunk, side), 1) >= col_in

        def below(start):
            return (lax.broadcasted_iota(jnp.int32, (chunk, side), 0) + start) >= row_in

        def patch(part, start):
            def at(i, j):
                return field[
                    part,
                    pl.ds(pl.multiple_of(row0 + i * side + start, chunk), chunk),
                    pl.ds(pl.multiple_of(col0 + j * side, side), side),
                ]

            return jnp.where(
                below(start),
                jnp.where(near, at(0, 0), at(0, 1)),
                jnp.where(near, at(1, 0), at(1, 1)),
            )

        def exits(start):
            real, imag = patch(0, start), patch(1, start)
            p_real = probes[w, 0, pl.ds(start, chunk), :]
            p_imag = probes[w, 1, pl.ds(start, chunk), :]
            return p_real * real - p_imag * imag, p_real * imag + p_imag * real

        for i in range(0, half, chunk):
            r0, i0 = exits(i)
            r1, i1 = exits(half + i)
            mixed[0, i : i + chunk, :] = (r0 + r1).astype(bf)
            mixed[0, half + i : half + i + chunk, :] = (i0 + i1).astype(bf)
            mixed[1, i : i + chunk, :] = (r0 - r1).astype(bf)
            mixed[1, half + i : half + i + chunk, :] = (i0 - i1).astype(bf)

        plus, minus = [], []
        for odd in (0, 1):
            h = dot(tables[w, 2 * odd], mixed[odd])
            re0, re1 = h[:half, :half], h[:half, half:]
            im0, im1 = h[half:, :half], h[half:, half:]
            plus.append(jnp.concatenate([re0 + re1, im0 + im1], axis=1).astype(bf))
            minus.append(jnp.concatenate([re0 - re1, im0 - im1], axis=1).astype(bf))

        backs = []
        for odd, sides in ((0, plus), (1, minus)):
            far = dot(jnp.concatenate(sides, axis=0), tables[w, 4 + 2 * odd + 1])
            re, im = far[:, :half], far[:, half:]
            power = jnp.maximum(re * re + im * im, amplitude_floor * amplitude_floor)
            factor = 1.0 - amps[w, :, odd * half : (odd + 1) * half] * lax.rsqrt(power)
            chi = jnp.concatenate([re * factor, im * factor], axis=1).astype(bf)
            backs.append(dot(chi, tables[w, 4 + 2 * odd]))
        left, right = backs[0] + backs[1], backs[0] - backs[1]

        outs = []
        for odd in (0, 1):
            at = slice(odd * half, (odd + 1) * half)
            real = jnp.concatenate([left[at, :half], right[at, :half]], axis=1)
            imag = jnp.concatenate([left[at, half:], right[at, half:]], axis=1)
            stacked = jnp.concatenate([real, imag], axis=0).astype(bf)
            outs.append(dot(tables[w, 2 * odd + 1], stacked))
        upper, lower = outs[0] + outs[1], outs[0] - outs[1]

        for start in range(0, side, chunk):
            back = upper if start < half else lower
            at = start % half
            b_real, b_imag = back[at : at + chunk], back[half + at : half + at + chunk]
            p_real = probes[w, 0, pl.ds(start, chunk), :]
            p_imag = probes[w, 1, pl.ds(start, chunk), :]
            terms = (p_real * b_real + p_imag * b_imag, p_real * b_imag - p_imag * b_real)
            rows_in = below(start)
            for part in (0, 1):
                for i, j in ((0, 0), (0, 1), (1, 0), (1, 1)):
                    keep = (rows_in if i == 0 else ~rows_in) & (near if j == 0 else ~near)
                    place = (
                        part,
                        pl.ds(pl.multiple_of(row0 + i * side + start, chunk), chunk),
                        pl.ds(pl.multiple_of(col0 + j * side, side), side),
                    )
                    total[place] = total[place] + jnp.where(keep & live, terms[part], zero)

    grad[...] = total[:, pl.ds(half, tile), :]
    odd_rows = pl.ds(at_odd, half)
    pack(total[0, odd_rows, :], total[1, odd_rows, :], rim_direct, rim_detour)
    rim_even[...] = total[:, pl.ds(at_even, half), :]
    for band, cols in (
        (band_odd, odd_side(meta, band_odd, wide)),
        (band_even, even_side(meta, band_even, wide)),
    ):
        band[...] = total[:, side:tile, cols]


def odd_side(meta, band, wide):
    return pl.ds(pl.multiple_of(meta[GX_ODD] * (wide - band.shape[2]), 128), band.shape[2])


def even_side(meta, band, wide):
    return pl.ds(pl.multiple_of((1 - meta[GX_ODD]) * (wide - band.shape[2]), 128), band.shape[2])


def rim_rows(meta, half):
    odd_row = meta[GY_ODD]
    return (
        pl.ds(pl.multiple_of(odd_row * half, half), half),
        pl.ds(pl.multiple_of((1 - odd_row) * half, half), half),
    )


def sides_kernel(meta, own, rim_odd, rim_even, mid_odd, mid_even, sems):
    tile, half = own.shape[1], rim_odd.shape[2]
    copies = []
    for rim, mid, cols in (
        (rim_odd, mid_odd, odd_side(meta, rim_odd, tile)),
        (rim_even, mid_even, even_side(meta, rim_even, tile)),
    ):
        for src, dst in (
            (own.at[:, pl.ds(0, half), cols], rim.at[:, pl.ds(0, half), :]),
            (own.at[:, pl.ds(tile - half, half), cols], rim.at[:, pl.ds(half, half), :]),
            (own.at[:, pl.ds(half, tile - 2 * half), cols], mid),
        ):
            copies.append(pltpu.make_async_copy(src, dst, sems.at[len(copies)]))
    for copy in copies:
        copy.start()
    for copy in copies:
        copy.wait()


def edges_kernel(meta, own, side_odd, side_even, _, direct, detour, even, lines):
    tile, half = own.shape[1], side_odd.shape[2]
    wide = lines.shape[2]
    for at, rows in ((0, slice(0, half)), (half, slice(tile - half, tile))):
        lines[:, at : at + half, half : half + tile] = own[:, rows, :]
    lines[:, :, odd_side(meta, side_odd, wide)] = side_odd[...]
    lines[:, :, even_side(meta, side_even, wide)] = side_even[...]
    odd_rows, even_rows = rim_rows(meta, half)
    pack(lines[0, odd_rows, :], lines[1, odd_rows, :], direct, detour)
    even[...] = lines[:, even_rows, :]


def centre_kernel(meta, own, lines, side_odd, side_even, centre):
    tile, half = own.shape[1], side_odd.shape[2]
    wide = lines.shape[2]
    mid = slice(half, tile - half)
    centre[:, :half, :] = lines[:, :half, :]
    centre[:, tile - half :, :] = lines[:, half:, :]
    centre[:, mid, half : half + tile] = own[:, mid, :]
    centre[:, mid, odd_side(meta, side_odd, wide)] = side_odd[...]
    centre[:, mid, even_side(meta, side_even, wide)] = side_even[...]


def bands_kernel(meta, grad, direct, detour, relayed, even, band_odd, band_even, line):
    (tile, wide), half = grad.shape[1:], even.shape[1]
    unpack(meta, direct, detour, relayed, line)
    odd_rows, even_rows = rim_rows(meta, half)
    for band, cols in ((band_odd, odd_side(meta, band_odd, wide)), (band_even, even_side(meta, band_even, wide))):
        band[:, :half, :] = grad[:, :half, cols]
        band[:, half:, :] = grad[:, tile - half :, cols]
        band[:, odd_rows, :] = band[:, odd_rows, :] + line[:, :, cols]
        band[:, even_rows, :] = band[:, even_rows, :] + even[:, :, cols]


def clear_outside(meta, cells, half):
    wide = cells.shape[2]

    @pl.when(meta[EDGE] == 1)
    def _():
        outside = pl.ds(pl.multiple_of(meta[GX_ODD] * (wide - half), half), half)
        cells[:, :, outside] = jnp.zeros((*cells.shape[:2], half), jnp.float32)


def update_edges_kernel(
    meta, centre, grad, line, even, band_odd, band_even, direct, detour, out_even, lines
):
    (tile, wide), half = grad.shape[1:], even.shape[1]
    odd_rows, even_rows = rim_rows(meta, half)
    for at, rows in ((0, slice(0, half)), (half, slice(tile - half, tile))):
        lines[:, at : at + half, :] = centre[:, rows, :] - step_size * grad[:, rows, :]
    lines[:, odd_rows, :] = lines[:, odd_rows, :] - step_size * line[...]
    lines[:, even_rows, :] = lines[:, even_rows, :] - step_size * even[...]
    for band, cols in ((band_odd, odd_side(meta, band_odd, wide)), (band_even, even_side(meta, band_even, wide))):
        lines[:, :, cols] = lines[:, :, cols] - step_size * band[...]
    clear_outside(meta, lines, half)
    pack(lines[0, odd_rows, :], lines[1, odd_rows, :], direct, detour)
    out_even[...] = lines[:, even_rows, :]


def update_centre_kernel(meta, centre, grad, lines, band_odd, band_even, fresh):
    tile, wide = grad.shape[1:]
    half = lines.shape[1] // 2
    mid = slice(half, tile - half)
    fresh[:, mid, :] = centre[:, mid, :] - step_size * grad[:, mid, :]
    for band, cols in ((band_odd, odd_side(meta, band_odd, wide)), (band_even, even_side(meta, band_even, wide))):
        fresh[:, mid, cols] = fresh[:, mid, cols] - step_size * band[...]
    clear_outside(meta, fresh, half)
    fresh[:, :half, :] = lines[:, :half, :]
    fresh[:, tile - half :, :] = lines[:, half:, :]


def final_kernel(meta, centre, grad, line, even, mid_odd, mid_even, rim_odd, rim_even, out):
    tile, half = grad.shape[1], even.shape[1]
    own = slice(half, half + tile)
    odd_row = meta[GY_ODD]
    far = tile - half
    out[...] = centre[:, :, own] - step_size * grad[:, :, own]
    for at, rim in ((odd_row * far, line), ((1 - odd_row) * far, even)):
        rows = pl.ds(pl.multiple_of(at, half), half)
        out[:, rows, :] = out[:, rows, :] - step_size * rim[:, :, own]
    for mid, rim, cols in (
        (mid_odd, rim_odd, odd_side(meta, mid_odd, tile)),
        (mid_even, rim_even, even_side(meta, mid_even, tile)),
    ):
        out[:, :half, cols] = out[:, :half, cols] - step_size * rim[:, :half, :]
        out[:, half:far, cols] = out[:, half:far, cols] - step_size * mid[...]
        out[:, far:, cols] = out[:, far:, cols] - step_size * rim[:, half:, :]


def call(kernel, meta, arrays, outs, scratch=(), flops=0, room=0, after=None, hbm=False):
    f32 = jnp.float32
    shapes = [
        jax.ShapeDtypeStruct(*o) if isinstance(o[0], tuple) else jax.ShapeDtypeStruct(o, f32)
        for o in outs
    ]
    shapes_in = [jax.ShapeDtypeStruct(x.shape, x.dtype) for x in arrays]
    moved = sum(math.prod(x.shape) * x.dtype.itemsize for x in [*shapes_in, *shapes])
    late = [] if after is None else [after]
    smem = pl.BlockSpec(memory_space=pltpu.SMEM)
    vmem = pl.BlockSpec(memory_space=pltpu.VMEM)
    anywhere = pl.BlockSpec(memory_space=pl.ANY)
    return pl.pallas_call(
        kernel,
        out_shape=shapes,
        in_specs=[smem] + [pl.BlockSpec(memory_space=pltpu.HBM) if hbm else vmem] * len(arrays) + [anywhere] * len(late),
        out_specs=[vmem] * len(shapes),
        scratch_shapes=list(scratch),
        compiler_params=pltpu.CompilerParams(vmem_limit_bytes=room or moved + MIB),
        cost_estimate=pl.CostEstimate(flops=flops, bytes_accessed=moved, transcendentals=0),
    )(meta, *arrays, *late)


def local(object_field, probe_field, measured, offsets, counts):
    tile = object_field.shape[1]
    side = probe_field.shape[1]
    half = side // 2
    windows = offsets.shape[2]
    wide = tile + side
    bf, f32 = jnp.bfloat16, jnp.float32
    place_col, columns_of_tiles = lax.axis_index("gx"), lax.axis_size("gx")
    odd_col = place_col % 2
    edge = (place_col == 0) | (place_col == columns_of_tiles - 1)
    place_row, rows_of_tiles = lax.axis_index("gy"), lax.axis_size("gy")
    odd_row = place_row % 2
    relay = (place_row == 0) | (place_row == rows_of_tiles - 1)
    places = jnp.stack([odd_col, odd_row, edge.astype(jnp.int32), relay.astype(jnp.int32)])
    meta = jnp.concatenate([places, counts[0], offsets[0, 0].reshape(-1)]).astype(jnp.int32)

    column, band = (2, 2 * half, half), (2, 2 * half, side)
    mid_column, mid_band = (2, tile - 2 * half, half), (2, tile - 2 * half, side)
    middle, lines = (2, tile, wide), (2, 2 * half, wide)
    line = (2, half, wide)
    sends = ((half, wide + CUT), (half, wide - CUT), line)

    *rims, mid_odd, mid_even = call(
        sides_kernel,
        places,
        (object_field,),
        (column, column, mid_column, mid_column),
        scratch=(pltpu.SemaphoreType.DMA((6,)),),
        hbm=True,
    )
    rims = swap_columns(*rims)
    mids = swap_columns(mid_odd, mid_even)
    probes, tables, amps = call(
        functools.partial(prepare_kernel, side, windows),
        meta,
        (probe_field, measured[0, 0]),
        ((windows, 2, side, side), ((windows, 8, side, side), bf), (windows, side, side)),
        flops=10**9,
        room=20 * MIB,
    )
    *edges, rows = call(edges_kernel, meta, (object_field, *rims), (*sends, lines), after=amps)
    halos = swap_rows(*edges)
    (centre,) = call(centre_kernel, meta, (object_field, rows, *mids), (middle,))
    for iteration in range(ITERS):
        last = iteration + 1 == ITERS
        grad, *rims, mid_odd, mid_even = call(
            functools.partial(gradient_kernel, side, windows),
            meta,
            (centre, *halos, probes, tables, amps),
            (middle, *sends, *((mid_column if last else mid_band),) * 2),
            scratch=(
                pltpu.VMEM((2, wide, wide), f32),
                pltpu.VMEM((2, wide, wide), f32),
                pltpu.VMEM((2, side, side), bf),
                pltpu.VMEM(line, f32),
            ),
            flops=windows * 16 * side**3,
            room=24 * MIB,
        )
        rims = swap_rows(*rims)
        shape = column if last else band
        *bands, odd_line = call(bands_kernel, meta, (grad, *rims), (shape, shape, line))
        bands = swap_columns(*bands)
        mids = swap_columns(mid_odd, mid_even)
        if last:
            break
        *edges, rows = call(
            update_edges_kernel,
            meta,
            (centre, grad, odd_line, rims[3], *bands),
            (*sends, lines),
        )
        halos = swap_rows(*edges)
        (centre,) = call(update_centre_kernel, meta, (centre, grad, rows, *mids), (middle,))
    (updated,) = call(
        final_kernel,
        meta,
        (centre, grad, odd_line, rims[3], *mids, *bands),
        (object_field.shape,),
    )
    return updated


def solution(mesh):
    return jax.shard_map(
        local,
        mesh=mesh,
        in_specs=(
            P(None, "gy", "gx"),
            P(),
            P("gy", "gx", None, None, None),
            P("gy", "gx", None, None),
            P("gy", "gx"),
        ),
        out_specs=P(None, "gy", "gx"),
        check_vma=False,
    )
```

profile of v0, /device:TPU:15, one launch (start us, length us, event | category | flops | bytes accessed | tf_op | source)
XLA Modules:
  0.0 217.9 jit_solution(9730422968316642199)
XLA Ops:
  0.1 1.6 copy-done
  1.7 1.5 shard_map.55
  3.1 6.1 %collective-permute-start = (f32[2,256,128]{2,1,0:T(8,128)}, f32[2,256,128]{2,1,0:T(8,128)S(1)}, u32[]{:S(2)}, u32[]{:S(2)}) collective-permute-start(f32[2,256,128]{2,1,0:T(8,128)} %get-tuple-element.38), channel_id=1, source_target_pairs={{16,32},{48,64},{80,96},{112,128},{144,160},{176,192},{208,224},{3... | collective-permute-start | bytes 786440 | tf_op jit(solution)/shard_map/ppermute | solution.py:40
  13.2 12.7 %shard_map.56 = (f32[4,2,256,256]{3,2,1,0:T(8,128)S(1)}, bf16[4,8,256,256]{3,2,1,0:T(8,128)(2,1)S(1)}, f32[4,256,256]{2,1,0:T(8,128)S(1)}) custom-call(s32[13]{0:T(128)S(1)} %concatenate.4.meta, f32[2,256,256]{2,1,0:T(8,128)S(1)} %copy-done.3, f32[4,256,256]{2,1,0:T(8,128)S(1)} %bitcast.7), custom_call_target="tpu_custom_call" | custom-call | flops 1000000000 | bytes 8912896 | tf_op jit(solution)/shard_map/pallas_call | solution.py:397
  27.7 2.0 collective-permute-start.5
  29.8 8.9 %collective-permute-start.4 = (f32[128,896]{1,0:T(8,128)S(1)}, f32[128,896]{1,0:T(8,128)S(1)}, u32[]{:S(2)}, u32[]{:S(2)}) collective-permute-start(f32[128,896]{1,0:T(8,128)S(1)} %get-tuple-element.44), channel_id=1, source_target_pairs={{1,2},{3,4},{5,6},{9,10},{11,12},{13,14},{2,1},{4,3},{6,5},{10,9},... | collective-permute-start | bytes 1376264 | tf_op jit(solution)/shard_map/ppermute | solution.py:32
  40.0 4.3 %collective-permute-start.2 = (f32[2,256,128]{2,1,0:T(8,128)S(1)}, f32[2,256,128]{2,1,0:T(8,128)S(1)}, u32[]{:S(2)}, u32[]{:S(2)}) collective-permute-start(f32[2,256,128]{2,1,0:T(8,128)S(1)} %get-tuple-element.42), channel_id=1, source_target_pairs={{16,32},{48,64},{80,96},{112,128},{144,160},{176,192},{208,224},{3... | collective-permute-start | bytes 786440 | tf_op jit(solution)/shard_map/ppermute | solution.py:40
  45.5 13.3 %collective-permute-done.2.side_odd = f32[2,256,128]{2,1,0:T(8,128)S(1)} collective-permute-done((f32[2,256,128]{2,1,0:T(8,128)S(1)}, f32[2,256,128]{2,1,0:T(8,128)S(1)}, u32[]{:S(2)}, u32[]{:S(2)}) %collective-permute-start.2) | collective-permute-done | bytes 262176 | tf_op jit(solution)/shard_map/ppermute | solution.py:40
  58.8 3.4 %collective-permute-done.3.side_even = f32[2,256,128]{2,1,0:T(8,128)S(1)} collective-permute-done((f32[2,256,128]{2,1,0:T(8,128)S(1)}, f32[2,256,128]{2,1,0:T(8,128)S(1)}, u32[]{:S(2)}, u32[]{:S(2)}) %collective-permute-start.3) | collective-permute-done | bytes 262176 | tf_op jit(solution)/shard_map/ppermute | solution.py:41
  63.0 7.2 %shard_map.59 = (f32[2,512,768]{2,1,0:T(8,128)S(1)}, f32[128,896]{1,0:T(8,128)S(1)}, f32[128,640]{1,0:T(8,128)S(1)}, f32[2,128,768]{2,1,0:T(8,128)S(1)}, f32[2,2...) custom-call(s32[13]{0:T(128)S(1)} %concatenate.4.meta, f32[2,512,768]{2,1,0:T(8,128)S(1)} %shard_map.58.centre, ...), custom_call_target="tpu_custom_call" | custom-call | flops 1073741824 | bytes 18153472 | tf_op jit(solution)/shard_map/pallas_call | solution.py:397
  71.6 9.7 %collective-permute-start.8 = (f32[128,896]{1,0:T(8,128)S(1)}, f32[128,896]{1,0:T(8,128)S(1)}, u32[]{:S(2)}, u32[]{:S(2)}) collective-permute-start(f32[128,896]{1,0:T(8,128)S(1)} %get-tuple-element.50), channel_id=1, source_target_pairs={{1,2},{3,4},{5,6},{9,10},{11,12},{13,14},{2,1},{4,3},{6,5},{10,9},... | collective-permute-start | bytes 1376264 | tf_op jit(solution)/shard_map/ppermute | solution.py:32
  82.6 4.9 %collective-permute-done.8.direct = f32[128,896]{1,0:T(8,128)S(1)} collective-permute-done((f32[128,896]{1,0:T(8,128)S(1)}, f32[128,896]{1,0:T(8,128)S(1)}, u32[]{:S(2)}, u32[]{:S(2)}) %collective-permute-start.8) | collective-permute-done | bytes 458784 | tf_op jit(solution)/shard_map/ppermute | solution.py:32
  87.6 6.4 %collective-permute-done.10.relayed = f32[128,640]{1,0:T(8,128)S(1)} collective-permute-done((f32[128,640]{1,0:T(8,128)S(1)}, f32[128,640]{1,0:T(8,128)S(1)}, u32[]{:S(2)}, u32[]{:S(2)}) %collective-permute-start.10) | collective-permute-done | bytes 327712 | tf_op jit(solution)/shard_map/ppermute | solution.py:34
  94.8 4.0 %collective-permute-start.12 = (f32[2,256,256]{2,1,0:T(8,128)S(1)}, f32[2,256,256]{2,1,0:T(8,128)S(1)}, u32[]{:S(2)}, u32[]{:S(2)}) collective-permute-start(f32[2,256,256]{2,1,0:T(8,128)S(1)} %get-tuple-element.54), channel_id=1, source_target_pairs={{16,32},{48,64},{80,96},{112,128},{144,160},{176,192},{208,224},{3... | collective-permute-start | bytes 1572872 | tf_op jit(solution)/shard_map/ppermute | solution.py:40
  98.8 13.2 %collective-permute-start.13 = (f32[2,256,256]{2,1,0:T(8,128)S(1)}, f32[2,256,256]{2,1,0:T(8,128)S(1)}, u32[]{:S(2)}, u32[]{:S(2)}) collective-permute-start(f32[2,256,256]{2,1,0:T(8,128)S(1)} %get-tuple-element.55), channel_id=1, source_target_pairs={{0,16},{32,48},{64,80},{96,112},{128,144},{160,176},{192,208},{224... | collective-permute-start | bytes 1572872 | tf_op jit(solution)/shard_map/ppermute | solution.py:41
  112.0 6.6 %collective-permute-done.13.band_even = f32[2,256,256]{2,1,0:T(8,128)S(1)} collective-permute-done((f32[2,256,256]{2,1,0:T(8,128)S(1)}, f32[2,256,256]{2,1,0:T(8,128)S(1)}, u32[]{:S(2)}, u32[]{:S(2)}) %collective-permute-start.13) | collective-permute-done | bytes 524320 | tf_op jit(solution)/shard_map/ppermute | solution.py:41
  120.0 2.9 %collective-permute-start.17 = (f32[128,640]{1,0:T(8,128)S(1)}, f32[128,640]{1,0:T(8,128)S(1)}, u32[]{:S(2)}, u32[]{:S(2)}) collective-permute-start(f32[128,640]{1,0:T(8,128)S(1)} %get-tuple-element.60), channel_id=1, source_target_pairs={{1,2},{3,4},{5,6},{9,10},{11,12},{13,14},{2,1},{4,3},{6,5},{10,9},... | collective-permute-start | bytes 983048 | tf_op jit(solution)/shard_map/ppermute | solution.py:31
  122.9 1.9 collective-permute-start.14
  124.8 1.6 collective-permute-start.15
  126.4 7.0 %collective-permute-start.16 = (f32[128,896]{1,0:T(8,128)S(1)}, f32[128,896]{1,0:T(8,128)S(1)}, u32[]{:S(2)}, u32[]{:S(2)}) collective-permute-start(f32[128,896]{1,0:T(8,128)S(1)} %get-tuple-element.59), channel_id=1, source_target_pairs={{1,2},{3,4},{5,6},{9,10},{11,12},{13,14},{2,1},{4,3},{6,5},{10,9},... | collective-permute-start | bytes 1376264 | tf_op jit(solution)/shard_map/ppermute | solution.py:32
  134.8 6.6 %collective-permute-done.14.band_odd = f32[2,256,256]{2,1,0:T(8,128)S(1)} collective-permute-done((f32[2,256,256]{2,1,0:T(8,128)S(1)}, f32[2,256,256]{2,1,0:T(8,128)S(1)}, u32[]{:S(2)}, u32[]{:S(2)}) %collective-permute-start.14) | collective-permute-done | bytes 524320 | tf_op jit(solution)/shard_map/ppermute | solution.py:40
  141.4 8.5 %collective-permute-done.15.band_even = f32[2,256,256]{2,1,0:T(8,128)S(1)} collective-permute-done((f32[2,256,256]{2,1,0:T(8,128)S(1)}, f32[2,256,256]{2,1,0:T(8,128)S(1)}, u32[]{:S(2)}, u32[]{:S(2)}) %collective-permute-start.15) | collective-permute-done | bytes 524320 | tf_op jit(solution)/shard_map/ppermute | solution.py:41
  151.2 11.2 %collective-permute-done.16.halo_direct = f32[128,896]{1,0:T(8,128)S(1)} collective-permute-done((f32[128,896]{1,0:T(8,128)S(1)}, f32[128,896]{1,0:T(8,128)S(1)}, u32[]{:S(2)}, u32[]{:S(2)}) %collective-permute-start.16) | collective-permute-done | bytes 458784 | tf_op jit(solution)/shard_map/ppermute | solution.py:32
  162.5 7.2 %shard_map.63 = (f32[2,512,768]{2,1,0:T(8,128)S(1)}, f32[128,896]{1,0:T(8,128)S(1)}, f32[128,640]{1,0:T(8,128)S(1)}, f32[2,128,768]{2,1,0:T(8,128)S(1)}, f32[2,2...) custom-call(s32[13]{0:T(128)S(1)} %concatenate.4.meta, f32[2,512,768]{2,1,0:T(8,128)S(1)} %shard_map.62.centre, ...), custom_call_target="tpu_custom_call" | custom-call | flops 1073741824 | bytes 17629184 | tf_op jit(solution)/shard_map/pallas_call | solution.py:397
  171.1 4.0 %collective-permute-start.20 = (f32[128,896]{1,0:T(8,128)S(1)}, f32[128,896]{1,0:T(8,128)S(1)}, u32[]{:S(2)}, u32[]{:S(2)}) collective-permute-start(f32[128,896]{1,0:T(8,128)S(1)} %get-tuple-element.63), channel_id=1, source_target_pairs={{1,2},{3,4},{5,6},{9,10},{11,12},{13,14},{2,1},{4,3},{6,5},{10,9},... | collective-permute-start | bytes 1376264 | tf_op jit(solution)/shard_map/ppermute | solution.py:32
  176.5 6.2 %collective-permute-start.24 = (f32[2,256,128]{2,1,0:T(8,128)S(1)}, f32[2,256,128]{2,1,0:T(8,128)S(1)}, u32[]{:S(2)}, u32[]{:S(2)}) collective-permute-start(f32[2,256,128]{2,1,0:T(8,128)S(1)} %get-tuple-element.67), channel_id=1, source_target_pairs={{16,32},{48,64},{80,96},{112,128},{144,160},{176,192},{208,224},{3... | collective-permute-start | bytes 786440 | tf_op jit(solution)/shard_map/ppermute | solution.py:40
  182.7 4.3 %collective-permute-done.20.direct = f32[128,896]{1,0:T(8,128)S(1)} collective-permute-done((f32[128,896]{1,0:T(8,128)S(1)}, f32[128,896]{1,0:T(8,128)S(1)}, u32[]{:S(2)}, u32[]{:S(2)}) %collective-permute-start.20) | collective-permute-done | bytes 458784 | tf_op jit(solution)/shard_map/ppermute | solution.py:32
  187.0 7.2 %collective-permute-done.22.relayed = f32[128,640]{1,0:T(8,128)S(1)} collective-permute-done((f32[128,640]{1,0:T(8,128)S(1)}, f32[128,640]{1,0:T(8,128)S(1)}, u32[]{:S(2)}, u32[]{:S(2)}) %collective-permute-start.22) | collective-permute-done | bytes 327712 | tf_op jit(solution)/shard_map/ppermute | solution.py:34
  194.9 5.6 %collective-permute-start.26 = (f32[2,256,128]{2,1,0:T(8,128)S(1)}, f32[2,256,128]{2,1,0:T(8,128)S(1)}, u32[]{:S(2)}, u32[]{:S(2)}) collective-permute-start(f32[2,256,128]{2,1,0:T(8,128)S(1)} %get-tuple-element.69), channel_id=1, source_target_pairs={{16,32},{48,64},{80,96},{112,128},{144,160},{176,192},{208,224},{3... | collective-permute-start | bytes 786440 | tf_op jit(solution)/shard_map/ppermute | solution.py:40
  200.5 11.0 %collective-permute-start.27 = (f32[2,256,128]{2,1,0:T(8,128)S(1)}, f32[2,256,128]{2,1,0:T(8,128)S(1)}, u32[]{:S(2)}, u32[]{:S(2)}) collective-permute-start(f32[2,256,128]{2,1,0:T(8,128)S(1)} %get-tuple-element.70), channel_id=1, source_target_pairs={{0,16},{32,48},{64,80},{96,112},{128,144},{160,176},{192,208},{224... | collective-permute-start | bytes 786440 | tf_op jit(solution)/shard_map/ppermute | solution.py:41
  211.5 3.8 %collective-permute-done.27.rim_even = f32[2,256,128]{2,1,0:T(8,128)S(1)} collective-permute-done((f32[2,256,128]{2,1,0:T(8,128)S(1)}, f32[2,256,128]{2,1,0:T(8,128)S(1)}, u32[]{:S(2)}, u32[]{:S(2)}) %collective-permute-start.27) | collective-permute-done | bytes 262176 | tf_op jit(solution)/shard_map/ppermute | solution.py:41
  215.2 2.6 %shard_map.65 = f32[2,512,512]{2,1,0:T(8,128)} custom-call(s32[13]{0:T(128)S(1)} %concatenate.4.meta, f32[2,512,768]{2,1,0:T(8,128)S(1)} %shard_map.62.centre, f32[2,512,768]{2,1,0:T(8,128)S(1)} %get-tuple-element.62.grad, f32[2,128,768]{2,1,0:T(8,128)S(1)} %get-tuple-element.66.line, f32[2,128,768]{2,1,0:T(8,128)S(1)} %collective-permute-done.23.even, ...), custom_call_target="tpu_custom_call" | custom-call | bytes 11010048 | tf_op jit(solution)/shard_map/pallas_call | solution.py:397
  (47 shorter events, 19.4 us)
Async XLA Ops:
  0.1 1.6 copy-start
  1.7 24.3 %copy-start.1 = (f32[2,512,512]{2,1,0:T(8,128)S(1)}, f32[2,512,512]{2,1,0:T(8,128)}, u32[]{:S(2)}) copy-start(f32[2,512,512]{2,1,0:T(8,128)} %own.5) | copy-start | bytes 6291460
  3.1 22.8 %collective-permute-start = (f32[2,256,128]{2,1,0:T(8,128)}, f32[2,256,128]{2,1,0:T(8,128)S(1)}, u32[]{:S(2)}, u32[]{:S(2)}) collective-permute-start(f32[2,256,128]{2,1,0:T(8,128)} %get-tuple-element.38), channel_id=1, source_target_pairs={{16,32},{48,64},{80,96},{112,128},{144,160},{176,192},{208,224},{3... | collective-permute-start | bytes 786440 | tf_op jit(solution)/shard_map/ppermute | solution.py:40
  9.3 16.6 %collective-permute-start.1 = (f32[2,256,128]{2,1,0:T(8,128)S(1)}, f32[2,256,128]{2,1,0:T(8,128)S(1)}, u32[]{:S(2)}, u32[]{:S(2)}) collective-permute-start(f32[2,256,128]{2,1,0:T(8,128)S(1)} %get-tuple-element.39), channel_id=1, source_target_pairs={{0,16},{32,48},{64,80},{96,112},{128,144},{160,176},{192,208},{224... | collective-permute-start | bytes 786440 | tf_op jit(solution)/shard_map/ppermute | solution.py:41
  11.0 1.2 copy-start.2
  12.2 1.0 copy-start.3
  26.7 36.3 %collective-permute-start.7 = (f32[2,128,768]{2,1,0:T(8,128)S(1)}, f32[2,128,768]{2,1,0:T(8,128)S(1)}, u32[]{:S(2)}, u32[]{:S(2)}) collective-permute-start(f32[2,128,768]{2,1,0:T(8,128)S(1)} %get-tuple-element.46), channel_id=1, source_target_pairs={{0,1},{2,3},{4,5},{6,7},{8,9},{10,11},{12,13},{14,15},{1,0},{3,2},... | collective-permute-start | bytes 2359304 | tf_op jit(solution)/shard_map/ppermute | solution.py:33
  27.7 10.9 %collective-permute-start.5 = (f32[128,640]{1,0:T(8,128)S(1)}, f32[128,640]{1,0:T(8,128)S(1)}, u32[]{:S(2)}, u32[]{:S(2)}) collective-permute-start(f32[128,640]{1,0:T(8,128)S(1)} %get-tuple-element.45), channel_id=1, source_target_pairs={{1,2},{3,4},{5,6},{9,10},{11,12},{13,14},{2,1},{4,3},{6,5},{10,9},... | collective-permute-start | bytes 983048 | tf_op jit(solution)/shard_map/ppermute | solution.py:31
  29.8 33.2 %collective-permute-start.4 = (f32[128,896]{1,0:T(8,128)S(1)}, f32[128,896]{1,0:T(8,128)S(1)}, u32[]{:S(2)}, u32[]{:S(2)}) collective-permute-start(f32[128,896]{1,0:T(8,128)S(1)} %get-tuple-element.44), channel_id=1, source_target_pairs={{1,2},{3,4},{5,6},{9,10},{11,12},{13,14},{2,1},{4,3},{6,5},{10,9},... | collective-permute-start | bytes 1376264 | tf_op jit(solution)/shard_map/ppermute | solution.py:32
  38.7 24.3 %collective-permute-start.6 = (f32[128,640]{1,0:T(8,128)S(1)}, f32[128,640]{1,0:T(8,128)S(1)}, u32[]{:S(2)}, u32[]{:S(2)}) collective-permute-start(f32[128,640]{1,0:T(8,128)S(1)} %collective-permute-done.5.halo_detour), channel_id=1, source_target_pairs={{0,8},{15,7},{16,24},{31,23},{32,40},{47,39},{48,56},{63,55},{64,7... | collective-permute-start | bytes 983048 | tf_op jit(solution)/shard_map/ppermute | solution.py:34
  40.0 18.8 %collective-permute-start.2 = (f32[2,256,128]{2,1,0:T(8,128)S(1)}, f32[2,256,128]{2,1,0:T(8,128)S(1)}, u32[]{:S(2)}, u32[]{:S(2)}) collective-permute-start(f32[2,256,128]{2,1,0:T(8,128)S(1)} %get-tuple-element.42), channel_id=1, source_target_pairs={{16,32},{48,64},{80,96},{112,128},{144,160},{176,192},{208,224},{3... | collective-permute-start | bytes 786440 | tf_op jit(solution)/shard_map/ppermute | solution.py:40
  44.3 17.9 %collective-permute-start.3 = (f32[2,256,128]{2,1,0:T(8,128)S(1)}, f32[2,256,128]{2,1,0:T(8,128)S(1)}, u32[]{:S(2)}, u32[]{:S(2)}) collective-permute-start(f32[2,256,128]{2,1,0:T(8,128)S(1)} %get-tuple-element.43), channel_id=1, source_target_pairs={{0,16},{32,48},{64,80},{96,112},{128,144},{160,176},{192,208},{224... | collective-permute-start | bytes 786440 | tf_op jit(solution)/shard_map/ppermute | solution.py:41
  70.2 23.8 %collective-permute-start.11 = (f32[2,128,768]{2,1,0:T(8,128)S(1)}, f32[2,128,768]{2,1,0:T(8,128)S(1)}, u32[]{:S(2)}, u32[]{:S(2)}) collective-permute-start(f32[2,128,768]{2,1,0:T(8,128)S(1)} %get-tuple-element.52), channel_id=1, source_target_pairs={{0,1},{2,3},{4,5},{6,7},{8,9},{10,11},{12,13},{14,15},{1,0},{3,2},... | collective-permute-start | bytes 2359304 | tf_op jit(solution)/shard_map/ppermute | solution.py:33
  70.3 11.0 %collective-permute-start.9 = (f32[128,640]{1,0:T(8,128)S(1)}, f32[128,640]{1,0:T(8,128)S(1)}, u32[]{:S(2)}, u32[]{:S(2)}) collective-permute-start(f32[128,640]{1,0:T(8,128)S(1)} %get-tuple-element.51), channel_id=1, source_target_pairs={{1,2},{3,4},{5,6},{9,10},{11,12},{13,14},{2,1},{4,3},{6,5},{10,9},... | collective-permute-start | bytes 983048 | tf_op jit(solution)/shard_map/ppermute | solution.py:31
  71.6 15.9 %collective-permute-start.8 = (f32[128,896]{1,0:T(8,128)S(1)}, f32[128,896]{1,0:T(8,128)S(1)}, u32[]{:S(2)}, u32[]{:S(2)}) collective-permute-start(f32[128,896]{1,0:T(8,128)S(1)} %get-tuple-element.50), channel_id=1, source_target_pairs={{1,2},{3,4},{5,6},{9,10},{11,12},{13,14},{2,1},{4,3},{6,5},{10,9},... | collective-permute-start | bytes 1376264 | tf_op jit(solution)/shard_map/ppermute | solution.py:32
  81.3 12.6 %collective-permute-start.10 = (f32[128,640]{1,0:T(8,128)S(1)}, f32[128,640]{1,0:T(8,128)S(1)}, u32[]{:S(2)}, u32[]{:S(2)}) collective-permute-start(f32[128,640]{1,0:T(8,128)S(1)} %collective-permute-done.9.detour), channel_id=1, source_target_pairs={{0,8},{15,7},{16,24},{31,23},{32,40},{47,39},{48,56},{63,55},{64,7... | collective-permute-start | bytes 983048 | tf_op jit(solution)/shard_map/ppermute | solution.py:34
  94.8 17.3 %collective-permute-start.12 = (f32[2,256,256]{2,1,0:T(8,128)S(1)}, f32[2,256,256]{2,1,0:T(8,128)S(1)}, u32[]{:S(2)}, u32[]{:S(2)}) collective-permute-start(f32[2,256,256]{2,1,0:T(8,128)S(1)} %get-tuple-element.54), channel_id=1, source_target_pairs={{16,32},{48,64},{80,96},{112,128},{144,160},{176,192},{208,224},{3... | collective-permute-start | bytes 1572872 | tf_op jit(solution)/shard_map/ppermute | solution.py:40
  98.8 19.8 %collective-permute-start.13 = (f32[2,256,256]{2,1,0:T(8,128)S(1)}, f32[2,256,256]{2,1,0:T(8,128)S(1)}, u32[]{:S(2)}, u32[]{:S(2)}) collective-permute-start(f32[2,256,256]{2,1,0:T(8,128)S(1)} %get-tuple-element.55), channel_id=1, source_target_pairs={{0,16},{32,48},{64,80},{96,112},{128,144},{160,176},{192,208},{224... | collective-permute-start | bytes 1572872 | tf_op jit(solution)/shard_map/ppermute | solution.py:41
  119.9 42.6 %collective-permute-start.19 = (f32[2,128,768]{2,1,0:T(8,128)S(1)}, f32[2,128,768]{2,1,0:T(8,128)S(1)}, u32[]{:S(2)}, u32[]{:S(2)}) collective-permute-start(f32[2,128,768]{2,1,0:T(8,128)S(1)} %get-tuple-element.61), channel_id=1, source_target_pairs={{0,1},{2,3},{4,5},{6,7},{8,9},{10,11},{12,13},{14,15},{1,0},{3,2},... | collective-permute-start | bytes 2359304 | tf_op jit(solution)/shard_map/ppermute | solution.py:33
  120.0 13.5 %collective-permute-start.17 = (f32[128,640]{1,0:T(8,128)S(1)}, f32[128,640]{1,0:T(8,128)S(1)}, u32[]{:S(2)}, u32[]{:S(2)}) collective-permute-start(f32[128,640]{1,0:T(8,128)S(1)} %get-tuple-element.60), channel_id=1, source_target_pairs={{1,2},{3,4},{5,6},{9,10},{11,12},{13,14},{2,1},{4,3},{6,5},{10,9},... | collective-permute-start | bytes 983048 | tf_op jit(solution)/shard_map/ppermute | solution.py:31
  122.9 18.5 %collective-permute-start.14 = (f32[2,256,256]{2,1,0:T(8,128)S(1)}, f32[2,256,256]{2,1,0:T(8,128)S(1)}, u32[]{:S(2)}, u32[]{:S(2)}) collective-permute-start(f32[2,256,256]{2,1,0:T(8,128)S(1)} %get-tuple-element.57), channel_id=1, source_target_pairs={{16,32},{48,64},{80,96},{112,128},{144,160},{176,192},{208,224},{3... | collective-permute-start | bytes 1572872 | tf_op jit(solution)/shard_map/ppermute | solution.py:40
  124.8 25.1 %collective-permute-start.15 = (f32[2,256,256]{2,1,0:T(8,128)S(1)}, f32[2,256,256]{2,1,0:T(8,128)S(1)}, u32[]{:S(2)}, u32[]{:S(2)}) collective-permute-start(f32[2,256,256]{2,1,0:T(8,128)S(1)} %get-tuple-element.58), channel_id=1, source_target_pairs={{0,16},{32,48},{64,80},{96,112},{128,144},{160,176},{192,208},{224... | collective-permute-start | bytes 1572872 | tf_op jit(solution)/shard_map/ppermute | solution.py:41
  126.4 36.0 %collective-permute-start.16 = (f32[128,896]{1,0:T(8,128)S(1)}, f32[128,896]{1,0:T(8,128)S(1)}, u32[]{:S(2)}, u32[]{:S(2)}) collective-permute-start(f32[128,896]{1,0:T(8,128)S(1)} %get-tuple-element.59), channel_id=1, source_target_pairs={{1,2},{3,4},{5,6},{9,10},{11,12},{13,14},{2,1},{4,3},{6,5},{10,9},... | collective-permute-start | bytes 1376264 | tf_op jit(solution)/shard_map/ppermute | solution.py:32
  133.5 29.0 %collective-permute-start.18 = (f32[128,640]{1,0:T(8,128)S(1)}, f32[128,640]{1,0:T(8,128)S(1)}, u32[]{:S(2)}, u32[]{:S(2)}) collective-permute-start(f32[128,640]{1,0:T(8,128)S(1)} %collective-permute-done.17.halo_detour), channel_id=1, source_target_pairs={{0,8},{15,7},{16,24},{31,23},{32,40},{47,39},{48,56},{63,55},{64,7... | collective-permute-start | bytes 983048 | tf_op jit(solution)/shard_map/ppermute | solution.py:34
  169.7 24.5 %collective-permute-start.23 = (f32[2,128,768]{2,1,0:T(8,128)S(1)}, f32[2,128,768]{2,1,0:T(8,128)S(1)}, u32[]{:S(2)}, u32[]{:S(2)}) collective-permute-start(f32[2,128,768]{2,1,0:T(8,128)S(1)} %get-tuple-element.65), channel_id=1, source_target_pairs={{0,1},{2,3},{4,5},{6,7},{8,9},{10,11},{12,13},{14,15},{1,0},{3,2},... | collective-permute-start | bytes 2359304 | tf_op jit(solution)/shard_map/ppermute | solution.py:33
  169.8 5.4 %collective-permute-start.21 = (f32[128,640]{1,0:T(8,128)S(1)}, f32[128,640]{1,0:T(8,128)S(1)}, u32[]{:S(2)}, u32[]{:S(2)}) collective-permute-start(f32[128,640]{1,0:T(8,128)S(1)} %get-tuple-element.64), channel_id=1, source_target_pairs={{1,2},{3,4},{5,6},{9,10},{11,12},{13,14},{2,1},{4,3},{6,5},{10,9},... | collective-permute-start | bytes 983048 | tf_op jit(solution)/shard_map/ppermute | solution.py:31
  171.1 15.9 %collective-permute-start.20 = (f32[128,896]{1,0:T(8,128)S(1)}, f32[128,896]{1,0:T(8,128)S(1)}, u32[]{:S(2)}, u32[]{:S(2)}) collective-permute-start(f32[128,896]{1,0:T(8,128)S(1)} %get-tuple-element.63), channel_id=1, source_target_pairs={{1,2},{3,4},{5,6},{9,10},{11,12},{13,14},{2,1},{4,3},{6,5},{10,9},... | collective-permute-start | bytes 1376264 | tf_op jit(solution)/shard_map/ppermute | solution.py:32
  175.2 19.0 %collective-permute-start.22 = (f32[128,640]{1,0:T(8,128)S(1)}, f32[128,640]{1,0:T(8,128)S(1)}, u32[]{:S(2)}, u32[]{:S(2)}) collective-permute-start(f32[128,640]{1,0:T(8,128)S(1)} %collective-permute-done.21.detour), channel_id=1, source_target_pairs={{0,8},{15,7},{16,24},{31,23},{32,40},{47,39},{48,56},{63,55},{64,7... | collective-permute-start | bytes 983048 | tf_op jit(solution)/shard_map/ppermute | solution.py:34
  176.5 35.0 %collective-permute-start.24 = (f32[2,256,128]{2,1,0:T(8,128)S(1)}, f32[2,256,128]{2,1,0:T(8,128)S(1)}, u32[]{:S(2)}, u32[]{:S(2)}) collective-permute-start(f32[2,256,128]{2,1,0:T(8,128)S(1)} %get-tuple-element.67), channel_id=1, source_target_pairs={{16,32},{48,64},{80,96},{112,128},{144,160},{176,192},{208,224},{3... | collective-permute-start | bytes 786440 | tf_op jit(solution)/shard_map/ppermute | solution.py:40
  182.6 28.9 %collective-permute-start.25 = (f32[2,256,128]{2,1,0:T(8,128)S(1)}, f32[2,256,128]{2,1,0:T(8,128)S(1)}, u32[]{:S(2)}, u32[]{:S(2)}) collective-permute-start(f32[2,256,128]{2,1,0:T(8,128)S(1)} %get-tuple-element.68), channel_id=1, source_target_pairs={{0,16},{32,48},{64,80},{96,112},{128,144},{160,176},{192,208},{224... | collective-permute-start | bytes 786440 | tf_op jit(solution)/shard_map/ppermute | solution.py:41
  194.9 16.6 %collective-permute-start.26 = (f32[2,256,128]{2,1,0:T(8,128)S(1)}, f32[2,256,128]{2,1,0:T(8,128)S(1)}, u32[]{:S(2)}, u32[]{:S(2)}) collective-permute-start(f32[2,256,128]{2,1,0:T(8,128)S(1)} %get-tuple-element.69), channel_id=1, source_target_pairs={{16,32},{48,64},{80,96},{112,128},{144,160},{176,192},{208,224},{3... | collective-permute-start | bytes 786440 | tf_op jit(solution)/shard_map/ppermute | solution.py:40
  200.5 14.8 %collective-permute-start.27 = (f32[2,256,128]{2,1,0:T(8,128)S(1)}, f32[2,256,128]{2,1,0:T(8,128)S(1)}, u32[]{:S(2)}, u32[]{:S(2)}) collective-permute-start(f32[2,256,128]{2,1,0:T(8,128)S(1)} %get-tuple-element.70), channel_id=1, source_target_pairs={{0,16},{32,48},{64,80},{96,112},{128,144},{160,176},{192,208},{224... | collective-permute-start | bytes 786440 | tf_op jit(solution)/shard_map/ppermute | solution.py:41
where the time goes:
time: 218 us
  starting transfers between devices  99.1 us (45%)
  waiting for transfers between devices  76.2 us (35%)
  Pallas kernels  36.7 us (17%)
  local copies, waits for them, and re-layouts  4.8 us (2%)
    pallas_call x11, Pallas kernels, call(): pl.pallas_call(kernel, out_shape=shapes, in_specs=[smem] + [pl.BlockSpec(...  36.7 us
    ppermute x4, starting transfers between devices, swap_rows(): straight = lax.ppermute(direct, 'gy', near + far)  29.7 us
    ppermute x6, starting transfers between devices, swap_columns(): from_odd = lax.ppermute(odd_cells, 'gx', pairs(count, 1))  28.1 us
    ppermute x6, starting transfers between devices, swap_columns(): from_even = lax.ppermute(even_cells, 'gx', pairs(count, 0))  27.3 us
    ppermute x6, waiting for transfers between devices, swap_columns(): from_even = lax.ppermute(even_cells, 'gx', pairs(count, 0))  22.3 us
    ppermute x4, waiting for transfers between devices, swap_rows(): straight = lax.ppermute(direct, 'gy', near + far)  20.5 us
    ppermute x6, waiting for transfers between devices, swap_columns(): from_odd = lax.ppermute(odd_cells, 'gx', pairs(count, 1))  19.9 us
    ppermute x4, waiting for transfers between devices, swap_rows(): second = lax.ppermute(first, 'gy', [(0, low + 1), (count - 1, low)])  13.6 us
  transfers between devices with their start and end apart: 28, of which 11 were waited for; matrix products, arithmetic and copies ran while one was open for 0% of the time, Pallas kernels for 7%

commit v1 on v0

--- a/solution.py
+++ b/solution.py
@@ -64,22 +64,31 @@
     return jnp.dot(a, b, preferred_element_type=jnp.float32)
 
 
+def waves(turn, side):
+    quarter = side // 4
+    moved = turn + quarter // 2
+    rest = (moved & (quarter - 1)) - quarter // 2
+    which = (moved >> (quarter.bit_length() - 1)) & 3
+    x = rest.astype(jnp.float32) * (2.0 * math.pi / side)
+    y = x * x
+    c = 1.0 + y * (-1 / 2 + y * (1 / 24 + y * (-1 / 720 + y * (1 / 40320))))
+    s = x * (1.0 + y * (-1 / 6 + y * (1 / 120 + y * (-1 / 5040 + y * (1 / 362880)))))
+    swapped = (which & 1) == 1
+    first, second = jnp.where(swapped, s, c), jnp.where(swapped, c, s)
+    cos = jnp.where((which == 1) | (which == 2), -first, first)
+    sin = jnp.where(which >= 2, -second, second)
+    return cos, sin
+
+
 def table_blocks(shift, half, side):
-    rows = lax.broadcasted_iota(jnp.int32, (half, half), 0)
-    cols = lax.broadcasted_iota(jnp.int32, (half, half), 1)
-    scale = 2.0 * math.pi / side
+    freq = 2 * lax.broadcasted_iota(jnp.int32, (half, half), 0)
+    cell = lax.broadcasted_iota(jnp.int32, (half, half), 1) - shift
     norm = 1.0 / math.sqrt(side)
-
-    def entries(freq, cell):
-        phase = (freq * (cell - shift + side)) & (side - 1)
-        angle = phase.astype(jnp.float32) * scale
-        return jnp.cos(angle) * norm, jnp.sin(angle) * norm
-
     out = []
     for odd in (0, 1):
-        c, s = entries(2 * rows + odd, cols)
-        ct, st = entries(2 * cols + odd, rows)
-        out.append((c, s, ct, st))
+        c, s = waves((freq + odd) * cell, side)
+        c, s = c * norm, s * norm
+        out.append((c, s, c.T, s.T))
     return out
 
 
@@ -274,23 +283,16 @@
     )
 
 
-def sides_kernel(meta, own, rim_odd, rim_even, mid_odd, mid_even, sems):
+def sides_kernel(meta, own, rim_odd, rim_even, mid_odd, mid_even):
     tile, half = own.shape[1], rim_odd.shape[2]
-    copies = []
+    far = tile - half
     for rim, mid, cols in (
         (rim_odd, mid_odd, odd_side(meta, rim_odd, tile)),
         (rim_even, mid_even, even_side(meta, rim_even, tile)),
     ):
-        for src, dst in (
-            (own.at[:, pl.ds(0, half), cols], rim.at[:, pl.ds(0, half), :]),
-            (own.at[:, pl.ds(tile - half, half), cols], rim.at[:, pl.ds(half, half), :]),
-            (own.at[:, pl.ds(half, tile - 2 * half), cols], mid),
-        ):
-            copies.append(pltpu.make_async_copy(src, dst, sems.at[len(copies)]))
-    for copy in copies:
-        copy.start()
-    for copy in copies:
-        copy.wait()
+        rim[:, :half, :] = own[:, :half, cols]
+        rim[:, half:, :] = own[:, far:, cols]
+        mid[...] = own[:, half:far, cols]
 
 
 def edges_kernel(meta, own, side_odd, side_even, _, direct, detour, even, lines):
@@ -382,7 +384,7 @@
         out[:, far:, cols] = out[:, far:, cols] - step_size * rim[:, half:, :]
 
 
-def call(kernel, meta, arrays, outs, scratch=(), flops=0, room=0, after=None, hbm=False):
+def call(kernel, meta, arrays, outs, scratch=(), flops=0, room=0, after=None):
     f32 = jnp.float32
     shapes = [
         jax.ShapeDtypeStruct(*o) if isinstance(o[0], tuple) else jax.ShapeDtypeStruct(o, f32)
@@ -397,7 +399,7 @@
     return pl.pallas_call(
         kernel,
         out_shape=shapes,
-        in_specs=[smem] + [pl.BlockSpec(memory_space=pltpu.HBM) if hbm else vmem] * len(arrays) + [anywhere] * len(late),
+        in_specs=[smem] + [vmem] * len(arrays) + [anywhere] * len(late),
         out_specs=[vmem] * len(shapes),
         scratch_shapes=list(scratch),
         compiler_params=pltpu.CompilerParams(vmem_limit_bytes=room or moved + MIB),
@@ -432,8 +434,6 @@
         places,
         (object_field,),
         (column, column, mid_column, mid_column),
-        scratch=(pltpu.SemaphoreType.DMA((6,)),),
-        hbm=True,
     )
     rims = swap_columns(*rims)
     mids = swap_columns(mid_odd, mid_even)

time: 218 us -> 210 us (0.963)
  Pallas kernels: 36.7 us -> 28.4 us
  waiting for transfers between devices: 76.2 us -> 83.5 us
  starting transfers between devices: 99.1 us -> 91.9 us
    ppermute x6, waiting for transfers between devices: 22.3 us -> 34.8 us  [swap_columns(): from_even = lax.ppermute(even_cells, 'gx', pairs(count, 0))]
    pallas_call x11, Pallas kernels: 36.7 us -> 28.4 us  [call(): pl.pallas_call(kernel, out_shape=shapes, in_specs=[smem] + [vmem] * len(a...]
    ppermute x6, waiting for transfers between devices: 19.9 us -> 14.6 us  [swap_columns(): from_odd = lax.ppermute(odd_cells, 'gx', pairs(count, 1))]
    ppermute x6, starting transfers between devices: 28.1 us -> 24.9 us  [swap_columns(): from_odd = lax.ppermute(odd_cells, 'gx', pairs(count, 1))]
    ppermute x6, starting transfers between devices: 27.3 us -> 24.5 us  [swap_columns(): from_even = lax.ppermute(even_cells, 'gx', pairs(count, 0))]
  transfers between devices with their start and end apart: 28 -> 28, of which waited for: 11 -> 13; matrix products, arithmetic and copies ran while one was open for 0% -> 0% of each run, Pallas kernels for 7% -> 3%
where the time goes in v1:
time: 210 us
  starting transfers between devices  91.9 us (44%)
  waiting for transfers between devices  83.5 us (40%)
  Pallas kernels  28.4 us (14%)
  local copies, waits for them, and re-layouts  4.8 us (2%)
    ppermute x6, waiting for transfers between devices, swap_columns(): from_even = lax.ppermute(even_cells, 'gx', pairs(count, 0))  34.8 us
    ppermute x4, starting transfers between devices, swap_rows(): straight = lax.ppermute(direct, 'gy', near + far)  30.6 us
    pallas_call x11, Pallas kernels, call(): pl.pallas_call(kernel, out_shape=shapes, in_specs=[smem] + [vmem] * len(a...  28.4 us
    ppermute x6, starting transfers between devices, swap_columns(): from_odd = lax.ppermute(odd_cells, 'gx', pairs(count, 1))  24.9 us
    ppermute x6, starting transfers between devices, swap_columns(): from_even = lax.ppermute(even_cells, 'gx', pairs(count, 0))  24.5 us
    ppermute x4, waiting for transfers between devices, swap_rows(): straight = lax.ppermute(direct, 'gy', near + far)  19.7 us
    ppermute x6, waiting for transfers between devices, swap_columns(): from_odd = lax.ppermute(odd_cells, 'gx', pairs(count, 1))  14.6 us
    ppermute x4, waiting for transfers between devices, swap_rows(): second = lax.ppermute(first, 'gy', [(0, low + 1), (count - 1, low)])  14.4 us
  transfers between devices with their start and end apart: 28, of which 13 were waited for; matrix products, arithmetic and copies ran while one was open for 0% of the time, Pallas kernels for 3%

profile of v1, /device:TPU:15, one launch (start us, length us, event | category | flops | bytes accessed | tf_op | source)
XLA Modules:
  0.0 209.7 jit_solution(8128870731798257586)
XLA Ops:
  0.1 1.6 copy-done
  3.1 6.1 %collective-permute-start = (f32[2,256,128]{2,1,0:T(8,128)}, f32[2,256,128]{2,1,0:T(8,128)S(1)}, u32[]{:S(2)}, u32[]{:S(2)}) collective-permute-start(f32[2,256,128]{2,1,0:T(8,128)} %get-tuple-element.38), channel_id=1, source_target_pairs={{16,32},{48,64},{80,96},{112,128},{144,160},{176,192},{208,224},{3... | collective-permute-start | bytes 786440 | tf_op jit(solution)/shard_map/ppermute | solution.py:40
  13.2 4.7 %shard_map.56 = (f32[4,2,256,256]{3,2,1,0:T(8,128)S(1)}, bf16[4,8,256,256]{3,2,1,0:T(8,128)(2,1)S(1)}, f32[4,256,256]{2,1,0:T(8,128)S(1)}) custom-call(s32[13]{0:T(128)S(1)} %concatenate.4.meta, f32[2,256,256]{2,1,0:T(8,128)S(1)} %copy-done.3, f32[4,256,256]{2,1,0:T(8,128)S(1)} %bitcast.7), custom_call_target="tpu_custom_call" | custom-call | flops 1000000000 | bytes 8912896 | tf_op jit(solution)/shard_map/pallas_call | solution.py:399
  17.8 4.2 %collective-permute-done.1.side_even = f32[2,256,128]{2,1,0:T(8,128)S(1)} collective-permute-done((f32[2,256,128]{2,1,0:T(8,128)S(1)}, f32[2,256,128]{2,1,0:T(8,128)S(1)}, u32[]{:S(2)}, u32[]{:S(2)}) %collective-permute-start.1) | collective-permute-done | bytes 262176 | tf_op jit(solution)/shard_map/ppermute | solution.py:41
  23.3 2.0 collective-permute-start.5
  25.4 9.8 %collective-permute-start.4 = (f32[128,896]{1,0:T(8,128)S(1)}, f32[128,896]{1,0:T(8,128)S(1)}, u32[]{:S(2)}, u32[]{:S(2)}) collective-permute-start(f32[128,896]{1,0:T(8,128)S(1)} %get-tuple-element.44), channel_id=1, source_target_pairs={{1,2},{3,4},{5,6},{9,10},{11,12},{13,14},{2,1},{4,3},{6,5},{10,9},... | collective-permute-start | bytes 1376264 | tf_op jit(solution)/shard_map/ppermute | solution.py:32
  36.5 2.5 %collective-permute-start.2 = (f32[2,256,128]{2,1,0:T(8,128)S(1)}, f32[2,256,128]{2,1,0:T(8,128)S(1)}, u32[]{:S(2)}, u32[]{:S(2)}) collective-permute-start(f32[2,256,128]{2,1,0:T(8,128)S(1)} %get-tuple-element.42), channel_id=1, source_target_pairs={{16,32},{48,64},{80,96},{112,128},{144,160},{176,192},{208,224},{3... | collective-permute-start | bytes 786440 | tf_op jit(solution)/shard_map/ppermute | solution.py:40
  40.5 9.8 %collective-permute-done.2.side_odd = f32[2,256,128]{2,1,0:T(8,128)S(1)} collective-permute-done((f32[2,256,128]{2,1,0:T(8,128)S(1)}, f32[2,256,128]{2,1,0:T(8,128)S(1)}, u32[]{:S(2)}, u32[]{:S(2)}) %collective-permute-start.2) | collective-permute-done | bytes 262176 | tf_op jit(solution)/shard_map/ppermute | solution.py:40
  50.3 7.1 %collective-permute-done.3.side_even = f32[2,256,128]{2,1,0:T(8,128)S(1)} collective-permute-done((f32[2,256,128]{2,1,0:T(8,128)S(1)}, f32[2,256,128]{2,1,0:T(8,128)S(1)}, u32[]{:S(2)}, u32[]{:S(2)}) %collective-permute-start.3) | collective-permute-done | bytes 262176 | tf_op jit(solution)/shard_map/ppermute | solution.py:41
  58.2 7.2 %shard_map.59 = (f32[2,512,768]{2,1,0:T(8,128)S(1)}, f32[128,896]{1,0:T(8,128)S(1)}, f32[128,640]{1,0:T(8,128)S(1)}, f32[2,128,768]{2,1,0:T(8,128)S(1)}, f32[2,2...) custom-call(s32[13]{0:T(128)S(1)} %concatenate.4.meta, f32[2,512,768]{2,1,0:T(8,128)S(1)} %shard_map.58.centre, ...), custom_call_target="tpu_custom_call" | custom-call | flops 1073741824 | bytes 18153472 | tf_op jit(solution)/shard_map/pallas_call | solution.py:399
  66.8 9.6 %collective-permute-start.8 = (f32[128,896]{1,0:T(8,128)S(1)}, f32[128,896]{1,0:T(8,128)S(1)}, u32[]{:S(2)}, u32[]{:S(2)}) collective-permute-start(f32[128,896]{1,0:T(8,128)S(1)} %get-tuple-element.50), channel_id=1, source_target_pairs={{1,2},{3,4},{5,6},{9,10},{11,12},{13,14},{2,1},{4,3},{6,5},{10,9},... | collective-permute-start | bytes 1376264 | tf_op jit(solution)/shard_map/ppermute | solution.py:32
  77.7 5.0 %collective-permute-done.8.direct = f32[128,896]{1,0:T(8,128)S(1)} collective-permute-done((f32[128,896]{1,0:T(8,128)S(1)}, f32[128,896]{1,0:T(8,128)S(1)}, u32[]{:S(2)}, u32[]{:S(2)}) %collective-permute-start.8) | collective-permute-done | bytes 458784 | tf_op jit(solution)/shard_map/ppermute | solution.py:32
  82.7 7.0 %collective-permute-done.10.relayed = f32[128,640]{1,0:T(8,128)S(1)} collective-permute-done((f32[128,640]{1,0:T(8,128)S(1)}, f32[128,640]{1,0:T(8,128)S(1)}, u32[]{:S(2)}, u32[]{:S(2)}) %collective-permute-start.10) | collective-permute-done | bytes 327712 | tf_op jit(solution)/shard_map/ppermute | solution.py:34
  90.6 1.9 collective-permute-start.12
  92.5 15.9 %collective-permute-start.13 = (f32[2,256,256]{2,1,0:T(8,128)S(1)}, f32[2,256,256]{2,1,0:T(8,128)S(1)}, u32[]{:S(2)}, u32[]{:S(2)}) collective-permute-start(f32[2,256,256]{2,1,0:T(8,128)S(1)} %get-tuple-element.55), channel_id=1, source_target_pairs={{0,16},{32,48},{64,80},{96,112},{128,144},{160,176},{192,208},{224... | collective-permute-start | bytes 1572872 | tf_op jit(solution)/shard_map/ppermute | solution.py:41
  108.4 6.6 %collective-permute-done.13.band_even = f32[2,256,256]{2,1,0:T(8,128)S(1)} collective-permute-done((f32[2,256,256]{2,1,0:T(8,128)S(1)}, f32[2,256,256]{2,1,0:T(8,128)S(1)}, u32[]{:S(2)}, u32[]{:S(2)}) %collective-permute-start.13) | collective-permute-done | bytes 524320 | tf_op jit(solution)/shard_map/ppermute | solution.py:41
  117.6 1.9 collective-permute-start.14
  119.6 2.5 %collective-permute-start.15 = (f32[2,256,256]{2,1,0:T(8,128)S(1)}, f32[2,256,256]{2,1,0:T(8,128)S(1)}, u32[]{:S(2)}, u32[]{:S(2)}) collective-permute-start(f32[2,256,256]{2,1,0:T(8,128)S(1)} %get-tuple-element.58), channel_id=1, source_target_pairs={{0,16},{32,48},{64,80},{96,112},{128,144},{160,176},{192,208},{224... | collective-permute-start | bytes 1572872 | tf_op jit(solution)/shard_map/ppermute | solution.py:41
  122.1 6.6 %collective-permute-start.16 = (f32[128,896]{1,0:T(8,128)S(1)}, f32[128,896]{1,0:T(8,128)S(1)}, u32[]{:S(2)}, u32[]{:S(2)}) collective-permute-start(f32[128,896]{1,0:T(8,128)S(1)} %get-tuple-element.59), channel_id=1, source_target_pairs={{1,2},{3,4},{5,6},{9,10},{11,12},{13,14},{2,1},{4,3},{6,5},{10,9},... | collective-permute-start | bytes 1376264 | tf_op jit(solution)/shard_map/ppermute | solution.py:32
  129.9 4.8 %collective-permute-done.14.band_odd = f32[2,256,256]{2,1,0:T(8,128)S(1)} collective-permute-done((f32[2,256,256]{2,1,0:T(8,128)S(1)}, f32[2,256,256]{2,1,0:T(8,128)S(1)}, u32[]{:S(2)}, u32[]{:S(2)}) %collective-permute-start.14) | collective-permute-done | bytes 524320 | tf_op jit(solution)/shard_map/ppermute | solution.py:40
  134.7 10.4 %collective-permute-done.15.band_even = f32[2,256,256]{2,1,0:T(8,128)S(1)} collective-permute-done((f32[2,256,256]{2,1,0:T(8,128)S(1)}, f32[2,256,256]{2,1,0:T(8,128)S(1)}, u32[]{:S(2)}, u32[]{:S(2)}) %collective-permute-start.15) | collective-permute-done | bytes 524320 | tf_op jit(solution)/shard_map/ppermute | solution.py:41
  146.2 10.7 %collective-permute-done.16.halo_direct = f32[128,896]{1,0:T(8,128)S(1)} collective-permute-done((f32[128,896]{1,0:T(8,128)S(1)}, f32[128,896]{1,0:T(8,128)S(1)}, u32[]{:S(2)}, u32[]{:S(2)}) %collective-permute-start.16) | collective-permute-done | bytes 458784 | tf_op jit(solution)/shard_map/ppermute | solution.py:32
  157.0 7.2 %shard_map.63 = (f32[2,512,768]{2,1,0:T(8,128)S(1)}, f32[128,896]{1,0:T(8,128)S(1)}, f32[128,640]{1,0:T(8,128)S(1)}, f32[2,128,768]{2,1,0:T(8,128)S(1)}, f32[2,2...) custom-call(s32[13]{0:T(128)S(1)} %concatenate.4.meta, f32[2,512,768]{2,1,0:T(8,128)S(1)} %shard_map.62.centre, ...), custom_call_target="tpu_custom_call" | custom-call | flops 1073741824 | bytes 17629184 | tf_op jit(solution)/shard_map/pallas_call | solution.py:399
  165.6 4.6 %collective-permute-start.20 = (f32[128,896]{1,0:T(8,128)S(1)}, f32[128,896]{1,0:T(8,128)S(1)}, u32[]{:S(2)}, u32[]{:S(2)}) collective-permute-start(f32[128,896]{1,0:T(8,128)S(1)} %get-tuple-element.63), channel_id=1, source_target_pairs={{1,2},{3,4},{5,6},{9,10},{11,12},{13,14},{2,1},{4,3},{6,5},{10,9},... | collective-permute-start | bytes 1376264 | tf_op jit(solution)/shard_map/ppermute | solution.py:32
  171.5 5.9 %collective-permute-start.24 = (f32[2,256,128]{2,1,0:T(8,128)S(1)}, f32[2,256,128]{2,1,0:T(8,128)S(1)}, u32[]{:S(2)}, u32[]{:S(2)}) collective-permute-start(f32[2,256,128]{2,1,0:T(8,128)S(1)} %get-tuple-element.67), channel_id=1, source_target_pairs={{16,32},{48,64},{80,96},{112,128},{144,160},{176,192},{208,224},{3... | collective-permute-start | bytes 786440 | tf_op jit(solution)/shard_map/ppermute | solution.py:40
  177.5 4.0 %collective-permute-done.20.direct = f32[128,896]{1,0:T(8,128)S(1)} collective-permute-done((f32[128,896]{1,0:T(8,128)S(1)}, f32[128,896]{1,0:T(8,128)S(1)}, u32[]{:S(2)}, u32[]{:S(2)}) %collective-permute-start.20) | collective-permute-done | bytes 458784 | tf_op jit(solution)/shard_map/ppermute | solution.py:32
  181.5 7.4 %collective-permute-done.22.relayed = f32[128,640]{1,0:T(8,128)S(1)} collective-permute-done((f32[128,640]{1,0:T(8,128)S(1)}, f32[128,640]{1,0:T(8,128)S(1)}, u32[]{:S(2)}, u32[]{:S(2)}) %collective-permute-start.22) | collective-permute-done | bytes 327712 | tf_op jit(solution)/shard_map/ppermute | solution.py:34
  189.6 6.5 %collective-permute-start.26 = (f32[2,256,128]{2,1,0:T(8,128)S(1)}, f32[2,256,128]{2,1,0:T(8,128)S(1)}, u32[]{:S(2)}, u32[]{:S(2)}) collective-permute-start(f32[2,256,128]{2,1,0:T(8,128)S(1)} %get-tuple-element.69), channel_id=1, source_target_pairs={{16,32},{48,64},{80,96},{112,128},{144,160},{176,192},{208,224},{3... | collective-permute-start | bytes 786440 | tf_op jit(solution)/shard_map/ppermute | solution.py:40
  196.1 4.5 %collective-permute-start.27 = (f32[2,256,128]{2,1,0:T(8,128)S(1)}, f32[2,256,128]{2,1,0:T(8,128)S(1)}, u32[]{:S(2)}, u32[]{:S(2)}) collective-permute-start(f32[2,256,128]{2,1,0:T(8,128)S(1)} %get-tuple-element.70), channel_id=1, source_target_pairs={{0,16},{32,48},{64,80},{96,112},{128,144},{160,176},{192,208},{224... | collective-permute-start | bytes 786440 | tf_op jit(solution)/shard_map/ppermute | solution.py:41
  200.6 3.7 %collective-permute-done.25.mid_even = f32[2,256,128]{2,1,0:T(8,128)S(1)} collective-permute-done((f32[2,256,128]{2,1,0:T(8,128)S(1)}, f32[2,256,128]{2,1,0:T(8,128)S(1)}, u32[]{:S(2)}, u32[]{:S(2)}) %collective-permute-start.25) | collective-permute-done | bytes 262176 | tf_op jit(solution)/shard_map/ppermute | solution.py:41
  204.3 2.8 %collective-permute-done.27.rim_even = f32[2,256,128]{2,1,0:T(8,128)S(1)} collective-permute-done((f32[2,256,128]{2,1,0:T(8,128)S(1)}, f32[2,256,128]{2,1,0:T(8,128)S(1)}, u32[]{:S(2)}, u32[]{:S(2)}) %collective-permute-start.27) | collective-permute-done | bytes 262176 | tf_op jit(solution)/shard_map/ppermute | solution.py:41
  207.1 2.6 %shard_map.65 = f32[2,512,512]{2,1,0:T(8,128)} custom-call(s32[13]{0:T(128)S(1)} %concatenate.4.meta, f32[2,512,768]{2,1,0:T(8,128)S(1)} %shard_map.62.centre, f32[2,512,768]{2,1,0:T(8,128)S(1)} %get-tuple-element.62.grad, f32[2,128,768]{2,1,0:T(8,128)S(1)} %get-tuple-element.66.line, f32[2,128,768]{2,1,0:T(8,128)S(1)} %collective-permute-done.23.even, ...), custom_call_target="tpu_custom_call" | custom-call | bytes 11010048 | tf_op jit(solution)/shard_map/pallas_call | solution.py:399
  (47 shorter events, 21.7 us)
Async XLA Ops:
  0.1 1.6 copy-start
  1.7 20.3 %copy-start.1 = (f32[2,512,512]{2,1,0:T(8,128)S(1)}, f32[2,512,512]{2,1,0:T(8,128)}, u32[]{:S(2)}) copy-start(f32[2,512,512]{2,1,0:T(8,128)} %own.5) | copy-start | bytes 6291460
  3.1 14.8 %collective-permute-start = (f32[2,256,128]{2,1,0:T(8,128)}, f32[2,256,128]{2,1,0:T(8,128)S(1)}, u32[]{:S(2)}, u32[]{:S(2)}) collective-permute-start(f32[2,256,128]{2,1,0:T(8,128)} %get-tuple-element.38), channel_id=1, source_target_pairs={{16,32},{48,64},{80,96},{112,128},{144,160},{176,192},{208,224},{3... | collective-permute-start | bytes 786440 | tf_op jit(solution)/shard_map/ppermute | solution.py:40
  9.2 12.8 %collective-permute-start.1 = (f32[2,256,128]{2,1,0:T(8,128)S(1)}, f32[2,256,128]{2,1,0:T(8,128)S(1)}, u32[]{:S(2)}, u32[]{:S(2)}) collective-permute-start(f32[2,256,128]{2,1,0:T(8,128)S(1)} %get-tuple-element.39), channel_id=1, source_target_pairs={{0,16},{32,48},{64,80},{96,112},{128,144},{160,176},{192,208},{224... | collective-permute-start | bytes 786440 | tf_op jit(solution)/shard_map/ppermute | solution.py:41
  10.9 1.2 copy-start.2
  12.1 1.0 copy-start.3
  22.7 35.4 %collective-permute-start.7 = (f32[2,128,768]{2,1,0:T(8,128)S(1)}, f32[2,128,768]{2,1,0:T(8,128)S(1)}, u32[]{:S(2)}, u32[]{:S(2)}) collective-permute-start(f32[2,128,768]{2,1,0:T(8,128)S(1)} %get-tuple-element.46), channel_id=1, source_target_pairs={{0,1},{2,3},{4,5},{6,7},{8,9},{10,11},{12,13},{14,15},{1,0},{3,2},... | collective-permute-start | bytes 2359304 | tf_op jit(solution)/shard_map/ppermute | solution.py:33
  23.3 11.9 %collective-permute-start.5 = (f32[128,640]{1,0:T(8,128)S(1)}, f32[128,640]{1,0:T(8,128)S(1)}, u32[]{:S(2)}, u32[]{:S(2)}) collective-permute-start(f32[128,640]{1,0:T(8,128)S(1)} %get-tuple-element.45), channel_id=1, source_target_pairs={{1,2},{3,4},{5,6},{9,10},{11,12},{13,14},{2,1},{4,3},{6,5},{10,9},... | collective-permute-start | bytes 983048 | tf_op jit(solution)/shard_map/ppermute | solution.py:31
  25.4 32.8 %collective-permute-start.4 = (f32[128,896]{1,0:T(8,128)S(1)}, f32[128,896]{1,0:T(8,128)S(1)}, u32[]{:S(2)}, u32[]{:S(2)}) collective-permute-start(f32[128,896]{1,0:T(8,128)S(1)} %get-tuple-element.44), channel_id=1, source_target_pairs={{1,2},{3,4},{5,6},{9,10},{11,12},{13,14},{2,1},{4,3},{6,5},{10,9},... | collective-permute-start | bytes 1376264 | tf_op jit(solution)/shard_map/ppermute | solution.py:32
  35.2 22.9 %collective-permute-start.6 = (f32[128,640]{1,0:T(8,128)S(1)}, f32[128,640]{1,0:T(8,128)S(1)}, u32[]{:S(2)}, u32[]{:S(2)}) collective-permute-start(f32[128,640]{1,0:T(8,128)S(1)} %collective-permute-done.5.halo_detour), channel_id=1, source_target_pairs={{0,8},{15,7},{16,24},{31,23},{32,40},{47,39},{48,56},{63,55},{64,7... | collective-permute-start | bytes 983048 | tf_op jit(solution)/shard_map/ppermute | solution.py:34
  36.5 13.8 %collective-permute-start.2 = (f32[2,256,128]{2,1,0:T(8,128)S(1)}, f32[2,256,128]{2,1,0:T(8,128)S(1)}, u32[]{:S(2)}, u32[]{:S(2)}) collective-permute-start(f32[2,256,128]{2,1,0:T(8,128)S(1)} %get-tuple-element.42), channel_id=1, source_target_pairs={{16,32},{48,64},{80,96},{112,128},{144,160},{176,192},{208,224},{3... | collective-permute-start | bytes 786440 | tf_op jit(solution)/shard_map/ppermute | solution.py:40
  39.0 18.4 %collective-permute-start.3 = (f32[2,256,128]{2,1,0:T(8,128)S(1)}, f32[2,256,128]{2,1,0:T(8,128)S(1)}, u32[]{:S(2)}, u32[]{:S(2)}) collective-permute-start(f32[2,256,128]{2,1,0:T(8,128)S(1)} %get-tuple-element.43), channel_id=1, source_target_pairs={{0,16},{32,48},{64,80},{96,112},{128,144},{160,176},{192,208},{224... | collective-permute-start | bytes 786440 | tf_op jit(solution)/shard_map/ppermute | solution.py:41
  65.4 24.4 %collective-permute-start.11 = (f32[2,128,768]{2,1,0:T(8,128)S(1)}, f32[2,128,768]{2,1,0:T(8,128)S(1)}, u32[]{:S(2)}, u32[]{:S(2)}) collective-permute-start(f32[2,128,768]{2,1,0:T(8,128)S(1)} %get-tuple-element.52), channel_id=1, source_target_pairs={{0,1},{2,3},{4,5},{6,7},{8,9},{10,11},{12,13},{14,15},{1,0},{3,2},... | collective-permute-start | bytes 2359304 | tf_op jit(solution)/shard_map/ppermute | solution.py:33
  65.5 10.9 %collective-permute-start.9 = (f32[128,640]{1,0:T(8,128)S(1)}, f32[128,640]{1,0:T(8,128)S(1)}, u32[]{:S(2)}, u32[]{:S(2)}) collective-permute-start(f32[128,640]{1,0:T(8,128)S(1)} %get-tuple-element.51), channel_id=1, source_target_pairs={{1,2},{3,4},{5,6},{9,10},{11,12},{13,14},{2,1},{4,3},{6,5},{10,9},... | collective-permute-start | bytes 983048 | tf_op jit(solution)/shard_map/ppermute | solution.py:31
  66.8 15.9 %collective-permute-start.8 = (f32[128,896]{1,0:T(8,128)S(1)}, f32[128,896]{1,0:T(8,128)S(1)}, u32[]{:S(2)}, u32[]{:S(2)}) collective-permute-start(f32[128,896]{1,0:T(8,128)S(1)} %get-tuple-element.50), channel_id=1, source_target_pairs={{1,2},{3,4},{5,6},{9,10},{11,12},{13,14},{2,1},{4,3},{6,5},{10,9},... | collective-permute-start | bytes 1376264 | tf_op jit(solution)/shard_map/ppermute | solution.py:32
  76.4 13.4 %collective-permute-start.10 = (f32[128,640]{1,0:T(8,128)S(1)}, f32[128,640]{1,0:T(8,128)S(1)}, u32[]{:S(2)}, u32[]{:S(2)}) collective-permute-start(f32[128,640]{1,0:T(8,128)S(1)} %collective-permute-done.9.detour), channel_id=1, source_target_pairs={{0,8},{15,7},{16,24},{31,23},{32,40},{47,39},{48,56},{63,55},{64,7... | collective-permute-start | bytes 983048 | tf_op jit(solution)/shard_map/ppermute | solution.py:34
  90.6 17.8 %collective-permute-start.12 = (f32[2,256,256]{2,1,0:T(8,128)S(1)}, f32[2,256,256]{2,1,0:T(8,128)S(1)}, u32[]{:S(2)}, u32[]{:S(2)}) collective-permute-start(f32[2,256,256]{2,1,0:T(8,128)S(1)} %get-tuple-element.54), channel_id=1, source_target_pairs={{16,32},{48,64},{80,96},{112,128},{144,160},{176,192},{208,224},{3... | collective-permute-start | bytes 1572872 | tf_op jit(solution)/shard_map/ppermute | solution.py:40
  92.5 22.5 %collective-permute-start.13 = (f32[2,256,256]{2,1,0:T(8,128)S(1)}, f32[2,256,256]{2,1,0:T(8,128)S(1)}, u32[]{:S(2)}, u32[]{:S(2)}) collective-permute-start(f32[2,256,256]{2,1,0:T(8,128)S(1)} %get-tuple-element.55), channel_id=1, source_target_pairs={{0,16},{32,48},{64,80},{96,112},{128,144},{160,176},{192,208},{224... | collective-permute-start | bytes 1572872 | tf_op jit(solution)/shard_map/ppermute | solution.py:41
  116.2 40.7 %collective-permute-start.19 = (f32[2,128,768]{2,1,0:T(8,128)S(1)}, f32[2,128,768]{2,1,0:T(8,128)S(1)}, u32[]{:S(2)}, u32[]{:S(2)}) collective-permute-start(f32[2,128,768]{2,1,0:T(8,128)S(1)} %get-tuple-element.61), channel_id=1, source_target_pairs={{0,1},{2,3},{4,5},{6,7},{8,9},{10,11},{12,13},{14,15},{1,0},{3,2},... | collective-permute-start | bytes 2359304 | tf_op jit(solution)/shard_map/ppermute | solution.py:33
  116.3 12.3 %collective-permute-start.17 = (f32[128,640]{1,0:T(8,128)S(1)}, f32[128,640]{1,0:T(8,128)S(1)}, u32[]{:S(2)}, u32[]{:S(2)}) collective-permute-start(f32[128,640]{1,0:T(8,128)S(1)} %get-tuple-element.60), channel_id=1, source_target_pairs={{1,2},{3,4},{5,6},{9,10},{11,12},{13,14},{2,1},{4,3},{6,5},{10,9},... | collective-permute-start | bytes 983048 | tf_op jit(solution)/shard_map/ppermute | solution.py:31
  117.6 17.1 %collective-permute-start.14 = (f32[2,256,256]{2,1,0:T(8,128)S(1)}, f32[2,256,256]{2,1,0:T(8,128)S(1)}, u32[]{:S(2)}, u32[]{:S(2)}) collective-permute-start(f32[2,256,256]{2,1,0:T(8,128)S(1)} %get-tuple-element.57), channel_id=1, source_target_pairs={{16,32},{48,64},{80,96},{112,128},{144,160},{176,192},{208,224},{3... | collective-permute-start | bytes 1572872 | tf_op jit(solution)/shard_map/ppermute | solution.py:40
  119.6 25.6 %collective-permute-start.15 = (f32[2,256,256]{2,1,0:T(8,128)S(1)}, f32[2,256,256]{2,1,0:T(8,128)S(1)}, u32[]{:S(2)}, u32[]{:S(2)}) collective-permute-start(f32[2,256,256]{2,1,0:T(8,128)S(1)} %get-tuple-element.58), channel_id=1, source_target_pairs={{0,16},{32,48},{64,80},{96,112},{128,144},{160,176},{192,208},{224... | collective-permute-start | bytes 1572872 | tf_op jit(solution)/shard_map/ppermute | solution.py:41
  122.1 34.9 %collective-permute-start.16 = (f32[128,896]{1,0:T(8,128)S(1)}, f32[128,896]{1,0:T(8,128)S(1)}, u32[]{:S(2)}, u32[]{:S(2)}) collective-permute-start(f32[128,896]{1,0:T(8,128)S(1)} %get-tuple-element.59), channel_id=1, source_target_pairs={{1,2},{3,4},{5,6},{9,10},{11,12},{13,14},{2,1},{4,3},{6,5},{10,9},... | collective-permute-start | bytes 1376264 | tf_op jit(solution)/shard_map/ppermute | solution.py:32
  128.6 28.3 %collective-permute-start.18 = (f32[128,640]{1,0:T(8,128)S(1)}, f32[128,640]{1,0:T(8,128)S(1)}, u32[]{:S(2)}, u32[]{:S(2)}) collective-permute-start(f32[128,640]{1,0:T(8,128)S(1)} %collective-permute-done.17.halo_detour), channel_id=1, source_target_pairs={{0,8},{15,7},{16,24},{31,23},{32,40},{47,39},{48,56},{63,55},{64,7... | collective-permute-start | bytes 983048 | tf_op jit(solution)/shard_map/ppermute | solution.py:34
  164.2 24.7 %collective-permute-start.23 = (f32[2,128,768]{2,1,0:T(8,128)S(1)}, f32[2,128,768]{2,1,0:T(8,128)S(1)}, u32[]{:S(2)}, u32[]{:S(2)}) collective-permute-start(f32[2,128,768]{2,1,0:T(8,128)S(1)} %get-tuple-element.65), channel_id=1, source_target_pairs={{0,1},{2,3},{4,5},{6,7},{8,9},{10,11},{12,13},{14,15},{1,0},{3,2},... | collective-permute-start | bytes 2359304 | tf_op jit(solution)/shard_map/ppermute | solution.py:33
  164.3 5.9 %collective-permute-start.21 = (f32[128,640]{1,0:T(8,128)S(1)}, f32[128,640]{1,0:T(8,128)S(1)}, u32[]{:S(2)}, u32[]{:S(2)}) collective-permute-start(f32[128,640]{1,0:T(8,128)S(1)} %get-tuple-element.64), channel_id=1, source_target_pairs={{1,2},{3,4},{5,6},{9,10},{11,12},{13,14},{2,1},{4,3},{6,5},{10,9},... | collective-permute-start | bytes 983048 | tf_op jit(solution)/shard_map/ppermute | solution.py:31
  165.6 15.9 %collective-permute-start.20 = (f32[128,896]{1,0:T(8,128)S(1)}, f32[128,896]{1,0:T(8,128)S(1)}, u32[]{:S(2)}, u32[]{:S(2)}) collective-permute-start(f32[128,896]{1,0:T(8,128)S(1)} %get-tuple-element.63), channel_id=1, source_target_pairs={{1,2},{3,4},{5,6},{9,10},{11,12},{13,14},{2,1},{4,3},{6,5},{10,9},... | collective-permute-start | bytes 1376264 | tf_op jit(solution)/shard_map/ppermute | solution.py:32
  170.2 18.7 %collective-permute-start.22 = (f32[128,640]{1,0:T(8,128)S(1)}, f32[128,640]{1,0:T(8,128)S(1)}, u32[]{:S(2)}, u32[]{:S(2)}) collective-permute-start(f32[128,640]{1,0:T(8,128)S(1)} %collective-permute-done.21.detour), channel_id=1, source_target_pairs={{0,8},{15,7},{16,24},{31,23},{32,40},{47,39},{48,56},{63,55},{64,7... | collective-permute-start | bytes 983048 | tf_op jit(solution)/shard_map/ppermute | solution.py:34
  171.5 29.1 %collective-permute-start.24 = (f32[2,256,128]{2,1,0:T(8,128)S(1)}, f32[2,256,128]{2,1,0:T(8,128)S(1)}, u32[]{:S(2)}, u32[]{:S(2)}) collective-permute-start(f32[2,256,128]{2,1,0:T(8,128)S(1)} %get-tuple-element.67), channel_id=1, source_target_pairs={{16,32},{48,64},{80,96},{112,128},{144,160},{176,192},{208,224},{3... | collective-permute-start | bytes 786440 | tf_op jit(solution)/shard_map/ppermute | solution.py:40
  177.4 26.8 %collective-permute-start.25 = (f32[2,256,128]{2,1,0:T(8,128)S(1)}, f32[2,256,128]{2,1,0:T(8,128)S(1)}, u32[]{:S(2)}, u32[]{:S(2)}) collective-permute-start(f32[2,256,128]{2,1,0:T(8,128)S(1)} %get-tuple-element.68), channel_id=1, source_target_pairs={{0,16},{32,48},{64,80},{96,112},{128,144},{160,176},{192,208},{224... | collective-permute-start | bytes 786440 | tf_op jit(solution)/shard_map/ppermute | solution.py:41
  189.6 14.7 %collective-permute-start.26 = (f32[2,256,128]{2,1,0:T(8,128)S(1)}, f32[2,256,128]{2,1,0:T(8,128)S(1)}, u32[]{:S(2)}, u32[]{:S(2)}) collective-permute-start(f32[2,256,128]{2,1,0:T(8,128)S(1)} %get-tuple-element.69), channel_id=1, source_target_pairs={{16,32},{48,64},{80,96},{112,128},{144,160},{176,192},{208,224},{3... | collective-permute-start | bytes 786440 | tf_op jit(solution)/shard_map/ppermute | solution.py:40
  196.1 11.0 %collective-permute-start.27 = (f32[2,256,128]{2,1,0:T(8,128)S(1)}, f32[2,256,128]{2,1,0:T(8,128)S(1)}, u32[]{:S(2)}, u32[]{:S(2)}) collective-permute-start(f32[2,256,128]{2,1,0:T(8,128)S(1)} %get-tuple-element.70), channel_id=1, source_target_pairs={{0,16},{32,48},{64,80},{96,112},{128,144},{160,176},{192,208},{224... | collective-permute-start | bytes 786440 | tf_op jit(solution)/shard_map/ppermute | solution.py:41

commit v2 on v1

--- a/solution.py
+++ b/solution.py
@@ -46,18 +46,19 @@
 
 
 def pack(real, imag, direct, detour):
-    wide = real.shape[1]
-    direct[:, :wide] = real
-    direct[:, wide:] = imag[:, :CUT]
-    detour[...] = imag[:, CUT:]
+    straight = direct.shape[1]
+    direct[...] = real[:, :straight]
+    detour[:, :CUT] = real[:, straight:]
+    detour[:, CUT:] = imag
 
 
 def unpack(meta, direct, detour, relayed, line):
-    wide = line.shape[2]
+    straight = direct.shape[1]
     own = meta[RELAY] == 0
-    line[0] = direct[:, :wide]
-    line[1, :, :CUT] = direct[:, wide:]
-    line[1, :, CUT:] = jnp.where(own, detour[...], jnp.zeros_like(detour)) + relayed[...]
+    line[0, :, :straight] = direct[...]
+    rest = jnp.where(own, detour[...], jnp.zeros_like(detour)) + relayed[...]
+    line[0, :, straight:] = rest[:, :CUT]
+    line[1] = rest[:, CUT:]
 
 
 def dot(a, b):
@@ -138,7 +139,8 @@
     side,
     windows,
     meta,
-    centre,
+    _field,
+    _total,
     halo_direct,
     halo_detour,
     halo_relayed,
@@ -146,29 +148,25 @@
     probes,
     tables,
     amps,
-    grad,
+    field,
+    total,
     rim_direct,
     rim_detour,
     rim_even,
     band_odd,
     band_even,
-    field,
-    total,
     mixed,
-    line,
 ):
     half = side // 2
-    tile, wide = centre.shape[1:]
+    wide = field.shape[2]
+    tile = wide - side
     bf = jnp.bfloat16
     odd_row = meta[GY_ODD]
     bottom = half + tile
-    at_odd = pl.multiple_of(odd_row * bottom, half)
-    at_even = pl.multiple_of((1 - odd_row) * bottom, half)
-    field[:, pl.ds(half, tile), :] = centre[...]
-    unpack(meta, halo_direct, halo_detour, halo_relayed, line)
-    field[:, pl.ds(at_odd, half), :] = line[...]
-    field[:, pl.ds(at_even, half), :] = halo_even[...]
-    total[...] = jnp.zeros_like(total)
+    odd_rows = pl.ds(pl.multiple_of(odd_row * bottom, half), half)
+    even_rows = pl.ds(pl.multiple_of((1 - odd_row) * bottom, half), half)
+    unpack(meta, halo_direct, halo_detour, halo_relayed, field.at[:, odd_rows, :])
+    field[:, even_rows, :] = halo_even[...]
     chunk = 32
     zero = jnp.float32(0)
 
@@ -256,10 +254,8 @@
                     )
                     total[place] = total[place] + jnp.where(keep & live, terms[part], zero)
 
-    grad[...] = total[:, pl.ds(half, tile), :]
-    odd_rows = pl.ds(at_odd, half)
     pack(total[0, odd_rows, :], total[1, odd_rows, :], rim_direct, rim_detour)
-    rim_even[...] = total[:, pl.ds(at_even, half), :]
+    rim_even[...] = total[:, even_rows, :]
     for band, cols in (
         (band_odd, odd_side(meta, band_odd, wide)),
         (band_even, even_side(meta, band_even, wide)),
@@ -307,24 +303,37 @@
     even[...] = lines[:, even_rows, :]
 
 
-def centre_kernel(meta, own, lines, side_odd, side_even, centre):
+def inner_rows(half, tile):
+    return (
+        (slice(half, 2 * half), slice(0, half)),
+        (slice(tile, half + tile), slice(half, 2 * half)),
+        slice(2 * half, tile),
+    )
+
+
+def centre_kernel(meta, own, lines, side_odd, side_even, field, total):
     tile, half = own.shape[1], side_odd.shape[2]
     wide = lines.shape[2]
-    mid = slice(half, tile - half)
-    centre[:, :half, :] = lines[:, :half, :]
-    centre[:, tile - half :, :] = lines[:, half:, :]
-    centre[:, mid, half : half + tile] = own[:, mid, :]
-    centre[:, mid, odd_side(meta, side_odd, wide)] = side_odd[...]
-    centre[:, mid, even_side(meta, side_even, wide)] = side_even[...]
-
-
-def bands_kernel(meta, grad, direct, detour, relayed, even, band_odd, band_even, line):
-    (tile, wide), half = grad.shape[1:], even.shape[1]
+    first, last, mid = inner_rows(half, tile)
+    for rows, outer in (first, last):
+        field[:, rows, :] = lines[:, outer, :]
+    field[:, mid, half : half + tile] = own[:, half : tile - half, :]
+    field[:, mid, odd_side(meta, side_odd, wide)] = side_odd[...]
+    field[:, mid, even_side(meta, side_even, wide)] = side_even[...]
+    total[...] = jnp.zeros_like(total)
+
+
+def bands_kernel(meta, total, direct, detour, relayed, even, band_odd, band_even, line):
+    wide, half = total.shape[2], even.shape[1]
     unpack(meta, direct, detour, relayed, line)
     odd_rows, even_rows = rim_rows(meta, half)
-    for band, cols in ((band_odd, odd_side(meta, band_odd, wide)), (band_even, even_side(meta, band_even, wide))):
-        band[:, :half, :] = grad[:, :half, cols]
-        band[:, half:, :] = grad[:, tile - half :, cols]
+    first, last, _ = inner_rows(half, wide - 2 * half)
+    for band, cols in (
+        (band_odd, odd_side(meta, band_odd, wide)),
+        (band_even, even_side(meta, band_even, wide)),
+    ):
+        for rows, outer in (first, last):
+            band[:, outer, :] = total[:, rows, cols]
         band[:, odd_rows, :] = band[:, odd_rows, :] + line[:, :, cols]
         band[:, even_rows, :] = band[:, even_rows, :] + even[:, :, cols]
 
@@ -339,39 +348,46 @@
 
 
 def update_edges_kernel(
-    meta, centre, grad, line, even, band_odd, band_even, direct, detour, out_even, lines
+    meta, field, total, line, even, band_odd, band_even, direct, detour, out_even, lines
 ):
-    (tile, wide), half = grad.shape[1:], even.shape[1]
+    wide, half = total.shape[2], even.shape[1]
     odd_rows, even_rows = rim_rows(meta, half)
-    for at, rows in ((0, slice(0, half)), (half, slice(tile - half, tile))):
-        lines[:, at : at + half, :] = centre[:, rows, :] - step_size * grad[:, rows, :]
+    first, last, _ = inner_rows(half, wide - 2 * half)
+    for rows, outer in (first, last):
+        lines[:, outer, :] = field[:, rows, :] - step_size * total[:, rows, :]
     lines[:, odd_rows, :] = lines[:, odd_rows, :] - step_size * line[...]
     lines[:, even_rows, :] = lines[:, even_rows, :] - step_size * even[...]
-    for band, cols in ((band_odd, odd_side(meta, band_odd, wide)), (band_even, even_side(meta, band_even, wide))):
+    for band, cols in (
+        (band_odd, odd_side(meta, band_odd, wide)),
+        (band_even, even_side(meta, band_even, wide)),
+    ):
         lines[:, :, cols] = lines[:, :, cols] - step_size * band[...]
     clear_outside(meta, lines, half)
     pack(lines[0, odd_rows, :], lines[1, odd_rows, :], direct, detour)
     out_even[...] = lines[:, even_rows, :]
 
 
-def update_centre_kernel(meta, centre, grad, lines, band_odd, band_even, fresh):
-    tile, wide = grad.shape[1:]
-    half = lines.shape[1] // 2
-    mid = slice(half, tile - half)
-    fresh[:, mid, :] = centre[:, mid, :] - step_size * grad[:, mid, :]
-    for band, cols in ((band_odd, odd_side(meta, band_odd, wide)), (band_even, even_side(meta, band_even, wide))):
+def update_centre_kernel(meta, field, total, lines, band_odd, band_even, fresh, zeros):
+    wide, half = total.shape[2], lines.shape[1] // 2
+    first, last, mid = inner_rows(half, wide - 2 * half)
+    fresh[:, mid, :] = field[:, mid, :] - step_size * total[:, mid, :]
+    for band, cols in (
+        (band_odd, odd_side(meta, band_odd, wide)),
+        (band_even, even_side(meta, band_even, wide)),
+    ):
         fresh[:, mid, cols] = fresh[:, mid, cols] - step_size * band[...]
-    clear_outside(meta, fresh, half)
-    fresh[:, :half, :] = lines[:, :half, :]
-    fresh[:, tile - half :, :] = lines[:, half:, :]
-
-
-def final_kernel(meta, centre, grad, line, even, mid_odd, mid_even, rim_odd, rim_even, out):
-    tile, half = grad.shape[1], even.shape[1]
+    clear_outside(meta, fresh.at[:, mid, :], half)
+    for rows, outer in (first, last):
+        fresh[:, rows, :] = lines[:, outer, :]
+    zeros[...] = jnp.zeros_like(zeros)
+
+
+def final_kernel(meta, field, total, line, even, mid_odd, mid_even, rim_odd, rim_even, out):
+    tile, half = out.shape[1], even.shape[1]
     own = slice(half, half + tile)
     odd_row = meta[GY_ODD]
     far = tile - half
-    out[...] = centre[:, :, own] - step_size * grad[:, :, own]
+    out[...] = field[:, own, own] - step_size * total[:, own, own]
     for at, rim in ((odd_row * far, line), ((1 - odd_row) * far, even)):
         rows = pl.ds(pl.multiple_of(at, half), half)
         out[:, rows, :] = out[:, rows, :] - step_size * rim[:, :, own]
@@ -384,7 +400,7 @@
         out[:, far:, cols] = out[:, far:, cols] - step_size * rim[:, half:, :]
 
 
-def call(kernel, meta, arrays, outs, scratch=(), flops=0, room=0, after=None):
+def call(kernel, meta, arrays, outs, scratch=(), flops=0, room=0, after=None, aliases=None):
     f32 = jnp.float32
     shapes = [
         jax.ShapeDtypeStruct(*o) if isinstance(o[0], tuple) else jax.ShapeDtypeStruct(o, f32)
@@ -402,7 +418,8 @@
         in_specs=[smem] + [vmem] * len(arrays) + [anywhere] * len(late),
         out_specs=[vmem] * len(shapes),
         scratch_shapes=list(scratch),
-        compiler_params=pltpu.CompilerParams(vmem_limit_bytes=room or moved + MIB),
+        input_output_aliases=aliases or {},
+        compiler_params=pltpu.CompilerParams(vmem_limit_bytes=room or min(moved + MIB, 6 * MIB)),
         cost_estimate=pl.CostEstimate(flops=flops, bytes_accessed=moved, transcendentals=0),
     )(meta, *arrays, *late)
 
@@ -413,7 +430,7 @@
     half = side // 2
     windows = offsets.shape[2]
     wide = tile + side
-    bf, f32 = jnp.bfloat16, jnp.float32
+    bf = jnp.bfloat16
     place_col, columns_of_tiles = lax.axis_index("gx"), lax.axis_size("gx")
     odd_col = place_col % 2
     edge = (place_col == 0) | (place_col == columns_of_tiles - 1)
@@ -425,9 +442,9 @@
 
     column, band = (2, 2 * half, half), (2, 2 * half, side)
     mid_column, mid_band = (2, tile - 2 * half, half), (2, tile - 2 * half, side)
-    middle, lines = (2, tile, wide), (2, 2 * half, wide)
+    whole, lines = (2, wide, wide), (2, 2 * half, wide)
     line = (2, half, wide)
-    sends = ((half, wide + CUT), (half, wide - CUT), line)
+    sends = ((half, wide - CUT), (half, wide + CUT), line)
 
     *rims, mid_odd, mid_even = call(
         sides_kernel,
@@ -443,30 +460,26 @@
         (probe_field, measured[0, 0]),
         ((windows, 2, side, side), ((windows, 8, side, side), bf), (windows, side, side)),
         flops=10**9,
-        room=20 * MIB,
+        room=12 * MIB,
     )
     *edges, rows = call(edges_kernel, meta, (object_field, *rims), (*sends, lines), after=amps)
     halos = swap_rows(*edges)
-    (centre,) = call(centre_kernel, meta, (object_field, rows, *mids), (middle,))
+    field, total = call(centre_kernel, meta, (object_field, rows, *mids), (whole, whole))
     for iteration in range(ITERS):
         last = iteration + 1 == ITERS
-        grad, *rims, mid_odd, mid_even = call(
+        field, total, *rims, mid_odd, mid_even = call(
             functools.partial(gradient_kernel, side, windows),
             meta,
-            (centre, *halos, probes, tables, amps),
-            (middle, *sends, *((mid_column if last else mid_band),) * 2),
-            scratch=(
-                pltpu.VMEM((2, wide, wide), f32),
-                pltpu.VMEM((2, wide, wide), f32),
-                pltpu.VMEM((2, side, side), bf),
-                pltpu.VMEM(line, f32),
-            ),
+            (field, total, *halos, probes, tables, amps),
+            (whole, whole, *sends, *((mid_column if last else mid_band),) * 2),
+            scratch=(pltpu.VMEM((2, side, side), bf),),
+            aliases={1: 0, 2: 1},
             flops=windows * 16 * side**3,
-            room=24 * MIB,
+            room=8 * MIB,
         )
         rims = swap_rows(*rims)
         shape = column if last else band
-        *bands, odd_line = call(bands_kernel, meta, (grad, *rims), (shape, shape, line))
+        *bands, odd_line = call(bands_kernel, meta, (total, *rims), (shape, shape, line))
         bands = swap_columns(*bands)
         mids = swap_columns(mid_odd, mid_even)
         if last:
@@ -474,15 +487,17 @@
         *edges, rows = call(
             update_edges_kernel,
             meta,
-            (centre, grad, odd_line, rims[3], *bands),
+            (field, total, odd_line, rims[3], *bands),
             (*sends, lines),
         )
         halos = swap_rows(*edges)
-        (centre,) = call(update_centre_kernel, meta, (centre, grad, rows, *mids), (middle,))
+        field, total = call(
+            update_centre_kernel, meta, (field, total, rows, *mids), (whole, whole)
+        )
     (updated,) = call(
         final_kernel,
         meta,
-        (centre, grad, odd_line, rims[3], *mids, *bands),
+        (field, total, odd_line, rims[3], *mids, *bands),
         (object_field.shape,),
     )
     return updated

time: 210 us -> 216 us (1.029)
  waiting for transfers between devices: 83.5 us -> 87.9 us
  starting transfers between devices: 91.9 us -> 94.3 us
    ppermute x4, waiting for transfers between devices: 0.01 us -> 17 us  [swap_rows(): first = lax.ppermute(detour, 'gy', near + [(low, 0), (low + 1, count - 1)])]
    ppermute x4, waiting for transfers between devices: 14.4 us -> 0.01 us  [swap_rows(): second = lax.ppermute(first, 'gy', [(0, low + 1), (count - 1, low)])]
    ppermute x4, waiting for transfers between devices: 19.7 us -> 29.5 us  [swap_rows(): straight = lax.ppermute(direct, 'gy', near + far)]
    ppermute x6, waiting for transfers between devices: 34.8 us -> 26.3 us  [swap_columns(): from_even = lax.ppermute(even_cells, 'gx', pairs(count, 0))]
    ppermute x4, starting transfers between devices: 30.6 us -> 22.5 us  [swap_rows(): straight = lax.ppermute(direct, 'gy', near + far)]
    ppermute x4, starting transfers between devices: 5.95 us -> 10.9 us  [swap_rows(): first = lax.ppermute(detour, 'gy', near + [(low, 0), (low + 1, count - 1)])]
    ppermute x6, starting transfers between devices: 24.5 us -> 28 us  [swap_columns(): from_even = lax.ppermute(even_cells, 'gx', pairs(count, 0))]
    ppermute x6, starting transfers between devices: 24.9 us -> 27.1 us  [swap_columns(): from_odd = lax.ppermute(odd_cells, 'gx', pairs(count, 1))]
  transfers between devices with their start and end apart: 28 -> 28, of which waited for: 13 -> 14; matrix products, arithmetic and copies ran while one was open for 0% -> 0% of each run, Pallas kernels for 3% -> 4%
where the time goes in v2:
time: 216 us
  starting transfers between devices  94.3 us (44%)
  waiting for transfers between devices  87.9 us (41%)
  Pallas kernels  27.8 us (13%)
  local copies, waits for them, and re-layouts  4.8 us (2%)
    ppermute x4, waiting for transfers between devices, swap_rows(): straight = lax.ppermute(direct, 'gy', near + far)  29.5 us
    ppermute x6, starting transfers between devices, swap_columns(): from_even = lax.ppermute(even_cells, 'gx', pairs(count, 0))  28 us
    pallas_call x11, Pallas kernels, call(): pl.pallas_call(kernel, out_shape=shapes, in_specs=[smem] + [vmem] * len(a...  27.8 us
    ppermute x6, starting transfers between devices, swap_columns(): from_odd = lax.ppermute(odd_cells, 'gx', pairs(count, 1))  27.1 us
    ppermute x6, waiting for transfers between devices, swap_columns(): from_even = lax.ppermute(even_cells, 'gx', pairs(count, 0))  26.3 us
    ppermute x4, starting transfers between devices, swap_rows(): straight = lax.ppermute(direct, 'gy', near + far)  22.5 us
    ppermute x4, waiting for transfers between devices, swap_rows(): first = lax.ppermute(detour, 'gy', near + [(low, 0), (low + 1, count - 1)])  17 us
    ppermute x6, waiting for transfers between devices, swap_columns(): from_odd = lax.ppermute(odd_cells, 'gx', pairs(count, 1))  15.1 us
  transfers between devices with their start and end apart: 28, of which 14 were waited for; matrix products, arithmetic and copies ran while one was open for 0% of the time, Pallas kernels for 4%

profile of v2, /device:TPU:15, one launch (start us, length us, event | category | flops | bytes accessed | tf_op | source)
XLA Modules:
  0.0 215.8 jit_solution(6740462389119971534)
XLA Ops:
  3.1 6.1 %collective-permute-start = (f32[2,256,128]{2,1,0:T(8,128)}, f32[2,256,128]{2,1,0:T(8,128)S(1)}, u32[]{:S(2)}, u32[]{:S(2)}) collective-permute-start(f32[2,256,128]{2,1,0:T(8,128)} %get-tuple-element.44), channel_id=1, source_target_pairs={{16,32},{48,64},{80,96},{112,128},{144,160},{176,192},{208,224},{3... | collective-permute-start | bytes 786440 | tf_op jit(solution)/shard_map/ppermute | solution.py:40
  13.2 4.7 %shard_map.56 = (f32[4,2,256,256]{3,2,1,0:T(8,128)S(1)}, bf16[4,8,256,256]{3,2,1,0:T(8,128)(2,1)S(1)}, f32[4,256,256]{2,1,0:T(8,128)S(1)}) custom-call(s32[13]{0:T(128)S(1)} %concatenate.4.meta, f32[2,256,256]{2,1,0:T(8,128)S(1)} %copy-done.3, f32[4,256,256]{2,1,0:T(8,128)S(1)} %bitcast.7), custom_call_target="tpu_custom_call" | custom-call | flops 1000000000 | bytes 8912896 | tf_op jit(solution)/shard_map/pallas_call | solution.py:415
  17.8 4.2 %collective-permute-done.1.side_even = f32[2,256,128]{2,1,0:T(8,128)S(1)} collective-permute-done((f32[2,256,128]{2,1,0:T(8,128)S(1)}, f32[2,256,128]{2,1,0:T(8,128)S(1)}, u32[]{:S(2)}, u32[]{:S(2)}) %collective-permute-start.1) | collective-permute-done | bytes 262176 | tf_op jit(solution)/shard_map/ppermute | solution.py:41
  22.7 2.5 %collective-permute-start.5 = (f32[128,896]{1,0:T(8,128)S(1)}, f32[128,896]{1,0:T(8,128)S(1)}, u32[]{:S(2)}, u32[]{:S(2)}) collective-permute-start(f32[128,896]{1,0:T(8,128)S(1)} %get-tuple-element.53), channel_id=1, source_target_pairs={{1,2},{3,4},{5,6},{9,10},{11,12},{13,14},{2,1},{4,3},{6,5},{10,9},... | collective-permute-start | bytes 1376264 | tf_op jit(solution)/shard_map/ppermute | solution.py:31
  25.7 4.9 %collective-permute-done.5.halo_detour = f32[128,896]{1,0:T(8,128)S(1)} collective-permute-done((f32[128,896]{1,0:T(8,128)S(1)}, f32[128,896]{1,0:T(8,128)S(1)}, u32[]{:S(2)}, u32[]{:S(2)}) %collective-permute-start.5) | collective-permute-done | bytes 458784 | tf_op jit(solution)/shard_map/ppermute | solution.py:31
  31.9 8.6 %collective-permute-start.4 = (f32[128,640]{1,0:T(8,128)S(1)}, f32[128,640]{1,0:T(8,128)S(1)}, u32[]{:S(2)}, u32[]{:S(2)}) collective-permute-start(f32[128,640]{1,0:T(8,128)S(1)} %get-tuple-element.52), channel_id=1, source_target_pairs={{1,2},{3,4},{5,6},{9,10},{11,12},{13,14},{2,1},{4,3},{6,5},{10,9},... | collective-permute-start | bytes 983048 | tf_op jit(solution)/shard_map/ppermute | solution.py:32
  40.6 2.8 %collective-permute-start.2 = (f32[2,256,128]{2,1,0:T(8,128)S(1)}, f32[2,256,128]{2,1,0:T(8,128)S(1)}, u32[]{:S(2)}, u32[]{:S(2)}) collective-permute-start(f32[2,256,128]{2,1,0:T(8,128)S(1)} %get-tuple-element.48), channel_id=1, source_target_pairs={{16,32},{48,64},{80,96},{112,128},{144,160},{176,192},{208,224},{3... | collective-permute-start | bytes 786440 | tf_op jit(solution)/shard_map/ppermute | solution.py:40
  44.9 12.2 %collective-permute-done.2.side_odd = f32[2,256,128]{2,1,0:T(8,128)S(1)} collective-permute-done((f32[2,256,128]{2,1,0:T(8,128)S(1)}, f32[2,256,128]{2,1,0:T(8,128)S(1)}, u32[]{:S(2)}, u32[]{:S(2)}) %collective-permute-start.2) | collective-permute-done | bytes 262176 | tf_op jit(solution)/shard_map/ppermute | solution.py:40
  57.1 2.3 %collective-permute-done.3.side_even = f32[2,256,128]{2,1,0:T(8,128)S(1)} collective-permute-done((f32[2,256,128]{2,1,0:T(8,128)S(1)}, f32[2,256,128]{2,1,0:T(8,128)S(1)}, u32[]{:S(2)}, u32[]{:S(2)}) %collective-permute-start.3) | collective-permute-done | bytes 262176 | tf_op jit(solution)/shard_map/ppermute | solution.py:41
  60.4 6.6 %shard_map.59 = (f32[2,768,768]{2,1,0:T(8,128)S(1)}, f32[2,768,768]{2,1,0:T(8,128)S(1)}, f32[128,640]{1,0:T(8,128)S(1)}, f32[128,896]{1,0:T(8,128)S(1)}, f32[2,1...) custom-call(s32[13]{0:T(128)S(1)} %concatenate.4.meta, ...), custom_call_target="tpu_custom_call", output_to_operand_aliasing={{0}: (1, {}), {1}: (2, {})} | custom-call | flops 1073741824 | bytes 30867456 | tf_op jit(solution)/shard_map/pallas_call | solution.py:415
  67.0 5.6 %collective-permute-start.9 = (f32[128,896]{1,0:T(8,128)S(1)}, f32[128,896]{1,0:T(8,128)S(1)}, u32[]{:S(2)}, u32[]{:S(2)}) collective-permute-start(f32[128,896]{1,0:T(8,128)S(1)} %get-tuple-element.60), channel_id=1, source_target_pairs={{1,2},{3,4},{5,6},{9,10},{11,12},{13,14},{2,1},{4,3},{6,5},{10,9},... | collective-permute-start | bytes 1376264 | tf_op jit(solution)/shard_map/ppermute | solution.py:31
  72.8 5.3 %collective-permute-done.9.detour = f32[128,896]{1,0:T(8,128)S(1)} collective-permute-done((f32[128,896]{1,0:T(8,128)S(1)}, f32[128,896]{1,0:T(8,128)S(1)}, u32[]{:S(2)}, u32[]{:S(2)}) %collective-permute-start.9) | collective-permute-done | bytes 458784 | tf_op jit(solution)/shard_map/ppermute | solution.py:31
  79.3 3.8 %collective-permute-start.8 = (f32[128,640]{1,0:T(8,128)S(1)}, f32[128,640]{1,0:T(8,128)S(1)}, u32[]{:S(2)}, u32[]{:S(2)}) collective-permute-start(f32[128,640]{1,0:T(8,128)S(1)} %get-tuple-element.59), channel_id=1, source_target_pairs={{1,2},{3,4},{5,6},{9,10},{11,12},{13,14},{2,1},{4,3},{6,5},{10,9},... | collective-permute-start | bytes 983048 | tf_op jit(solution)/shard_map/ppermute | solution.py:32
  83.1 10.8 %collective-permute-done.8.direct = f32[128,640]{1,0:T(8,128)S(1)} collective-permute-done((f32[128,640]{1,0:T(8,128)S(1)}, f32[128,640]{1,0:T(8,128)S(1)}, u32[]{:S(2)}, u32[]{:S(2)}) %collective-permute-start.8) | collective-permute-done | bytes 327712 | tf_op jit(solution)/shard_map/ppermute | solution.py:32
  94.7 1.9 collective-permute-start.12
  96.6 17.9 %collective-permute-start.13 = (f32[2,256,256]{2,1,0:T(8,128)S(1)}, f32[2,256,256]{2,1,0:T(8,128)S(1)}, u32[]{:S(2)}, u32[]{:S(2)}) collective-permute-start(f32[2,256,256]{2,1,0:T(8,128)S(1)} %get-tuple-element.64), channel_id=1, source_target_pairs={{0,16},{32,48},{64,80},{96,112},{128,144},{160,176},{192,208},{224... | collective-permute-start | bytes 1572872 | tf_op jit(solution)/shard_map/ppermute | solution.py:41
  114.5 6.6 %collective-permute-done.13.band_even = f32[2,256,256]{2,1,0:T(8,128)S(1)} collective-permute-done((f32[2,256,256]{2,1,0:T(8,128)S(1)}, f32[2,256,256]{2,1,0:T(8,128)S(1)}, u32[]{:S(2)}, u32[]{:S(2)}) %collective-permute-start.13) | collective-permute-done | bytes 524320 | tf_op jit(solution)/shard_map/ppermute | solution.py:41
  123.9 1.9 collective-permute-start.14
  125.8 1.8 collective-permute-start.15
  130.5 8.2 %collective-permute-start.16 = (f32[128,640]{1,0:T(8,128)S(1)}, f32[128,640]{1,0:T(8,128)S(1)}, u32[]{:S(2)}, u32[]{:S(2)}) collective-permute-start(f32[128,640]{1,0:T(8,128)S(1)} %get-tuple-element.70), channel_id=1, source_target_pairs={{1,2},{3,4},{5,6},{9,10},{11,12},{13,14},{2,1},{4,3},{6,5},{10,9},... | collective-permute-start | bytes 983048 | tf_op jit(solution)/shard_map/ppermute | solution.py:32
  138.7 2.9 %collective-permute-done.14.band_odd = f32[2,256,256]{2,1,0:T(8,128)S(1)} collective-permute-done((f32[2,256,256]{2,1,0:T(8,128)S(1)}, f32[2,256,256]{2,1,0:T(8,128)S(1)}, u32[]{:S(2)}, u32[]{:S(2)}) %collective-permute-start.14) | collective-permute-done | bytes 524320 | tf_op jit(solution)/shard_map/ppermute | solution.py:40
  141.5 9.6 %collective-permute-done.15.band_even = f32[2,256,256]{2,1,0:T(8,128)S(1)} collective-permute-done((f32[2,256,256]{2,1,0:T(8,128)S(1)}, f32[2,256,256]{2,1,0:T(8,128)S(1)}, u32[]{:S(2)}, u32[]{:S(2)}) %collective-permute-start.15) | collective-permute-done | bytes 524320 | tf_op jit(solution)/shard_map/ppermute | solution.py:41
  152.5 11.0 %collective-permute-done.16.halo_direct = f32[128,640]{1,0:T(8,128)S(1)} collective-permute-done((f32[128,640]{1,0:T(8,128)S(1)}, f32[128,640]{1,0:T(8,128)S(1)}, u32[]{:S(2)}, u32[]{:S(2)}) %collective-permute-start.16) | collective-permute-done | bytes 327712 | tf_op jit(solution)/shard_map/ppermute | solution.py:32
  163.5 6.6 %shard_map.63 = (f32[2,768,768]{2,1,0:T(8,128)S(1)}, f32[2,768,768]{2,1,0:T(8,128)S(1)}, f32[128,640]{1,0:T(8,128)S(1)}, f32[128,896]{1,0:T(8,128)S(1)}, f32[2,1...) custom-call(s32[13]{0:T(128)S(1)} %concatenate.4.meta, ...), custom_call_target="tpu_custom_call", output_to_operand_aliasing={{0}: (1, {}), {1}: (2, {})} | custom-call | flops 1073741824 | bytes 30343168 | tf_op jit(solution)/shard_map/pallas_call | solution.py:415
  171.5 5.3 %collective-permute-done.21.detour = f32[128,896]{1,0:T(8,128)S(1)} collective-permute-done((f32[128,896]{1,0:T(8,128)S(1)}, f32[128,896]{1,0:T(8,128)S(1)}, u32[]{:S(2)}, u32[]{:S(2)}) %collective-permute-start.21) | collective-permute-done | bytes 458784 | tf_op jit(solution)/shard_map/ppermute | solution.py:31
  178.1 1.9 collective-permute-start.20
  180.0 8.8 %collective-permute-start.24 = (f32[2,256,128]{2,1,0:T(8,128)S(1)}, f32[2,256,128]{2,1,0:T(8,128)S(1)}, u32[]{:S(2)}, u32[]{:S(2)}) collective-permute-start(f32[2,256,128]{2,1,0:T(8,128)S(1)} %get-tuple-element.79), channel_id=1, source_target_pairs={{16,32},{48,64},{80,96},{112,128},{144,160},{176,192},{208,224},{3... | collective-permute-start | bytes 786440 | tf_op jit(solution)/shard_map/ppermute | solution.py:40
  189.0 7.7 %collective-permute-done.20.direct = f32[128,640]{1,0:T(8,128)S(1)} collective-permute-done((f32[128,640]{1,0:T(8,128)S(1)}, f32[128,640]{1,0:T(8,128)S(1)}, u32[]{:S(2)}, u32[]{:S(2)}) %collective-permute-start.20) | collective-permute-done | bytes 327712 | tf_op jit(solution)/shard_map/ppermute | solution.py:32
  197.4 5.5 %collective-permute-start.26 = (f32[2,256,128]{2,1,0:T(8,128)S(1)}, f32[2,256,128]{2,1,0:T(8,128)S(1)}, u32[]{:S(2)}, u32[]{:S(2)}) collective-permute-start(f32[2,256,128]{2,1,0:T(8,128)S(1)} %get-tuple-element.81), channel_id=1, source_target_pairs={{16,32},{48,64},{80,96},{112,128},{144,160},{176,192},{208,224},{3... | collective-permute-start | bytes 786440 | tf_op jit(solution)/shard_map/ppermute | solution.py:40
  202.9 6.6 %collective-permute-start.27 = (f32[2,256,128]{2,1,0:T(8,128)S(1)}, f32[2,256,128]{2,1,0:T(8,128)S(1)}, u32[]{:S(2)}, u32[]{:S(2)}) collective-permute-start(f32[2,256,128]{2,1,0:T(8,128)S(1)} %get-tuple-element.82), channel_id=1, source_target_pairs={{0,16},{32,48},{64,80},{96,112},{128,144},{160,176},{192,208},{224... | collective-permute-start | bytes 786440 | tf_op jit(solution)/shard_map/ppermute | solution.py:41
  209.5 3.8 %collective-permute-done.27.rim_even = f32[2,256,128]{2,1,0:T(8,128)S(1)} collective-permute-done((f32[2,256,128]{2,1,0:T(8,128)S(1)}, f32[2,256,128]{2,1,0:T(8,128)S(1)}, u32[]{:S(2)}, u32[]{:S(2)}) %collective-permute-start.27) | collective-permute-done | bytes 262176 | tf_op jit(solution)/shard_map/ppermute | solution.py:41
  213.2 2.6 %shard_map.65 = f32[2,512,512]{2,1,0:T(8,128)} custom-call(s32[13]{0:T(128)S(1)} %concatenate.4.meta, f32[2,768,768]{2,1,0:T(8,128)S(1)} %get-tuple-element.73.field, f32[2,768,768]{2,1,0:T(8,128)S(1)} %get-tuple-element.74.total, f32[2,128,768]{2,1,0:T(8,128)S(1)} %get-tuple-element.78.line, f32[2,128,768]{2,1,0:T(8,128)S(1)} %collective-permute-done.23.even, ...), custom_call_target="tpu_custom_call" | custom-call | bytes 14155776 | tf_op jit(solution)/shard_map/pallas_call | solution.py:415
  (47 shorter events, 24.1 us)
Async XLA Ops:
  0.1 1.6 copy-start
  1.7 20.3 %copy-start.1 = (f32[2,512,512]{2,1,0:T(8,128)S(1)}, f32[2,512,512]{2,1,0:T(8,128)}, u32[]{:S(2)}) copy-start(f32[2,512,512]{2,1,0:T(8,128)} %own.5) | copy-start | bytes 6291460
  3.1 14.8 %collective-permute-start = (f32[2,256,128]{2,1,0:T(8,128)}, f32[2,256,128]{2,1,0:T(8,128)S(1)}, u32[]{:S(2)}, u32[]{:S(2)}) collective-permute-start(f32[2,256,128]{2,1,0:T(8,128)} %get-tuple-element.44), channel_id=1, source_target_pairs={{16,32},{48,64},{80,96},{112,128},{144,160},{176,192},{208,224},{3... | collective-permute-start | bytes 786440 | tf_op jit(solution)/shard_map/ppermute | solution.py:40
  9.2 12.8 %collective-permute-start.1 = (f32[2,256,128]{2,1,0:T(8,128)S(1)}, f32[2,256,128]{2,1,0:T(8,128)S(1)}, u32[]{:S(2)}, u32[]{:S(2)}) collective-permute-start(f32[2,256,128]{2,1,0:T(8,128)S(1)} %get-tuple-element.45), channel_id=1, source_target_pairs={{0,16},{32,48},{64,80},{96,112},{128,144},{160,176},{192,208},{224... | collective-permute-start | bytes 786440 | tf_op jit(solution)/shard_map/ppermute | solution.py:41
  10.9 1.2 copy-start.2
  12.1 1.0 copy-start.3
  22.7 7.9 %collective-permute-start.5 = (f32[128,896]{1,0:T(8,128)S(1)}, f32[128,896]{1,0:T(8,128)S(1)}, u32[]{:S(2)}, u32[]{:S(2)}) collective-permute-start(f32[128,896]{1,0:T(8,128)S(1)} %get-tuple-element.53), channel_id=1, source_target_pairs={{1,2},{3,4},{5,6},{9,10},{11,12},{13,14},{2,1},{4,3},{6,5},{10,9},... | collective-permute-start | bytes 1376264 | tf_op jit(solution)/shard_map/ppermute | solution.py:31
  25.3 35.1 %collective-permute-start.7 = (f32[2,128,768]{2,1,0:T(8,128)S(1)}, f32[2,128,768]{2,1,0:T(8,128)S(1)}, u32[]{:S(2)}, u32[]{:S(2)}) collective-permute-start(f32[2,128,768]{2,1,0:T(8,128)S(1)} %get-tuple-element.54), channel_id=1, source_target_pairs={{0,1},{2,3},{4,5},{6,7},{8,9},{10,11},{12,13},{14,15},{1,0},{3,2},... | collective-permute-start | bytes 2359304 | tf_op jit(solution)/shard_map/ppermute | solution.py:33
  30.6 29.8 %collective-permute-start.6 = (f32[128,896]{1,0:T(8,128)S(1)}, f32[128,896]{1,0:T(8,128)S(1)}, u32[]{:S(2)}, u32[]{:S(2)}) collective-permute-start(f32[128,896]{1,0:T(8,128)S(1)} %collective-permute-done.5.halo_detour), channel_id=1, source_target_pairs={{0,8},{15,7},{16,24},{31,23},{32,40},{47,39},{48,56},{63,55},{64,7... | collective-permute-start | bytes 1376264 | tf_op jit(solution)/shard_map/ppermute | solution.py:34
  31.9 28.5 %collective-permute-start.4 = (f32[128,640]{1,0:T(8,128)S(1)}, f32[128,640]{1,0:T(8,128)S(1)}, u32[]{:S(2)}, u32[]{:S(2)}) collective-permute-start(f32[128,640]{1,0:T(8,128)S(1)} %get-tuple-element.52), channel_id=1, source_target_pairs={{1,2},{3,4},{5,6},{9,10},{11,12},{13,14},{2,1},{4,3},{6,5},{10,9},... | collective-permute-start | bytes 983048 | tf_op jit(solution)/shard_map/ppermute | solution.py:32
  40.6 16.5 %collective-permute-start.2 = (f32[2,256,128]{2,1,0:T(8,128)S(1)}, f32[2,256,128]{2,1,0:T(8,128)S(1)}, u32[]{:S(2)}, u32[]{:S(2)}) collective-permute-start(f32[2,256,128]{2,1,0:T(8,128)S(1)} %get-tuple-element.48), channel_id=1, source_target_pairs={{16,32},{48,64},{80,96},{112,128},{144,160},{176,192},{208,224},{3... | collective-permute-start | bytes 786440 | tf_op jit(solution)/shard_map/ppermute | solution.py:40
  43.4 16.0 %collective-permute-start.3 = (f32[2,256,128]{2,1,0:T(8,128)S(1)}, f32[2,256,128]{2,1,0:T(8,128)S(1)}, u32[]{:S(2)}, u32[]{:S(2)}) collective-permute-start(f32[2,256,128]{2,1,0:T(8,128)S(1)} %get-tuple-element.49), channel_id=1, source_target_pairs={{0,16},{32,48},{64,80},{96,112},{128,144},{160,176},{192,208},{224... | collective-permute-start | bytes 786440 | tf_op jit(solution)/shard_map/ppermute | solution.py:41
  67.0 11.0 %collective-permute-start.9 = (f32[128,896]{1,0:T(8,128)S(1)}, f32[128,896]{1,0:T(8,128)S(1)}, u32[]{:S(2)}, u32[]{:S(2)}) collective-permute-start(f32[128,896]{1,0:T(8,128)S(1)} %get-tuple-element.60), channel_id=1, source_target_pairs={{1,2},{3,4},{5,6},{9,10},{11,12},{13,14},{2,1},{4,3},{6,5},{10,9},... | collective-permute-start | bytes 1376264 | tf_op jit(solution)/shard_map/ppermute | solution.py:31
  72.6 21.2 %collective-permute-start.11 = (f32[2,128,768]{2,1,0:T(8,128)S(1)}, f32[2,128,768]{2,1,0:T(8,128)S(1)}, u32[]{:S(2)}, u32[]{:S(2)}) collective-permute-start(f32[2,128,768]{2,1,0:T(8,128)S(1)} %get-tuple-element.61), channel_id=1, source_target_pairs={{0,1},{2,3},{4,5},{6,7},{8,9},{10,11},{12,13},{14,15},{1,0},{3,2},... | collective-permute-start | bytes 2359304 | tf_op jit(solution)/shard_map/ppermute | solution.py:33
  78.0 15.8 %collective-permute-start.10 = (f32[128,896]{1,0:T(8,128)S(1)}, f32[128,896]{1,0:T(8,128)S(1)}, u32[]{:S(2)}, u32[]{:S(2)}) collective-permute-start(f32[128,896]{1,0:T(8,128)S(1)} %collective-permute-done.9.detour), channel_id=1, source_target_pairs={{0,8},{15,7},{16,24},{31,23},{32,40},{47,39},{48,56},{63,55},{64,7... | collective-permute-start | bytes 1376264 | tf_op jit(solution)/shard_map/ppermute | solution.py:34
  79.3 14.5 %collective-permute-start.8 = (f32[128,640]{1,0:T(8,128)S(1)}, f32[128,640]{1,0:T(8,128)S(1)}, u32[]{:S(2)}, u32[]{:S(2)}) collective-permute-start(f32[128,640]{1,0:T(8,128)S(1)} %get-tuple-element.59), channel_id=1, source_target_pairs={{1,2},{3,4},{5,6},{9,10},{11,12},{13,14},{2,1},{4,3},{6,5},{10,9},... | collective-permute-start | bytes 983048 | tf_op jit(solution)/shard_map/ppermute | solution.py:32
  94.7 19.8 %collective-permute-start.12 = (f32[2,256,256]{2,1,0:T(8,128)S(1)}, f32[2,256,256]{2,1,0:T(8,128)S(1)}, u32[]{:S(2)}, u32[]{:S(2)}) collective-permute-start(f32[2,256,256]{2,1,0:T(8,128)S(1)} %get-tuple-element.63), channel_id=1, source_target_pairs={{16,32},{48,64},{80,96},{112,128},{144,160},{176,192},{208,224},{3... | collective-permute-start | bytes 1572872 | tf_op jit(solution)/shard_map/ppermute | solution.py:40
  96.6 24.5 %collective-permute-start.13 = (f32[2,256,256]{2,1,0:T(8,128)S(1)}, f32[2,256,256]{2,1,0:T(8,128)S(1)}, u32[]{:S(2)}, u32[]{:S(2)}) collective-permute-start(f32[2,256,256]{2,1,0:T(8,128)S(1)} %get-tuple-element.64), channel_id=1, source_target_pairs={{0,16},{32,48},{64,80},{96,112},{128,144},{160,176},{192,208},{224... | collective-permute-start | bytes 1572872 | tf_op jit(solution)/shard_map/ppermute | solution.py:41
  122.3 6.8 %collective-permute-start.17 = (f32[128,896]{1,0:T(8,128)S(1)}, f32[128,896]{1,0:T(8,128)S(1)}, u32[]{:S(2)}, u32[]{:S(2)}) collective-permute-start(f32[128,896]{1,0:T(8,128)S(1)} %get-tuple-element.71), channel_id=1, source_target_pairs={{1,2},{3,4},{5,6},{9,10},{11,12},{13,14},{2,1},{4,3},{6,5},{10,9},... | collective-permute-start | bytes 1376264 | tf_op jit(solution)/shard_map/ppermute | solution.py:31
  123.8 39.7 %collective-permute-start.19 = (f32[2,128,768]{2,1,0:T(8,128)S(1)}, f32[2,128,768]{2,1,0:T(8,128)S(1)}, u32[]{:S(2)}, u32[]{:S(2)}) collective-permute-start(f32[2,128,768]{2,1,0:T(8,128)S(1)} %get-tuple-element.72), channel_id=1, source_target_pairs={{0,1},{2,3},{4,5},{6,7},{8,9},{10,11},{12,13},{14,15},{1,0},{3,2},... | collective-permute-start | bytes 2359304 | tf_op jit(solution)/shard_map/ppermute | solution.py:33
  123.9 17.6 %collective-permute-start.14 = (f32[2,256,256]{2,1,0:T(8,128)S(1)}, f32[2,256,256]{2,1,0:T(8,128)S(1)}, u32[]{:S(2)}, u32[]{:S(2)}) collective-permute-start(f32[2,256,256]{2,1,0:T(8,128)S(1)} %get-tuple-element.66), channel_id=1, source_target_pairs={{16,32},{48,64},{80,96},{112,128},{144,160},{176,192},{208,224},{3... | collective-permute-start | bytes 1572872 | tf_op jit(solution)/shard_map/ppermute | solution.py:40
  125.8 25.3 %collective-permute-start.15 = (f32[2,256,256]{2,1,0:T(8,128)S(1)}, f32[2,256,256]{2,1,0:T(8,128)S(1)}, u32[]{:S(2)}, u32[]{:S(2)}) collective-permute-start(f32[2,256,256]{2,1,0:T(8,128)S(1)} %get-tuple-element.67), channel_id=1, source_target_pairs={{0,16},{32,48},{64,80},{96,112},{128,144},{160,176},{192,208},{224... | collective-permute-start | bytes 1572872 | tf_op jit(solution)/shard_map/ppermute | solution.py:41
  129.2 34.4 %collective-permute-start.18 = (f32[128,896]{1,0:T(8,128)S(1)}, f32[128,896]{1,0:T(8,128)S(1)}, u32[]{:S(2)}, u32[]{:S(2)}) collective-permute-start(f32[128,896]{1,0:T(8,128)S(1)} %collective-permute-done.17.halo_detour), channel_id=1, source_target_pairs={{0,8},{15,7},{16,24},{31,23},{32,40},{47,39},{48,56},{63,55},{64,7... | collective-permute-start | bytes 1376264 | tf_op jit(solution)/shard_map/ppermute | solution.py:34
  130.5 33.1 %collective-permute-start.16 = (f32[128,640]{1,0:T(8,128)S(1)}, f32[128,640]{1,0:T(8,128)S(1)}, u32[]{:S(2)}, u32[]{:S(2)}) collective-permute-start(f32[128,640]{1,0:T(8,128)S(1)} %get-tuple-element.70), channel_id=1, source_target_pairs={{1,2},{3,4},{5,6},{9,10},{11,12},{13,14},{2,1},{4,3},{6,5},{10,9},... | collective-permute-start | bytes 983048 | tf_op jit(solution)/shard_map/ppermute | solution.py:32
  170.1 6.7 %collective-permute-start.21 = (f32[128,896]{1,0:T(8,128)S(1)}, f32[128,896]{1,0:T(8,128)S(1)}, u32[]{:S(2)}, u32[]{:S(2)}) collective-permute-start(f32[128,896]{1,0:T(8,128)S(1)} %get-tuple-element.76), channel_id=1, source_target_pairs={{1,2},{3,4},{5,6},{9,10},{11,12},{13,14},{2,1},{4,3},{6,5},{10,9},... | collective-permute-start | bytes 1376264 | tf_op jit(solution)/shard_map/ppermute | solution.py:31
  171.4 25.2 %collective-permute-start.23 = (f32[2,128,768]{2,1,0:T(8,128)S(1)}, f32[2,128,768]{2,1,0:T(8,128)S(1)}, u32[]{:S(2)}, u32[]{:S(2)}) collective-permute-start(f32[2,128,768]{2,1,0:T(8,128)S(1)} %get-tuple-element.77), channel_id=1, source_target_pairs={{0,1},{2,3},{4,5},{6,7},{8,9},{10,11},{12,13},{14,15},{1,0},{3,2},... | collective-permute-start | bytes 2359304 | tf_op jit(solution)/shard_map/ppermute | solution.py:33
  176.8 19.8 %collective-permute-start.22 = (f32[128,896]{1,0:T(8,128)S(1)}, f32[128,896]{1,0:T(8,128)S(1)}, u32[]{:S(2)}, u32[]{:S(2)}) collective-permute-start(f32[128,896]{1,0:T(8,128)S(1)} %collective-permute-done.21.detour), channel_id=1, source_target_pairs={{0,8},{15,7},{16,24},{31,23},{32,40},{47,39},{48,56},{63,55},{64,7... | collective-permute-start | bytes 1376264 | tf_op jit(solution)/shard_map/ppermute | solution.py:34
  178.1 18.5 %collective-permute-start.20 = (f32[128,640]{1,0:T(8,128)S(1)}, f32[128,640]{1,0:T(8,128)S(1)}, u32[]{:S(2)}, u32[]{:S(2)}) collective-permute-start(f32[128,640]{1,0:T(8,128)S(1)} %get-tuple-element.75), channel_id=1, source_target_pairs={{1,2},{3,4},{5,6},{9,10},{11,12},{13,14},{2,1},{4,3},{6,5},{10,9},... | collective-permute-start | bytes 983048 | tf_op jit(solution)/shard_map/ppermute | solution.py:32
  180.0 29.5 %collective-permute-start.24 = (f32[2,256,128]{2,1,0:T(8,128)S(1)}, f32[2,256,128]{2,1,0:T(8,128)S(1)}, u32[]{:S(2)}, u32[]{:S(2)}) collective-permute-start(f32[2,256,128]{2,1,0:T(8,128)S(1)} %get-tuple-element.79), channel_id=1, source_target_pairs={{16,32},{48,64},{80,96},{112,128},{144,160},{176,192},{208,224},{3... | collective-permute-start | bytes 786440 | tf_op jit(solution)/shard_map/ppermute | solution.py:40
  188.9 20.6 %collective-permute-start.25 = (f32[2,256,128]{2,1,0:T(8,128)S(1)}, f32[2,256,128]{2,1,0:T(8,128)S(1)}, u32[]{:S(2)}, u32[]{:S(2)}) collective-permute-start(f32[2,256,128]{2,1,0:T(8,128)S(1)} %get-tuple-element.80), channel_id=1, source_target_pairs={{0,16},{32,48},{64,80},{96,112},{128,144},{160,176},{192,208},{224... | collective-permute-start | bytes 786440 | tf_op jit(solution)/shard_map/ppermute | solution.py:41
  197.4 12.1 %collective-permute-start.26 = (f32[2,256,128]{2,1,0:T(8,128)S(1)}, f32[2,256,128]{2,1,0:T(8,128)S(1)}, u32[]{:S(2)}, u32[]{:S(2)}) collective-permute-start(f32[2,256,128]{2,1,0:T(8,128)S(1)} %get-tuple-element.81), channel_id=1, source_target_pairs={{16,32},{48,64},{80,96},{112,128},{144,160},{176,192},{208,224},{3... | collective-permute-start | bytes 786440 | tf_op jit(solution)/shard_map/ppermute | solution.py:40
  202.9 10.4 %collective-permute-start.27 = (f32[2,256,128]{2,1,0:T(8,128)S(1)}, f32[2,256,128]{2,1,0:T(8,128)S(1)}, u32[]{:S(2)}, u32[]{:S(2)}) collective-permute-start(f32[2,256,128]{2,1,0:T(8,128)S(1)} %get-tuple-element.82), channel_id=1, source_target_pairs={{0,16},{32,48},{64,80},{96,112},{128,144},{160,176},{192,208},{224... | collective-permute-start | bytes 786440 | tf_op jit(solution)/shard_map/ppermute | solution.py:41

commit v3 on v2

--- a/solution.py
+++ b/solution.py
@@ -46,19 +46,18 @@
 
 
 def pack(real, imag, direct, detour):
-    straight = direct.shape[1]
-    direct[...] = real[:, :straight]
-    detour[:, :CUT] = real[:, straight:]
-    detour[:, CUT:] = imag
+    wide = real.shape[1]
+    direct[:, :wide] = real
+    direct[:, wide:] = imag[:, :CUT]
+    detour[...] = imag[:, CUT:]
 
 
 def unpack(meta, direct, detour, relayed, line):
-    straight = direct.shape[1]
+    wide = line.shape[2]
     own = meta[RELAY] == 0
-    line[0, :, :straight] = direct[...]
-    rest = jnp.where(own, detour[...], jnp.zeros_like(detour)) + relayed[...]
-    line[0, :, straight:] = rest[:, :CUT]
-    line[1] = rest[:, CUT:]
+    line[0] = direct[:, :wide]
+    line[1, :, :CUT] = direct[:, wide:]
+    line[1, :, CUT:] = jnp.where(own, detour[...], jnp.zeros_like(detour)) + relayed[...]
 
 
 def dot(a, b):
@@ -153,10 +152,9 @@
     rim_direct,
     rim_detour,
     rim_even,
-    band_odd,
-    band_even,
-    mixed,
+    *rest,
 ):
+    *bands, mixed = rest
     half = side // 2
     wide = field.shape[2]
     tile = wide - side
@@ -256,11 +254,12 @@
 
     pack(total[0, odd_rows, :], total[1, odd_rows, :], rim_direct, rim_detour)
     rim_even[...] = total[:, even_rows, :]
-    for band, cols in (
-        (band_odd, odd_side(meta, band_odd, wide)),
-        (band_even, even_side(meta, band_even, wide)),
-    ):
-        band[...] = total[:, side:tile, cols]
+    first = side
+    for band_odd, band_even in zip(bands[::2], bands[1::2]):
+        rows = slice(first, first + band_odd.shape[1])
+        band_odd[...] = total[:, rows, odd_side(meta, band_odd, wide)]
+        band_even[...] = total[:, rows, even_side(meta, band_even, wide)]
+        first += band_odd.shape[1]
 
 
 def odd_side(meta, band, wide):
@@ -367,22 +366,25 @@
     out_even[...] = lines[:, even_rows, :]
 
 
-def update_centre_kernel(meta, field, total, lines, band_odd, band_even, fresh, zeros):
+def update_centre_kernel(
+    meta, field, total, lines, upper_odd, upper_even, lower_odd, lower_even, fresh, zeros
+):
     wide, half = total.shape[2], lines.shape[1] // 2
     first, last, mid = inner_rows(half, wide - 2 * half)
     fresh[:, mid, :] = field[:, mid, :] - step_size * total[:, mid, :]
-    for band, cols in (
-        (band_odd, odd_side(meta, band_odd, wide)),
-        (band_even, even_side(meta, band_even, wide)),
-    ):
-        fresh[:, mid, cols] = fresh[:, mid, cols] - step_size * band[...]
+    start = mid.start
+    for odd, even in ((upper_odd, upper_even), (lower_odd, lower_even)):
+        rows = slice(start, start + odd.shape[1])
+        for band, cols in ((odd, odd_side(meta, odd, wide)), (even, even_side(meta, even, wide))):
+            fresh[:, rows, cols] = fresh[:, rows, cols] - step_size * band[...]
+        start += odd.shape[1]
     clear_outside(meta, fresh.at[:, mid, :], half)
     for rows, outer in (first, last):
         fresh[:, rows, :] = lines[:, outer, :]
     zeros[...] = jnp.zeros_like(zeros)
 
 
-def final_kernel(meta, field, total, line, even, mid_odd, mid_even, rim_odd, rim_even, out):
+def almost_final_kernel(meta, field, total, line, even, mid_odd, mid_even, out, part_odd, part_even):
     tile, half = out.shape[1], even.shape[1]
     own = slice(half, half + tile)
     odd_row = meta[GY_ODD]
@@ -391,16 +393,39 @@
     for at, rim in ((odd_row * far, line), ((1 - odd_row) * far, even)):
         rows = pl.ds(pl.multiple_of(at, half), half)
         out[:, rows, :] = out[:, rows, :] - step_size * rim[:, :, own]
-    for mid, rim, cols in (
-        (mid_odd, rim_odd, odd_side(meta, mid_odd, tile)),
-        (mid_even, rim_even, even_side(meta, mid_even, tile)),
+    for mid, part, cols in (
+        (mid_odd, part_odd, odd_side(meta, mid_odd, tile)),
+        (mid_even, part_even, even_side(meta, mid_even, tile)),
     ):
-        out[:, :half, cols] = out[:, :half, cols] - step_size * rim[:, :half, :]
         out[:, half:far, cols] = out[:, half:far, cols] - step_size * mid[...]
-        out[:, far:, cols] = out[:, far:, cols] - step_size * rim[:, half:, :]
-
-
-def call(kernel, meta, arrays, outs, scratch=(), flops=0, room=0, after=None, aliases=None):
+        part[:, :half, :] = out[:, :half, cols]
+        part[:, half:, :] = out[:, far:, cols]
+
+
+def final_kernel(meta, _, part_odd, part_even, rim_odd, rim_even, out, ready, sems):
+    tile, half = out.shape[1], part_odd.shape[2]
+    copies = []
+    for i, (part, rim, cols) in enumerate(
+        (
+            (part_odd, rim_odd, odd_side(meta, part_odd, tile)),
+            (part_even, rim_even, even_side(meta, part_even, tile)),
+        )
+    ):
+        ready[i] = part[...] - step_size * rim[...]
+        for j, first in enumerate((0, tile - half)):
+            copies.append(
+                pltpu.make_async_copy(
+                    ready.at[i, :, pl.ds(j * half, half), :],
+                    out.at[:, pl.ds(first, half), cols],
+                    sems.at[len(copies)],
+                )
+            )
+            copies[-1].start()
+    for copy in copies:
+        copy.wait()
+
+
+def call(kernel, meta, arrays, outs, scratch=(), flops=0, room=0, after=None, aliases=None, far=False):
     f32 = jnp.float32
     shapes = [
         jax.ShapeDtypeStruct(*o) if isinstance(o[0], tuple) else jax.ShapeDtypeStruct(o, f32)
@@ -415,8 +440,8 @@
     return pl.pallas_call(
         kernel,
         out_shape=shapes,
-        in_specs=[smem] + [vmem] * len(arrays) + [anywhere] * len(late),
-        out_specs=[vmem] * len(shapes),
+        in_specs=[smem, anywhere if far else vmem, *[vmem] * (len(arrays) - 1), *[anywhere] * len(late)],
+        out_specs=[anywhere if far else vmem] * len(shapes),
         scratch_shapes=list(scratch),
         input_output_aliases=aliases or {},
         compiler_params=pltpu.CompilerParams(vmem_limit_bytes=room or min(moved + MIB, 6 * MIB)),
@@ -441,10 +466,10 @@
     meta = jnp.concatenate([places, counts[0], offsets[0, 0].reshape(-1)]).astype(jnp.int32)
 
     column, band = (2, 2 * half, half), (2, 2 * half, side)
-    mid_column, mid_band = (2, tile - 2 * half, half), (2, tile - 2 * half, side)
+    mid_column, mid_band = (2, tile - 2 * half, half), (2, tile // 2 - half, side)
     whole, lines = (2, wide, wide), (2, 2 * half, wide)
     line = (2, half, wide)
-    sends = ((half, wide - CUT), (half, wide + CUT), line)
+    sends = ((half, wide + CUT), (half, wide - CUT), line)
 
     *rims, mid_odd, mid_even = call(
         sides_kernel,
@@ -467,23 +492,24 @@
     field, total = call(centre_kernel, meta, (object_field, rows, *mids), (whole, whole))
     for iteration in range(ITERS):
         last = iteration + 1 == ITERS
-        field, total, *rims, mid_odd, mid_even = call(
+        field, total, *rest = call(
             functools.partial(gradient_kernel, side, windows),
             meta,
             (field, total, *halos, probes, tables, amps),
-            (whole, whole, *sends, *((mid_column if last else mid_band),) * 2),
+            (whole, whole, *sends, *((mid_column,) * 2 if last else (mid_band,) * 4)),
             scratch=(pltpu.VMEM((2, side, side), bf),),
             aliases={1: 0, 2: 1},
             flops=windows * 16 * side**3,
             room=8 * MIB,
         )
-        rims = swap_rows(*rims)
+        rims = swap_rows(*rest[:3])
         shape = column if last else band
         *bands, odd_line = call(bands_kernel, meta, (total, *rims), (shape, shape, line))
         bands = swap_columns(*bands)
-        mids = swap_columns(mid_odd, mid_even)
+        mids = swap_columns(*rest[3:5])
         if last:
             break
+        mids += swap_columns(*rest[5:])
         *edges, rows = call(
             update_edges_kernel,
             meta,
@@ -494,11 +520,20 @@
         field, total = call(
             update_centre_kernel, meta, (field, total, rows, *mids), (whole, whole)
         )
+    updated, *parts = call(
+        almost_final_kernel,
+        meta,
+        (field, total, odd_line, rims[3], *mids),
+        (object_field.shape, column, column),
+    )
     (updated,) = call(
         final_kernel,
         meta,
-        (field, total, odd_line, rims[3], *mids, *bands),
+        (updated, *parts, *bands),
         (object_field.shape,),
+        scratch=(pltpu.VMEM((2, *column), jnp.float32), pltpu.SemaphoreType.DMA((4,))),
+        aliases={1: 0},
+        far=True,
     )
     return updated
 

time: 216 us -> 212 us (0.981); the launches traced: 216 us -> 209 us
  waiting for transfers between devices: 87.9 us -> 67.5 us
  starting transfers between devices: 94.3 us -> 107 us
    ppermute x4, waiting for transfers between devices: 29.5 us -> 8.1 us  [swap_rows(): straight = lax.ppermute(direct, 'gy', near + far)]
    ppermute x4, waiting for transfers between devices: 17 us -> 0.01 us  [swap_rows(): first = lax.ppermute(detour, 'gy', near + [(low, 0), (low + 1, count - 1)])]
    ppermute x4, waiting for transfers between devices: 0.01 us -> 13 us  [swap_rows(): second = lax.ppermute(first, 'gy', [(0, low + 1), (count - 1, low)])]
    ppermute x6 -> x7, starting transfers between devices: 28 us -> 39 us  [swap_columns(): from_even = lax.ppermute(even_cells, 'gx', pairs(count, 0))]
    ppermute x4, starting transfers between devices: 22.5 us -> 33 us  [swap_rows(): straight = lax.ppermute(direct, 'gy', near + far)]
    ppermute x6 -> x7, waiting for transfers between devices: 15.1 us -> 24.8 us  [swap_columns(): from_odd = lax.ppermute(odd_cells, 'gx', pairs(count, 1))]
    ppermute x4, starting transfers between devices: 10.9 us -> 5.95 us  [swap_rows(): first = lax.ppermute(detour, 'gy', near + [(low, 0), (low + 1, count - 1)])]
    ppermute x6 -> x7, waiting for transfers between devices: 26.3 us -> 21.6 us  [swap_columns(): from_even = lax.ppermute(even_cells, 'gx', pairs(count, 0))]
  transfers between devices with their start and end apart: 28 -> 30, of which waited for: 14 -> 11; matrix products, arithmetic and copies ran while one was open for 0% -> 0% of each run, Pallas kernels for 4% -> 5%
where the time goes in v3:
time: 212 us; the launch traced here: 209 us
  starting transfers between devices  107 us (50%)
  waiting for transfers between devices  67.5 us (32%)
  Pallas kernels  29.1 us (14%)
  local copies, waits for them, and re-layouts  4.8 us (2%)
    ppermute x7, starting transfers between devices, swap_columns(): from_even = lax.ppermute(even_cells, 'gx', pairs(count, 0))  39 us
    ppermute x4, starting transfers between devices, swap_rows(): straight = lax.ppermute(direct, 'gy', near + far)  33 us
    pallas_call x12, Pallas kernels, call(): pl.pallas_call(kernel, out_shape=shapes, in_specs=[smem, anywhere if far...  29.1 us
    ppermute x7, waiting for transfers between devices, swap_columns(): from_odd = lax.ppermute(odd_cells, 'gx', pairs(count, 1))  24.8 us
    ppermute x7, starting transfers between devices, swap_columns(): from_odd = lax.ppermute(odd_cells, 'gx', pairs(count, 1))  22.9 us
    ppermute x7, waiting for transfers between devices, swap_columns(): from_even = lax.ppermute(even_cells, 'gx', pairs(count, 0))  21.6 us
    ppermute x4, waiting for transfers between devices, swap_rows(): second = lax.ppermute(first, 'gy', [(0, low + 1), (count - 1, low)])  13 us
    ppermute x4, waiting for transfers between devices, swap_rows(): straight = lax.ppermute(direct, 'gy', near + far)  8.1 us
  transfers between devices with their start and end apart: 30, of which 11 were waited for; matrix products, arithmetic and copies ran while one was open for 0% of the time, Pallas kernels for 5%

profile of v3, /device:TPU:15, one launch (start us, length us, event | category | flops | bytes accessed | tf_op | source)
XLA Modules:
  0.0 209.5 jit_solution(15594340432074622892)
XLA Ops:
  0.1 1.6 copy-done
  3.1 6.1 %collective-permute-start = (f32[2,256,128]{2,1,0:T(8,128)}, f32[2,256,128]{2,1,0:T(8,128)S(1)}, u32[]{:S(2)}, u32[]{:S(2)}) collective-permute-start(f32[2,256,128]{2,1,0:T(8,128)} %get-tuple-element.49), channel_id=1, source_target_pairs={{16,32},{48,64},{80,96},{112,128},{144,160},{176,192},{208,224},{3... | collective-permute-start | bytes 786440 | tf_op jit(solution)/shard_map/ppermute | solution.py:40
  13.2 4.7 %shard_map.56 = (f32[4,2,256,256]{3,2,1,0:T(8,128)S(1)}, bf16[4,8,256,256]{3,2,1,0:T(8,128)(2,1)S(1)}, f32[4,256,256]{2,1,0:T(8,128)S(1)}) custom-call(s32[13]{0:T(128)S(1)} %concatenate.4.meta, f32[2,256,256]{2,1,0:T(8,128)S(1)} %copy-done.3, f32[4,256,256]{2,1,0:T(8,128)S(1)} %bitcast.7), custom_call_target="tpu_custom_call" | custom-call | flops 1000000000 | bytes 8912896 | tf_op jit(solution)/shard_map/pallas_call | solution.py:440
  17.8 4.2 %collective-permute-done.1.side_even = f32[2,256,128]{2,1,0:T(8,128)S(1)} collective-permute-done((f32[2,256,128]{2,1,0:T(8,128)S(1)}, f32[2,256,128]{2,1,0:T(8,128)S(1)}, u32[]{:S(2)}, u32[]{:S(2)}) %collective-permute-start.1) | collective-permute-done | bytes 262176 | tf_op jit(solution)/shard_map/ppermute | solution.py:41
  23.3 2.0 collective-permute-start.5
  25.4 9.8 %collective-permute-start.4 = (f32[128,896]{1,0:T(8,128)S(1)}, f32[128,896]{1,0:T(8,128)S(1)}, u32[]{:S(2)}, u32[]{:S(2)}) collective-permute-start(f32[128,896]{1,0:T(8,128)S(1)} %get-tuple-element.57), channel_id=1, source_target_pairs={{1,2},{3,4},{5,6},{9,10},{11,12},{13,14},{2,1},{4,3},{6,5},{10,9},... | collective-permute-start | bytes 1376264 | tf_op jit(solution)/shard_map/ppermute | solution.py:32
  36.5 2.5 %collective-permute-start.2 = (f32[2,256,128]{2,1,0:T(8,128)S(1)}, f32[2,256,128]{2,1,0:T(8,128)S(1)}, u32[]{:S(2)}, u32[]{:S(2)}) collective-permute-start(f32[2,256,128]{2,1,0:T(8,128)S(1)} %get-tuple-element.53), channel_id=1, source_target_pairs={{16,32},{48,64},{80,96},{112,128},{144,160},{176,192},{208,224},{3... | collective-permute-start | bytes 786440 | tf_op jit(solution)/shard_map/ppermute | solution.py:40
  40.5 9.8 %collective-permute-done.2.side_odd = f32[2,256,128]{2,1,0:T(8,128)S(1)} collective-permute-done((f32[2,256,128]{2,1,0:T(8,128)S(1)}, f32[2,256,128]{2,1,0:T(8,128)S(1)}, u32[]{:S(2)}, u32[]{:S(2)}) %collective-permute-start.2) | collective-permute-done | bytes 262176 | tf_op jit(solution)/shard_map/ppermute | solution.py:40
  50.3 7.1 %collective-permute-done.3.side_even = f32[2,256,128]{2,1,0:T(8,128)S(1)} collective-permute-done((f32[2,256,128]{2,1,0:T(8,128)S(1)}, f32[2,256,128]{2,1,0:T(8,128)S(1)}, u32[]{:S(2)}, u32[]{:S(2)}) %collective-permute-start.3) | collective-permute-done | bytes 262176 | tf_op jit(solution)/shard_map/ppermute | solution.py:41
  58.5 6.6 %shard_map.59 = (f32[2,768,768]{2,1,0:T(8,128)S(1)}, f32[2,768,768]{2,1,0:T(8,128)S(1)}, f32[128,896]{1,0:T(8,128)S(1)}, f32[128,640]{1,0:T(8,128)S(1)}, f32[2,1...) custom-call(s32[13]{0:T(128)S(1)} %concatenate.4.meta, ...), custom_call_target="tpu_custom_call", output_to_operand_aliasing={{0}: (1, {}), {1}: (2, {})} | custom-call | flops 1073741824 | bytes 30736384 | tf_op jit(solution)/shard_map/pallas_call | solution.py:440
  66.5 9.6 %collective-permute-start.8 = (f32[128,896]{1,0:T(8,128)S(1)}, f32[128,896]{1,0:T(8,128)S(1)}, u32[]{:S(2)}, u32[]{:S(2)}) collective-permute-start(f32[128,896]{1,0:T(8,128)S(1)} %get-tuple-element.64), channel_id=1, source_target_pairs={{1,2},{3,4},{5,6},{9,10},{11,12},{13,14},{2,1},{4,3},{6,5},{10,9},... | collective-permute-start | bytes 1376264 | tf_op jit(solution)/shard_map/ppermute | solution.py:32
  77.4 5.0 %collective-permute-done.8.direct = f32[128,896]{1,0:T(8,128)S(1)} collective-permute-done((f32[128,896]{1,0:T(8,128)S(1)}, f32[128,896]{1,0:T(8,128)S(1)}, u32[]{:S(2)}, u32[]{:S(2)}) %collective-permute-start.8) | collective-permute-done | bytes 458784 | tf_op jit(solution)/shard_map/ppermute | solution.py:32
  82.4 7.0 %collective-permute-done.10.relayed = f32[128,640]{1,0:T(8,128)S(1)} collective-permute-done((f32[128,640]{1,0:T(8,128)S(1)}, f32[128,640]{1,0:T(8,128)S(1)}, u32[]{:S(2)}, u32[]{:S(2)}) %collective-permute-start.10) | collective-permute-done | bytes 327712 | tf_op jit(solution)/shard_map/ppermute | solution.py:34
  90.2 1.9 collective-permute-start.12
  92.2 15.8 %collective-permute-start.13 = (f32[2,256,256]{2,1,0:T(8,128)S(1)}, f32[2,256,256]{2,1,0:T(8,128)S(1)}, u32[]{:S(2)}, u32[]{:S(2)}) collective-permute-start(f32[2,256,256]{2,1,0:T(8,128)S(1)} %get-tuple-element.69), channel_id=1, source_target_pairs={{0,16},{32,48},{64,80},{96,112},{128,144},{160,176},{192,208},{224... | collective-permute-start | bytes 1572872 | tf_op jit(solution)/shard_map/ppermute | solution.py:41
  108.0 6.6 %collective-permute-done.13.band_even = f32[2,256,256]{2,1,0:T(8,128)S(1)} collective-permute-done((f32[2,256,256]{2,1,0:T(8,128)S(1)}, f32[2,256,256]{2,1,0:T(8,128)S(1)}, u32[]{:S(2)}, u32[]{:S(2)}) %collective-permute-start.13) | collective-permute-done | bytes 524320 | tf_op jit(solution)/shard_map/ppermute | solution.py:41
  117.2 1.9 collective-permute-start.14
  119.2 2.5 %collective-permute-start.15 = (f32[2,128,256]{2,1,0:T(8,128)S(1)}, f32[2,128,256]{2,1,0:T(8,128)S(1)}, u32[]{:S(2)}, u32[]{:S(2)}) collective-permute-start(f32[2,128,256]{2,1,0:T(8,128)S(1)} %get-tuple-element.72), channel_id=1, source_target_pairs={{0,16},{32,48},{64,80},{96,112},{128,144},{160,176},{192,208},{224... | collective-permute-start | bytes 786440 | tf_op jit(solution)/shard_map/ppermute | solution.py:41
  121.7 6.5 %collective-permute-start.18 = (f32[128,896]{1,0:T(8,128)S(1)}, f32[128,896]{1,0:T(8,128)S(1)}, u32[]{:S(2)}, u32[]{:S(2)}) collective-permute-start(f32[128,896]{1,0:T(8,128)S(1)} %get-tuple-element.77), channel_id=1, source_target_pairs={{1,2},{3,4},{5,6},{9,10},{11,12},{13,14},{2,1},{4,3},{6,5},{10,9},... | collective-permute-start | bytes 1376264 | tf_op jit(solution)/shard_map/ppermute | solution.py:32
  129.5 4.3 %collective-permute-start.16 = (f32[2,128,256]{2,1,0:T(8,128)S(1)}, f32[2,128,256]{2,1,0:T(8,128)S(1)}, u32[]{:S(2)}, u32[]{:S(2)}) collective-permute-start(f32[2,128,256]{2,1,0:T(8,128)S(1)} %get-tuple-element.73), channel_id=1, source_target_pairs={{16,32},{48,64},{80,96},{112,128},{144,160},{176,192},{208,224},{3... | collective-permute-start | bytes 786440 | tf_op jit(solution)/shard_map/ppermute | solution.py:40
  133.9 3.5 %collective-permute-start.17 = (f32[2,128,256]{2,1,0:T(8,128)S(1)}, f32[2,128,256]{2,1,0:T(8,128)S(1)}, u32[]{:S(2)}, u32[]{:S(2)}) collective-permute-start(f32[2,128,256]{2,1,0:T(8,128)S(1)} %get-tuple-element.74), channel_id=1, source_target_pairs={{0,16},{32,48},{64,80},{96,112},{128,144},{160,176},{192,208},{224... | collective-permute-start | bytes 786440 | tf_op jit(solution)/shard_map/ppermute | solution.py:41
  137.4 15.0 %collective-permute-done.16.lower_odd = f32[2,128,256]{2,1,0:T(8,128)S(1)} collective-permute-done((f32[2,128,256]{2,1,0:T(8,128)S(1)}, f32[2,128,256]{2,1,0:T(8,128)S(1)}, u32[]{:S(2)}, u32[]{:S(2)}) %collective-permute-start.16) | collective-permute-done | bytes 262176 | tf_op jit(solution)/shard_map/ppermute | solution.py:40
  152.4 2.6 %collective-permute-done.17.lower_even = f32[2,128,256]{2,1,0:T(8,128)S(1)} collective-permute-done((f32[2,128,256]{2,1,0:T(8,128)S(1)}, f32[2,128,256]{2,1,0:T(8,128)S(1)}, u32[]{:S(2)}, u32[]{:S(2)}) %collective-permute-start.17) | collective-permute-done | bytes 262176 | tf_op jit(solution)/shard_map/ppermute | solution.py:41
  156.4 6.6 %shard_map.63 = (f32[2,768,768]{2,1,0:T(8,128)S(1)}, f32[2,768,768]{2,1,0:T(8,128)S(1)}, f32[128,896]{1,0:T(8,128)S(1)}, f32[128,640]{1,0:T(8,128)S(1)}, f32[2,1...) custom-call(s32[13]{0:T(128)S(1)} %concatenate.4.meta, ...), custom_call_target="tpu_custom_call", output_to_operand_aliasing={{0}: (1, {}), {1}: (2, {})} | custom-call | flops 1073741824 | bytes 30212096 | tf_op jit(solution)/shard_map/pallas_call | solution.py:440
  164.4 7.1 %collective-permute-start.22 = (f32[128,896]{1,0:T(8,128)S(1)}, f32[128,896]{1,0:T(8,128)S(1)}, u32[]{:S(2)}, u32[]{:S(2)}) collective-permute-start(f32[128,896]{1,0:T(8,128)S(1)} %get-tuple-element.82), channel_id=1, source_target_pairs={{1,2},{3,4},{5,6},{9,10},{11,12},{13,14},{2,1},{4,3},{6,5},{10,9},... | collective-permute-start | bytes 1376264 | tf_op jit(solution)/shard_map/ppermute | solution.py:32
  172.8 2.4 %collective-permute-start.26 = (f32[2,256,128]{2,1,0:T(8,128)S(1)}, f32[2,256,128]{2,1,0:T(8,128)S(1)}, u32[]{:S(2)}, u32[]{:S(2)}) collective-permute-start(f32[2,256,128]{2,1,0:T(8,128)S(1)} %get-tuple-element.86), channel_id=1, source_target_pairs={{16,32},{48,64},{80,96},{112,128},{144,160},{176,192},{208,224},{3... | collective-permute-start | bytes 786440 | tf_op jit(solution)/shard_map/ppermute | solution.py:40
  175.2 2.0 collective-permute-start.27
  177.2 3.1 %collective-permute-done.22.direct = f32[128,896]{1,0:T(8,128)S(1)} collective-permute-done((f32[128,896]{1,0:T(8,128)S(1)}, f32[128,896]{1,0:T(8,128)S(1)}, u32[]{:S(2)}, u32[]{:S(2)}) %collective-permute-start.22) | collective-permute-done | bytes 458784 | tf_op jit(solution)/shard_map/ppermute | solution.py:32
  180.3 6.0 %collective-permute-done.24.relayed = f32[128,640]{1,0:T(8,128)S(1)} collective-permute-done((f32[128,640]{1,0:T(8,128)S(1)}, f32[128,640]{1,0:T(8,128)S(1)}, u32[]{:S(2)}, u32[]{:S(2)}) %collective-permute-start.24) | collective-permute-done | bytes 327712 | tf_op jit(solution)/shard_map/ppermute | solution.py:34
  187.0 3.7 %collective-permute-start.28 = (f32[2,256,128]{2,1,0:T(8,128)S(1)}, f32[2,256,128]{2,1,0:T(8,128)S(1)}, u32[]{:S(2)}, u32[]{:S(2)}) collective-permute-start(f32[2,256,128]{2,1,0:T(8,128)S(1)} %get-tuple-element.91), channel_id=1, source_target_pairs={{16,32},{48,64},{80,96},{112,128},{144,160},{176,192},{208,224},{3... | collective-permute-start | bytes 786440 | tf_op jit(solution)/shard_map/ppermute | solution.py:40
  190.7 13.5 %collective-permute-start.29 = (f32[2,256,128]{2,1,0:T(8,128)S(1)}, f32[2,256,128]{2,1,0:T(8,128)S(1)}, u32[]{:S(2)}, u32[]{:S(2)}) collective-permute-start(f32[2,256,128]{2,1,0:T(8,128)S(1)} %get-tuple-element.92), channel_id=1, source_target_pairs={{0,16},{32,48},{64,80},{96,112},{128,144},{160,176},{192,208},{224... | collective-permute-start | bytes 786440 | tf_op jit(solution)/shard_map/ppermute | solution.py:41
  204.2 2.6 %shard_map.65 = (f32[2,512,512]{2,1,0:T(8,128)}, f32[2,256,128]{2,1,0:T(8,128)S(1)}, f32[2,256,128]{2,1,0:T(8,128)S(1)}) custom-call(s32[13]{0:T(128)S(1)} %concatenate.4.meta, f32[2,768,768]{2,1,0:T(8,128)S(1)} %get-tuple-element.80.field, f32[2,768,768]{2,1,0:T(8,128)S(1)} %get-tuple-element.81.total, f32[2,128,768]{2,1,0:T(8,128)S(1)} %get-tuple-element.85.line, ...), custom_call_target="tpu_custom_call" | custom-call | bytes 14155776 | tf_op jit(solution)/shard_map/pallas_call | solution.py:440
  (52 shorter events, 24.8 us)
Async XLA Ops:
  0.1 1.6 copy-start
  1.7 20.3 %copy-start.1 = (f32[2,512,512]{2,1,0:T(8,128)S(1)}, f32[2,512,512]{2,1,0:T(8,128)}, u32[]{:S(2)}) copy-start(f32[2,512,512]{2,1,0:T(8,128)} %own.5) | copy-start | bytes 6291460
  3.1 14.8 %collective-permute-start = (f32[2,256,128]{2,1,0:T(8,128)}, f32[2,256,128]{2,1,0:T(8,128)S(1)}, u32[]{:S(2)}, u32[]{:S(2)}) collective-permute-start(f32[2,256,128]{2,1,0:T(8,128)} %get-tuple-element.49), channel_id=1, source_target_pairs={{16,32},{48,64},{80,96},{112,128},{144,160},{176,192},{208,224},{3... | collective-permute-start | bytes 786440 | tf_op jit(solution)/shard_map/ppermute | solution.py:40
  9.2 12.8 %collective-permute-start.1 = (f32[2,256,128]{2,1,0:T(8,128)S(1)}, f32[2,256,128]{2,1,0:T(8,128)S(1)}, u32[]{:S(2)}, u32[]{:S(2)}) collective-permute-start(f32[2,256,128]{2,1,0:T(8,128)S(1)} %get-tuple-element.50), channel_id=1, source_target_pairs={{0,16},{32,48},{64,80},{96,112},{128,144},{160,176},{192,208},{224... | collective-permute-start | bytes 786440 | tf_op jit(solution)/shard_map/ppermute | solution.py:41
  22.7 35.7 %collective-permute-start.7 = (f32[2,128,768]{2,1,0:T(8,128)S(1)}, f32[2,128,768]{2,1,0:T(8,128)S(1)}, u32[]{:S(2)}, u32[]{:S(2)}) collective-permute-start(f32[2,128,768]{2,1,0:T(8,128)S(1)} %get-tuple-element.59), channel_id=1, source_target_pairs={{0,1},{2,3},{4,5},{6,7},{8,9},{10,11},{12,13},{14,15},{1,0},{3,2},... | collective-permute-start | bytes 2359304 | tf_op jit(solution)/shard_map/ppermute | solution.py:33
  23.3 11.9 %collective-permute-start.5 = (f32[128,640]{1,0:T(8,128)S(1)}, f32[128,640]{1,0:T(8,128)S(1)}, u32[]{:S(2)}, u32[]{:S(2)}) collective-permute-start(f32[128,640]{1,0:T(8,128)S(1)} %get-tuple-element.58), channel_id=1, source_target_pairs={{1,2},{3,4},{5,6},{9,10},{11,12},{13,14},{2,1},{4,3},{6,5},{10,9},... | collective-permute-start | bytes 983048 | tf_op jit(solution)/shard_map/ppermute | solution.py:31
  25.4 33.1 %collective-permute-start.4 = (f32[128,896]{1,0:T(8,128)S(1)}, f32[128,896]{1,0:T(8,128)S(1)}, u32[]{:S(2)}, u32[]{:S(2)}) collective-permute-start(f32[128,896]{1,0:T(8,128)S(1)} %get-tuple-element.57), channel_id=1, source_target_pairs={{1,2},{3,4},{5,6},{9,10},{11,12},{13,14},{2,1},{4,3},{6,5},{10,9},... | collective-permute-start | bytes 1376264 | tf_op jit(solution)/shard_map/ppermute | solution.py:32
  35.2 23.2 %collective-permute-start.6 = (f32[128,640]{1,0:T(8,128)S(1)}, f32[128,640]{1,0:T(8,128)S(1)}, u32[]{:S(2)}, u32[]{:S(2)}) collective-permute-start(f32[128,640]{1,0:T(8,128)S(1)} %collective-permute-done.5.halo_detour), channel_id=1, source_target_pairs={{0,8},{15,7},{16,24},{31,23},{32,40},{47,39},{48,56},{63,55},{64,7... | collective-permute-start | bytes 983048 | tf_op jit(solution)/shard_map/ppermute | solution.py:34
  36.5 13.8 %collective-permute-start.2 = (f32[2,256,128]{2,1,0:T(8,128)S(1)}, f32[2,256,128]{2,1,0:T(8,128)S(1)}, u32[]{:S(2)}, u32[]{:S(2)}) collective-permute-start(f32[2,256,128]{2,1,0:T(8,128)S(1)} %get-tuple-element.53), channel_id=1, source_target_pairs={{16,32},{48,64},{80,96},{112,128},{144,160},{176,192},{208,224},{3... | collective-permute-start | bytes 786440 | tf_op jit(solution)/shard_map/ppermute | solution.py:40
  39.0 18.4 %collective-permute-start.3 = (f32[2,256,128]{2,1,0:T(8,128)S(1)}, f32[2,256,128]{2,1,0:T(8,128)S(1)}, u32[]{:S(2)}, u32[]{:S(2)}) collective-permute-start(f32[2,256,128]{2,1,0:T(8,128)S(1)} %get-tuple-element.54), channel_id=1, source_target_pairs={{0,16},{32,48},{64,80},{96,112},{128,144},{160,176},{192,208},{224... | collective-permute-start | bytes 786440 | tf_op jit(solution)/shard_map/ppermute | solution.py:41
  65.1 24.4 %collective-permute-start.11 = (f32[2,128,768]{2,1,0:T(8,128)S(1)}, f32[2,128,768]{2,1,0:T(8,128)S(1)}, u32[]{:S(2)}, u32[]{:S(2)}) collective-permute-start(f32[2,128,768]{2,1,0:T(8,128)S(1)} %get-tuple-element.66), channel_id=1, source_target_pairs={{0,1},{2,3},{4,5},{6,7},{8,9},{10,11},{12,13},{14,15},{1,0},{3,2},... | collective-permute-start | bytes 2359304 | tf_op jit(solution)/shard_map/ppermute | solution.py:33
  65.2 10.9 %collective-permute-start.9 = (f32[128,640]{1,0:T(8,128)S(1)}, f32[128,640]{1,0:T(8,128)S(1)}, u32[]{:S(2)}, u32[]{:S(2)}) collective-permute-start(f32[128,640]{1,0:T(8,128)S(1)} %get-tuple-element.65), channel_id=1, source_target_pairs={{1,2},{3,4},{5,6},{9,10},{11,12},{13,14},{2,1},{4,3},{6,5},{10,9},... | collective-permute-start | bytes 983048 | tf_op jit(solution)/shard_map/ppermute | solution.py:31
  66.5 15.9 %collective-permute-start.8 = (f32[128,896]{1,0:T(8,128)S(1)}, f32[128,896]{1,0:T(8,128)S(1)}, u32[]{:S(2)}, u32[]{:S(2)}) collective-permute-start(f32[128,896]{1,0:T(8,128)S(1)} %get-tuple-element.64), channel_id=1, source_target_pairs={{1,2},{3,4},{5,6},{9,10},{11,12},{13,14},{2,1},{4,3},{6,5},{10,9},... | collective-permute-start | bytes 1376264 | tf_op jit(solution)/shard_map/ppermute | solution.py:32
  76.1 13.4 %collective-permute-start.10 = (f32[128,640]{1,0:T(8,128)S(1)}, f32[128,640]{1,0:T(8,128)S(1)}, u32[]{:S(2)}, u32[]{:S(2)}) collective-permute-start(f32[128,640]{1,0:T(8,128)S(1)} %collective-permute-done.9.detour), channel_id=1, source_target_pairs={{0,8},{15,7},{16,24},{31,23},{32,40},{47,39},{48,56},{63,55},{64,7... | collective-permute-start | bytes 983048 | tf_op jit(solution)/shard_map/ppermute | solution.py:34
  90.2 17.7 %collective-permute-start.12 = (f32[2,256,256]{2,1,0:T(8,128)S(1)}, f32[2,256,256]{2,1,0:T(8,128)S(1)}, u32[]{:S(2)}, u32[]{:S(2)}) collective-permute-start(f32[2,256,256]{2,1,0:T(8,128)S(1)} %get-tuple-element.68), channel_id=1, source_target_pairs={{16,32},{48,64},{80,96},{112,128},{144,160},{176,192},{208,224},{3... | collective-permute-start | bytes 1572872 | tf_op jit(solution)/shard_map/ppermute | solution.py:40
  92.2 22.4 %collective-permute-start.13 = (f32[2,256,256]{2,1,0:T(8,128)S(1)}, f32[2,256,256]{2,1,0:T(8,128)S(1)}, u32[]{:S(2)}, u32[]{:S(2)}) collective-permute-start(f32[2,256,256]{2,1,0:T(8,128)S(1)} %get-tuple-element.69), channel_id=1, source_target_pairs={{0,16},{32,48},{64,80},{96,112},{128,144},{160,176},{192,208},{224... | collective-permute-start | bytes 1572872 | tf_op jit(solution)/shard_map/ppermute | solution.py:41
  115.8 40.5 %collective-permute-start.21 = (f32[2,128,768]{2,1,0:T(8,128)S(1)}, f32[2,128,768]{2,1,0:T(8,128)S(1)}, u32[]{:S(2)}, u32[]{:S(2)}) collective-permute-start(f32[2,128,768]{2,1,0:T(8,128)S(1)} %get-tuple-element.79), channel_id=1, source_target_pairs={{0,1},{2,3},{4,5},{6,7},{8,9},{10,11},{12,13},{14,15},{1,0},{3,2},... | collective-permute-start | bytes 2359304 | tf_op jit(solution)/shard_map/ppermute | solution.py:33
  115.9 12.3 %collective-permute-start.19 = (f32[128,640]{1,0:T(8,128)S(1)}, f32[128,640]{1,0:T(8,128)S(1)}, u32[]{:S(2)}, u32[]{:S(2)}) collective-permute-start(f32[128,640]{1,0:T(8,128)S(1)} %get-tuple-element.78), channel_id=1, source_target_pairs={{1,2},{3,4},{5,6},{9,10},{11,12},{13,14},{2,1},{4,3},{6,5},{10,9},... | collective-permute-start | bytes 983048 | tf_op jit(solution)/shard_map/ppermute | solution.py:31
  117.2 12.3 %collective-permute-start.14 = (f32[2,128,256]{2,1,0:T(8,128)S(1)}, f32[2,128,256]{2,1,0:T(8,128)S(1)}, u32[]{:S(2)}, u32[]{:S(2)}) collective-permute-start(f32[2,128,256]{2,1,0:T(8,128)S(1)} %get-tuple-element.71), channel_id=1, source_target_pairs={{16,32},{48,64},{80,96},{112,128},{144,160},{176,192},{208,224},{3... | collective-permute-start | bytes 786440 | tf_op jit(solution)/shard_map/ppermute | solution.py:40
  119.2 14.7 %collective-permute-start.15 = (f32[2,128,256]{2,1,0:T(8,128)S(1)}, f32[2,128,256]{2,1,0:T(8,128)S(1)}, u32[]{:S(2)}, u32[]{:S(2)}) collective-permute-start(f32[2,128,256]{2,1,0:T(8,128)S(1)} %get-tuple-element.72), channel_id=1, source_target_pairs={{0,16},{32,48},{64,80},{96,112},{128,144},{160,176},{192,208},{224... | collective-permute-start | bytes 786440 | tf_op jit(solution)/shard_map/ppermute | solution.py:41
  121.7 34.6 %collective-permute-start.18 = (f32[128,896]{1,0:T(8,128)S(1)}, f32[128,896]{1,0:T(8,128)S(1)}, u32[]{:S(2)}, u32[]{:S(2)}) collective-permute-start(f32[128,896]{1,0:T(8,128)S(1)} %get-tuple-element.77), channel_id=1, source_target_pairs={{1,2},{3,4},{5,6},{9,10},{11,12},{13,14},{2,1},{4,3},{6,5},{10,9},... | collective-permute-start | bytes 1376264 | tf_op jit(solution)/shard_map/ppermute | solution.py:32
  128.2 28.1 %collective-permute-start.20 = (f32[128,640]{1,0:T(8,128)S(1)}, f32[128,640]{1,0:T(8,128)S(1)}, u32[]{:S(2)}, u32[]{:S(2)}) collective-permute-start(f32[128,640]{1,0:T(8,128)S(1)} %collective-permute-done.19.halo_detour), channel_id=1, source_target_pairs={{0,8},{15,7},{16,24},{31,23},{32,40},{47,39},{48,56},{63,55},{64,7... | collective-permute-start | bytes 983048 | tf_op jit(solution)/shard_map/ppermute | solution.py:34
  129.5 22.8 %collective-permute-start.16 = (f32[2,128,256]{2,1,0:T(8,128)S(1)}, f32[2,128,256]{2,1,0:T(8,128)S(1)}, u32[]{:S(2)}, u32[]{:S(2)}) collective-permute-start(f32[2,128,256]{2,1,0:T(8,128)S(1)} %get-tuple-element.73), channel_id=1, source_target_pairs={{16,32},{48,64},{80,96},{112,128},{144,160},{176,192},{208,224},{3... | collective-permute-start | bytes 786440 | tf_op jit(solution)/shard_map/ppermute | solution.py:40
  133.9 21.1 %collective-permute-start.17 = (f32[2,128,256]{2,1,0:T(8,128)S(1)}, f32[2,128,256]{2,1,0:T(8,128)S(1)}, u32[]{:S(2)}, u32[]{:S(2)}) collective-permute-start(f32[2,128,256]{2,1,0:T(8,128)S(1)} %get-tuple-element.74), channel_id=1, source_target_pairs={{0,16},{32,48},{64,80},{96,112},{128,144},{160,176},{192,208},{224... | collective-permute-start | bytes 786440 | tf_op jit(solution)/shard_map/ppermute | solution.py:41
  163.0 23.3 %collective-permute-start.25 = (f32[2,128,768]{2,1,0:T(8,128)S(1)}, f32[2,128,768]{2,1,0:T(8,128)S(1)}, u32[]{:S(2)}, u32[]{:S(2)}) collective-permute-start(f32[2,128,768]{2,1,0:T(8,128)S(1)} %get-tuple-element.84), channel_id=1, source_target_pairs={{0,1},{2,3},{4,5},{6,7},{8,9},{10,11},{12,13},{14,15},{1,0},{3,2},... | collective-permute-start | bytes 2359304 | tf_op jit(solution)/shard_map/ppermute | solution.py:33
  163.1 8.4 %collective-permute-start.23 = (f32[128,640]{1,0:T(8,128)S(1)}, f32[128,640]{1,0:T(8,128)S(1)}, u32[]{:S(2)}, u32[]{:S(2)}) collective-permute-start(f32[128,640]{1,0:T(8,128)S(1)} %get-tuple-element.83), channel_id=1, source_target_pairs={{1,2},{3,4},{5,6},{9,10},{11,12},{13,14},{2,1},{4,3},{6,5},{10,9},... | collective-permute-start | bytes 983048 | tf_op jit(solution)/shard_map/ppermute | solution.py:31
  164.4 15.9 %collective-permute-start.22 = (f32[128,896]{1,0:T(8,128)S(1)}, f32[128,896]{1,0:T(8,128)S(1)}, u32[]{:S(2)}, u32[]{:S(2)}) collective-permute-start(f32[128,896]{1,0:T(8,128)S(1)} %get-tuple-element.82), channel_id=1, source_target_pairs={{1,2},{3,4},{5,6},{9,10},{11,12},{13,14},{2,1},{4,3},{6,5},{10,9},... | collective-permute-start | bytes 1376264 | tf_op jit(solution)/shard_map/ppermute | solution.py:32
  171.5 14.8 %collective-permute-start.24 = (f32[128,640]{1,0:T(8,128)S(1)}, f32[128,640]{1,0:T(8,128)S(1)}, u32[]{:S(2)}, u32[]{:S(2)}) collective-permute-start(f32[128,640]{1,0:T(8,128)S(1)} %collective-permute-done.23.detour), channel_id=1, source_target_pairs={{0,8},{15,7},{16,24},{31,23},{32,40},{47,39},{48,56},{63,55},{64,7... | collective-permute-start | bytes 983048 | tf_op jit(solution)/shard_map/ppermute | solution.py:34
  172.8 31.4 %collective-permute-start.26 = (f32[2,256,128]{2,1,0:T(8,128)S(1)}, f32[2,256,128]{2,1,0:T(8,128)S(1)}, u32[]{:S(2)}, u32[]{:S(2)}) collective-permute-start(f32[2,256,128]{2,1,0:T(8,128)S(1)} %get-tuple-element.86), channel_id=1, source_target_pairs={{16,32},{48,64},{80,96},{112,128},{144,160},{176,192},{208,224},{3... | collective-permute-start | bytes 786440 | tf_op jit(solution)/shard_map/ppermute | solution.py:40
  175.2 29.0 %collective-permute-start.27 = (f32[2,256,128]{2,1,0:T(8,128)S(1)}, f32[2,256,128]{2,1,0:T(8,128)S(1)}, u32[]{:S(2)}, u32[]{:S(2)}) collective-permute-start(f32[2,256,128]{2,1,0:T(8,128)S(1)} %get-tuple-element.87), channel_id=1, source_target_pairs={{0,16},{32,48},{64,80},{96,112},{128,144},{160,176},{192,208},{224... | collective-permute-start | bytes 786440 | tf_op jit(solution)/shard_map/ppermute | solution.py:41
  187.0 19.8 %collective-permute-start.28 = (f32[2,256,128]{2,1,0:T(8,128)S(1)}, f32[2,256,128]{2,1,0:T(8,128)S(1)}, u32[]{:S(2)}, u32[]{:S(2)}) collective-permute-start(f32[2,256,128]{2,1,0:T(8,128)S(1)} %get-tuple-element.91), channel_id=1, source_target_pairs={{16,32},{48,64},{80,96},{112,128},{144,160},{176,192},{208,224},{3... | collective-permute-start | bytes 786440 | tf_op jit(solution)/shard_map/ppermute | solution.py:40
  190.7 17.3 %collective-permute-start.29 = (f32[2,256,128]{2,1,0:T(8,128)S(1)}, f32[2,256,128]{2,1,0:T(8,128)S(1)}, u32[]{:S(2)}, u32[]{:S(2)}) collective-permute-start(f32[2,256,128]{2,1,0:T(8,128)S(1)} %get-tuple-element.92), channel_id=1, source_target_pairs={{0,16},{32,48},{64,80},{96,112},{128,144},{160,176},{192,208},{224... | collective-permute-start | bytes 786440 | tf_op jit(solution)/shard_map/ppermute | solution.py:41
  (2 other events, 2.3 us)

commit v4 on v3

--- a/solution.py
+++ b/solution.py
@@ -23,16 +23,19 @@
     return ups + [(b, a) for a, b in ups]
 
 
-def swap_rows(direct, detour, even_cells):
+def swap_odd(direct, detour):
     count = lax.axis_size("gy")
     low = count // 2 - 1
     far = [(low, low + 1), (low + 1, low)]
     near = [p for p in pairs(count, 1) if p not in far]
     first = lax.ppermute(detour, "gy", near + [(low, 0), (low + 1, count - 1)])
     straight = lax.ppermute(direct, "gy", near + far)
-    even = lax.ppermute(even_cells, "gy", pairs(count, 0))
     second = lax.ppermute(first, "gy", [(0, low + 1), (count - 1, low)])
-    return straight, first, second, even
+    return straight, first, second
+
+
+def swap_even(cells):
+    return lax.ppermute(cells, "gy", pairs(lax.axis_size("gy"), 0))
 
 
 def swap_columns(odd_cells, even_cells):
@@ -270,71 +273,62 @@
     return pl.ds(pl.multiple_of((1 - meta[GX_ODD]) * (wide - band.shape[2]), 128), band.shape[2])
 
 
-def rim_rows(meta, half):
-    odd_row = meta[GY_ODD]
-    return (
-        pl.ds(pl.multiple_of(odd_row * half, half), half),
-        pl.ds(pl.multiple_of((1 - odd_row) * half, half), half),
-    )
-
-
-def sides_kernel(meta, own, rim_odd, rim_even, mid_odd, mid_even):
-    tile, half = own.shape[1], rim_odd.shape[2]
-    far = tile - half
-    for rim, mid, cols in (
-        (rim_odd, mid_odd, odd_side(meta, rim_odd, tile)),
-        (rim_even, mid_even, even_side(meta, rim_even, tile)),
+def both_sides(meta, odd, even, wide):
+    return (odd, odd_side(meta, odd, wide)), (even, even_side(meta, even, wide))
+
+
+def strip(meta, odd, half, tile, margin):
+    low = meta[GY_ODD] if odd else 1 - meta[GY_ODD]
+    return pl.ds(pl.multiple_of(margin + low * (tile - half), half), half)
+
+
+def sides_kernel(meta, own, odd_a, odd_b, even_a, even_b, mid_a, mid_b):
+    tile, half = own.shape[1], odd_a.shape[1]
+    for rows, pair in (
+        (strip(meta, True, half, tile, 0), (odd_a, odd_b)),
+        (strip(meta, False, half, tile, 0), (even_a, even_b)),
+        (slice(half, tile - half), (mid_a, mid_b)),
     ):
-        rim[:, :half, :] = own[:, :half, cols]
-        rim[:, half:, :] = own[:, far:, cols]
-        mid[...] = own[:, half:far, cols]
-
-
-def edges_kernel(meta, own, side_odd, side_even, _, direct, detour, even, lines):
+        for out, cols in both_sides(meta, *pair, tile):
+            out[...] = own[:, rows, cols]
+
+
+def edge_kernel(odd, meta, own, side_odd, side_even, _, *outs):
+    *sends, line = outs
     tile, half = own.shape[1], side_odd.shape[2]
-    wide = lines.shape[2]
-    for at, rows in ((0, slice(0, half)), (half, slice(tile - half, tile))):
-        lines[:, at : at + half, half : half + tile] = own[:, rows, :]
-    lines[:, :, odd_side(meta, side_odd, wide)] = side_odd[...]
-    lines[:, :, even_side(meta, side_even, wide)] = side_even[...]
-    odd_rows, even_rows = rim_rows(meta, half)
-    pack(lines[0, odd_rows, :], lines[1, odd_rows, :], direct, detour)
-    even[...] = lines[:, even_rows, :]
-
-
-def inner_rows(half, tile):
-    return (
-        (slice(half, 2 * half), slice(0, half)),
-        (slice(tile, half + tile), slice(half, 2 * half)),
-        slice(2 * half, tile),
-    )
-
-
-def centre_kernel(meta, own, lines, side_odd, side_even, field, total):
+    wide = line.shape[2]
+    line[:, :, half : half + tile] = own[:, strip(meta, odd, half, tile, 0), :]
+    for side, cols in both_sides(meta, side_odd, side_even, wide):
+        line[:, :, cols] = side[...]
+    if odd:
+        pack(line[0], line[1], *sends)
+
+
+def centre_kernel(meta, own, odd_line, even_line, side_odd, side_even, field, total):
     tile, half = own.shape[1], side_odd.shape[2]
-    wide = lines.shape[2]
-    first, last, mid = inner_rows(half, tile)
-    for rows, outer in (first, last):
-        field[:, rows, :] = lines[:, outer, :]
+    wide = field.shape[2]
+    mid = slice(2 * half, tile)
+    field[:, strip(meta, True, half, tile, half), :] = odd_line[...]
+    field[:, strip(meta, False, half, tile, half), :] = even_line[...]
     field[:, mid, half : half + tile] = own[:, half : tile - half, :]
-    field[:, mid, odd_side(meta, side_odd, wide)] = side_odd[...]
-    field[:, mid, even_side(meta, side_even, wide)] = side_even[...]
+    for side, cols in both_sides(meta, side_odd, side_even, wide):
+        field[:, mid, cols] = side[...]
     total[...] = jnp.zeros_like(total)
 
 
-def bands_kernel(meta, total, direct, detour, relayed, even, band_odd, band_even, line):
-    wide, half = total.shape[2], even.shape[1]
+def odd_bands_kernel(meta, total, direct, detour, relayed, band_odd, band_even, line):
+    wide, half = total.shape[2], line.shape[1]
     unpack(meta, direct, detour, relayed, line)
-    odd_rows, even_rows = rim_rows(meta, half)
-    first, last, _ = inner_rows(half, wide - 2 * half)
-    for band, cols in (
-        (band_odd, odd_side(meta, band_odd, wide)),
-        (band_even, even_side(meta, band_even, wide)),
-    ):
-        for rows, outer in (first, last):
-            band[:, outer, :] = total[:, rows, cols]
-        band[:, odd_rows, :] = band[:, odd_rows, :] + line[:, :, cols]
-        band[:, even_rows, :] = band[:, even_rows, :] + even[:, :, cols]
+    rows = strip(meta, True, half, wide - 2 * half, half)
+    for band, cols in both_sides(meta, band_odd, band_even, wide):
+        band[...] = total[:, rows, cols] + line[:, :, cols]
+
+
+def even_bands_kernel(meta, total, line, band_odd, band_even):
+    wide, half = total.shape[2], line.shape[1]
+    rows = strip(meta, False, half, wide - 2 * half, half)
+    for band, cols in both_sides(meta, band_odd, band_even, wide):
+        band[...] = total[:, rows, cols] + line[:, :, cols]
 
 
 def clear_outside(meta, cells, half):
@@ -346,81 +340,87 @@
         cells[:, :, outside] = jnp.zeros((*cells.shape[:2], half), jnp.float32)
 
 
-def update_edges_kernel(
-    meta, field, total, line, even, band_odd, band_even, direct, detour, out_even, lines
+def update_edge_kernel(odd, meta, field, total, line, band_odd, band_even, *outs):
+    *sends, fresh = outs
+    wide, half = total.shape[2], line.shape[1]
+    rows = strip(meta, odd, half, wide - 2 * half, half)
+    fresh[...] = field[:, rows, :] - step_size * (total[:, rows, :] + line[...])
+    for band, cols in both_sides(meta, band_odd, band_even, wide):
+        fresh[:, :, cols] = fresh[:, :, cols] - step_size * band[...]
+    clear_outside(meta, fresh, half)
+    if odd:
+        pack(fresh[0], fresh[1], *sends)
+
+
+def update_centre_kernel(
+    meta,
+    field,
+    total,
+    odd_line,
+    even_line,
+    upper_odd,
+    upper_even,
+    lower_odd,
+    lower_even,
+    fresh,
+    zeros,
 ):
-    wide, half = total.shape[2], even.shape[1]
-    odd_rows, even_rows = rim_rows(meta, half)
-    first, last, _ = inner_rows(half, wide - 2 * half)
-    for rows, outer in (first, last):
-        lines[:, outer, :] = field[:, rows, :] - step_size * total[:, rows, :]
-    lines[:, odd_rows, :] = lines[:, odd_rows, :] - step_size * line[...]
-    lines[:, even_rows, :] = lines[:, even_rows, :] - step_size * even[...]
-    for band, cols in (
-        (band_odd, odd_side(meta, band_odd, wide)),
-        (band_even, even_side(meta, band_even, wide)),
-    ):
-        lines[:, :, cols] = lines[:, :, cols] - step_size * band[...]
-    clear_outside(meta, lines, half)
-    pack(lines[0, odd_rows, :], lines[1, odd_rows, :], direct, detour)
-    out_even[...] = lines[:, even_rows, :]
-
-
-def update_centre_kernel(
-    meta, field, total, lines, upper_odd, upper_even, lower_odd, lower_even, fresh, zeros
-):
-    wide, half = total.shape[2], lines.shape[1] // 2
-    first, last, mid = inner_rows(half, wide - 2 * half)
+    wide, half = total.shape[2], odd_line.shape[1]
+    tile = wide - 2 * half
+    mid = slice(2 * half, tile)
     fresh[:, mid, :] = field[:, mid, :] - step_size * total[:, mid, :]
     start = mid.start
-    for odd, even in ((upper_odd, upper_even), (lower_odd, lower_even)):
-        rows = slice(start, start + odd.shape[1])
-        for band, cols in ((odd, odd_side(meta, odd, wide)), (even, even_side(meta, even, wide))):
+    for pair in ((upper_odd, upper_even), (lower_odd, lower_even)):
+        rows = slice(start, start + pair[0].shape[1])
+        for band, cols in both_sides(meta, *pair, wide):
             fresh[:, rows, cols] = fresh[:, rows, cols] - step_size * band[...]
-        start += odd.shape[1]
+        start = rows.stop
     clear_outside(meta, fresh.at[:, mid, :], half)
-    for rows, outer in (first, last):
-        fresh[:, rows, :] = lines[:, outer, :]
+    fresh[:, strip(meta, True, half, tile, half), :] = odd_line[...]
+    fresh[:, strip(meta, False, half, tile, half), :] = even_line[...]
     zeros[...] = jnp.zeros_like(zeros)
 
 
-def almost_final_kernel(meta, field, total, line, even, mid_odd, mid_even, out, part_odd, part_even):
-    tile, half = out.shape[1], even.shape[1]
+def almost_final_kernel(
+    meta,
+    field,
+    total,
+    odd_line,
+    even_line,
+    mid_odd,
+    mid_even,
+    even_odd,
+    even_even,
+    out,
+    part_odd,
+    part_even,
+):
+    tile, half = out.shape[1], odd_line.shape[1]
     own = slice(half, half + tile)
-    odd_row = meta[GY_ODD]
-    far = tile - half
     out[...] = field[:, own, own] - step_size * total[:, own, own]
-    for at, rim in ((odd_row * far, line), ((1 - odd_row) * far, even)):
-        rows = pl.ds(pl.multiple_of(at, half), half)
-        out[:, rows, :] = out[:, rows, :] - step_size * rim[:, :, own]
-    for mid, part, cols in (
-        (mid_odd, part_odd, odd_side(meta, mid_odd, tile)),
-        (mid_even, part_even, even_side(meta, mid_even, tile)),
+    odd_rows = strip(meta, True, half, tile, 0)
+    even_rows = strip(meta, False, half, tile, 0)
+    for rows, line in ((odd_rows, odd_line), (even_rows, even_line)):
+        out[:, rows, :] = out[:, rows, :] - step_size * line[:, :, own]
+    mid = slice(half, tile - half)
+    for rows, pair in ((mid, (mid_odd, mid_even)), (even_rows, (even_odd, even_even))):
+        for band, cols in both_sides(meta, *pair, tile):
+            out[:, rows, cols] = out[:, rows, cols] - step_size * band[...]
+    for part, cols in both_sides(meta, part_odd, part_even, tile):
+        part[...] = out[:, odd_rows, cols]
+
+
+def final_kernel(meta, _, part_odd, part_even, band_odd, band_even, out, ready, sems):
+    tile, half = out.shape[1], part_odd.shape[1]
+    rows = strip(meta, True, half, tile, 0)
+    copies = []
+    for (part, cols), band in zip(
+        both_sides(meta, part_odd, part_even, tile), (band_odd, band_even)
     ):
-        out[:, half:far, cols] = out[:, half:far, cols] - step_size * mid[...]
-        part[:, :half, :] = out[:, :half, cols]
-        part[:, half:, :] = out[:, far:, cols]
-
-
-def final_kernel(meta, _, part_odd, part_even, rim_odd, rim_even, out, ready, sems):
-    tile, half = out.shape[1], part_odd.shape[2]
-    copies = []
-    for i, (part, rim, cols) in enumerate(
-        (
-            (part_odd, rim_odd, odd_side(meta, part_odd, tile)),
-            (part_even, rim_even, even_side(meta, part_even, tile)),
-        )
-    ):
-        ready[i] = part[...] - step_size * rim[...]
-        for j, first in enumerate((0, tile - half)):
-            copies.append(
-                pltpu.make_async_copy(
-                    ready.at[i, :, pl.ds(j * half, half), :],
-                    out.at[:, pl.ds(first, half), cols],
-                    sems.at[len(copies)],
-                )
-            )
-            copies[-1].start()
+        i = len(copies)
+        ready[i] = part[...] - step_size * band[...]
+        copies.append(pltpu.make_async_copy(ready.at[i], out.at[:, rows, cols], sems.at[i]))
+        copies[-1].start()
     for copy in copies:
         copy.wait()
 
@@ -465,73 +465,69 @@
     places = jnp.stack([odd_col, odd_row, edge.astype(jnp.int32), relay.astype(jnp.int32)])
     meta = jnp.concatenate([places, counts[0], offsets[0, 0].reshape(-1)]).astype(jnp.int32)
 
-    column, band = (2, 2 * half, half), (2, 2 * half, side)
+    column, band = (2, half, half), (2, half, side)
     mid_column, mid_band = (2, tile - 2 * half, half), (2, tile // 2 - half, side)
-    whole, lines = (2, wide, wide), (2, 2 * half, wide)
-    line = (2, half, wide)
-    sends = ((half, wide + CUT), (half, wide - CUT), line)
-
-    *rims, mid_odd, mid_even = call(
-        sides_kernel,
-        places,
-        (object_field,),
-        (column, column, mid_column, mid_column),
-    )
-    rims = swap_columns(*rims)
-    mids = swap_columns(mid_odd, mid_even)
-    probes, tables, amps = call(
+    whole, line = (2, wide, wide), (2, half, wide)
+    parts = ((half, wide + CUT), (half, wide - CUT))
+
+    def step(kernel, *args, **kwargs):
+        return call(kernel, meta, *args, **kwargs)
+
+    sides = call(sides_kernel, places, (object_field,), (column,) * 4 + (mid_column,) * 2)
+    odd_sides = swap_columns(*sides[:2])
+    even_sides = swap_columns(*sides[2:4])
+    mids = swap_columns(*sides[4:])
+    probes, tables, amps = step(
         functools.partial(prepare_kernel, side, windows),
-        meta,
         (probe_field, measured[0, 0]),
         ((windows, 2, side, side), ((windows, 8, side, side), bf), (windows, side, side)),
         flops=10**9,
         room=12 * MIB,
     )
-    *edges, rows = call(edges_kernel, meta, (object_field, *rims), (*sends, lines), after=amps)
-    halos = swap_rows(*edges)
-    field, total = call(centre_kernel, meta, (object_field, rows, *mids), (whole, whole))
-    for iteration in range(ITERS):
-        last = iteration + 1 == ITERS
-        field, total, *rest = call(
+    *sends, odd_line = step(
+        functools.partial(edge_kernel, True), (object_field, *odd_sides), (*parts, line), after=amps
+    )
+    odd_halo = swap_odd(*sends)
+    (even_line,) = step(functools.partial(edge_kernel, False), (object_field, *even_sides), (line,), after=amps)
+    even_halo = swap_even(even_line)
+    field, total = step(centre_kernel, (object_field, odd_line, even_line, *mids), (whole, whole))
+    for i in range(1, ITERS + 1):
+        last = i == ITERS
+        field, total, *rest = step(
             functools.partial(gradient_kernel, side, windows),
-            meta,
-            (field, total, *halos, probes, tables, amps),
-            (whole, whole, *sends, *((mid_column,) * 2 if last else (mid_band,) * 4)),
+            (field, total, *odd_halo, even_halo, probes, tables, amps),
+            (whole, whole, *parts, line, *((mid_column,) * 2 if last else (mid_band,) * 4)),
             scratch=(pltpu.VMEM((2, side, side), bf),),
             aliases={1: 0, 2: 1},
             flops=windows * 16 * side**3,
             room=8 * MIB,
         )
-        rims = swap_rows(*rest[:3])
+        odd_rim = swap_odd(*rest[:2])
+        even_rim = swap_even(rest[2])
+        mids = swap_columns(*rest[3:5])
         shape = column if last else band
-        *bands, odd_line = call(bands_kernel, meta, (total, *rims), (shape, shape, line))
-        bands = swap_columns(*bands)
-        mids = swap_columns(*rest[3:5])
+        evens = step(even_bands_kernel, (total, even_rim), (shape, shape))
+        evens = swap_columns(*evens)
+        *odds, odd_rim = step(odd_bands_kernel, (total, *odd_rim), (shape, shape, line))
+        odds = swap_columns(*odds)
         if last:
             break
-        mids += swap_columns(*rest[5:])
-        *edges, rows = call(
-            update_edges_kernel,
-            meta,
-            (field, total, odd_line, rims[3], *bands),
-            (*sends, lines),
+        lower = swap_columns(*rest[5:])
+        (even_line,) = step(functools.partial(update_edge_kernel, False), (field, total, even_rim, *evens), (line,))
+        even_halo = swap_even(even_line)
+        *sends, odd_line = step(
+            functools.partial(update_edge_kernel, True), (field, total, odd_rim, *odds), (*parts, line)
         )
-        halos = swap_rows(*edges)
-        field, total = call(
-            update_centre_kernel, meta, (field, total, rows, *mids), (whole, whole)
-        )
-    updated, *parts = call(
-        almost_final_kernel,
-        meta,
-        (field, total, odd_line, rims[3], *mids),
-        (object_field.shape, column, column),
+        odd_halo = swap_odd(*sends)
+        field, total = step(update_centre_kernel, (field, total, odd_line, even_line, *mids, *lower), (whole, whole))
+    updated, *ends = step(
+        almost_final_kernel, (field, total, odd_rim, even_rim, *mids, *evens), (object_field.shape, column, column)
     )
-    (updated,) = call(
+    (updated,) = step(
         final_kernel,
-        meta,
-        (updated, *parts, *bands),
+        (updated, *ends, *odds),
         (object_field.shape,),
-        scratch=(pltpu.VMEM((2, *column), jnp.float32), pltpu.SemaphoreType.DMA((4,))),
+        scratch=(pltpu.VMEM((2, *column), jnp.float32), pltpu.SemaphoreType.DMA((2,))),
         aliases={1: 0},
         far=True,
     )

time: 212 us -> 211 us (level)
  waiting for transfers between devices: 67.5 us -> 58.7 us
  starting transfers between devices: 107 us -> 114 us
    ppermute x7 -> x10, waiting for transfers between devices: 21.6 us -> 11.8 us  [swap_columns(): from_even = lax.ppermute(even_cells, 'gx', pairs(count, 0))]
    ppermute x16, starting transfers between devices: 44.9 us -> 51.9 us  [the longest x4 37.3 us: swap_odd(): straight = lax.ppermute(direct, 'gy', near + far)]
    ppermute x7 -> x10, starting transfers between devices: 22.9 us -> 29.2 us  [swap_columns(): from_odd = lax.ppermute(odd_cells, 'gx', pairs(count, 1))]
    ppermute x7 -> x10, starting transfers between devices: 39 us -> 33.2 us  [swap_columns(): from_even = lax.ppermute(even_cells, 'gx', pairs(count, 0))]
    pallas_call x12 -> x16, Pallas kernels: 29.1 us -> 30.9 us  [call(): pl.pallas_call(kernel, out_shape=shapes, in_specs=[smem, anywhere if far...]
    ppermute x7 -> x10, waiting for transfers between devices: 24.8 us -> 26.4 us  [swap_columns(): from_odd = lax.ppermute(odd_cells, 'gx', pairs(count, 1))]
  transfers between devices with their start and end apart: 30 -> 36, of which waited for: 11 -> 11; matrix products, arithmetic and copies ran while one was open for 0% -> 0% of each run, Pallas kernels for 5% -> 7%
where the time goes in v4:
time: 211 us; the launch traced here: 210 us
  starting transfers between devices  114 us (54%)
  waiting for transfers between devices  58.7 us (28%)
  Pallas kernels  30.9 us (15%)
  local copies, waits for them, and re-layouts  4.8 us (2%)
    ppermute x4, starting transfers between devices, swap_odd(): straight = lax.ppermute(direct, 'gy', near + far)  37.3 us
    ppermute x10, starting transfers between devices, swap_columns(): from_even = lax.ppermute(even_cells, 'gx', pairs(count, 0))  33.2 us
    pallas_call x16, Pallas kernels, call(): pl.pallas_call(kernel, out_shape=shapes, in_specs=[smem, anywhere if far...  30.9 us
    ppermute x10, starting transfers between devices, swap_columns(): from_odd = lax.ppermute(odd_cells, 'gx', pairs(count, 1))  29.2 us
    ppermute x10, waiting for transfers between devices, swap_columns(): from_odd = lax.ppermute(odd_cells, 'gx', pairs(count, 1))  26.4 us
    ppermute x4, waiting for transfers between devices, swap_odd(): second = lax.ppermute(first, 'gy', [(0, low + 1), (count - 1, low)])  12.2 us
    ppermute x10, waiting for transfers between devices, swap_columns(): from_even = lax.ppermute(even_cells, 'gx', pairs(count, 0))  11.8 us
    ppermute x4, waiting for transfers between devices, swap_odd(): straight = lax.ppermute(direct, 'gy', near + far)  8.31 us
  transfers between devices with their start and end apart: 36, of which 11 were waited for; matrix products, arithmetic and copies ran while one was open for 0% of the time, Pallas kernels for 7%

profile of v4, /device:TPU:15, one launch (start us, length us, event | category | flops | bytes accessed | tf_op | source)
XLA Modules:
  0.0 210.0 jit_solution(9919687614903810106)
XLA Ops:
  3.0 6.1 %collective-permute-start.2 = (f32[2,128,128]{2,1,0:T(8,128)}, f32[2,128,128]{2,1,0:T(8,128)S(1)}, u32[]{:S(2)}, u32[]{:S(2)}) collective-permute-start(f32[2,128,128]{2,1,0:T(8,128)} %get-tuple-element.57), channel_id=1, source_target_pairs={{16,32},{48,64},{80,96},{112,128},{144,160},{176,192},{208,224},{3... | collective-permute-start | bytes 393224 | tf_op jit(solution)/shard_map/ppermute | solution.py:43
  16.6 4.7 %shard_map.56 = (f32[4,2,256,256]{3,2,1,0:T(8,128)S(1)}, bf16[4,8,256,256]{3,2,1,0:T(8,128)(2,1)S(1)}, f32[4,256,256]{2,1,0:T(8,128)S(1)}) custom-call(s32[13]{0:T(128)S(1)} %concatenate.4.meta, f32[2,256,256]{2,1,0:T(8,128)S(1)} %copy-done.3, f32[4,256,256]{2,1,0:T(8,128)S(1)} %bitcast.7), custom_call_target="tpu_custom_call" | custom-call | flops 1000000000 | bytes 8912896 | tf_op jit(solution)/shard_map/pallas_call | solution.py:440
  24.2 2.0 collective-permute-start.7
  26.2 10.8 %collective-permute-start.6 = (f32[128,896]{1,0:T(8,128)S(1)}, f32[128,896]{1,0:T(8,128)S(1)}, u32[]{:S(2)}, u32[]{:S(2)}) collective-permute-start(f32[128,896]{1,0:T(8,128)S(1)} %get-tuple-element.63), channel_id=1, source_target_pairs={{1,2},{3,4},{5,6},{9,10},{11,12},{13,14},{2,1},{4,3},{6,5},{10,9},... | collective-permute-start | bytes 1376264 | tf_op jit(solution)/shard_map/ppermute | solution.py:32
  38.3 2.4 %collective-permute-start.4 = (f32[2,256,128]{2,1,0:T(8,128)S(1)}, f32[2,256,128]{2,1,0:T(8,128)S(1)}, u32[]{:S(2)}, u32[]{:S(2)}) collective-permute-start(f32[2,256,128]{2,1,0:T(8,128)S(1)} %get-tuple-element.59), channel_id=1, source_target_pairs={{16,32},{48,64},{80,96},{112,128},{144,160},{176,192},{208,224},{3... | collective-permute-start | bytes 786440 | tf_op jit(solution)/shard_map/ppermute | solution.py:43
  41.8 10.8 %collective-permute-done.4.side_odd = f32[2,256,128]{2,1,0:T(8,128)S(1)} collective-permute-done((f32[2,256,128]{2,1,0:T(8,128)S(1)}, f32[2,256,128]{2,1,0:T(8,128)S(1)}, u32[]{:S(2)}, u32[]{:S(2)}) %collective-permute-start.4) | collective-permute-done | bytes 262176 | tf_op jit(solution)/shard_map/ppermute | solution.py:43
  52.6 6.9 %collective-permute-done.5.side_even = f32[2,256,128]{2,1,0:T(8,128)S(1)} collective-permute-done((f32[2,256,128]{2,1,0:T(8,128)S(1)}, f32[2,256,128]{2,1,0:T(8,128)S(1)}, u32[]{:S(2)}, u32[]{:S(2)}) %collective-permute-start.5) | collective-permute-done | bytes 262176 | tf_op jit(solution)/shard_map/ppermute | solution.py:44
  60.6 6.6 %shard_map.60 = (f32[2,768,768]{2,1,0:T(8,128)S(1)}, f32[2,768,768]{2,1,0:T(8,128)S(1)}, f32[128,896]{1,0:T(8,128)S(1)}, f32[128,640]{1,0:T(8,128)S(1)}, f32[2,1...) custom-call(s32[13]{0:T(128)S(1)} %concatenate.4.meta, ...), custom_call_target="tpu_custom_call", output_to_operand_aliasing={{0}: (1, {}), {1}: (2, {})} | custom-call | flops 1073741824 | bytes 30736384 | tf_op jit(solution)/shard_map/pallas_call | solution.py:440
  69.1 8.7 %collective-permute-start.10 = (f32[128,896]{1,0:T(8,128)S(1)}, f32[128,896]{1,0:T(8,128)S(1)}, u32[]{:S(2)}, u32[]{:S(2)}) collective-permute-start(f32[128,896]{1,0:T(8,128)S(1)} %get-tuple-element.69), channel_id=1, source_target_pairs={{1,2},{3,4},{5,6},{9,10},{11,12},{13,14},{2,1},{4,3},{6,5},{10,9},... | collective-permute-start | bytes 1376264 | tf_op jit(solution)/shard_map/ppermute | solution.py:32
  79.8 2.4 %collective-permute-start.16 = (f32[2,128,256]{2,1,0:T(8,128)S(1)}, f32[2,128,256]{2,1,0:T(8,128)S(1)}, u32[]{:S(2)}, u32[]{:S(2)}) collective-permute-start(f32[2,128,256]{2,1,0:T(8,128)S(1)} %get-tuple-element.76), channel_id=1, source_target_pairs={{16,32},{48,64},{80,96},{112,128},{144,160},{176,192},{208,224},{3... | collective-permute-start | bytes 786440 | tf_op jit(solution)/shard_map/ppermute | solution.py:43
  82.2 2.0 collective-permute-start.17
  84.2 4.3 %collective-permute-done.10.direct = f32[128,896]{1,0:T(8,128)S(1)} collective-permute-done((f32[128,896]{1,0:T(8,128)S(1)}, f32[128,896]{1,0:T(8,128)S(1)}, u32[]{:S(2)}, u32[]{:S(2)}) %collective-permute-start.10) | collective-permute-done | bytes 458784 | tf_op jit(solution)/shard_map/ppermute | solution.py:32
  88.5 5.2 %collective-permute-done.12.relayed = f32[128,640]{1,0:T(8,128)S(1)} collective-permute-done((f32[128,640]{1,0:T(8,128)S(1)}, f32[128,640]{1,0:T(8,128)S(1)}, u32[]{:S(2)}, u32[]{:S(2)}) %collective-permute-start.12) | collective-permute-done | bytes 327712 | tf_op jit(solution)/shard_map/ppermute | solution.py:33
  94.4 2.1 %collective-permute-start.13 = (f32[2,128,256]{2,1,0:T(8,128)S(1)}, f32[2,128,256]{2,1,0:T(8,128)S(1)}, u32[]{:S(2)}, u32[]{:S(2)}) collective-permute-start(f32[2,128,256]{2,1,0:T(8,128)S(1)} %get-tuple-element.72), channel_id=1, source_target_pairs={{16,32},{48,64},{80,96},{112,128},{144,160},{176,192},{208,224},{3... | collective-permute-start | bytes 786440 | tf_op jit(solution)/shard_map/ppermute | solution.py:43
  96.5 12.2 %collective-permute-start.14 = (f32[2,128,256]{2,1,0:T(8,128)S(1)}, f32[2,128,256]{2,1,0:T(8,128)S(1)}, u32[]{:S(2)}, u32[]{:S(2)}) collective-permute-start(f32[2,128,256]{2,1,0:T(8,128)S(1)} %get-tuple-element.73), channel_id=1, source_target_pairs={{0,16},{32,48},{64,80},{96,112},{128,144},{160,176},{192,208},{224... | collective-permute-start | bytes 786440 | tf_op jit(solution)/shard_map/ppermute | solution.py:44
  110.0 2.4 %collective-permute-done.14.band_even = f32[2,128,256]{2,1,0:T(8,128)S(1)} collective-permute-done((f32[2,128,256]{2,1,0:T(8,128)S(1)}, f32[2,128,256]{2,1,0:T(8,128)S(1)}, u32[]{:S(2)}, u32[]{:S(2)}) %collective-permute-start.14) | collective-permute-done | bytes 262176 | tf_op jit(solution)/shard_map/ppermute | solution.py:44
  113.3 2.4 %collective-permute-start.23 = (f32[128,640]{1,0:T(8,128)S(1)}, f32[128,640]{1,0:T(8,128)S(1)}, u32[]{:S(2)}, u32[]{:S(2)}) collective-permute-start(f32[128,640]{1,0:T(8,128)S(1)} %get-tuple-element.85), channel_id=1, source_target_pairs={{1,2},{3,4},{5,6},{9,10},{11,12},{13,14},{2,1},{4,3},{6,5},{10,9},... | collective-permute-start | bytes 983048 | tf_op jit(solution)/shard_map/ppermute | solution.py:31
  115.6 3.4 %collective-permute-start.18 = (f32[2,128,256]{2,1,0:T(8,128)S(1)}, f32[2,128,256]{2,1,0:T(8,128)S(1)}, u32[]{:S(2)}, u32[]{:S(2)}) collective-permute-start(f32[2,128,256]{2,1,0:T(8,128)S(1)} %get-tuple-element.78), channel_id=1, source_target_pairs={{16,32},{48,64},{80,96},{112,128},{144,160},{176,192},{208,224},{3... | collective-permute-start | bytes 786440 | tf_op jit(solution)/shard_map/ppermute | solution.py:43
  120.7 8.2 %collective-permute-start.22 = (f32[128,896]{1,0:T(8,128)S(1)}, f32[128,896]{1,0:T(8,128)S(1)}, u32[]{:S(2)}, u32[]{:S(2)}) collective-permute-start(f32[128,896]{1,0:T(8,128)S(1)} %get-tuple-element.84), channel_id=1, source_target_pairs={{1,2},{3,4},{5,6},{9,10},{11,12},{13,14},{2,1},{4,3},{6,5},{10,9},... | collective-permute-start | bytes 1376264 | tf_op jit(solution)/shard_map/ppermute | solution.py:32
  130.2 4.1 %collective-permute-start.20 = (f32[2,128,256]{2,1,0:T(8,128)S(1)}, f32[2,128,256]{2,1,0:T(8,128)S(1)}, u32[]{:S(2)}, u32[]{:S(2)}) collective-permute-start(f32[2,128,256]{2,1,0:T(8,128)S(1)} %get-tuple-element.80), channel_id=1, source_target_pairs={{16,32},{48,64},{80,96},{112,128},{144,160},{176,192},{208,224},{3... | collective-permute-start | bytes 786440 | tf_op jit(solution)/shard_map/ppermute | solution.py:43
  134.3 2.4 %collective-permute-start.21 = (f32[2,128,256]{2,1,0:T(8,128)S(1)}, f32[2,128,256]{2,1,0:T(8,128)S(1)}, u32[]{:S(2)}, u32[]{:S(2)}) collective-permute-start(f32[2,128,256]{2,1,0:T(8,128)S(1)} %get-tuple-element.81), channel_id=1, source_target_pairs={{0,16},{32,48},{64,80},{96,112},{128,144},{160,176},{192,208},{224... | collective-permute-start | bytes 786440 | tf_op jit(solution)/shard_map/ppermute | solution.py:44
  136.7 12.2 %collective-permute-done.20.lower_odd = f32[2,128,256]{2,1,0:T(8,128)S(1)} collective-permute-done((f32[2,128,256]{2,1,0:T(8,128)S(1)}, f32[2,128,256]{2,1,0:T(8,128)S(1)}, u32[]{:S(2)}, u32[]{:S(2)}) %collective-permute-start.20) | collective-permute-done | bytes 262176 | tf_op jit(solution)/shard_map/ppermute | solution.py:43
  149.0 2.0 collective-permute-done.21.lower_even
  152.4 6.6 %shard_map.66 = (f32[2,768,768]{2,1,0:T(8,128)S(1)}, f32[2,768,768]{2,1,0:T(8,128)S(1)}, f32[128,896]{1,0:T(8,128)S(1)}, f32[128,640]{1,0:T(8,128)S(1)}, f32[2,1...) custom-call(s32[13]{0:T(128)S(1)} %concatenate.4.meta, ...), custom_call_target="tpu_custom_call", output_to_operand_aliasing={{0}: (1, {}), {1}: (2, {})} | custom-call | flops 1073741824 | bytes 30212096 | tf_op jit(solution)/shard_map/pallas_call | solution.py:440
  160.4 9.7 %collective-permute-start.26 = (f32[128,896]{1,0:T(8,128)S(1)}, f32[128,896]{1,0:T(8,128)S(1)}, u32[]{:S(2)}, u32[]{:S(2)}) collective-permute-start(f32[128,896]{1,0:T(8,128)S(1)} %get-tuple-element.88), channel_id=1, source_target_pairs={{1,2},{3,4},{5,6},{9,10},{11,12},{13,14},{2,1},{4,3},{6,5},{10,9},... | collective-permute-start | bytes 1376264 | tf_op jit(solution)/shard_map/ppermute | solution.py:32
  171.4 2.4 %collective-permute-start.30 = (f32[2,256,128]{2,1,0:T(8,128)S(1)}, f32[2,256,128]{2,1,0:T(8,128)S(1)}, u32[]{:S(2)}, u32[]{:S(2)}) collective-permute-start(f32[2,256,128]{2,1,0:T(8,128)S(1)} %get-tuple-element.92), channel_id=1, source_target_pairs={{16,32},{48,64},{80,96},{112,128},{144,160},{176,192},{208,224},{3... | collective-permute-start | bytes 786440 | tf_op jit(solution)/shard_map/ppermute | solution.py:43
  175.2 4.0 %collective-permute-done.26.direct = f32[128,896]{1,0:T(8,128)S(1)} collective-permute-done((f32[128,896]{1,0:T(8,128)S(1)}, f32[128,896]{1,0:T(8,128)S(1)}, u32[]{:S(2)}, u32[]{:S(2)}) %collective-permute-start.26) | collective-permute-done | bytes 458784 | tf_op jit(solution)/shard_map/ppermute | solution.py:32
  179.2 6.9 %collective-permute-done.28.relayed = f32[128,640]{1,0:T(8,128)S(1)} collective-permute-done((f32[128,640]{1,0:T(8,128)S(1)}, f32[128,640]{1,0:T(8,128)S(1)}, u32[]{:S(2)}, u32[]{:S(2)}) %collective-permute-start.28) | collective-permute-done | bytes 327712 | tf_op jit(solution)/shard_map/ppermute | solution.py:33
  189.3 10.8 %collective-permute-start.33 = (f32[2,128,128]{2,1,0:T(8,128)S(1)}, f32[2,128,128]{2,1,0:T(8,128)S(1)}, u32[]{:S(2)}, u32[]{:S(2)}) collective-permute-start(f32[2,128,128]{2,1,0:T(8,128)S(1)} %get-tuple-element.95), channel_id=1, source_target_pairs={{0,16},{32,48},{64,80},{96,112},{128,144},{160,176},{192,208},{224... | collective-permute-start | bytes 393224 | tf_op jit(solution)/shard_map/ppermute | solution.py:44
  200.2 2.4 %collective-permute-start.34 = (f32[2,128,128]{2,1,0:T(8,128)S(1)}, f32[2,128,128]{2,1,0:T(8,128)S(1)}, u32[]{:S(2)}, u32[]{:S(2)}) collective-permute-start(f32[2,128,128]{2,1,0:T(8,128)S(1)} %get-tuple-element.99), channel_id=1, source_target_pairs={{16,32},{48,64},{80,96},{112,128},{144,160},{176,192},{208,224},{3... | collective-permute-start | bytes 393224 | tf_op jit(solution)/shard_map/ppermute | solution.py:43
  202.7 2.6 %shard_map.69 = (f32[2,512,512]{2,1,0:T(8,128)}, f32[2,128,128]{2,1,0:T(8,128)S(1)}, f32[2,128,128]{2,1,0:T(8,128)S(1)}) custom-call(s32[13]{0:T(128)S(1)} %concatenate.4.meta, f32[2,768,768]{2,1,0:T(8,128)S(1)} %get-tuple-element.86.field, f32[2,768,768]{2,1,0:T(8,128)S(1)} %get-tuple-element.87.total, f32[2,128,768]{2,1,0:T(8,128)S(1)} %get-tuple-element.90.odd_line, ...), custom_call_target="tpu_custom_call" | custom-call | bytes 14155776 | tf_op jit(solution)/shard_map/pallas_call | solution.py:440
  205.2 3.3 %collective-permute-done.34.band_odd = f32[2,128,128]{2,1,0:T(8,128)S(1)} collective-permute-done((f32[2,128,128]{2,1,0:T(8,128)S(1)}, f32[2,128,128]{2,1,0:T(8,128)S(1)}, u32[]{:S(2)}, u32[]{:S(2)}) %collective-permute-start.34) | collective-permute-done | bytes 131104 | tf_op jit(solution)/shard_map/ppermute | solution.py:43
  (68 shorter events, 35.6 us)
Async XLA Ops:
  3.0 18.2 %collective-permute-start.2 = (f32[2,128,128]{2,1,0:T(8,128)}, f32[2,128,128]{2,1,0:T(8,128)S(1)}, u32[]{:S(2)}, u32[]{:S(2)}) collective-permute-start(f32[2,128,128]{2,1,0:T(8,128)} %get-tuple-element.57), channel_id=1, source_target_pairs={{16,32},{48,64},{80,96},{112,128},{144,160},{176,192},{208,224},{3... | collective-permute-start | bytes 393224 | tf_op jit(solution)/shard_map/ppermute | solution.py:43
  9.1 12.1 %collective-permute-start.3 = (f32[2,128,128]{2,1,0:T(8,128)S(1)}, f32[2,128,128]{2,1,0:T(8,128)S(1)}, u32[]{:S(2)}, u32[]{:S(2)}) collective-permute-start(f32[2,128,128]{2,1,0:T(8,128)S(1)} %get-tuple-element.58), channel_id=1, source_target_pairs={{0,16},{32,48},{64,80},{96,112},{128,144},{160,176},{192,208},{224... | collective-permute-start | bytes 393224 | tf_op jit(solution)/shard_map/ppermute | solution.py:44
  9.2 14.2 %collective-permute-start = (f32[2,128,128]{2,1,0:T(8,128)S(1)}, f32[2,128,128]{2,1,0:T(8,128)S(1)}, u32[]{:S(2)}, u32[]{:S(2)}) collective-permute-start(f32[2,128,128]{2,1,0:T(8,128)S(1)} %get-tuple-element.53), channel_id=1, source_target_pairs={{16,32},{48,64},{80,96},{112,128},{144,160},{176,192},{208,224},{3... | collective-permute-start | bytes 393224 | tf_op jit(solution)/shard_map/ppermute | solution.py:43
  11.2 12.3 %collective-permute-start.1 = (f32[2,128,128]{2,1,0:T(8,128)S(1)}, f32[2,128,128]{2,1,0:T(8,128)S(1)}, u32[]{:S(2)}, u32[]{:S(2)}) collective-permute-start(f32[2,128,128]{2,1,0:T(8,128)S(1)} %get-tuple-element.54), channel_id=1, source_target_pairs={{0,16},{32,48},{64,80},{96,112},{128,144},{160,176},{192,208},{224... | collective-permute-start | bytes 393224 | tf_op jit(solution)/shard_map/ppermute | solution.py:44
  21.9 38.7 %collective-permute-start.9 = (f32[2,128,768]{2,1,0:T(8,128)S(1)}, f32[2,128,768]{2,1,0:T(8,128)S(1)}, u32[]{:S(2)}, u32[]{:S(2)}) collective-permute-start(f32[2,128,768]{2,1,0:T(8,128)S(1)} %shard_map.58.even_line), channel_id=1, source_target_pairs={{0,1},{2,3},{4,5},{6,7},{8,9},{10,11},{12,13},{14,15},{1,0},{3,2},... | collective-permute-start | bytes 2359304 | tf_op jit(solution)/shard_map/ppermute | solution.py:38
  24.2 12.8 %collective-permute-start.7 = (f32[128,640]{1,0:T(8,128)S(1)}, f32[128,640]{1,0:T(8,128)S(1)}, u32[]{:S(2)}, u32[]{:S(2)}) collective-permute-start(f32[128,640]{1,0:T(8,128)S(1)} %get-tuple-element.64), channel_id=1, source_target_pairs={{1,2},{3,4},{5,6},{9,10},{11,12},{13,14},{2,1},{4,3},{6,5},{10,9},... | collective-permute-start | bytes 983048 | tf_op jit(solution)/shard_map/ppermute | solution.py:31
  26.2 34.4 %collective-permute-start.6 = (f32[128,896]{1,0:T(8,128)S(1)}, f32[128,896]{1,0:T(8,128)S(1)}, u32[]{:S(2)}, u32[]{:S(2)}) collective-permute-start(f32[128,896]{1,0:T(8,128)S(1)} %get-tuple-element.63), channel_id=1, source_target_pairs={{1,2},{3,4},{5,6},{9,10},{11,12},{13,14},{2,1},{4,3},{6,5},{10,9},... | collective-permute-start | bytes 1376264 | tf_op jit(solution)/shard_map/ppermute | solution.py:32
  37.0 23.6 %collective-permute-start.8 = (f32[128,640]{1,0:T(8,128)S(1)}, f32[128,640]{1,0:T(8,128)S(1)}, u32[]{:S(2)}, u32[]{:S(2)}) collective-permute-start(f32[128,640]{1,0:T(8,128)S(1)} %collective-permute-done.7.halo_detour), channel_id=1, source_target_pairs={{0,8},{15,7},{16,24},{31,23},{32,40},{47,39},{48,56},{63,55},{64,7... | collective-permute-start | bytes 983048 | tf_op jit(solution)/shard_map/ppermute | solution.py:33
  38.3 14.3 %collective-permute-start.4 = (f32[2,256,128]{2,1,0:T(8,128)S(1)}, f32[2,256,128]{2,1,0:T(8,128)S(1)}, u32[]{:S(2)}, u32[]{:S(2)}) collective-permute-start(f32[2,256,128]{2,1,0:T(8,128)S(1)} %get-tuple-element.59), channel_id=1, source_target_pairs={{16,32},{48,64},{80,96},{112,128},{144,160},{176,192},{208,224},{3... | collective-permute-start | bytes 786440 | tf_op jit(solution)/shard_map/ppermute | solution.py:43
  40.7 18.8 %collective-permute-start.5 = (f32[2,256,128]{2,1,0:T(8,128)S(1)}, f32[2,256,128]{2,1,0:T(8,128)S(1)}, u32[]{:S(2)}, u32[]{:S(2)}) collective-permute-start(f32[2,256,128]{2,1,0:T(8,128)S(1)} %get-tuple-element.60), channel_id=1, source_target_pairs={{0,16},{32,48},{64,80},{96,112},{128,144},{160,176},{192,208},{224... | collective-permute-start | bytes 786440 | tf_op jit(solution)/shard_map/ppermute | solution.py:44
  67.2 11.9 %collective-permute-start.15 = (f32[2,128,768]{2,1,0:T(8,128)S(1)}, f32[2,128,768]{2,1,0:T(8,128)S(1)}, u32[]{:S(2)}, u32[]{:S(2)}) collective-permute-start(f32[2,128,768]{2,1,0:T(8,128)S(1)} %get-tuple-element.75), channel_id=1, source_target_pairs={{0,1},{2,3},{4,5},{6,7},{8,9},{10,11},{12,13},{14,15},{1,0},{3,2},... | collective-permute-start | bytes 2359304 | tf_op jit(solution)/shard_map/ppermute | solution.py:38
  69.1 19.3 %collective-permute-start.10 = (f32[128,896]{1,0:T(8,128)S(1)}, f32[128,896]{1,0:T(8,128)S(1)}, u32[]{:S(2)}, u32[]{:S(2)}) collective-permute-start(f32[128,896]{1,0:T(8,128)S(1)} %get-tuple-element.69), channel_id=1, source_target_pairs={{1,2},{3,4},{5,6},{9,10},{11,12},{13,14},{2,1},{4,3},{6,5},{10,9},... | collective-permute-start | bytes 1376264 | tf_op jit(solution)/shard_map/ppermute | solution.py:32
  77.8 15.9 %collective-permute-start.12 = (f32[128,640]{1,0:T(8,128)S(1)}, f32[128,640]{1,0:T(8,128)S(1)}, u32[]{:S(2)}, u32[]{:S(2)}) collective-permute-start(f32[128,640]{1,0:T(8,128)S(1)} %collective-permute-done.11.detour), channel_id=1, source_target_pairs={{0,8},{15,7},{16,24},{31,23},{32,40},{47,39},{48,56},{63,55},{64,7... | collective-permute-start | bytes 983048 | tf_op jit(solution)/shard_map/ppermute | solution.py:33
  79.8 28.9 %collective-permute-start.16 = (f32[2,128,256]{2,1,0:T(8,128)S(1)}, f32[2,128,256]{2,1,0:T(8,128)S(1)}, u32[]{:S(2)}, u32[]{:S(2)}) collective-permute-start(f32[2,128,256]{2,1,0:T(8,128)S(1)} %get-tuple-element.76), channel_id=1, source_target_pairs={{16,32},{48,64},{80,96},{112,128},{144,160},{176,192},{208,224},{3... | collective-permute-start | bytes 786440 | tf_op jit(solution)/shard_map/ppermute | solution.py:43
  82.2 26.9 %collective-permute-start.17 = (f32[2,128,256]{2,1,0:T(8,128)S(1)}, f32[2,128,256]{2,1,0:T(8,128)S(1)}, u32[]{:S(2)}, u32[]{:S(2)}) collective-permute-start(f32[2,128,256]{2,1,0:T(8,128)S(1)} %get-tuple-element.77), channel_id=1, source_target_pairs={{0,16},{32,48},{64,80},{96,112},{128,144},{160,176},{192,208},{224... | collective-permute-start | bytes 786440 | tf_op jit(solution)/shard_map/ppermute | solution.py:44
  94.4 15.6 %collective-permute-start.13 = (f32[2,128,256]{2,1,0:T(8,128)S(1)}, f32[2,128,256]{2,1,0:T(8,128)S(1)}, u32[]{:S(2)}, u32[]{:S(2)}) collective-permute-start(f32[2,128,256]{2,1,0:T(8,128)S(1)} %get-tuple-element.72), channel_id=1, source_target_pairs={{16,32},{48,64},{80,96},{112,128},{144,160},{176,192},{208,224},{3... | collective-permute-start | bytes 786440 | tf_op jit(solution)/shard_map/ppermute | solution.py:43
  96.5 15.9 %collective-permute-start.14 = (f32[2,128,256]{2,1,0:T(8,128)S(1)}, f32[2,128,256]{2,1,0:T(8,128)S(1)}, u32[]{:S(2)}, u32[]{:S(2)}) collective-permute-start(f32[2,128,256]{2,1,0:T(8,128)S(1)} %get-tuple-element.73), channel_id=1, source_target_pairs={{0,16},{32,48},{64,80},{96,112},{128,144},{160,176},{192,208},{224... | collective-permute-start | bytes 786440 | tf_op jit(solution)/shard_map/ppermute | solution.py:44
  109.9 42.5 %collective-permute-start.25 = (f32[2,128,768]{2,1,0:T(8,128)S(1)}, f32[2,128,768]{2,1,0:T(8,128)S(1)}, u32[]{:S(2)}, u32[]{:S(2)}) collective-permute-start(f32[2,128,768]{2,1,0:T(8,128)S(1)} %shard_map.64.even_line), channel_id=1, source_target_pairs={{0,1},{2,3},{4,5},{6,7},{8,9},{10,11},{12,13},{14,15},{1,0},{3,2},... | collective-permute-start | bytes 2359304 | tf_op jit(solution)/shard_map/ppermute | solution.py:38
  113.3 15.6 %collective-permute-start.23 = (f32[128,640]{1,0:T(8,128)S(1)}, f32[128,640]{1,0:T(8,128)S(1)}, u32[]{:S(2)}, u32[]{:S(2)}) collective-permute-start(f32[128,640]{1,0:T(8,128)S(1)} %get-tuple-element.85), channel_id=1, source_target_pairs={{1,2},{3,4},{5,6},{9,10},{11,12},{13,14},{2,1},{4,3},{6,5},{10,9},... | collective-permute-start | bytes 983048 | tf_op jit(solution)/shard_map/ppermute | solution.py:31
  115.6 14.5 %collective-permute-start.18 = (f32[2,128,256]{2,1,0:T(8,128)S(1)}, f32[2,128,256]{2,1,0:T(8,128)S(1)}, u32[]{:S(2)}, u32[]{:S(2)}) collective-permute-start(f32[2,128,256]{2,1,0:T(8,128)S(1)} %get-tuple-element.78), channel_id=1, source_target_pairs={{16,32},{48,64},{80,96},{112,128},{144,160},{176,192},{208,224},{3... | collective-permute-start | bytes 786440 | tf_op jit(solution)/shard_map/ppermute | solution.py:43
  119.1 15.2 %collective-permute-start.19 = (f32[2,128,256]{2,1,0:T(8,128)S(1)}, f32[2,128,256]{2,1,0:T(8,128)S(1)}, u32[]{:S(2)}, u32[]{:S(2)}) collective-permute-start(f32[2,128,256]{2,1,0:T(8,128)S(1)} %get-tuple-element.79), channel_id=1, source_target_pairs={{0,16},{32,48},{64,80},{96,112},{128,144},{160,176},{192,208},{224... | collective-permute-start | bytes 786440 | tf_op jit(solution)/shard_map/ppermute | solution.py:44
  120.7 31.7 %collective-permute-start.22 = (f32[128,896]{1,0:T(8,128)S(1)}, f32[128,896]{1,0:T(8,128)S(1)}, u32[]{:S(2)}, u32[]{:S(2)}) collective-permute-start(f32[128,896]{1,0:T(8,128)S(1)} %get-tuple-element.84), channel_id=1, source_target_pairs={{1,2},{3,4},{5,6},{9,10},{11,12},{13,14},{2,1},{4,3},{6,5},{10,9},... | collective-permute-start | bytes 1376264 | tf_op jit(solution)/shard_map/ppermute | solution.py:32
  128.9 23.5 %collective-permute-start.24 = (f32[128,640]{1,0:T(8,128)S(1)}, f32[128,640]{1,0:T(8,128)S(1)}, u32[]{:S(2)}, u32[]{:S(2)}) collective-permute-start(f32[128,640]{1,0:T(8,128)S(1)} %collective-permute-done.23.halo_detour), channel_id=1, source_target_pairs={{0,8},{15,7},{16,24},{31,23},{32,40},{47,39},{48,56},{63,55},{64,7... | collective-permute-start | bytes 983048 | tf_op jit(solution)/shard_map/ppermute | solution.py:33
  130.2 18.8 %collective-permute-start.20 = (f32[2,128,256]{2,1,0:T(8,128)S(1)}, f32[2,128,256]{2,1,0:T(8,128)S(1)}, u32[]{:S(2)}, u32[]{:S(2)}) collective-permute-start(f32[2,128,256]{2,1,0:T(8,128)S(1)} %get-tuple-element.80), channel_id=1, source_target_pairs={{16,32},{48,64},{80,96},{112,128},{144,160},{176,192},{208,224},{3... | collective-permute-start | bytes 786440 | tf_op jit(solution)/shard_map/ppermute | solution.py:43
  134.3 16.6 %collective-permute-start.21 = (f32[2,128,256]{2,1,0:T(8,128)S(1)}, f32[2,128,256]{2,1,0:T(8,128)S(1)}, u32[]{:S(2)}, u32[]{:S(2)}) collective-permute-start(f32[2,128,256]{2,1,0:T(8,128)S(1)} %get-tuple-element.81), channel_id=1, source_target_pairs={{0,16},{32,48},{64,80},{96,112},{128,144},{160,176},{192,208},{224... | collective-permute-start | bytes 786440 | tf_op jit(solution)/shard_map/ppermute | solution.py:44
  159.0 27.8 %collective-permute-start.29 = (f32[2,128,768]{2,1,0:T(8,128)S(1)}, f32[2,128,768]{2,1,0:T(8,128)S(1)}, u32[]{:S(2)}, u32[]{:S(2)}) collective-permute-start(f32[2,128,768]{2,1,0:T(8,128)S(1)} %get-tuple-element.91), channel_id=1, source_target_pairs={{0,1},{2,3},{4,5},{6,7},{8,9},{10,11},{12,13},{14,15},{1,0},{3,2},... | collective-permute-start | bytes 2359304 | tf_op jit(solution)/shard_map/ppermute | solution.py:38
  160.4 18.8 %collective-permute-start.26 = (f32[128,896]{1,0:T(8,128)S(1)}, f32[128,896]{1,0:T(8,128)S(1)}, u32[]{:S(2)}, u32[]{:S(2)}) collective-permute-start(f32[128,896]{1,0:T(8,128)S(1)} %get-tuple-element.88), channel_id=1, source_target_pairs={{1,2},{3,4},{5,6},{9,10},{11,12},{13,14},{2,1},{4,3},{6,5},{10,9},... | collective-permute-start | bytes 1376264 | tf_op jit(solution)/shard_map/ppermute | solution.py:32
  170.1 16.1 %collective-permute-start.28 = (f32[128,640]{1,0:T(8,128)S(1)}, f32[128,640]{1,0:T(8,128)S(1)}, u32[]{:S(2)}, u32[]{:S(2)}) collective-permute-start(f32[128,640]{1,0:T(8,128)S(1)} %collective-permute-done.27.detour), channel_id=1, source_target_pairs={{0,8},{15,7},{16,24},{31,23},{32,40},{47,39},{48,56},{63,55},{64,7... | collective-permute-start | bytes 983048 | tf_op jit(solution)/shard_map/ppermute | solution.py:33
  171.4 31.2 %collective-permute-start.30 = (f32[2,256,128]{2,1,0:T(8,128)S(1)}, f32[2,256,128]{2,1,0:T(8,128)S(1)}, u32[]{:S(2)}, u32[]{:S(2)}) collective-permute-start(f32[2,256,128]{2,1,0:T(8,128)S(1)} %get-tuple-element.92), channel_id=1, source_target_pairs={{16,32},{48,64},{80,96},{112,128},{144,160},{176,192},{208,224},{3... | collective-permute-start | bytes 786440 | tf_op jit(solution)/shard_map/ppermute | solution.py:43
  173.8 28.9 %collective-permute-start.31 = (f32[2,256,128]{2,1,0:T(8,128)S(1)}, f32[2,256,128]{2,1,0:T(8,128)S(1)}, u32[]{:S(2)}, u32[]{:S(2)}) collective-permute-start(f32[2,256,128]{2,1,0:T(8,128)S(1)} %get-tuple-element.93), channel_id=1, source_target_pairs={{0,16},{32,48},{64,80},{96,112},{128,144},{160,176},{192,208},{224... | collective-permute-start | bytes 786440 | tf_op jit(solution)/shard_map/ppermute | solution.py:44
  187.4 15.3 %collective-permute-start.32 = (f32[2,128,128]{2,1,0:T(8,128)S(1)}, f32[2,128,128]{2,1,0:T(8,128)S(1)}, u32[]{:S(2)}, u32[]{:S(2)}) collective-permute-start(f32[2,128,128]{2,1,0:T(8,128)S(1)} %get-tuple-element.94), channel_id=1, source_target_pairs={{16,32},{48,64},{80,96},{112,128},{144,160},{176,192},{208,224},{3... | collective-permute-start | bytes 393224 | tf_op jit(solution)/shard_map/ppermute | solution.py:43
  189.3 13.3 %collective-permute-start.33 = (f32[2,128,128]{2,1,0:T(8,128)S(1)}, f32[2,128,128]{2,1,0:T(8,128)S(1)}, u32[]{:S(2)}, u32[]{:S(2)}) collective-permute-start(f32[2,128,128]{2,1,0:T(8,128)S(1)} %get-tuple-element.95), channel_id=1, source_target_pairs={{0,16},{32,48},{64,80},{96,112},{128,144},{160,176},{192,208},{224... | collective-permute-start | bytes 393224 | tf_op jit(solution)/shard_map/ppermute | solution.py:44
  (8 other events, 59.4 us)

commit v5 on v3

--- a/solution.py
+++ b/solution.py
@@ -42,22 +42,23 @@
     return from_odd, from_even
 
 
-CUT = 128
+STRAIGHT = 512
 
 
 def pack(real, imag, direct, detour):
-    wide = real.shape[1]
-    direct[:, :wide] = real
-    direct[:, wide:] = imag[:, :CUT]
-    detour[...] = imag[:, CUT:]
+    rest = real.shape[1] - STRAIGHT
+    direct[...] = real[:, :STRAIGHT]
+    detour[:, :rest] = real[:, STRAIGHT:]
+    detour[:, rest:] = imag
 
 
 def unpack(meta, direct, detour, relayed, line):
-    wide = line.shape[2]
+    rest = line.shape[2] - STRAIGHT
     own = meta[RELAY] == 0
-    line[0] = direct[:, :wide]
-    line[1, :, :CUT] = direct[:, wide:]
-    line[1, :, CUT:] = jnp.where(own, detour[...], jnp.zeros_like(detour)) + relayed[...]
+    line[0, :, :STRAIGHT] = direct[...]
+    cells = jnp.where(own, detour[...], jnp.zeros_like(detour)) + relayed[...]
+    line[0, :, STRAIGHT:] = cells[:, :rest]
+    line[1] = cells[:, rest:]
 
 
 def dot(a, b):
@@ -469,7 +470,7 @@
     mid_column, mid_band = (2, tile - 2 * half, half), (2, tile // 2 - half, side)
     whole, lines = (2, wide, wide), (2, 2 * half, wide)
     line = (2, half, wide)
-    sends = ((half, wide + CUT), (half, wide - CUT), line)
+    sends = ((half, STRAIGHT), (half, 2 * wide - STRAIGHT), line)
 
     *rims, mid_odd, mid_even = call(
         sides_kernel,

time: 212 us -> 221 us (1.042)
  waiting for transfers between devices: 67.5 us -> 89.2 us
  starting transfers between devices: 107 us -> 95.8 us
    ppermute x4, waiting for transfers between devices: 8.1 us -> 40.7 us  [swap_rows(): straight = lax.ppermute(direct, 'gy', near + far)]
    ppermute x4, waiting for transfers between devices: 0.01 us -> 19.8 us  [swap_rows(): first = lax.ppermute(detour, 'gy', near + [(low, 0), (low + 1, count - 1)])]
    ppermute x7, waiting for transfers between devices: 24.8 us -> 9.36 us  [swap_columns(): from_odd = lax.ppermute(odd_cells, 'gx', pairs(count, 1))]
    ppermute x7, starting transfers between devices: 39 us -> 24.2 us  [swap_columns(): from_even = lax.ppermute(even_cells, 'gx', pairs(count, 0))]
    ppermute x4, waiting for transfers between devices: 13 us -> 3.47 us  [swap_rows(): second = lax.ppermute(first, 'gy', [(0, low + 1), (count - 1, low)])]
    ppermute x4, starting transfers between devices: 5.95 us -> 13.6 us  [swap_rows(): first = lax.ppermute(detour, 'gy', near + [(low, 0), (low + 1, count - 1)])]
    ppermute x7, waiting for transfers between devices: 21.6 us -> 15.9 us  [swap_columns(): from_even = lax.ppermute(even_cells, 'gx', pairs(count, 0))]
    ppermute x4, starting transfers between devices: 33 us -> 28.1 us  [swap_rows(): straight = lax.ppermute(direct, 'gy', near + far)]
  transfers between devices with their start and end apart: 30 -> 30, of which waited for: 11 -> 16; matrix products, arithmetic and copies ran while one was open for 0% -> 0% of each run, Pallas kernels for 5% -> 5%
where the time goes in v5:
time: 221 us; the launch traced here: 220 us
  starting transfers between devices  95.8 us (43%)
  waiting for transfers between devices  89.2 us (40%)
  Pallas kernels  29.1 us (13%)
  local copies, waits for them, and re-layouts  4.8 us (2%)
    ppermute x4, waiting for transfers between devices, swap_rows(): straight = lax.ppermute(direct, 'gy', near + far)  40.7 us
    pallas_call x12, Pallas kernels, call(): pl.pallas_call(kernel, out_shape=shapes, in_specs=[smem, anywhere if far...  29.1 us
    ppermute x4, starting transfers between devices, swap_rows(): straight = lax.ppermute(direct, 'gy', near + far)  28.1 us
    ppermute x7, starting transfers between devices, swap_columns(): from_even = lax.ppermute(even_cells, 'gx', pairs(count, 0))  24.2 us
    ppermute x7, starting transfers between devices, swap_columns(): from_odd = lax.ppermute(odd_cells, 'gx', pairs(count, 1))  24.1 us
    ppermute x4, waiting for transfers between devices, swap_rows(): first = lax.ppermute(detour, 'gy', near + [(low, 0), (low + 1, count - 1)])  19.8 us
    ppermute x7, waiting for transfers between devices, swap_columns(): from_even = lax.ppermute(even_cells, 'gx', pairs(count, 0))  15.9 us
    ppermute x4, starting transfers between devices, swap_rows(): first = lax.ppermute(detour, 'gy', near + [(low, 0), (low + 1, count - 1)])  13.6 us
  transfers between devices with their start and end apart: 30, of which 16 were waited for; matrix products, arithmetic and copies ran while one was open for 0% of the time, Pallas kernels for 5%

profile of v5, /device:TPU:15, one launch (start us, length us, event | category | flops | bytes accessed | tf_op | source)
XLA Modules:
  0.0 220.2 jit_solution(11313683420175124285)
XLA Ops:
  3.1 6.1 %collective-permute-start = (f32[2,256,128]{2,1,0:T(8,128)}, f32[2,256,128]{2,1,0:T(8,128)S(1)}, u32[]{:S(2)}, u32[]{:S(2)}) collective-permute-start(f32[2,256,128]{2,1,0:T(8,128)} %get-tuple-element.49), channel_id=1, source_target_pairs={{16,32},{48,64},{80,96},{112,128},{144,160},{176,192},{208,224},{3... | collective-permute-start | bytes 786440 | tf_op jit(solution)/shard_map/ppermute | solution.py:40
  13.2 4.7 %shard_map.56 = (f32[4,2,256,256]{3,2,1,0:T(8,128)S(1)}, bf16[4,8,256,256]{3,2,1,0:T(8,128)(2,1)S(1)}, f32[4,256,256]{2,1,0:T(8,128)S(1)}) custom-call(s32[13]{0:T(128)S(1)} %concatenate.4.meta, f32[2,256,256]{2,1,0:T(8,128)S(1)} %copy-done.3, f32[4,256,256]{2,1,0:T(8,128)S(1)} %bitcast.7), custom_call_target="tpu_custom_call" | custom-call | flops 1000000000 | bytes 8912896 | tf_op jit(solution)/shard_map/pallas_call | solution.py:441
  17.8 4.2 %collective-permute-done.1.side_even = f32[2,256,128]{2,1,0:T(8,128)S(1)} collective-permute-done((f32[2,256,128]{2,1,0:T(8,128)S(1)}, f32[2,256,128]{2,1,0:T(8,128)S(1)}, u32[]{:S(2)}, u32[]{:S(2)}) %collective-permute-start.1) | collective-permute-done | bytes 262176 | tf_op jit(solution)/shard_map/ppermute | solution.py:41
  22.7 2.5 %collective-permute-start.5 = (f32[128,1024]{1,0:T(8,128)S(1)}, f32[128,1024]{1,0:T(8,128)S(1)}, u32[]{:S(2)}, u32[]{:S(2)}) collective-permute-start(f32[128,1024]{1,0:T(8,128)S(1)} %get-tuple-element.58), channel_id=1, source_target_pairs={{1,2},{3,4},{5,6},{9,10},{11,12},{13,14},{2,1},{4,3},{6,5},{10,9},... | collective-permute-start | bytes 1572872 | tf_op jit(solution)/shard_map/ppermute | solution.py:31
  25.7 5.7 %collective-permute-done.5.halo_detour = f32[128,1024]{1,0:T(8,128)S(1)} collective-permute-done((f32[128,1024]{1,0:T(8,128)S(1)}, f32[128,1024]{1,0:T(8,128)S(1)}, u32[]{:S(2)}, u32[]{:S(2)}) %collective-permute-start.5) | collective-permute-done | bytes 524320 | tf_op jit(solution)/shard_map/ppermute | solution.py:31
  35.9 10.2 %collective-permute-start.4 = (f32[128,512]{1,0:T(8,128)S(1)}, f32[128,512]{1,0:T(8,128)S(1)}, u32[]{:S(2)}, u32[]{:S(2)}) collective-permute-start(f32[128,512]{1,0:T(8,128)S(1)} %get-tuple-element.57), channel_id=1, source_target_pairs={{1,2},{3,4},{5,6},{9,10},{11,12},{13,14},{2,1},{4,3},{6,5},{10,9},... | collective-permute-start | bytes 786440 | tf_op jit(solution)/shard_map/ppermute | solution.py:32
  47.5 14.7 %collective-permute-done.4.halo_direct = f32[128,512]{1,0:T(8,128)S(1)} collective-permute-done((f32[128,512]{1,0:T(8,128)S(1)}, f32[128,512]{1,0:T(8,128)S(1)}, u32[]{:S(2)}, u32[]{:S(2)}) %collective-permute-start.4) | collective-permute-done | bytes 262176 | tf_op jit(solution)/shard_map/ppermute | solution.py:32
  62.2 6.6 %shard_map.59 = (f32[2,768,768]{2,1,0:T(8,128)S(1)}, f32[2,768,768]{2,1,0:T(8,128)S(1)}, f32[128,512]{1,0:T(8,128)S(1)}, f32[128,1024]{1,0:T(8,128)S(1)}, f32[2,...) custom-call(s32[13]{0:T(128)S(1)} %concatenate.4.meta, ...), custom_call_target="tpu_custom_call", output_to_operand_aliasing={{0}: (1, {}), {1}: (2, {})} | custom-call | flops 1073741824 | bytes 30932992 | tf_op jit(solution)/shard_map/pallas_call | solution.py:441
  68.8 2.7 %collective-permute-start.9 = (f32[128,1024]{1,0:T(8,128)S(1)}, f32[128,1024]{1,0:T(8,128)S(1)}, u32[]{:S(2)}, u32[]{:S(2)}) collective-permute-start(f32[128,1024]{1,0:T(8,128)S(1)} %get-tuple-element.65), channel_id=1, source_target_pairs={{1,2},{3,4},{5,6},{9,10},{11,12},{13,14},{2,1},{4,3},{6,5},{10,9},... | collective-permute-start | bytes 1572872 | tf_op jit(solution)/shard_map/ppermute | solution.py:31
  71.6 6.0 %collective-permute-done.9.detour = f32[128,1024]{1,0:T(8,128)S(1)} collective-permute-done((f32[128,1024]{1,0:T(8,128)S(1)}, f32[128,1024]{1,0:T(8,128)S(1)}, u32[]{:S(2)}, u32[]{:S(2)}) %collective-permute-start.9) | collective-permute-done | bytes 524320 | tf_op jit(solution)/shard_map/ppermute | solution.py:31
  78.9 7.0 %collective-permute-start.8 = (f32[128,512]{1,0:T(8,128)S(1)}, f32[128,512]{1,0:T(8,128)S(1)}, u32[]{:S(2)}, u32[]{:S(2)}) collective-permute-start(f32[128,512]{1,0:T(8,128)S(1)} %get-tuple-element.64), channel_id=1, source_target_pairs={{1,2},{3,4},{5,6},{9,10},{11,12},{13,14},{2,1},{4,3},{6,5},{10,9},... | collective-permute-start | bytes 786440 | tf_op jit(solution)/shard_map/ppermute | solution.py:32
  85.9 11.2 %collective-permute-done.8.direct = f32[128,512]{1,0:T(8,128)S(1)} collective-permute-done((f32[128,512]{1,0:T(8,128)S(1)}, f32[128,512]{1,0:T(8,128)S(1)}, u32[]{:S(2)}, u32[]{:S(2)}) %collective-permute-start.8) | collective-permute-done | bytes 262176 | tf_op jit(solution)/shard_map/ppermute | solution.py:32
  97.9 3.6 %collective-permute-start.12 = (f32[2,256,256]{2,1,0:T(8,128)S(1)}, f32[2,256,256]{2,1,0:T(8,128)S(1)}, u32[]{:S(2)}, u32[]{:S(2)}) collective-permute-start(f32[2,256,256]{2,1,0:T(8,128)S(1)} %get-tuple-element.68), channel_id=1, source_target_pairs={{16,32},{48,64},{80,96},{112,128},{144,160},{176,192},{208,224},{3... | collective-permute-start | bytes 1572872 | tf_op jit(solution)/shard_map/ppermute | solution.py:40
  101.5 12.0 %collective-permute-start.13 = (f32[2,256,256]{2,1,0:T(8,128)S(1)}, f32[2,256,256]{2,1,0:T(8,128)S(1)}, u32[]{:S(2)}, u32[]{:S(2)}) collective-permute-start(f32[2,256,256]{2,1,0:T(8,128)S(1)} %get-tuple-element.69), channel_id=1, source_target_pairs={{0,16},{32,48},{64,80},{96,112},{128,144},{160,176},{192,208},{224... | collective-permute-start | bytes 1572872 | tf_op jit(solution)/shard_map/ppermute | solution.py:41
  113.5 6.6 %collective-permute-done.13.band_even = f32[2,256,256]{2,1,0:T(8,128)S(1)} collective-permute-done((f32[2,256,256]{2,1,0:T(8,128)S(1)}, f32[2,256,256]{2,1,0:T(8,128)S(1)}, u32[]{:S(2)}, u32[]{:S(2)}) %collective-permute-start.13) | collective-permute-done | bytes 524320 | tf_op jit(solution)/shard_map/ppermute | solution.py:41
  121.3 6.1 %collective-permute-start.19 = (f32[128,1024]{1,0:T(8,128)S(1)}, f32[128,1024]{1,0:T(8,128)S(1)}, u32[]{:S(2)}, u32[]{:S(2)}) collective-permute-start(f32[128,1024]{1,0:T(8,128)S(1)} %get-tuple-element.78), channel_id=1, source_target_pairs={{1,2},{3,4},{5,6},{9,10},{11,12},{13,14},{2,1},{4,3},{6,5},{10,9},... | collective-permute-start | bytes 1572872 | tf_op jit(solution)/shard_map/ppermute | solution.py:31
  136.9 4.5 %collective-permute-done.14.upper_odd = f32[2,128,256]{2,1,0:T(8,128)S(1)} collective-permute-done((f32[2,128,256]{2,1,0:T(8,128)S(1)}, f32[2,128,256]{2,1,0:T(8,128)S(1)}, u32[]{:S(2)}, u32[]{:S(2)}) %collective-permute-start.14) | collective-permute-done | bytes 262176 | tf_op jit(solution)/shard_map/ppermute | solution.py:40
  141.4 2.8 %collective-permute-start.17 = (f32[2,128,256]{2,1,0:T(8,128)S(1)}, f32[2,128,256]{2,1,0:T(8,128)S(1)}, u32[]{:S(2)}, u32[]{:S(2)}) collective-permute-start(f32[2,128,256]{2,1,0:T(8,128)S(1)} %get-tuple-element.74), channel_id=1, source_target_pairs={{0,16},{32,48},{64,80},{96,112},{128,144},{160,176},{192,208},{224... | collective-permute-start | bytes 786440 | tf_op jit(solution)/shard_map/ppermute | solution.py:41
  144.2 6.7 %collective-permute-start.18 = (f32[128,512]{1,0:T(8,128)S(1)}, f32[128,512]{1,0:T(8,128)S(1)}, u32[]{:S(2)}, u32[]{:S(2)}) collective-permute-start(f32[128,512]{1,0:T(8,128)S(1)} %get-tuple-element.77), channel_id=1, source_target_pairs={{1,2},{3,4},{5,6},{9,10},{11,12},{13,14},{2,1},{4,3},{6,5},{10,9},... | collective-permute-start | bytes 786440 | tf_op jit(solution)/shard_map/ppermute | solution.py:32
  150.8 4.6 %collective-permute-done.16.lower_odd = f32[2,128,256]{2,1,0:T(8,128)S(1)} collective-permute-done((f32[2,128,256]{2,1,0:T(8,128)S(1)}, f32[2,128,256]{2,1,0:T(8,128)S(1)}, u32[]{:S(2)}, u32[]{:S(2)}) %collective-permute-start.16) | collective-permute-done | bytes 262176 | tf_op jit(solution)/shard_map/ppermute | solution.py:40
  158.8 7.8 %collective-permute-done.18.halo_direct = f32[128,512]{1,0:T(8,128)S(1)} collective-permute-done((f32[128,512]{1,0:T(8,128)S(1)}, f32[128,512]{1,0:T(8,128)S(1)}, u32[]{:S(2)}, u32[]{:S(2)}) %collective-permute-start.18) | collective-permute-done | bytes 262176 | tf_op jit(solution)/shard_map/ppermute | solution.py:32
  166.6 6.6 %shard_map.63 = (f32[2,768,768]{2,1,0:T(8,128)S(1)}, f32[2,768,768]{2,1,0:T(8,128)S(1)}, f32[128,512]{1,0:T(8,128)S(1)}, f32[128,1024]{1,0:T(8,128)S(1)}, f32[2,...) custom-call(s32[13]{0:T(128)S(1)} %concatenate.4.meta, ...), custom_call_target="tpu_custom_call", output_to_operand_aliasing={{0}: (1, {}), {1}: (2, {})} | custom-call | flops 1073741824 | bytes 30408704 | tf_op jit(solution)/shard_map/pallas_call | solution.py:441
  173.2 2.2 %collective-permute-start.23 = (f32[128,1024]{1,0:T(8,128)S(1)}, f32[128,1024]{1,0:T(8,128)S(1)}, u32[]{:S(2)}, u32[]{:S(2)}) collective-permute-start(f32[128,1024]{1,0:T(8,128)S(1)} %get-tuple-element.83), channel_id=1, source_target_pairs={{1,2},{3,4},{5,6},{9,10},{11,12},{13,14},{2,1},{4,3},{6,5},{10,9},... | collective-permute-start | bytes 1572872 | tf_op jit(solution)/shard_map/ppermute | solution.py:31
  175.5 6.0 %collective-permute-done.23.detour = f32[128,1024]{1,0:T(8,128)S(1)} collective-permute-done((f32[128,1024]{1,0:T(8,128)S(1)}, f32[128,1024]{1,0:T(8,128)S(1)}, u32[]{:S(2)}, u32[]{:S(2)}) %collective-permute-start.23) | collective-permute-done | bytes 524320 | tf_op jit(solution)/shard_map/ppermute | solution.py:31
  182.8 4.3 %collective-permute-start.22 = (f32[128,512]{1,0:T(8,128)S(1)}, f32[128,512]{1,0:T(8,128)S(1)}, u32[]{:S(2)}, u32[]{:S(2)}) collective-permute-start(f32[128,512]{1,0:T(8,128)S(1)} %get-tuple-element.82), channel_id=1, source_target_pairs={{1,2},{3,4},{5,6},{9,10},{11,12},{13,14},{2,1},{4,3},{6,5},{10,9},... | collective-permute-start | bytes 786440 | tf_op jit(solution)/shard_map/ppermute | solution.py:32
  187.1 6.0 %collective-permute-start.26 = (f32[2,256,128]{2,1,0:T(8,128)S(1)}, f32[2,256,128]{2,1,0:T(8,128)S(1)}, u32[]{:S(2)}, u32[]{:S(2)}) collective-permute-start(f32[2,256,128]{2,1,0:T(8,128)S(1)} %get-tuple-element.86), channel_id=1, source_target_pairs={{16,32},{48,64},{80,96},{112,128},{144,160},{176,192},{208,224},{3... | collective-permute-start | bytes 786440 | tf_op jit(solution)/shard_map/ppermute | solution.py:40
  193.3 7.0 %collective-permute-done.22.direct = f32[128,512]{1,0:T(8,128)S(1)} collective-permute-done((f32[128,512]{1,0:T(8,128)S(1)}, f32[128,512]{1,0:T(8,128)S(1)}, u32[]{:S(2)}, u32[]{:S(2)}) %collective-permute-start.22) | collective-permute-done | bytes 262176 | tf_op jit(solution)/shard_map/ppermute | solution.py:32
  200.2 3.5 %collective-permute-done.24.relayed = f32[128,1024]{1,0:T(8,128)S(1)} collective-permute-done((f32[128,1024]{1,0:T(8,128)S(1)}, f32[128,1024]{1,0:T(8,128)S(1)}, u32[]{:S(2)}, u32[]{:S(2)}) %collective-permute-start.24) | collective-permute-done | bytes 524320 | tf_op jit(solution)/shard_map/ppermute | solution.py:34
  204.4 2.4 %collective-permute-start.28 = (f32[2,256,128]{2,1,0:T(8,128)S(1)}, f32[2,256,128]{2,1,0:T(8,128)S(1)}, u32[]{:S(2)}, u32[]{:S(2)}) collective-permute-start(f32[2,256,128]{2,1,0:T(8,128)S(1)} %get-tuple-element.91), channel_id=1, source_target_pairs={{16,32},{48,64},{80,96},{112,128},{144,160},{176,192},{208,224},{3... | collective-permute-start | bytes 786440 | tf_op jit(solution)/shard_map/ppermute | solution.py:40
  206.8 6.1 %collective-permute-start.29 = (f32[2,256,128]{2,1,0:T(8,128)S(1)}, f32[2,256,128]{2,1,0:T(8,128)S(1)}, u32[]{:S(2)}, u32[]{:S(2)}) collective-permute-start(f32[2,256,128]{2,1,0:T(8,128)S(1)} %get-tuple-element.92), channel_id=1, source_target_pairs={{0,16},{32,48},{64,80},{96,112},{128,144},{160,176},{192,208},{224... | collective-permute-start | bytes 786440 | tf_op jit(solution)/shard_map/ppermute | solution.py:41
  212.9 2.6 %shard_map.65 = (f32[2,512,512]{2,1,0:T(8,128)}, f32[2,256,128]{2,1,0:T(8,128)S(1)}, f32[2,256,128]{2,1,0:T(8,128)S(1)}) custom-call(s32[13]{0:T(128)S(1)} %concatenate.4.meta, f32[2,768,768]{2,1,0:T(8,128)S(1)} %get-tuple-element.80.field, f32[2,768,768]{2,1,0:T(8,128)S(1)} %get-tuple-element.81.total, f32[2,128,768]{2,1,0:T(8,128)S(1)} %get-tuple-element.85.line, ...), custom_call_target="tpu_custom_call" | custom-call | bytes 14155776 | tf_op jit(solution)/shard_map/pallas_call | solution.py:441
  215.5 3.1 %collective-permute-done.29.rim_even = f32[2,256,128]{2,1,0:T(8,128)S(1)} collective-permute-done((f32[2,256,128]{2,1,0:T(8,128)S(1)}, f32[2,256,128]{2,1,0:T(8,128)S(1)}, u32[]{:S(2)}, u32[]{:S(2)}) %collective-permute-start.29) | collective-permute-done | bytes 262176 | tf_op jit(solution)/shard_map/ppermute | solution.py:41
  (52 shorter events, 33.4 us)
Async XLA Ops:
  0.1 1.6 copy-start
  1.7 20.3 %copy-start.1 = (f32[2,512,512]{2,1,0:T(8,128)S(1)}, f32[2,512,512]{2,1,0:T(8,128)}, u32[]{:S(2)}) copy-start(f32[2,512,512]{2,1,0:T(8,128)} %own.5) | copy-start | bytes 6291460
  3.1 14.8 %collective-permute-start = (f32[2,256,128]{2,1,0:T(8,128)}, f32[2,256,128]{2,1,0:T(8,128)S(1)}, u32[]{:S(2)}, u32[]{:S(2)}) collective-permute-start(f32[2,256,128]{2,1,0:T(8,128)} %get-tuple-element.49), channel_id=1, source_target_pairs={{16,32},{48,64},{80,96},{112,128},{144,160},{176,192},{208,224},{3... | collective-permute-start | bytes 786440 | tf_op jit(solution)/shard_map/ppermute | solution.py:40
  9.2 12.8 %collective-permute-start.1 = (f32[2,256,128]{2,1,0:T(8,128)S(1)}, f32[2,256,128]{2,1,0:T(8,128)S(1)}, u32[]{:S(2)}, u32[]{:S(2)}) collective-permute-start(f32[2,256,128]{2,1,0:T(8,128)S(1)} %get-tuple-element.50), channel_id=1, source_target_pairs={{0,16},{32,48},{64,80},{96,112},{128,144},{160,176},{192,208},{224... | collective-permute-start | bytes 786440 | tf_op jit(solution)/shard_map/ppermute | solution.py:41
  22.7 8.6 %collective-permute-start.5 = (f32[128,1024]{1,0:T(8,128)S(1)}, f32[128,1024]{1,0:T(8,128)S(1)}, u32[]{:S(2)}, u32[]{:S(2)}) collective-permute-start(f32[128,1024]{1,0:T(8,128)S(1)} %get-tuple-element.58), channel_id=1, source_target_pairs={{1,2},{3,4},{5,6},{9,10},{11,12},{13,14},{2,1},{4,3},{6,5},{10,9},... | collective-permute-start | bytes 1572872 | tf_op jit(solution)/shard_map/ppermute | solution.py:31
  25.3 37.0 %collective-permute-start.7 = (f32[2,128,768]{2,1,0:T(8,128)S(1)}, f32[2,128,768]{2,1,0:T(8,128)S(1)}, u32[]{:S(2)}, u32[]{:S(2)}) collective-permute-start(f32[2,128,768]{2,1,0:T(8,128)S(1)} %get-tuple-element.59), channel_id=1, source_target_pairs={{0,1},{2,3},{4,5},{6,7},{8,9},{10,11},{12,13},{14,15},{1,0},{3,2},... | collective-permute-start | bytes 2359304 | tf_op jit(solution)/shard_map/ppermute | solution.py:33
  31.3 30.9 %collective-permute-start.6 = (f32[128,1024]{1,0:T(8,128)S(1)}, f32[128,1024]{1,0:T(8,128)S(1)}, u32[]{:S(2)}, u32[]{:S(2)}) collective-permute-start(f32[128,1024]{1,0:T(8,128)S(1)} %collective-permute-done.5.halo_detour), channel_id=1, source_target_pairs={{0,8},{15,7},{16,24},{31,23},{32,40},{47,39},{48,56},{63,55},{64,7... | collective-permute-start | bytes 1572872 | tf_op jit(solution)/shard_map/ppermute | solution.py:34
  32.6 13.8 %collective-permute-start.2 = (f32[2,256,128]{2,1,0:T(8,128)S(1)}, f32[2,256,128]{2,1,0:T(8,128)S(1)}, u32[]{:S(2)}, u32[]{:S(2)}) collective-permute-start(f32[2,256,128]{2,1,0:T(8,128)S(1)} %get-tuple-element.53), channel_id=1, source_target_pairs={{16,32},{48,64},{80,96},{112,128},{144,160},{176,192},{208,224},{3... | collective-permute-start | bytes 786440 | tf_op jit(solution)/shard_map/ppermute | solution.py:40
  34.6 11.9 %collective-permute-start.3 = (f32[2,256,128]{2,1,0:T(8,128)S(1)}, f32[2,256,128]{2,1,0:T(8,128)S(1)}, u32[]{:S(2)}, u32[]{:S(2)}) collective-permute-start(f32[2,256,128]{2,1,0:T(8,128)S(1)} %get-tuple-element.54), channel_id=1, source_target_pairs={{0,16},{32,48},{64,80},{96,112},{128,144},{160,176},{192,208},{224... | collective-permute-start | bytes 786440 | tf_op jit(solution)/shard_map/ppermute | solution.py:41
  35.9 26.3 %collective-permute-start.4 = (f32[128,512]{1,0:T(8,128)S(1)}, f32[128,512]{1,0:T(8,128)S(1)}, u32[]{:S(2)}, u32[]{:S(2)}) collective-permute-start(f32[128,512]{1,0:T(8,128)S(1)} %get-tuple-element.57), channel_id=1, source_target_pairs={{1,2},{3,4},{5,6},{9,10},{11,12},{13,14},{2,1},{4,3},{6,5},{10,9},... | collective-permute-start | bytes 786440 | tf_op jit(solution)/shard_map/ppermute | solution.py:32
  68.8 8.8 %collective-permute-start.9 = (f32[128,1024]{1,0:T(8,128)S(1)}, f32[128,1024]{1,0:T(8,128)S(1)}, u32[]{:S(2)}, u32[]{:S(2)}) collective-permute-start(f32[128,1024]{1,0:T(8,128)S(1)} %get-tuple-element.65), channel_id=1, source_target_pairs={{1,2},{3,4},{5,6},{9,10},{11,12},{13,14},{2,1},{4,3},{6,5},{10,9},... | collective-permute-start | bytes 1572872 | tf_op jit(solution)/shard_map/ppermute | solution.py:31
  71.5 25.5 %collective-permute-start.11 = (f32[2,128,768]{2,1,0:T(8,128)S(1)}, f32[2,128,768]{2,1,0:T(8,128)S(1)}, u32[]{:S(2)}, u32[]{:S(2)}) collective-permute-start(f32[2,128,768]{2,1,0:T(8,128)S(1)} %get-tuple-element.66), channel_id=1, source_target_pairs={{0,1},{2,3},{4,5},{6,7},{8,9},{10,11},{12,13},{14,15},{1,0},{3,2},... | collective-permute-start | bytes 2359304 | tf_op jit(solution)/shard_map/ppermute | solution.py:33
  77.6 19.5 %collective-permute-start.10 = (f32[128,1024]{1,0:T(8,128)S(1)}, f32[128,1024]{1,0:T(8,128)S(1)}, u32[]{:S(2)}, u32[]{:S(2)}) collective-permute-start(f32[128,1024]{1,0:T(8,128)S(1)} %collective-permute-done.9.detour), channel_id=1, source_target_pairs={{0,8},{15,7},{16,24},{31,23},{32,40},{47,39},{48,56},{63,55},{64,7... | collective-permute-start | bytes 1572872 | tf_op jit(solution)/shard_map/ppermute | solution.py:34
  78.9 18.2 %collective-permute-start.8 = (f32[128,512]{1,0:T(8,128)S(1)}, f32[128,512]{1,0:T(8,128)S(1)}, u32[]{:S(2)}, u32[]{:S(2)}) collective-permute-start(f32[128,512]{1,0:T(8,128)S(1)} %get-tuple-element.64), channel_id=1, source_target_pairs={{1,2},{3,4},{5,6},{9,10},{11,12},{13,14},{2,1},{4,3},{6,5},{10,9},... | collective-permute-start | bytes 786440 | tf_op jit(solution)/shard_map/ppermute | solution.py:32
  97.9 15.6 %collective-permute-start.12 = (f32[2,256,256]{2,1,0:T(8,128)S(1)}, f32[2,256,256]{2,1,0:T(8,128)S(1)}, u32[]{:S(2)}, u32[]{:S(2)}) collective-permute-start(f32[2,256,256]{2,1,0:T(8,128)S(1)} %get-tuple-element.68), channel_id=1, source_target_pairs={{16,32},{48,64},{80,96},{112,128},{144,160},{176,192},{208,224},{3... | collective-permute-start | bytes 1572872 | tf_op jit(solution)/shard_map/ppermute | solution.py:40
  101.5 18.6 %collective-permute-start.13 = (f32[2,256,256]{2,1,0:T(8,128)S(1)}, f32[2,256,256]{2,1,0:T(8,128)S(1)}, u32[]{:S(2)}, u32[]{:S(2)}) collective-permute-start(f32[2,256,256]{2,1,0:T(8,128)S(1)} %get-tuple-element.69), channel_id=1, source_target_pairs={{0,16},{32,48},{64,80},{96,112},{128,144},{160,176},{192,208},{224... | collective-permute-start | bytes 1572872 | tf_op jit(solution)/shard_map/ppermute | solution.py:41
  121.3 12.2 %collective-permute-start.19 = (f32[128,1024]{1,0:T(8,128)S(1)}, f32[128,1024]{1,0:T(8,128)S(1)}, u32[]{:S(2)}, u32[]{:S(2)}) collective-permute-start(f32[128,1024]{1,0:T(8,128)S(1)} %get-tuple-element.78), channel_id=1, source_target_pairs={{1,2},{3,4},{5,6},{9,10},{11,12},{13,14},{2,1},{4,3},{6,5},{10,9},... | collective-permute-start | bytes 1572872 | tf_op jit(solution)/shard_map/ppermute | solution.py:31
  127.4 39.2 %collective-permute-start.21 = (f32[2,128,768]{2,1,0:T(8,128)S(1)}, f32[2,128,768]{2,1,0:T(8,128)S(1)}, u32[]{:S(2)}, u32[]{:S(2)}) collective-permute-start(f32[2,128,768]{2,1,0:T(8,128)S(1)} %get-tuple-element.79), channel_id=1, source_target_pairs={{0,1},{2,3},{4,5},{6,7},{8,9},{10,11},{12,13},{14,15},{1,0},{3,2},... | collective-permute-start | bytes 2359304 | tf_op jit(solution)/shard_map/ppermute | solution.py:33
  127.5 13.9 %collective-permute-start.14 = (f32[2,128,256]{2,1,0:T(8,128)S(1)}, f32[2,128,256]{2,1,0:T(8,128)S(1)}, u32[]{:S(2)}, u32[]{:S(2)}) collective-permute-start(f32[2,128,256]{2,1,0:T(8,128)S(1)} %get-tuple-element.71), channel_id=1, source_target_pairs={{16,32},{48,64},{80,96},{112,128},{144,160},{176,192},{208,224},{3... | collective-permute-start | bytes 786440 | tf_op jit(solution)/shard_map/ppermute | solution.py:40
  129.4 14.7 %collective-permute-start.15 = (f32[2,128,256]{2,1,0:T(8,128)S(1)}, f32[2,128,256]{2,1,0:T(8,128)S(1)}, u32[]{:S(2)}, u32[]{:S(2)}) collective-permute-start(f32[2,128,256]{2,1,0:T(8,128)S(1)} %get-tuple-element.72), channel_id=1, source_target_pairs={{0,16},{32,48},{64,80},{96,112},{128,144},{160,176},{192,208},{224... | collective-permute-start | bytes 786440 | tf_op jit(solution)/shard_map/ppermute | solution.py:41
  133.5 33.1 %collective-permute-start.20 = (f32[128,1024]{1,0:T(8,128)S(1)}, f32[128,1024]{1,0:T(8,128)S(1)}, u32[]{:S(2)}, u32[]{:S(2)}) collective-permute-start(f32[128,1024]{1,0:T(8,128)S(1)} %collective-permute-done.19.halo_detour), channel_id=1, source_target_pairs={{0,8},{15,7},{16,24},{31,23},{32,40},{47,39},{48,56},{63,55},{64,7... | collective-permute-start | bytes 1572872 | tf_op jit(solution)/shard_map/ppermute | solution.py:34
  134.8 20.6 %collective-permute-start.16 = (f32[2,128,256]{2,1,0:T(8,128)S(1)}, f32[2,128,256]{2,1,0:T(8,128)S(1)}, u32[]{:S(2)}, u32[]{:S(2)}) collective-permute-start(f32[2,128,256]{2,1,0:T(8,128)S(1)} %get-tuple-element.73), channel_id=1, source_target_pairs={{16,32},{48,64},{80,96},{112,128},{144,160},{176,192},{208,224},{3... | collective-permute-start | bytes 786440 | tf_op jit(solution)/shard_map/ppermute | solution.py:40
  141.4 16.0 %collective-permute-start.17 = (f32[2,128,256]{2,1,0:T(8,128)S(1)}, f32[2,128,256]{2,1,0:T(8,128)S(1)}, u32[]{:S(2)}, u32[]{:S(2)}) collective-permute-start(f32[2,128,256]{2,1,0:T(8,128)S(1)} %get-tuple-element.74), channel_id=1, source_target_pairs={{0,16},{32,48},{64,80},{96,112},{128,144},{160,176},{192,208},{224... | collective-permute-start | bytes 786440 | tf_op jit(solution)/shard_map/ppermute | solution.py:41
  144.2 22.5 %collective-permute-start.18 = (f32[128,512]{1,0:T(8,128)S(1)}, f32[128,512]{1,0:T(8,128)S(1)}, u32[]{:S(2)}, u32[]{:S(2)}) collective-permute-start(f32[128,512]{1,0:T(8,128)S(1)} %get-tuple-element.77), channel_id=1, source_target_pairs={{1,2},{3,4},{5,6},{9,10},{11,12},{13,14},{2,1},{4,3},{6,5},{10,9},... | collective-permute-start | bytes 786440 | tf_op jit(solution)/shard_map/ppermute | solution.py:32
  173.2 8.3 %collective-permute-start.23 = (f32[128,1024]{1,0:T(8,128)S(1)}, f32[128,1024]{1,0:T(8,128)S(1)}, u32[]{:S(2)}, u32[]{:S(2)}) collective-permute-start(f32[128,1024]{1,0:T(8,128)S(1)} %get-tuple-element.83), channel_id=1, source_target_pairs={{1,2},{3,4},{5,6},{9,10},{11,12},{13,14},{2,1},{4,3},{6,5},{10,9},... | collective-permute-start | bytes 1572872 | tf_op jit(solution)/shard_map/ppermute | solution.py:31
  175.4 24.8 %collective-permute-start.25 = (f32[2,128,768]{2,1,0:T(8,128)S(1)}, f32[2,128,768]{2,1,0:T(8,128)S(1)}, u32[]{:S(2)}, u32[]{:S(2)}) collective-permute-start(f32[2,128,768]{2,1,0:T(8,128)S(1)} %get-tuple-element.84), channel_id=1, source_target_pairs={{0,1},{2,3},{4,5},{6,7},{8,9},{10,11},{12,13},{14,15},{1,0},{3,2},... | collective-permute-start | bytes 2359304 | tf_op jit(solution)/shard_map/ppermute | solution.py:33
  181.5 22.2 %collective-permute-start.24 = (f32[128,1024]{1,0:T(8,128)S(1)}, f32[128,1024]{1,0:T(8,128)S(1)}, u32[]{:S(2)}, u32[]{:S(2)}) collective-permute-start(f32[128,1024]{1,0:T(8,128)S(1)} %collective-permute-done.23.detour), channel_id=1, source_target_pairs={{0,8},{15,7},{16,24},{31,23},{32,40},{47,39},{48,56},{63,55},{64,7... | collective-permute-start | bytes 1572872 | tf_op jit(solution)/shard_map/ppermute | solution.py:34
  182.8 17.4 %collective-permute-start.22 = (f32[128,512]{1,0:T(8,128)S(1)}, f32[128,512]{1,0:T(8,128)S(1)}, u32[]{:S(2)}, u32[]{:S(2)}) collective-permute-start(f32[128,512]{1,0:T(8,128)S(1)} %get-tuple-element.82), channel_id=1, source_target_pairs={{1,2},{3,4},{5,6},{9,10},{11,12},{13,14},{2,1},{4,3},{6,5},{10,9},... | collective-permute-start | bytes 786440 | tf_op jit(solution)/shard_map/ppermute | solution.py:32
  187.1 25.8 %collective-permute-start.26 = (f32[2,256,128]{2,1,0:T(8,128)S(1)}, f32[2,256,128]{2,1,0:T(8,128)S(1)}, u32[]{:S(2)}, u32[]{:S(2)}) collective-permute-start(f32[2,256,128]{2,1,0:T(8,128)S(1)} %get-tuple-element.86), channel_id=1, source_target_pairs={{16,32},{48,64},{80,96},{112,128},{144,160},{176,192},{208,224},{3... | collective-permute-start | bytes 786440 | tf_op jit(solution)/shard_map/ppermute | solution.py:40
  193.2 19.8 %collective-permute-start.27 = (f32[2,256,128]{2,1,0:T(8,128)S(1)}, f32[2,256,128]{2,1,0:T(8,128)S(1)}, u32[]{:S(2)}, u32[]{:S(2)}) collective-permute-start(f32[2,256,128]{2,1,0:T(8,128)S(1)} %get-tuple-element.87), channel_id=1, source_target_pairs={{0,16},{32,48},{64,80},{96,112},{128,144},{160,176},{192,208},{224... | collective-permute-start | bytes 786440 | tf_op jit(solution)/shard_map/ppermute | solution.py:41
  204.4 11.1 %collective-permute-start.28 = (f32[2,256,128]{2,1,0:T(8,128)S(1)}, f32[2,256,128]{2,1,0:T(8,128)S(1)}, u32[]{:S(2)}, u32[]{:S(2)}) collective-permute-start(f32[2,256,128]{2,1,0:T(8,128)S(1)} %get-tuple-element.91), channel_id=1, source_target_pairs={{16,32},{48,64},{80,96},{112,128},{144,160},{176,192},{208,224},{3... | collective-permute-start | bytes 786440 | tf_op jit(solution)/shard_map/ppermute | solution.py:40
  206.8 11.8 %collective-permute-start.29 = (f32[2,256,128]{2,1,0:T(8,128)S(1)}, f32[2,256,128]{2,1,0:T(8,128)S(1)}, u32[]{:S(2)}, u32[]{:S(2)}) collective-permute-start(f32[2,256,128]{2,1,0:T(8,128)S(1)} %get-tuple-element.92), channel_id=1, source_target_pairs={{0,16},{32,48},{64,80},{96,112},{128,144},{160,176},{192,208},{224... | collective-permute-start | bytes 786440 | tf_op jit(solution)/shard_map/ppermute | solution.py:41
  (2 other events, 2.3 us)

commit v6 on v3

--- a/solution.py
+++ b/solution.py
@@ -23,16 +23,23 @@
     return ups + [(b, a) for a, b in ups]
 
 
-def swap_rows(direct, detour, even_cells):
+def swap_odd(direct, detour):
     count = lax.axis_size("gy")
     low = count // 2 - 1
     far = [(low, low + 1), (low + 1, low)]
     near = [p for p in pairs(count, 1) if p not in far]
     first = lax.ppermute(detour, "gy", near + [(low, 0), (low + 1, count - 1)])
     straight = lax.ppermute(direct, "gy", near + far)
-    even = lax.ppermute(even_cells, "gy", pairs(count, 0))
     second = lax.ppermute(first, "gy", [(0, low + 1), (count - 1, low)])
-    return straight, first, second, even
+    return straight, first, second
+
+
+def swap_even(cells):
+    return lax.ppermute(cells, "gy", pairs(lax.axis_size("gy"), 0))
+
+
+def swap_rows(direct, detour, even_cells):
+    return *swap_odd(direct, detour), swap_even(even_cells)
 
 
 def swap_columns(odd_cells, even_cells):
@@ -154,7 +161,7 @@
     rim_even,
     *rest,
 ):
-    *bands, mixed = rest
+    *bands, mixed, terms = rest
     half = side // 2
     wide = field.shape[2]
     tile = wide - side
@@ -165,7 +172,7 @@
     even_rows = pl.ds(pl.multiple_of((1 - odd_row) * bottom, half), half)
     unpack(meta, halo_direct, halo_detour, halo_relayed, field.at[:, odd_rows, :])
     field[:, even_rows, :] = halo_even[...]
-    chunk = 32
+    chunk, lanes = 32, 128
     zero = jnp.float32(0)
 
     for w in range(windows):
@@ -234,23 +241,54 @@
             outs.append(dot(tables[w, 2 * odd + 1], stacked))
         upper, lower = outs[0] + outs[1], outs[0] - outs[1]
 
+        never = 2 * side
+        cut_row, cut_col = jnp.minimum(row_in // chunk, side // chunk - 1), jnp.minimum(col_in // lanes, side // lanes - 1)
+        cut_row, cut_col = pl.multiple_of(cut_row * chunk, chunk), pl.multiple_of(cut_col * lanes, lanes)
+        rows_before = jnp.where((cut_row + chunk > row_in) & live, row_in, -1) - cut_row
+        cols_before = jnp.where(cut_col + lanes > col_in, col_in, -1) - cut_col
+        iota_r = lax.broadcasted_iota(jnp.int32, (chunk, lanes), 0)
+        iota_c = lax.broadcasted_iota(jnp.int32, (chunk, lanes), 1)
+
+        def placed(first, size, cut):
+            moved = first + size <= cut
+            return jnp.where(moved, side, 0) + first, jnp.where(moved, 0, cut) - first
+
+        columns = []
+        for first in range(0, side, lanes):
+            at, least = placed(first, lanes, col_in)
+            columns.append((first, pl.multiple_of(col0 + at, lanes), iota_c >= least))
+        columns.append((cut_col, pl.multiple_of(col0 + side + cut_col, lanes), iota_c < cols_before))
+
+        def add(part, row, col, term, keep):
+            cells = (part, pl.ds(row, chunk), pl.ds(col, lanes))
+            total[cells] = total[cells] + jnp.where(keep, term, zero)
+
         for start in range(0, side, chunk):
             back = upper if start < half else lower
             at = start % half
             b_real, b_imag = back[at : at + chunk], back[half + at : half + at + chunk]
             p_real = probes[w, 0, pl.ds(start, chunk), :]
             p_imag = probes[w, 1, pl.ds(start, chunk), :]
-            terms = (p_real * b_real + p_imag * b_imag, p_real * b_imag - p_imag * b_real)
-            rows_in = below(start)
+            both = (p_real * b_real + p_imag * b_imag, p_real * b_imag - p_imag * b_real)
+            row, least = placed(start, chunk, row_in)
+            row, keep = pl.multiple_of(row0 + row, chunk), iota_r >= jnp.where(live, least, never)
             for part in (0, 1):
-                for i, j in ((0, 0), (0, 1), (1, 0), (1, 1)):
-                    keep = (rows_in if i == 0 else ~rows_in) & (near if j == 0 else ~near)
-                    place = (
-                        part,
-                        pl.ds(pl.multiple_of(row0 + i * side + start, chunk), chunk),
-                        pl.ds(pl.multiple_of(col0 + j * side, side), side),
-                    )
-                    total[place] = total[place] + jnp.where(keep & live, terms[part], zero)
+                terms[part, start : start + chunk, :] = both[part]
+                for first, col, wanted in columns[:-1]:
+                    add(part, row, col, both[part][:, first : first + lanes], keep & wanted)
+        first, col, wanted = columns[-1]
+        for start in range(0, side, chunk):
+            row, least = placed(start, chunk, row_in)
+            row, keep = pl.multiple_of(row0 + row, chunk), iota_r >= jnp.where(live, least, never)
+            for part in (0, 1):
+                term = terms[part, start : start + chunk, pl.ds(first, lanes)]
+                add(part, row, col, term, keep & wanted)
+        row = pl.multiple_of(row0 + side + cut_row, chunk)
+        keep = iota_r < rows_before
+        for part in (0, 1):
+            for first, col, wanted in columns:
+                term = terms[part, pl.ds(cut_row, chunk), pl.ds(first, lanes)]
+                add(part, row, col, term, keep & wanted)
 
     pack(total[0, odd_rows, :], total[1, odd_rows, :], rim_direct, rim_detour)
     rim_even[...] = total[:, even_rows, :]
@@ -278,28 +316,39 @@
     )
 
 
-def sides_kernel(meta, own, rim_odd, rim_even, mid_odd, mid_even):
-    tile, half = own.shape[1], rim_odd.shape[2]
-    far = tile - half
-    for rim, mid, cols in (
-        (rim_odd, mid_odd, odd_side(meta, rim_odd, tile)),
-        (rim_even, mid_even, even_side(meta, rim_even, tile)),
+def both_sides(meta, odd, even, wide):
+    return (odd, odd_side(meta, odd, wide)), (even, even_side(meta, even, wide))
+
+
+def strip(meta, odd, half, tile, margin):
+    low = meta[GY_ODD] if odd else 1 - meta[GY_ODD]
+    return pl.ds(pl.multiple_of(margin + low * (tile - half), half), half)
+
+
+def sides_kernel(meta, own, odd_a, odd_b, even_a, even_b, mid_a, mid_b, odd_own):
+    tile, half = own.shape[1], odd_a.shape[1]
+    for rows, pair in (
+        (strip(meta, True, half, tile, 0), (odd_a, odd_b)),
+        (strip(meta, False, half, tile, 0), (even_a, even_b)),
+        (slice(half, tile - half), (mid_a, mid_b)),
     ):
-        rim[:, :half, :] = own[:, :half, cols]
-        rim[:, half:, :] = own[:, far:, cols]
-        mid[...] = own[:, half:far, cols]
-
-
-def edges_kernel(meta, own, side_odd, side_even, _, direct, detour, even, lines):
-    tile, half = own.shape[1], side_odd.shape[2]
-    wide = lines.shape[2]
-    for at, rows in ((0, slice(0, half)), (half, slice(tile - half, tile))):
-        lines[:, at : at + half, half : half + tile] = own[:, rows, :]
-    lines[:, :, odd_side(meta, side_odd, wide)] = side_odd[...]
-    lines[:, :, even_side(meta, side_even, wide)] = side_even[...]
-    odd_rows, even_rows = rim_rows(meta, half)
-    pack(lines[0, odd_rows, :], lines[1, odd_rows, :], direct, detour)
-    even[...] = lines[:, even_rows, :]
+        for out, cols in both_sides(meta, *pair, tile):
+            out[...] = own[:, rows, cols]
+    odd_own[...] = own[:, strip(meta, True, half, tile, 0), :]
+
+
+def edge_kernel(odd, meta, own, side_odd, side_even, *outs):
+    *sends, line = outs
+    tile, half = own.shape[2], side_odd.shape[2]
+    wide = line.shape[2]
+    if odd:
+        line[:, :, half : half + tile] = own[...]
+    else:
+        line[:, :, half : half + tile] = own[:, strip(meta, False, half, tile, 0), :]
+    for side, cols in both_sides(meta, side_odd, side_even, wide):
+        line[:, :, cols] = side[...]
+    if odd:
+        pack(line[0], line[1], *sends)
 
 
 def inner_rows(half, tile):
@@ -310,15 +359,15 @@
     )
 
 
-def centre_kernel(meta, own, lines, side_odd, side_even, field, total):
+def centre_kernel(meta, own, odd_line, even_line, side_odd, side_even, field, total):
     tile, half = own.shape[1], side_odd.shape[2]
-    wide = lines.shape[2]
-    first, last, mid = inner_rows(half, tile)
-    for rows, outer in (first, last):
-        field[:, rows, :] = lines[:, outer, :]
+    wide = field.shape[2]
+    mid = slice(2 * half, tile)
+    field[:, strip(meta, True, half, tile, half), :] = odd_line[...]
+    field[:, strip(meta, False, half, tile, half), :] = even_line[...]
     field[:, mid, half : half + tile] = own[:, half : tile - half, :]
-    field[:, mid, odd_side(meta, side_odd, wide)] = side_odd[...]
-    field[:, mid, even_side(meta, side_even, wide)] = side_even[...]
+    for side, cols in both_sides(meta, side_odd, side_even, wide):
+        field[:, mid, cols] = side[...]
     total[...] = jnp.zeros_like(total)
 
 
@@ -471,14 +520,27 @@
     line = (2, half, wide)
     sends = ((half, wide + CUT), (half, wide - CUT), line)
 
-    *rims, mid_odd, mid_even = call(
+    block = (2, half, half)
+    *sides, odd_own = call(
         sides_kernel,
         places,
         (object_field,),
-        (column, column, mid_column, mid_column),
-    )
-    rims = swap_columns(*rims)
-    mids = swap_columns(mid_odd, mid_even)
+        (*(block,) * 4, *(mid_column,) * 2, (2, half, tile)),
+    )
+    odd_sides = swap_columns(*sides[:2])
+    even_sides = swap_columns(*sides[2:4])
+    mids = swap_columns(*sides[4:])
+    *parts, odd_line = call(
+        functools.partial(edge_kernel, True),
+        meta,
+        (odd_own, *odd_sides),
+        (*sends[:2], line),
+    )
+    odd_halo = swap_odd(*parts)
+    (even_line,) = call(
+        functools.partial(edge_kernel, False), meta, (object_field, *even_sides), (line,)
+    )
+    halos = (*odd_halo, swap_even(even_line))
     probes, tables, amps = call(
         functools.partial(prepare_kernel, side, windows),
         meta,
@@ -487,9 +549,9 @@
         flops=10**9,
         room=12 * MIB,
     )
-    *edges, rows = call(edges_kernel, meta, (object_field, *rims), (*sends, lines), after=amps)
-    halos = swap_rows(*edges)
-    field, total = call(centre_kernel, meta, (object_field, rows, *mids), (whole, whole))
+    field, total = call(
+        centre_kernel, meta, (object_field, odd_line, even_line, *mids), (whole, whole)
+    )
     for iteration in range(ITERS):
         last = iteration + 1 == ITERS
         field, total, *rest = call(
@@ -497,7 +559,7 @@
             meta,
             (field, total, *halos, probes, tables, amps),
             (whole, whole, *sends, *((mid_column,) * 2 if last else (mid_band,) * 4)),
-            scratch=(pltpu.VMEM((2, side, side), bf),),
+            scratch=(pltpu.VMEM((2, side, side), bf), pltpu.VMEM((2, side, side), jnp.float32)),
             aliases={1: 0, 2: 1},
             flops=windows * 16 * side**3,
             room=8 * MIB,

time: 212 us -> 207 us (0.976)
  waiting for transfers between devices: 67.5 us -> 63 us
  Pallas kernels: 29.1 us -> 26.1 us
  local copies, waits for them, and re-layouts: 4.8 us -> 7.09 us
    ppermute x7 -> x8, starting transfers between devices: 39 us -> 30.6 us  [swap_columns(): from_even = lax.ppermute(even_cells, 'gx', pairs(count, 0))]
    ppermute x16, starting transfers between devices: 44.9 us -> 52.6 us  [the longest x4 33.3 us: swap_odd(): straight = lax.ppermute(direct, 'gy', near + far)]
    ppermute x7 -> x8, waiting for transfers between devices: 24.8 us -> 20 us  [swap_columns(): from_odd = lax.ppermute(odd_cells, 'gx', pairs(count, 1))]
    pallas_call x12 -> x13, Pallas kernels: 29.1 us -> 26.1 us  [call(): pl.pallas_call(kernel, out_shape=shapes, in_specs=[smem, anywhere if far...]
    ppermute x16, waiting for transfers between devices: 21.2 us -> 23.8 us  [the longest x4 13.3 us: swap_odd(): straight = lax.ppermute(direct, 'gy', near + far)]
    ppermute x7 -> x8, waiting for transfers between devices: 21.6 us -> 19.3 us  [swap_columns(): from_even = lax.ppermute(even_cells, 'gx', pairs(count, 0))]
    unnamed x9 -> x13, local copies, waits for them, and re-layouts: 4.63 us -> 6.92 us
    ppermute x7 -> x8, starting transfers between devices: 22.9 us -> 23.3 us  [swap_columns(): from_odd = lax.ppermute(odd_cells, 'gx', pairs(count, 1))]
  transfers between devices with their start and end apart: 30 -> 32, of which waited for: 11 -> 13; matrix products, arithmetic and copies ran while one was open for 0% -> 0% of each run, Pallas kernels for 5% -> 6%
where the time goes in v6:
time: 207 us; the launch traced here: 204 us
  starting transfers between devices  106 us (51%)
  waiting for transfers between devices  63 us (30%)
  Pallas kernels  26.1 us (13%)
  local copies, waits for them, and re-layouts  7.09 us (3%)
    ppermute x4, starting transfers between devices, swap_odd(): straight = lax.ppermute(direct, 'gy', near + far)  33.3 us
    ppermute x8, starting transfers between devices, swap_columns(): from_even = lax.ppermute(even_cells, 'gx', pairs(count, 0))  30.6 us
    pallas_call x13, Pallas kernels, call(): pl.pallas_call(kernel, out_shape=shapes, in_specs=[smem, anywhere if far...  26.1 us
    ppermute x8, starting transfers between devices, swap_columns(): from_odd = lax.ppermute(odd_cells, 'gx', pairs(count, 1))  23.3 us
    ppermute x8, waiting for transfers between devices, swap_columns(): from_odd = lax.ppermute(odd_cells, 'gx', pairs(count, 1))  20 us
    ppermute x8, waiting for transfers between devices, swap_columns(): from_even = lax.ppermute(even_cells, 'gx', pairs(count, 0))  19.3 us
    ppermute x4, waiting for transfers between devices, swap_odd(): straight = lax.ppermute(direct, 'gy', near + far)  13.3 us
    ppermute x4, starting transfers between devices, swap_odd(): first = lax.ppermute(detour, 'gy', near + [(low, 0), (low + 1, count - 1)])  12.5 us
  transfers between devices with their start and end apart: 32, of which 13 were waited for; matrix products, arithmetic and copies ran while one was open for 0% of the time, Pallas kernels for 6%

profile of v6, /device:TPU:15, one launch (start us, length us, event | category | flops | bytes accessed | tf_op | source)
XLA Modules:
  0.0 203.9 jit_solution(8173385179369861509)
XLA Ops:
  3.8 6.1 %collective-permute-start.2 = (f32[2,128,128]{2,1,0:T(8,128)}, f32[2,128,128]{2,1,0:T(8,128)S(1)}, u32[]{:S(2)}, u32[]{:S(2)}) collective-permute-start(f32[2,128,128]{2,1,0:T(8,128)} %get-tuple-element.55), channel_id=1, source_target_pairs={{16,32},{48,64},{80,96},{112,128},{144,160},{176,192},{208,224},{3... | collective-permute-start | bytes 393224 | tf_op jit(solution)/shard_map/ppermute | solution.py:47
  20.4 2.0 collective-permute-done.1.side_even
  23.0 2.9 %collective-permute-start.7 = (f32[128,640]{1,0:T(8,128)S(1)}, f32[128,640]{1,0:T(8,128)S(1)}, u32[]{:S(2)}, u32[]{:S(2)}) collective-permute-start(f32[128,640]{1,0:T(8,128)S(1)} %get-tuple-element.62), channel_id=1, source_target_pairs={{1,2},{3,4},{5,6},{9,10},{11,12},{13,14},{2,1},{4,3},{6,5},{10,9},... | collective-permute-start | bytes 983048 | tf_op jit(solution)/shard_map/ppermute | solution.py:31
  25.9 8.5 %collective-permute-start.6 = (f32[128,896]{1,0:T(8,128)S(1)}, f32[128,896]{1,0:T(8,128)S(1)}, u32[]{:S(2)}, u32[]{:S(2)}) collective-permute-start(f32[128,896]{1,0:T(8,128)S(1)} %get-tuple-element.61), channel_id=1, source_target_pairs={{1,2},{3,4},{5,6},{9,10},{11,12},{13,14},{2,1},{4,3},{6,5},{10,9},... | collective-permute-start | bytes 1376264 | tf_op jit(solution)/shard_map/ppermute | solution.py:32
  35.7 2.4 %collective-permute-start.4 = (f32[2,256,128]{2,1,0:T(8,128)}, f32[2,256,128]{2,1,0:T(8,128)S(1)}, u32[]{:S(2)}, u32[]{:S(2)}) collective-permute-start(f32[2,256,128]{2,1,0:T(8,128)} %copy-done.5), channel_id=1, source_target_pairs={{16,32},{48,64},{80,96},{112,128},{144,160},{176,192},{208,224},{3... | collective-permute-start | bytes 786440 | tf_op jit(solution)/shard_map/ppermute | solution.py:47
  41.8 4.7 %shard_map.59 = (f32[4,2,256,256]{3,2,1,0:T(8,128)S(1)}, bf16[4,8,256,256]{3,2,1,0:T(8,128)(2,1)S(1)}, f32[4,256,256]{2,1,0:T(8,128)S(1)}) custom-call(s32[13]{0:T(128)S(1)} %concatenate.4.meta, f32[2,256,256]{2,1,0:T(8,128)S(1)} %copy-done.4, f32[4,256,256]{2,1,0:T(8,128)S(1)} %bitcast.7), custom_call_target="tpu_custom_call" | custom-call | flops 1000000000 | bytes 8912896 | tf_op jit(solution)/shard_map/pallas_call | solution.py:489
  46.5 4.1 %collective-permute-done.4.side_odd = f32[2,256,128]{2,1,0:T(8,128)S(1)} collective-permute-done((f32[2,256,128]{2,1,0:T(8,128)}, f32[2,256,128]{2,1,0:T(8,128)S(1)}, u32[]{:S(2)}, u32[]{:S(2)}) %collective-permute-start.4) | collective-permute-done | bytes 262176 | tf_op jit(solution)/shard_map/ppermute | solution.py:47
  50.6 5.9 %collective-permute-done.5.side_even = f32[2,256,128]{2,1,0:T(8,128)S(1)} collective-permute-done((f32[2,256,128]{2,1,0:T(8,128)S(1)}, f32[2,256,128]{2,1,0:T(8,128)S(1)}, u32[]{:S(2)}, u32[]{:S(2)}) %collective-permute-start.5) | collective-permute-done | bytes 262176 | tf_op jit(solution)/shard_map/ppermute | solution.py:48
  57.6 4.8 %shard_map.60 = (f32[2,768,768]{2,1,0:T(8,128)S(1)}, f32[2,768,768]{2,1,0:T(8,128)S(1)}, f32[128,896]{1,0:T(8,128)S(1)}, f32[128,640]{1,0:T(8,128)S(1)}, f32[2,1...) custom-call(s32[13]{0:T(128)S(1)} %concatenate.4.meta, ...), custom_call_target="tpu_custom_call", output_to_operand_aliasing={{0}: (1, {}), {1}: (2, {})} | custom-call | flops 1073741824 | bytes 30736384 | tf_op jit(solution)/shard_map/pallas_call | solution.py:489
  62.5 3.8 %collective-permute-start.11 = (f32[128,640]{1,0:T(8,128)S(1)}, f32[128,640]{1,0:T(8,128)S(1)}, u32[]{:S(2)}, u32[]{:S(2)}) collective-permute-start(f32[128,640]{1,0:T(8,128)S(1)} %get-tuple-element.69), channel_id=1, source_target_pairs={{1,2},{3,4},{5,6},{9,10},{11,12},{13,14},{2,1},{4,3},{6,5},{10,9},... | collective-permute-start | bytes 983048 | tf_op jit(solution)/shard_map/ppermute | solution.py:31
  66.2 7.5 %collective-permute-start.10 = (f32[128,896]{1,0:T(8,128)S(1)}, f32[128,896]{1,0:T(8,128)S(1)}, u32[]{:S(2)}, u32[]{:S(2)}) collective-permute-start(f32[128,896]{1,0:T(8,128)S(1)} %get-tuple-element.68), channel_id=1, source_target_pairs={{1,2},{3,4},{5,6},{9,10},{11,12},{13,14},{2,1},{4,3},{6,5},{10,9},... | collective-permute-start | bytes 1376264 | tf_op jit(solution)/shard_map/ppermute | solution.py:32
  75.1 7.1 %collective-permute-done.10.direct = f32[128,896]{1,0:T(8,128)S(1)} collective-permute-done((f32[128,896]{1,0:T(8,128)S(1)}, f32[128,896]{1,0:T(8,128)S(1)}, u32[]{:S(2)}, u32[]{:S(2)}) %collective-permute-start.10) | collective-permute-done | bytes 458784 | tf_op jit(solution)/shard_map/ppermute | solution.py:32
  82.2 3.8 %collective-permute-done.12.relayed = f32[128,640]{1,0:T(8,128)S(1)} collective-permute-done((f32[128,640]{1,0:T(8,128)S(1)}, f32[128,640]{1,0:T(8,128)S(1)}, u32[]{:S(2)}, u32[]{:S(2)}) %collective-permute-start.12) | collective-permute-done | bytes 327712 | tf_op jit(solution)/shard_map/ppermute | solution.py:33
  86.7 4.5 %collective-permute-start.14 = (f32[2,256,256]{2,1,0:T(8,128)S(1)}, f32[2,256,256]{2,1,0:T(8,128)S(1)}, u32[]{:S(2)}, u32[]{:S(2)}) collective-permute-start(f32[2,256,256]{2,1,0:T(8,128)S(1)} %get-tuple-element.72), channel_id=1, source_target_pairs={{16,32},{48,64},{80,96},{112,128},{144,160},{176,192},{208,224},{3... | collective-permute-start | bytes 1572872 | tf_op jit(solution)/shard_map/ppermute | solution.py:47
  91.2 12.4 %collective-permute-start.15 = (f32[2,256,256]{2,1,0:T(8,128)S(1)}, f32[2,256,256]{2,1,0:T(8,128)S(1)}, u32[]{:S(2)}, u32[]{:S(2)}) collective-permute-start(f32[2,256,256]{2,1,0:T(8,128)S(1)} %get-tuple-element.73), channel_id=1, source_target_pairs={{0,16},{32,48},{64,80},{96,112},{128,144},{160,176},{192,208},{224... | collective-permute-start | bytes 1572872 | tf_op jit(solution)/shard_map/ppermute | solution.py:48
  103.7 6.6 %collective-permute-done.15.band_even = f32[2,256,256]{2,1,0:T(8,128)S(1)} collective-permute-done((f32[2,256,256]{2,1,0:T(8,128)S(1)}, f32[2,256,256]{2,1,0:T(8,128)S(1)}, u32[]{:S(2)}, u32[]{:S(2)}) %collective-permute-start.15) | collective-permute-done | bytes 524320 | tf_op jit(solution)/shard_map/ppermute | solution.py:48
  111.6 3.8 %collective-permute-start.21 = (f32[128,640]{1,0:T(8,128)S(1)}, f32[128,640]{1,0:T(8,128)S(1)}, u32[]{:S(2)}, u32[]{:S(2)}) collective-permute-start(f32[128,640]{1,0:T(8,128)S(1)} %get-tuple-element.82), channel_id=1, source_target_pairs={{1,2},{3,4},{5,6},{9,10},{11,12},{13,14},{2,1},{4,3},{6,5},{10,9},... | collective-permute-start | bytes 983048 | tf_op jit(solution)/shard_map/ppermute | solution.py:31
  115.3 1.9 collective-permute-start.16
  117.3 2.3 %collective-permute-start.17 = (f32[2,128,256]{2,1,0:T(8,128)S(1)}, f32[2,128,256]{2,1,0:T(8,128)S(1)}, u32[]{:S(2)}, u32[]{:S(2)}) collective-permute-start(f32[2,128,256]{2,1,0:T(8,128)S(1)} %get-tuple-element.76), channel_id=1, source_target_pairs={{0,16},{32,48},{64,80},{96,112},{128,144},{160,176},{192,208},{224... | collective-permute-start | bytes 786440 | tf_op jit(solution)/shard_map/ppermute | solution.py:48
  119.5 8.2 %collective-permute-start.20 = (f32[128,896]{1,0:T(8,128)S(1)}, f32[128,896]{1,0:T(8,128)S(1)}, u32[]{:S(2)}, u32[]{:S(2)}) collective-permute-start(f32[128,896]{1,0:T(8,128)S(1)} %get-tuple-element.81), channel_id=1, source_target_pairs={{1,2},{3,4},{5,6},{9,10},{11,12},{13,14},{2,1},{4,3},{6,5},{10,9},... | collective-permute-start | bytes 1376264 | tf_op jit(solution)/shard_map/ppermute | solution.py:32
  129.0 2.6 %collective-permute-start.18 = (f32[2,128,256]{2,1,0:T(8,128)S(1)}, f32[2,128,256]{2,1,0:T(8,128)S(1)}, u32[]{:S(2)}, u32[]{:S(2)}) collective-permute-start(f32[2,128,256]{2,1,0:T(8,128)S(1)} %get-tuple-element.77), channel_id=1, source_target_pairs={{16,32},{48,64},{80,96},{112,128},{144,160},{176,192},{208,224},{3... | collective-permute-start | bytes 786440 | tf_op jit(solution)/shard_map/ppermute | solution.py:47
  131.6 2.1 %collective-permute-start.19 = (f32[2,128,256]{2,1,0:T(8,128)S(1)}, f32[2,128,256]{2,1,0:T(8,128)S(1)}, u32[]{:S(2)}, u32[]{:S(2)}) collective-permute-start(f32[2,128,256]{2,1,0:T(8,128)S(1)} %get-tuple-element.78), channel_id=1, source_target_pairs={{0,16},{32,48},{64,80},{96,112},{128,144},{160,176},{192,208},{224... | collective-permute-start | bytes 786440 | tf_op jit(solution)/shard_map/ppermute | solution.py:48
  133.7 15.9 %collective-permute-done.18.lower_odd = f32[2,128,256]{2,1,0:T(8,128)S(1)} collective-permute-done((f32[2,128,256]{2,1,0:T(8,128)S(1)}, f32[2,128,256]{2,1,0:T(8,128)S(1)}, u32[]{:S(2)}, u32[]{:S(2)}) %collective-permute-start.18) | collective-permute-done | bytes 262176 | tf_op jit(solution)/shard_map/ppermute | solution.py:47
  149.6 2.0 collective-permute-done.19.lower_even
  153.0 4.8 %shard_map.64 = (f32[2,768,768]{2,1,0:T(8,128)S(1)}, f32[2,768,768]{2,1,0:T(8,128)S(1)}, f32[128,896]{1,0:T(8,128)S(1)}, f32[128,640]{1,0:T(8,128)S(1)}, f32[2,1...) custom-call(s32[13]{0:T(128)S(1)} %concatenate.4.meta, ...), custom_call_target="tpu_custom_call", output_to_operand_aliasing={{0}: (1, {}), {1}: (2, {})} | custom-call | flops 1073741824 | bytes 30212096 | tf_op jit(solution)/shard_map/pallas_call | solution.py:489
  157.9 2.1 %collective-permute-start.25 = (f32[128,640]{1,0:T(8,128)S(1)}, f32[128,640]{1,0:T(8,128)S(1)}, u32[]{:S(2)}, u32[]{:S(2)}) collective-permute-start(f32[128,640]{1,0:T(8,128)S(1)} %get-tuple-element.87), channel_id=1, source_target_pairs={{1,2},{3,4},{5,6},{9,10},{11,12},{13,14},{2,1},{4,3},{6,5},{10,9},... | collective-permute-start | bytes 983048 | tf_op jit(solution)/shard_map/ppermute | solution.py:31
  160.0 9.2 %collective-permute-start.24 = (f32[128,896]{1,0:T(8,128)S(1)}, f32[128,896]{1,0:T(8,128)S(1)}, u32[]{:S(2)}, u32[]{:S(2)}) collective-permute-start(f32[128,896]{1,0:T(8,128)S(1)} %get-tuple-element.86), channel_id=1, source_target_pairs={{1,2},{3,4},{5,6},{9,10},{11,12},{13,14},{2,1},{4,3},{6,5},{10,9},... | collective-permute-start | bytes 1376264 | tf_op jit(solution)/shard_map/ppermute | solution.py:32
  170.4 1.9 collective-permute-start.28
  172.7 6.2 %collective-permute-done.24.direct = f32[128,896]{1,0:T(8,128)S(1)} collective-permute-done((f32[128,896]{1,0:T(8,128)S(1)}, f32[128,896]{1,0:T(8,128)S(1)}, u32[]{:S(2)}, u32[]{:S(2)}) %collective-permute-start.24) | collective-permute-done | bytes 458784 | tf_op jit(solution)/shard_map/ppermute | solution.py:32
  178.9 6.7 %collective-permute-done.26.relayed = f32[128,640]{1,0:T(8,128)S(1)} collective-permute-done((f32[128,640]{1,0:T(8,128)S(1)}, f32[128,640]{1,0:T(8,128)S(1)}, u32[]{:S(2)}, u32[]{:S(2)}) %collective-permute-start.26) | collective-permute-done | bytes 327712 | tf_op jit(solution)/shard_map/ppermute | solution.py:33
  188.2 10.4 %collective-permute-start.31 = (f32[2,256,128]{2,1,0:T(8,128)S(1)}, f32[2,256,128]{2,1,0:T(8,128)S(1)}, u32[]{:S(2)}, u32[]{:S(2)}) collective-permute-start(f32[2,256,128]{2,1,0:T(8,128)S(1)} %get-tuple-element.96), channel_id=1, source_target_pairs={{0,16},{32,48},{64,80},{96,112},{128,144},{160,176},{192,208},{224... | collective-permute-start | bytes 786440 | tf_op jit(solution)/shard_map/ppermute | solution.py:48
  199.0 2.6 %shard_map.66 = (f32[2,512,512]{2,1,0:T(8,128)}, f32[2,256,128]{2,1,0:T(8,128)S(1)}, f32[2,256,128]{2,1,0:T(8,128)S(1)}) custom-call(s32[13]{0:T(128)S(1)} %concatenate.4.meta, f32[2,768,768]{2,1,0:T(8,128)S(1)} %get-tuple-element.84.field, f32[2,768,768]{2,1,0:T(8,128)S(1)} %get-tuple-element.85.total, f32[2,128,768]{2,1,0:T(8,128)S(1)} %get-tuple-element.89.line, ...), custom_call_target="tpu_custom_call" | custom-call | bytes 14155776 | tf_op jit(solution)/shard_map/pallas_call | solution.py:489
  (61 shorter events, 33.4 us)
Async XLA Ops:
  3.8 11.3 %collective-permute-start.2 = (f32[2,128,128]{2,1,0:T(8,128)}, f32[2,128,128]{2,1,0:T(8,128)S(1)}, u32[]{:S(2)}, u32[]{:S(2)}) collective-permute-start(f32[2,128,128]{2,1,0:T(8,128)} %get-tuple-element.55), channel_id=1, source_target_pairs={{16,32},{48,64},{80,96},{112,128},{144,160},{176,192},{208,224},{3... | collective-permute-start | bytes 393224 | tf_op jit(solution)/shard_map/ppermute | solution.py:47
  9.9 6.8 %collective-permute-start.3 = (f32[2,128,128]{2,1,0:T(8,128)}, f32[2,128,128]{2,1,0:T(8,128)S(1)}, u32[]{:S(2)}, u32[]{:S(2)}) collective-permute-start(f32[2,128,128]{2,1,0:T(8,128)} %get-tuple-element.56), channel_id=1, source_target_pairs={{0,16},{32,48},{64,80},{96,112},{128,144},{160,176},{192,208},{224... | collective-permute-start | bytes 393224 | tf_op jit(solution)/shard_map/ppermute | solution.py:48
  10.0 10.3 %collective-permute-start = (f32[2,128,128]{2,1,0:T(8,128)}, f32[2,128,128]{2,1,0:T(8,128)S(1)}, u32[]{:S(2)}, u32[]{:S(2)}) collective-permute-start(f32[2,128,128]{2,1,0:T(8,128)} %get-tuple-element.52), channel_id=1, source_target_pairs={{16,32},{48,64},{80,96},{112,128},{144,160},{176,192},{208,224},{3... | collective-permute-start | bytes 393224 | tf_op jit(solution)/shard_map/ppermute | solution.py:47
  12.0 10.4 %collective-permute-start.1 = (f32[2,128,128]{2,1,0:T(8,128)S(1)}, f32[2,128,128]{2,1,0:T(8,128)S(1)}, u32[]{:S(2)}, u32[]{:S(2)}) collective-permute-start(f32[2,128,128]{2,1,0:T(8,128)S(1)} %get-tuple-element.53), channel_id=1, source_target_pairs={{0,16},{32,48},{64,80},{96,112},{128,144},{160,176},{192,208},{224... | collective-permute-start | bytes 393224 | tf_op jit(solution)/shard_map/ppermute | solution.py:48
  18.9 38.6 %collective-permute-start.9 = (f32[2,128,768]{2,1,0:T(8,128)S(1)}, f32[2,128,768]{2,1,0:T(8,128)S(1)}, u32[]{:S(2)}, u32[]{:S(2)}) collective-permute-start(f32[2,128,768]{2,1,0:T(8,128)S(1)} %shard_map.57.even_line), channel_id=1, source_target_pairs={{0,1},{2,3},{4,5},{6,7},{8,9},{10,11},{12,13},{14,15},{1,0},{3,2},... | collective-permute-start | bytes 2359304 | tf_op jit(solution)/shard_map/ppermute | solution.py:38
  23.0 11.4 %collective-permute-start.7 = (f32[128,640]{1,0:T(8,128)S(1)}, f32[128,640]{1,0:T(8,128)S(1)}, u32[]{:S(2)}, u32[]{:S(2)}) collective-permute-start(f32[128,640]{1,0:T(8,128)S(1)} %get-tuple-element.62), channel_id=1, source_target_pairs={{1,2},{3,4},{5,6},{9,10},{11,12},{13,14},{2,1},{4,3},{6,5},{10,9},... | collective-permute-start | bytes 983048 | tf_op jit(solution)/shard_map/ppermute | solution.py:31
  25.9 31.6 %collective-permute-start.6 = (f32[128,896]{1,0:T(8,128)S(1)}, f32[128,896]{1,0:T(8,128)S(1)}, u32[]{:S(2)}, u32[]{:S(2)}) collective-permute-start(f32[128,896]{1,0:T(8,128)S(1)} %get-tuple-element.61), channel_id=1, source_target_pairs={{1,2},{3,4},{5,6},{9,10},{11,12},{13,14},{2,1},{4,3},{6,5},{10,9},... | collective-permute-start | bytes 1376264 | tf_op jit(solution)/shard_map/ppermute | solution.py:32
  34.4 23.2 %collective-permute-start.8 = (f32[128,640]{1,0:T(8,128)S(1)}, f32[128,640]{1,0:T(8,128)S(1)}, u32[]{:S(2)}, u32[]{:S(2)}) collective-permute-start(f32[128,640]{1,0:T(8,128)S(1)} %collective-permute-done.7.halo_detour), channel_id=1, source_target_pairs={{0,8},{15,7},{16,24},{31,23},{32,40},{47,39},{48,56},{63,55},{64,7... | collective-permute-start | bytes 983048 | tf_op jit(solution)/shard_map/ppermute | solution.py:33
  35.7 14.9 %collective-permute-start.4 = (f32[2,256,128]{2,1,0:T(8,128)}, f32[2,256,128]{2,1,0:T(8,128)S(1)}, u32[]{:S(2)}, u32[]{:S(2)}) collective-permute-start(f32[2,256,128]{2,1,0:T(8,128)} %copy-done.5), channel_id=1, source_target_pairs={{16,32},{48,64},{80,96},{112,128},{144,160},{176,192},{208,224},{3... | collective-permute-start | bytes 786440 | tf_op jit(solution)/shard_map/ppermute | solution.py:47
  38.1 18.4 %collective-permute-start.5 = (f32[2,256,128]{2,1,0:T(8,128)S(1)}, f32[2,256,128]{2,1,0:T(8,128)S(1)}, u32[]{:S(2)}, u32[]{:S(2)}) collective-permute-start(f32[2,256,128]{2,1,0:T(8,128)S(1)} %get-tuple-element.58), channel_id=1, source_target_pairs={{0,16},{32,48},{64,80},{96,112},{128,144},{160,176},{192,208},{224... | collective-permute-start | bytes 786440 | tf_op jit(solution)/shard_map/ppermute | solution.py:48
  62.4 23.5 %collective-permute-start.13 = (f32[2,128,768]{2,1,0:T(8,128)S(1)}, f32[2,128,768]{2,1,0:T(8,128)S(1)}, u32[]{:S(2)}, u32[]{:S(2)}) collective-permute-start(f32[2,128,768]{2,1,0:T(8,128)S(1)} %get-tuple-element.70), channel_id=1, source_target_pairs={{0,1},{2,3},{4,5},{6,7},{8,9},{10,11},{12,13},{14,15},{1,0},{3,2},... | collective-permute-start | bytes 2359304 | tf_op jit(solution)/shard_map/ppermute | solution.py:38
  62.5 11.3 %collective-permute-start.11 = (f32[128,640]{1,0:T(8,128)S(1)}, f32[128,640]{1,0:T(8,128)S(1)}, u32[]{:S(2)}, u32[]{:S(2)}) collective-permute-start(f32[128,640]{1,0:T(8,128)S(1)} %get-tuple-element.69), channel_id=1, source_target_pairs={{1,2},{3,4},{5,6},{9,10},{11,12},{13,14},{2,1},{4,3},{6,5},{10,9},... | collective-permute-start | bytes 983048 | tf_op jit(solution)/shard_map/ppermute | solution.py:31
  66.2 15.9 %collective-permute-start.10 = (f32[128,896]{1,0:T(8,128)S(1)}, f32[128,896]{1,0:T(8,128)S(1)}, u32[]{:S(2)}, u32[]{:S(2)}) collective-permute-start(f32[128,896]{1,0:T(8,128)S(1)} %get-tuple-element.68), channel_id=1, source_target_pairs={{1,2},{3,4},{5,6},{9,10},{11,12},{13,14},{2,1},{4,3},{6,5},{10,9},... | collective-permute-start | bytes 1376264 | tf_op jit(solution)/shard_map/ppermute | solution.py:32
  73.8 12.1 %collective-permute-start.12 = (f32[128,640]{1,0:T(8,128)S(1)}, f32[128,640]{1,0:T(8,128)S(1)}, u32[]{:S(2)}, u32[]{:S(2)}) collective-permute-start(f32[128,640]{1,0:T(8,128)S(1)} %collective-permute-done.11.detour), channel_id=1, source_target_pairs={{0,8},{15,7},{16,24},{31,23},{32,40},{47,39},{48,56},{63,55},{64,7... | collective-permute-start | bytes 983048 | tf_op jit(solution)/shard_map/ppermute | solution.py:33
  86.7 16.9 %collective-permute-start.14 = (f32[2,256,256]{2,1,0:T(8,128)S(1)}, f32[2,256,256]{2,1,0:T(8,128)S(1)}, u32[]{:S(2)}, u32[]{:S(2)}) collective-permute-start(f32[2,256,256]{2,1,0:T(8,128)S(1)} %get-tuple-element.72), channel_id=1, source_target_pairs={{16,32},{48,64},{80,96},{112,128},{144,160},{176,192},{208,224},{3... | collective-permute-start | bytes 1572872 | tf_op jit(solution)/shard_map/ppermute | solution.py:47
  91.2 19.0 %collective-permute-start.15 = (f32[2,256,256]{2,1,0:T(8,128)S(1)}, f32[2,256,256]{2,1,0:T(8,128)S(1)}, u32[]{:S(2)}, u32[]{:S(2)}) collective-permute-start(f32[2,256,256]{2,1,0:T(8,128)S(1)} %get-tuple-element.73), channel_id=1, source_target_pairs={{0,16},{32,48},{64,80},{96,112},{128,144},{160,176},{192,208},{224... | collective-permute-start | bytes 1572872 | tf_op jit(solution)/shard_map/ppermute | solution.py:48
  111.5 41.5 %collective-permute-start.23 = (f32[2,128,768]{2,1,0:T(8,128)S(1)}, f32[2,128,768]{2,1,0:T(8,128)S(1)}, u32[]{:S(2)}, u32[]{:S(2)}) collective-permute-start(f32[2,128,768]{2,1,0:T(8,128)S(1)} %get-tuple-element.83), channel_id=1, source_target_pairs={{0,1},{2,3},{4,5},{6,7},{8,9},{10,11},{12,13},{14,15},{1,0},{3,2},... | collective-permute-start | bytes 2359304 | tf_op jit(solution)/shard_map/ppermute | solution.py:38
  111.6 16.1 %collective-permute-start.21 = (f32[128,640]{1,0:T(8,128)S(1)}, f32[128,640]{1,0:T(8,128)S(1)}, u32[]{:S(2)}, u32[]{:S(2)}) collective-permute-start(f32[128,640]{1,0:T(8,128)S(1)} %get-tuple-element.82), channel_id=1, source_target_pairs={{1,2},{3,4},{5,6},{9,10},{11,12},{13,14},{2,1},{4,3},{6,5},{10,9},... | collective-permute-start | bytes 983048 | tf_op jit(solution)/shard_map/ppermute | solution.py:31
  115.3 13.7 %collective-permute-start.16 = (f32[2,128,256]{2,1,0:T(8,128)S(1)}, f32[2,128,256]{2,1,0:T(8,128)S(1)}, u32[]{:S(2)}, u32[]{:S(2)}) collective-permute-start(f32[2,128,256]{2,1,0:T(8,128)S(1)} %get-tuple-element.75), channel_id=1, source_target_pairs={{16,32},{48,64},{80,96},{112,128},{144,160},{176,192},{208,224},{3... | collective-permute-start | bytes 786440 | tf_op jit(solution)/shard_map/ppermute | solution.py:47
  117.3 14.4 %collective-permute-start.17 = (f32[2,128,256]{2,1,0:T(8,128)S(1)}, f32[2,128,256]{2,1,0:T(8,128)S(1)}, u32[]{:S(2)}, u32[]{:S(2)}) collective-permute-start(f32[2,128,256]{2,1,0:T(8,128)S(1)} %get-tuple-element.76), channel_id=1, source_target_pairs={{0,16},{32,48},{64,80},{96,112},{128,144},{160,176},{192,208},{224... | collective-permute-start | bytes 786440 | tf_op jit(solution)/shard_map/ppermute | solution.py:48
  119.5 33.5 %collective-permute-start.20 = (f32[128,896]{1,0:T(8,128)S(1)}, f32[128,896]{1,0:T(8,128)S(1)}, u32[]{:S(2)}, u32[]{:S(2)}) collective-permute-start(f32[128,896]{1,0:T(8,128)S(1)} %get-tuple-element.81), channel_id=1, source_target_pairs={{1,2},{3,4},{5,6},{9,10},{11,12},{13,14},{2,1},{4,3},{6,5},{10,9},... | collective-permute-start | bytes 1376264 | tf_op jit(solution)/shard_map/ppermute | solution.py:32
  127.7 25.3 %collective-permute-start.22 = (f32[128,640]{1,0:T(8,128)S(1)}, f32[128,640]{1,0:T(8,128)S(1)}, u32[]{:S(2)}, u32[]{:S(2)}) collective-permute-start(f32[128,640]{1,0:T(8,128)S(1)} %collective-permute-done.21.halo_detour), channel_id=1, source_target_pairs={{0,8},{15,7},{16,24},{31,23},{32,40},{47,39},{48,56},{63,55},{64,7... | collective-permute-start | bytes 983048 | tf_op jit(solution)/shard_map/ppermute | solution.py:33
  129.0 20.6 %collective-permute-start.18 = (f32[2,128,256]{2,1,0:T(8,128)S(1)}, f32[2,128,256]{2,1,0:T(8,128)S(1)}, u32[]{:S(2)}, u32[]{:S(2)}) collective-permute-start(f32[2,128,256]{2,1,0:T(8,128)S(1)} %get-tuple-element.77), channel_id=1, source_target_pairs={{16,32},{48,64},{80,96},{112,128},{144,160},{176,192},{208,224},{3... | collective-permute-start | bytes 786440 | tf_op jit(solution)/shard_map/ppermute | solution.py:47
  131.6 20.0 %collective-permute-start.19 = (f32[2,128,256]{2,1,0:T(8,128)S(1)}, f32[2,128,256]{2,1,0:T(8,128)S(1)}, u32[]{:S(2)}, u32[]{:S(2)}) collective-permute-start(f32[2,128,256]{2,1,0:T(8,128)S(1)} %get-tuple-element.78), channel_id=1, source_target_pairs={{0,16},{32,48},{64,80},{96,112},{128,144},{160,176},{192,208},{224... | collective-permute-start | bytes 786440 | tf_op jit(solution)/shard_map/ppermute | solution.py:48
  157.8 27.8 %collective-permute-start.27 = (f32[2,128,768]{2,1,0:T(8,128)S(1)}, f32[2,128,768]{2,1,0:T(8,128)S(1)}, u32[]{:S(2)}, u32[]{:S(2)}) collective-permute-start(f32[2,128,768]{2,1,0:T(8,128)S(1)} %get-tuple-element.88), channel_id=1, source_target_pairs={{0,1},{2,3},{4,5},{6,7},{8,9},{10,11},{12,13},{14,15},{1,0},{3,2},... | collective-permute-start | bytes 2359304 | tf_op jit(solution)/shard_map/ppermute | solution.py:38
  157.9 11.2 %collective-permute-start.25 = (f32[128,640]{1,0:T(8,128)S(1)}, f32[128,640]{1,0:T(8,128)S(1)}, u32[]{:S(2)}, u32[]{:S(2)}) collective-permute-start(f32[128,640]{1,0:T(8,128)S(1)} %get-tuple-element.87), channel_id=1, source_target_pairs={{1,2},{3,4},{5,6},{9,10},{11,12},{13,14},{2,1},{4,3},{6,5},{10,9},... | collective-permute-start | bytes 983048 | tf_op jit(solution)/shard_map/ppermute | solution.py:31
  160.0 18.9 %collective-permute-start.24 = (f32[128,896]{1,0:T(8,128)S(1)}, f32[128,896]{1,0:T(8,128)S(1)}, u32[]{:S(2)}, u32[]{:S(2)}) collective-permute-start(f32[128,896]{1,0:T(8,128)S(1)} %get-tuple-element.86), channel_id=1, source_target_pairs={{1,2},{3,4},{5,6},{9,10},{11,12},{13,14},{2,1},{4,3},{6,5},{10,9},... | collective-permute-start | bytes 1376264 | tf_op jit(solution)/shard_map/ppermute | solution.py:32
  169.1 16.4 %collective-permute-start.26 = (f32[128,640]{1,0:T(8,128)S(1)}, f32[128,640]{1,0:T(8,128)S(1)}, u32[]{:S(2)}, u32[]{:S(2)}) collective-permute-start(f32[128,640]{1,0:T(8,128)S(1)} %collective-permute-done.25.detour), channel_id=1, source_target_pairs={{0,8},{15,7},{16,24},{31,23},{32,40},{47,39},{48,56},{63,55},{64,7... | collective-permute-start | bytes 983048 | tf_op jit(solution)/shard_map/ppermute | solution.py:33
  170.4 28.2 %collective-permute-start.28 = (f32[2,256,128]{2,1,0:T(8,128)S(1)}, f32[2,256,128]{2,1,0:T(8,128)S(1)}, u32[]{:S(2)}, u32[]{:S(2)}) collective-permute-start(f32[2,256,128]{2,1,0:T(8,128)S(1)} %get-tuple-element.90), channel_id=1, source_target_pairs={{16,32},{48,64},{80,96},{112,128},{144,160},{176,192},{208,224},{3... | collective-permute-start | bytes 786440 | tf_op jit(solution)/shard_map/ppermute | solution.py:47
  172.4 26.7 %collective-permute-start.29 = (f32[2,256,128]{2,1,0:T(8,128)S(1)}, f32[2,256,128]{2,1,0:T(8,128)S(1)}, u32[]{:S(2)}, u32[]{:S(2)}) collective-permute-start(f32[2,256,128]{2,1,0:T(8,128)S(1)} %get-tuple-element.91), channel_id=1, source_target_pairs={{0,16},{32,48},{64,80},{96,112},{128,144},{160,176},{192,208},{224... | collective-permute-start | bytes 786440 | tf_op jit(solution)/shard_map/ppermute | solution.py:48
  186.3 15.4 %collective-permute-start.30 = (f32[2,256,128]{2,1,0:T(8,128)S(1)}, f32[2,256,128]{2,1,0:T(8,128)S(1)}, u32[]{:S(2)}, u32[]{:S(2)}) collective-permute-start(f32[2,256,128]{2,1,0:T(8,128)S(1)} %get-tuple-element.95), channel_id=1, source_target_pairs={{16,32},{48,64},{80,96},{112,128},{144,160},{176,192},{208,224},{3... | collective-permute-start | bytes 786440 | tf_op jit(solution)/shard_map/ppermute | solution.py:47
  188.2 14.2 %collective-permute-start.31 = (f32[2,256,128]{2,1,0:T(8,128)S(1)}, f32[2,256,128]{2,1,0:T(8,128)S(1)}, u32[]{:S(2)}, u32[]{:S(2)}) collective-permute-start(f32[2,256,128]{2,1,0:T(8,128)S(1)} %get-tuple-element.96), channel_id=1, source_target_pairs={{0,16},{32,48},{64,80},{96,112},{128,144},{160,176},{192,208},{224... | collective-permute-start | bytes 786440 | tf_op jit(solution)/shard_map/ppermute | solution.py:48
  (6 other events, 61.0 us)

commit v7 on v6

--- a/solution.py
+++ b/solution.py
@@ -325,10 +325,9 @@
     return pl.ds(pl.multiple_of(margin + low * (tile - half), half), half)
 
 
-def sides_kernel(meta, own, odd_a, odd_b, even_a, even_b, mid_a, mid_b, odd_own):
-    tile, half = own.shape[1], odd_a.shape[1]
+def sides_kernel(meta, own, even_a, even_b, mid_a, mid_b, odd_own):
+    tile, half = own.shape[1], even_a.shape[1]
     for rows, pair in (
-        (strip(meta, True, half, tile, 0), (odd_a, odd_b)),
         (strip(meta, False, half, tile, 0), (even_a, even_b)),
         (slice(half, tile - half), (mid_a, mid_b)),
     ):
@@ -521,15 +520,22 @@
     sends = ((half, wide + CUT), (half, wide - CUT), line)
 
     block = (2, half, half)
+
+    def corner(low, right):
+        return object_field[:, low * (tile - half) :, right * (tile - half) :][:, :half, :half]
+
+    right, left = [
+        jnp.where(odd_row == 1, corner(1, at), corner(0, at)) for at in (1, 0)
+    ]
+    odd_sides = swap_columns(jnp.where(odd_col == 1, right, left), jnp.where(odd_col == 1, left, right))
     *sides, odd_own = call(
         sides_kernel,
         places,
         (object_field,),
-        (*(block,) * 4, *(mid_column,) * 2, (2, half, tile)),
-    )
-    odd_sides = swap_columns(*sides[:2])
-    even_sides = swap_columns(*sides[2:4])
-    mids = swap_columns(*sides[4:])
+        (block, block, mid_column, mid_column, (2, half, tile)),
+    )
+    even_sides = swap_columns(*sides[:2])
+    mids = swap_columns(*sides[2:])
     *parts, odd_line = call(
         functools.partial(edge_kernel, True),
         meta,

time: 207 us -> 206 us (level); the launches traced: 204 us -> 205 us
    ppermute x4, starting transfers between devices: 33.3 us -> 27.6 us  [swap_odd(): straight = lax.ppermute(direct, 'gy', near + far)]
    ppermute x8, waiting for transfers between devices: 20 us -> 24.3 us  [swap_columns(): from_odd = lax.ppermute(odd_cells, 'gx', pairs(count, 1))]
    ppermute x8, starting transfers between devices: 30.6 us -> 34.9 us  [swap_columns(): from_even = lax.ppermute(even_cells, 'gx', pairs(count, 0))]
    ppermute x8, waiting for transfers between devices: 19.3 us -> 15 us  [swap_columns(): from_even = lax.ppermute(even_cells, 'gx', pairs(count, 0))]
    ppermute x4, starting transfers between devices: 12.5 us -> 15.5 us  [swap_odd(): first = lax.ppermute(detour, 'gy', near + [(low, 0), (low + 1, count - 1)])]
  transfers between devices with their start and end apart: 32 -> 32, of which waited for: 13 -> 13; matrix products, arithmetic and copies ran while one was open for 0% -> 1% of each run, Pallas kernels for 6% -> 6%
where the time goes in v7:
time: 206 us; the launch traced here: 205 us
  starting transfers between devices  108 us (52%)
  waiting for transfers between devices  61.2 us (30%)
  Pallas kernels  26 us (13%)
  local copies, waits for them, and re-layouts  7.09 us (3%)
    ppermute x8, starting transfers between devices, swap_columns(): from_even = lax.ppermute(even_cells, 'gx', pairs(count, 0))  34.9 us
    ppermute x4, starting transfers between devices, swap_odd(): straight = lax.ppermute(direct, 'gy', near + far)  27.6 us
    pallas_call x13, Pallas kernels, call(): pl.pallas_call(kernel, out_shape=shapes, in_specs=[smem, anywhere if far...  26 us
    ppermute x8, waiting for transfers between devices, swap_columns(): from_odd = lax.ppermute(odd_cells, 'gx', pairs(count, 1))  24.3 us
    ppermute x8, starting transfers between devices, swap_columns(): from_odd = lax.ppermute(odd_cells, 'gx', pairs(count, 1))  22.8 us
    ppermute x4, starting transfers between devices, swap_odd(): first = lax.ppermute(detour, 'gy', near + [(low, 0), (low + 1, count - 1)])  15.5 us
    ppermute x8, waiting for transfers between devices, swap_columns(): from_even = lax.ppermute(even_cells, 'gx', pairs(count, 0))  15 us
    ppermute x4, waiting for transfers between devices, swap_odd(): straight = lax.ppermute(direct, 'gy', near + far)  11.7 us
  transfers between devices with their start and end apart: 32, of which 13 were waited for; matrix products, arithmetic and copies ran while one was open for 1% of the time, Pallas kernels for 6%

profile of v7, /device:TPU:15, one launch (start us, length us, event | category | flops | bytes accessed | tf_op | source)
XLA Modules:
  0.0 205.4 jit_solution(4067254874131787743)
XLA Ops:
  3.7 6.1 %collective-permute-start.2 = (f32[2,128,128]{2,1,0:T(8,128)}, f32[2,128,128]{2,1,0:T(8,128)S(1)}, u32[]{:S(2)}, u32[]{:S(2)}) collective-permute-start(f32[2,128,128]{2,1,0:T(8,128)} %get-tuple-element.51), channel_id=1, source_target_pairs={{16,32},{48,64},{80,96},{112,128},{144,160},{176,192},{208,224},{3... | collective-permute-start | bytes 393224 | tf_op jit(solution)/shard_map/ppermute | solution.py:47
  13.2 1.9 collective-permute-start
  22.5 4.7 %collective-permute-start.7 = (f32[128,640]{1,0:T(8,128)S(1)}, f32[128,640]{1,0:T(8,128)S(1)}, u32[]{:S(2)}, u32[]{:S(2)}) collective-permute-start(f32[128,640]{1,0:T(8,128)S(1)} %get-tuple-element.58), channel_id=1, source_target_pairs={{1,2},{3,4},{5,6},{9,10},{11,12},{13,14},{2,1},{4,3},{6,5},{10,9},... | collective-permute-start | bytes 983048 | tf_op jit(solution)/shard_map/ppermute | solution.py:31
  27.1 8.3 %collective-permute-start.6 = (f32[128,896]{1,0:T(8,128)S(1)}, f32[128,896]{1,0:T(8,128)S(1)}, u32[]{:S(2)}, u32[]{:S(2)}) collective-permute-start(f32[128,896]{1,0:T(8,128)S(1)} %get-tuple-element.57), channel_id=1, source_target_pairs={{1,2},{3,4},{5,6},{9,10},{11,12},{13,14},{2,1},{4,3},{6,5},{10,9},... | collective-permute-start | bytes 1376264 | tf_op jit(solution)/shard_map/ppermute | solution.py:32
  36.8 2.9 %collective-permute-start.4 = (f32[2,256,128]{2,1,0:T(8,128)}, f32[2,256,128]{2,1,0:T(8,128)S(1)}, u32[]{:S(2)}, u32[]{:S(2)}) collective-permute-start(f32[2,256,128]{2,1,0:T(8,128)} %copy-done.5), channel_id=1, source_target_pairs={{16,32},{48,64},{80,96},{112,128},{144,160},{176,192},{208,224},{3... | collective-permute-start | bytes 786440 | tf_op jit(solution)/shard_map/ppermute | solution.py:47
  42.1 4.7 %shard_map.59 = (f32[4,2,256,256]{3,2,1,0:T(8,128)S(1)}, bf16[4,8,256,256]{3,2,1,0:T(8,128)(2,1)S(1)}, f32[4,256,256]{2,1,0:T(8,128)S(1)}) custom-call(s32[13]{0:T(128)S(1)} %concatenate.4.meta, f32[2,256,256]{2,1,0:T(8,128)S(1)} %copy-done.4, f32[4,256,256]{2,1,0:T(8,128)S(1)} %bitcast.7), custom_call_target="tpu_custom_call" | custom-call | flops 1000000000 | bytes 8912896 | tf_op jit(solution)/shard_map/pallas_call | solution.py:488
  46.8 4.1 %collective-permute-done.4.side_odd = f32[2,256,128]{2,1,0:T(8,128)S(1)} collective-permute-done((f32[2,256,128]{2,1,0:T(8,128)}, f32[2,256,128]{2,1,0:T(8,128)S(1)}, u32[]{:S(2)}, u32[]{:S(2)}) %collective-permute-start.4) | collective-permute-done | bytes 262176 | tf_op jit(solution)/shard_map/ppermute | solution.py:47
  50.9 4.9 %collective-permute-done.5.side_even = f32[2,256,128]{2,1,0:T(8,128)S(1)} collective-permute-done((f32[2,256,128]{2,1,0:T(8,128)S(1)}, f32[2,256,128]{2,1,0:T(8,128)S(1)}, u32[]{:S(2)}, u32[]{:S(2)}) %collective-permute-start.5) | collective-permute-done | bytes 262176 | tf_op jit(solution)/shard_map/ppermute | solution.py:48
  56.9 4.8 %shard_map.60 = (f32[2,768,768]{2,1,0:T(8,128)S(1)}, f32[2,768,768]{2,1,0:T(8,128)S(1)}, f32[128,896]{1,0:T(8,128)S(1)}, f32[128,640]{1,0:T(8,128)S(1)}, f32[2,1...) custom-call(s32[13]{0:T(128)S(1)} %concatenate.4.meta, ...), custom_call_target="tpu_custom_call", output_to_operand_aliasing={{0}: (1, {}), {1}: (2, {})} | custom-call | flops 1073741824 | bytes 30736384 | tf_op jit(solution)/shard_map/pallas_call | solution.py:488
  61.8 5.1 %collective-permute-start.11 = (f32[128,640]{1,0:T(8,128)S(1)}, f32[128,640]{1,0:T(8,128)S(1)}, u32[]{:S(2)}, u32[]{:S(2)}) collective-permute-start(f32[128,640]{1,0:T(8,128)S(1)} %get-tuple-element.65), channel_id=1, source_target_pairs={{1,2},{3,4},{5,6},{9,10},{11,12},{13,14},{2,1},{4,3},{6,5},{10,9},... | collective-permute-start | bytes 983048 | tf_op jit(solution)/shard_map/ppermute | solution.py:31
  66.9 6.1 %collective-permute-start.10 = (f32[128,896]{1,0:T(8,128)S(1)}, f32[128,896]{1,0:T(8,128)S(1)}, u32[]{:S(2)}, u32[]{:S(2)}) collective-permute-start(f32[128,896]{1,0:T(8,128)S(1)} %get-tuple-element.64), channel_id=1, source_target_pairs={{1,2},{3,4},{5,6},{9,10},{11,12},{13,14},{2,1},{4,3},{6,5},{10,9},... | collective-permute-start | bytes 1376264 | tf_op jit(solution)/shard_map/ppermute | solution.py:32
  74.3 8.5 %collective-permute-done.10.direct = f32[128,896]{1,0:T(8,128)S(1)} collective-permute-done((f32[128,896]{1,0:T(8,128)S(1)}, f32[128,896]{1,0:T(8,128)S(1)}, u32[]{:S(2)}, u32[]{:S(2)}) %collective-permute-start.10) | collective-permute-done | bytes 458784 | tf_op jit(solution)/shard_map/ppermute | solution.py:32
  82.8 4.9 %collective-permute-done.12.relayed = f32[128,640]{1,0:T(8,128)S(1)} collective-permute-done((f32[128,640]{1,0:T(8,128)S(1)}, f32[128,640]{1,0:T(8,128)S(1)}, u32[]{:S(2)}, u32[]{:S(2)}) %collective-permute-start.12) | collective-permute-done | bytes 327712 | tf_op jit(solution)/shard_map/ppermute | solution.py:33
  88.5 2.6 %collective-permute-start.14 = (f32[2,256,256]{2,1,0:T(8,128)S(1)}, f32[2,256,256]{2,1,0:T(8,128)S(1)}, u32[]{:S(2)}, u32[]{:S(2)}) collective-permute-start(f32[2,256,256]{2,1,0:T(8,128)S(1)} %get-tuple-element.68), channel_id=1, source_target_pairs={{16,32},{48,64},{80,96},{112,128},{144,160},{176,192},{208,224},{3... | collective-permute-start | bytes 1572872 | tf_op jit(solution)/shard_map/ppermute | solution.py:47
  91.1 9.5 %collective-permute-start.15 = (f32[2,256,256]{2,1,0:T(8,128)S(1)}, f32[2,256,256]{2,1,0:T(8,128)S(1)}, u32[]{:S(2)}, u32[]{:S(2)}) collective-permute-start(f32[2,256,256]{2,1,0:T(8,128)S(1)} %get-tuple-element.69), channel_id=1, source_target_pairs={{0,16},{32,48},{64,80},{96,112},{128,144},{160,176},{192,208},{224... | collective-permute-start | bytes 1572872 | tf_op jit(solution)/shard_map/ppermute | solution.py:48
  102.2 7.2 %collective-permute-done.15.band_even = f32[2,256,256]{2,1,0:T(8,128)S(1)} collective-permute-done((f32[2,256,256]{2,1,0:T(8,128)S(1)}, f32[2,256,256]{2,1,0:T(8,128)S(1)}, u32[]{:S(2)}, u32[]{:S(2)}) %collective-permute-start.15) | collective-permute-done | bytes 524320 | tf_op jit(solution)/shard_map/ppermute | solution.py:48
  110.8 3.8 %collective-permute-start.21 = (f32[128,640]{1,0:T(8,128)S(1)}, f32[128,640]{1,0:T(8,128)S(1)}, u32[]{:S(2)}, u32[]{:S(2)}) collective-permute-start(f32[128,640]{1,0:T(8,128)S(1)} %get-tuple-element.78), channel_id=1, source_target_pairs={{1,2},{3,4},{5,6},{9,10},{11,12},{13,14},{2,1},{4,3},{6,5},{10,9},... | collective-permute-start | bytes 983048 | tf_op jit(solution)/shard_map/ppermute | solution.py:31
  114.5 1.9 collective-permute-start.16
  116.5 1.9 collective-permute-start.17
  118.3 6.8 %collective-permute-start.20 = (f32[128,896]{1,0:T(8,128)S(1)}, f32[128,896]{1,0:T(8,128)S(1)}, u32[]{:S(2)}, u32[]{:S(2)}) collective-permute-start(f32[128,896]{1,0:T(8,128)S(1)} %get-tuple-element.77), channel_id=1, source_target_pairs={{1,2},{3,4},{5,6},{9,10},{11,12},{13,14},{2,1},{4,3},{6,5},{10,9},... | collective-permute-start | bytes 1376264 | tf_op jit(solution)/shard_map/ppermute | solution.py:32
  127.2 3.1 %collective-permute-start.18 = (f32[2,128,256]{2,1,0:T(8,128)S(1)}, f32[2,128,256]{2,1,0:T(8,128)S(1)}, u32[]{:S(2)}, u32[]{:S(2)}) collective-permute-start(f32[2,128,256]{2,1,0:T(8,128)S(1)} %get-tuple-element.73), channel_id=1, source_target_pairs={{16,32},{48,64},{80,96},{112,128},{144,160},{176,192},{208,224},{3... | collective-permute-start | bytes 786440 | tf_op jit(solution)/shard_map/ppermute | solution.py:47
  132.0 16.7 %collective-permute-done.18.lower_odd = f32[2,128,256]{2,1,0:T(8,128)S(1)} collective-permute-done((f32[2,128,256]{2,1,0:T(8,128)S(1)}, f32[2,128,256]{2,1,0:T(8,128)S(1)}, u32[]{:S(2)}, u32[]{:S(2)}) %collective-permute-start.18) | collective-permute-done | bytes 262176 | tf_op jit(solution)/shard_map/ppermute | solution.py:47
  151.9 4.8 %shard_map.64 = (f32[2,768,768]{2,1,0:T(8,128)S(1)}, f32[2,768,768]{2,1,0:T(8,128)S(1)}, f32[128,896]{1,0:T(8,128)S(1)}, f32[128,640]{1,0:T(8,128)S(1)}, f32[2,1...) custom-call(s32[13]{0:T(128)S(1)} %concatenate.4.meta, ...), custom_call_target="tpu_custom_call", output_to_operand_aliasing={{0}: (1, {}), {1}: (2, {})} | custom-call | flops 1073741824 | bytes 30212096 | tf_op jit(solution)/shard_map/pallas_call | solution.py:488
  156.8 1.9 collective-permute-start.25
  158.8 6.5 %collective-permute-start.24 = (f32[128,896]{1,0:T(8,128)S(1)}, f32[128,896]{1,0:T(8,128)S(1)}, u32[]{:S(2)}, u32[]{:S(2)}) collective-permute-start(f32[128,896]{1,0:T(8,128)S(1)} %get-tuple-element.82), channel_id=1, source_target_pairs={{1,2},{3,4},{5,6},{9,10},{11,12},{13,14},{2,1},{4,3},{6,5},{10,9},... | collective-permute-start | bytes 1376264 | tf_op jit(solution)/shard_map/ppermute | solution.py:32
  166.5 2.3 %collective-permute-start.28 = (f32[2,256,128]{2,1,0:T(8,128)S(1)}, f32[2,256,128]{2,1,0:T(8,128)S(1)}, u32[]{:S(2)}, u32[]{:S(2)}) collective-permute-start(f32[2,256,128]{2,1,0:T(8,128)S(1)} %get-tuple-element.86), channel_id=1, source_target_pairs={{16,32},{48,64},{80,96},{112,128},{144,160},{176,192},{208,224},{3... | collective-permute-start | bytes 786440 | tf_op jit(solution)/shard_map/ppermute | solution.py:47
  168.8 3.4 %collective-permute-start.29 = (f32[2,256,128]{2,1,0:T(8,128)S(1)}, f32[2,256,128]{2,1,0:T(8,128)S(1)}, u32[]{:S(2)}, u32[]{:S(2)}) collective-permute-start(f32[2,256,128]{2,1,0:T(8,128)S(1)} %get-tuple-element.87), channel_id=1, source_target_pairs={{0,16},{32,48},{64,80},{96,112},{128,144},{160,176},{192,208},{224... | collective-permute-start | bytes 786440 | tf_op jit(solution)/shard_map/ppermute | solution.py:48
  172.1 3.1 %collective-permute-done.24.direct = f32[128,896]{1,0:T(8,128)S(1)} collective-permute-done((f32[128,896]{1,0:T(8,128)S(1)}, f32[128,896]{1,0:T(8,128)S(1)}, u32[]{:S(2)}, u32[]{:S(2)}) %collective-permute-start.24) | collective-permute-done | bytes 458784 | tf_op jit(solution)/shard_map/ppermute | solution.py:32
  175.3 5.3 %collective-permute-done.26.relayed = f32[128,640]{1,0:T(8,128)S(1)} collective-permute-done((f32[128,640]{1,0:T(8,128)S(1)}, f32[128,640]{1,0:T(8,128)S(1)}, u32[]{:S(2)}, u32[]{:S(2)}) %collective-permute-start.26) | collective-permute-done | bytes 327712 | tf_op jit(solution)/shard_map/ppermute | solution.py:33
  181.3 1.9 collective-permute-start.30
  183.2 16.9 %collective-permute-start.31 = (f32[2,256,128]{2,1,0:T(8,128)S(1)}, f32[2,256,128]{2,1,0:T(8,128)S(1)}, u32[]{:S(2)}, u32[]{:S(2)}) collective-permute-start(f32[2,256,128]{2,1,0:T(8,128)S(1)} %get-tuple-element.92), channel_id=1, source_target_pairs={{0,16},{32,48},{64,80},{96,112},{128,144},{160,176},{192,208},{224... | collective-permute-start | bytes 786440 | tf_op jit(solution)/shard_map/ppermute | solution.py:48
  200.1 2.6 %shard_map.66 = (f32[2,512,512]{2,1,0:T(8,128)}, f32[2,256,128]{2,1,0:T(8,128)S(1)}, f32[2,256,128]{2,1,0:T(8,128)S(1)}) custom-call(s32[13]{0:T(128)S(1)} %concatenate.4.meta, f32[2,768,768]{2,1,0:T(8,128)S(1)} %get-tuple-element.80.field, f32[2,768,768]{2,1,0:T(8,128)S(1)} %get-tuple-element.81.total, f32[2,128,768]{2,1,0:T(8,128)S(1)} %get-tuple-element.85.line, ...), custom_call_target="tpu_custom_call" | custom-call | bytes 14155776 | tf_op jit(solution)/shard_map/pallas_call | solution.py:488
  (62 shorter events, 35.1 us)
Async XLA Ops:
  3.7 13.0 %collective-permute-start.2 = (f32[2,128,128]{2,1,0:T(8,128)}, f32[2,128,128]{2,1,0:T(8,128)S(1)}, u32[]{:S(2)}, u32[]{:S(2)}) collective-permute-start(f32[2,128,128]{2,1,0:T(8,128)} %get-tuple-element.51), channel_id=1, source_target_pairs={{16,32},{48,64},{80,96},{112,128},{144,160},{176,192},{208,224},{3... | collective-permute-start | bytes 393224 | tf_op jit(solution)/shard_map/ppermute | solution.py:47
  9.8 6.9 %collective-permute-start.3 = (f32[2,128,128]{2,1,0:T(8,128)S(1)}, f32[2,128,128]{2,1,0:T(8,128)S(1)}, u32[]{:S(2)}, u32[]{:S(2)}) collective-permute-start(f32[2,128,128]{2,1,0:T(8,128)S(1)} %get-tuple-element.52), channel_id=1, source_target_pairs={{0,16},{32,48},{64,80},{96,112},{128,144},{160,176},{192,208},{224... | collective-permute-start | bytes 393224 | tf_op jit(solution)/shard_map/ppermute | solution.py:48
  11.8 9.0 %collective-permute-start.1 = (f32[2,128,128]{2,1,0:T(8,128)}, f32[2,128,128]{2,1,0:T(8,128)S(1)}, u32[]{:S(2)}, u32[]{:S(2)}) collective-permute-start(f32[2,128,128]{2,1,0:T(8,128)} %get-tuple-element.93), channel_id=1, source_target_pairs={{0,16},{32,48},{64,80},{96,112},{128,144},{160,176},{192,208},{224... | collective-permute-start | bytes 393224 | tf_op jit(solution)/shard_map/ppermute | solution.py:48
  13.2 8.6 %collective-permute-start = (f32[2,128,128]{2,1,0:T(8,128)}, f32[2,128,128]{2,1,0:T(8,128)S(1)}, u32[]{:S(2)}, u32[]{:S(2)}) collective-permute-start(f32[2,128,128]{2,1,0:T(8,128)} %get-tuple-element.94), channel_id=1, source_target_pairs={{16,32},{48,64},{80,96},{112,128},{144,160},{176,192},{208,224},{3... | collective-permute-start | bytes 393224 | tf_op jit(solution)/shard_map/ppermute | solution.py:47
  19.0 37.9 %collective-permute-start.9 = (f32[2,128,768]{2,1,0:T(8,128)S(1)}, f32[2,128,768]{2,1,0:T(8,128)S(1)}, u32[]{:S(2)}, u32[]{:S(2)}) collective-permute-start(f32[2,128,768]{2,1,0:T(8,128)S(1)} %shard_map.57.even_line), channel_id=1, source_target_pairs={{0,1},{2,3},{4,5},{6,7},{8,9},{10,11},{12,13},{14,15},{1,0},{3,2},... | collective-permute-start | bytes 2359304 | tf_op jit(solution)/shard_map/ppermute | solution.py:38
  22.5 13.0 %collective-permute-start.7 = (f32[128,640]{1,0:T(8,128)S(1)}, f32[128,640]{1,0:T(8,128)S(1)}, u32[]{:S(2)}, u32[]{:S(2)}) collective-permute-start(f32[128,640]{1,0:T(8,128)S(1)} %get-tuple-element.58), channel_id=1, source_target_pairs={{1,2},{3,4},{5,6},{9,10},{11,12},{13,14},{2,1},{4,3},{6,5},{10,9},... | collective-permute-start | bytes 983048 | tf_op jit(solution)/shard_map/ppermute | solution.py:31
  27.1 29.7 %collective-permute-start.6 = (f32[128,896]{1,0:T(8,128)S(1)}, f32[128,896]{1,0:T(8,128)S(1)}, u32[]{:S(2)}, u32[]{:S(2)}) collective-permute-start(f32[128,896]{1,0:T(8,128)S(1)} %get-tuple-element.57), channel_id=1, source_target_pairs={{1,2},{3,4},{5,6},{9,10},{11,12},{13,14},{2,1},{4,3},{6,5},{10,9},... | collective-permute-start | bytes 1376264 | tf_op jit(solution)/shard_map/ppermute | solution.py:32
  35.5 21.4 %collective-permute-start.8 = (f32[128,640]{1,0:T(8,128)S(1)}, f32[128,640]{1,0:T(8,128)S(1)}, u32[]{:S(2)}, u32[]{:S(2)}) collective-permute-start(f32[128,640]{1,0:T(8,128)S(1)} %collective-permute-done.7.halo_detour), channel_id=1, source_target_pairs={{0,8},{15,7},{16,24},{31,23},{32,40},{47,39},{48,56},{63,55},{64,7... | collective-permute-start | bytes 983048 | tf_op jit(solution)/shard_map/ppermute | solution.py:33
  36.8 14.1 %collective-permute-start.4 = (f32[2,256,128]{2,1,0:T(8,128)}, f32[2,256,128]{2,1,0:T(8,128)S(1)}, u32[]{:S(2)}, u32[]{:S(2)}) collective-permute-start(f32[2,256,128]{2,1,0:T(8,128)} %copy-done.5), channel_id=1, source_target_pairs={{16,32},{48,64},{80,96},{112,128},{144,160},{176,192},{208,224},{3... | collective-permute-start | bytes 786440 | tf_op jit(solution)/shard_map/ppermute | solution.py:47
  39.7 16.1 %collective-permute-start.5 = (f32[2,256,128]{2,1,0:T(8,128)S(1)}, f32[2,256,128]{2,1,0:T(8,128)S(1)}, u32[]{:S(2)}, u32[]{:S(2)}) collective-permute-start(f32[2,256,128]{2,1,0:T(8,128)S(1)} %get-tuple-element.54), channel_id=1, source_target_pairs={{0,16},{32,48},{64,80},{96,112},{128,144},{160,176},{192,208},{224... | collective-permute-start | bytes 786440 | tf_op jit(solution)/shard_map/ppermute | solution.py:48
  61.7 26.0 %collective-permute-start.13 = (f32[2,128,768]{2,1,0:T(8,128)S(1)}, f32[2,128,768]{2,1,0:T(8,128)S(1)}, u32[]{:S(2)}, u32[]{:S(2)}) collective-permute-start(f32[2,128,768]{2,1,0:T(8,128)S(1)} %get-tuple-element.66), channel_id=1, source_target_pairs={{0,1},{2,3},{4,5},{6,7},{8,9},{10,11},{12,13},{14,15},{1,0},{3,2},... | collective-permute-start | bytes 2359304 | tf_op jit(solution)/shard_map/ppermute | solution.py:38
  61.8 11.2 %collective-permute-start.11 = (f32[128,640]{1,0:T(8,128)S(1)}, f32[128,640]{1,0:T(8,128)S(1)}, u32[]{:S(2)}, u32[]{:S(2)}) collective-permute-start(f32[128,640]{1,0:T(8,128)S(1)} %get-tuple-element.65), channel_id=1, source_target_pairs={{1,2},{3,4},{5,6},{9,10},{11,12},{13,14},{2,1},{4,3},{6,5},{10,9},... | collective-permute-start | bytes 983048 | tf_op jit(solution)/shard_map/ppermute | solution.py:31
  66.9 15.9 %collective-permute-start.10 = (f32[128,896]{1,0:T(8,128)S(1)}, f32[128,896]{1,0:T(8,128)S(1)}, u32[]{:S(2)}, u32[]{:S(2)}) collective-permute-start(f32[128,896]{1,0:T(8,128)S(1)} %get-tuple-element.64), channel_id=1, source_target_pairs={{1,2},{3,4},{5,6},{9,10},{11,12},{13,14},{2,1},{4,3},{6,5},{10,9},... | collective-permute-start | bytes 1376264 | tf_op jit(solution)/shard_map/ppermute | solution.py:32
  73.0 14.7 %collective-permute-start.12 = (f32[128,640]{1,0:T(8,128)S(1)}, f32[128,640]{1,0:T(8,128)S(1)}, u32[]{:S(2)}, u32[]{:S(2)}) collective-permute-start(f32[128,640]{1,0:T(8,128)S(1)} %collective-permute-done.11.detour), channel_id=1, source_target_pairs={{0,8},{15,7},{16,24},{31,23},{32,40},{47,39},{48,56},{63,55},{64,7... | collective-permute-start | bytes 983048 | tf_op jit(solution)/shard_map/ppermute | solution.py:33
  88.5 13.7 %collective-permute-start.14 = (f32[2,256,256]{2,1,0:T(8,128)S(1)}, f32[2,256,256]{2,1,0:T(8,128)S(1)}, u32[]{:S(2)}, u32[]{:S(2)}) collective-permute-start(f32[2,256,256]{2,1,0:T(8,128)S(1)} %get-tuple-element.68), channel_id=1, source_target_pairs={{16,32},{48,64},{80,96},{112,128},{144,160},{176,192},{208,224},{3... | collective-permute-start | bytes 1572872 | tf_op jit(solution)/shard_map/ppermute | solution.py:47
  91.1 18.3 %collective-permute-start.15 = (f32[2,256,256]{2,1,0:T(8,128)S(1)}, f32[2,256,256]{2,1,0:T(8,128)S(1)}, u32[]{:S(2)}, u32[]{:S(2)}) collective-permute-start(f32[2,256,256]{2,1,0:T(8,128)S(1)} %get-tuple-element.69), channel_id=1, source_target_pairs={{0,16},{32,48},{64,80},{96,112},{128,144},{160,176},{192,208},{224... | collective-permute-start | bytes 1572872 | tf_op jit(solution)/shard_map/ppermute | solution.py:48
  110.7 41.3 %collective-permute-start.23 = (f32[2,128,768]{2,1,0:T(8,128)S(1)}, f32[2,128,768]{2,1,0:T(8,128)S(1)}, u32[]{:S(2)}, u32[]{:S(2)}) collective-permute-start(f32[2,128,768]{2,1,0:T(8,128)S(1)} %get-tuple-element.79), channel_id=1, source_target_pairs={{0,1},{2,3},{4,5},{6,7},{8,9},{10,11},{12,13},{14,15},{1,0},{3,2},... | collective-permute-start | bytes 2359304 | tf_op jit(solution)/shard_map/ppermute | solution.py:38
  110.8 14.4 %collective-permute-start.21 = (f32[128,640]{1,0:T(8,128)S(1)}, f32[128,640]{1,0:T(8,128)S(1)}, u32[]{:S(2)}, u32[]{:S(2)}) collective-permute-start(f32[128,640]{1,0:T(8,128)S(1)} %get-tuple-element.78), channel_id=1, source_target_pairs={{1,2},{3,4},{5,6},{9,10},{11,12},{13,14},{2,1},{4,3},{6,5},{10,9},... | collective-permute-start | bytes 983048 | tf_op jit(solution)/shard_map/ppermute | solution.py:31
  114.5 12.7 %collective-permute-start.16 = (f32[2,128,256]{2,1,0:T(8,128)S(1)}, f32[2,128,256]{2,1,0:T(8,128)S(1)}, u32[]{:S(2)}, u32[]{:S(2)}) collective-permute-start(f32[2,128,256]{2,1,0:T(8,128)S(1)} %get-tuple-element.71), channel_id=1, source_target_pairs={{16,32},{48,64},{80,96},{112,128},{144,160},{176,192},{208,224},{3... | collective-permute-start | bytes 786440 | tf_op jit(solution)/shard_map/ppermute | solution.py:47
  116.5 13.9 %collective-permute-start.17 = (f32[2,128,256]{2,1,0:T(8,128)S(1)}, f32[2,128,256]{2,1,0:T(8,128)S(1)}, u32[]{:S(2)}, u32[]{:S(2)}) collective-permute-start(f32[2,128,256]{2,1,0:T(8,128)S(1)} %get-tuple-element.72), channel_id=1, source_target_pairs={{0,16},{32,48},{64,80},{96,112},{128,144},{160,176},{192,208},{224... | collective-permute-start | bytes 786440 | tf_op jit(solution)/shard_map/ppermute | solution.py:48
  118.3 33.6 %collective-permute-start.20 = (f32[128,896]{1,0:T(8,128)S(1)}, f32[128,896]{1,0:T(8,128)S(1)}, u32[]{:S(2)}, u32[]{:S(2)}) collective-permute-start(f32[128,896]{1,0:T(8,128)S(1)} %get-tuple-element.77), channel_id=1, source_target_pairs={{1,2},{3,4},{5,6},{9,10},{11,12},{13,14},{2,1},{4,3},{6,5},{10,9},... | collective-permute-start | bytes 1376264 | tf_op jit(solution)/shard_map/ppermute | solution.py:32
  125.2 26.8 %collective-permute-start.22 = (f32[128,640]{1,0:T(8,128)S(1)}, f32[128,640]{1,0:T(8,128)S(1)}, u32[]{:S(2)}, u32[]{:S(2)}) collective-permute-start(f32[128,640]{1,0:T(8,128)S(1)} %collective-permute-done.21.halo_detour), channel_id=1, source_target_pairs={{0,8},{15,7},{16,24},{31,23},{32,40},{47,39},{48,56},{63,55},{64,7... | collective-permute-start | bytes 983048 | tf_op jit(solution)/shard_map/ppermute | solution.py:33
  127.2 21.5 %collective-permute-start.18 = (f32[2,128,256]{2,1,0:T(8,128)S(1)}, f32[2,128,256]{2,1,0:T(8,128)S(1)}, u32[]{:S(2)}, u32[]{:S(2)}) collective-permute-start(f32[2,128,256]{2,1,0:T(8,128)S(1)} %get-tuple-element.73), channel_id=1, source_target_pairs={{16,32},{48,64},{80,96},{112,128},{144,160},{176,192},{208,224},{3... | collective-permute-start | bytes 786440 | tf_op jit(solution)/shard_map/ppermute | solution.py:47
  130.3 20.2 %collective-permute-start.19 = (f32[2,128,256]{2,1,0:T(8,128)S(1)}, f32[2,128,256]{2,1,0:T(8,128)S(1)}, u32[]{:S(2)}, u32[]{:S(2)}) collective-permute-start(f32[2,128,256]{2,1,0:T(8,128)S(1)} %get-tuple-element.74), channel_id=1, source_target_pairs={{0,16},{32,48},{64,80},{96,112},{128,144},{160,176},{192,208},{224... | collective-permute-start | bytes 786440 | tf_op jit(solution)/shard_map/ppermute | solution.py:48
  156.7 23.8 %collective-permute-start.27 = (f32[2,128,768]{2,1,0:T(8,128)S(1)}, f32[2,128,768]{2,1,0:T(8,128)S(1)}, u32[]{:S(2)}, u32[]{:S(2)}) collective-permute-start(f32[2,128,768]{2,1,0:T(8,128)S(1)} %get-tuple-element.84), channel_id=1, source_target_pairs={{0,1},{2,3},{4,5},{6,7},{8,9},{10,11},{12,13},{14,15},{1,0},{3,2},... | collective-permute-start | bytes 2359304 | tf_op jit(solution)/shard_map/ppermute | solution.py:38
  156.8 8.4 %collective-permute-start.25 = (f32[128,640]{1,0:T(8,128)S(1)}, f32[128,640]{1,0:T(8,128)S(1)}, u32[]{:S(2)}, u32[]{:S(2)}) collective-permute-start(f32[128,640]{1,0:T(8,128)S(1)} %get-tuple-element.83), channel_id=1, source_target_pairs={{1,2},{3,4},{5,6},{9,10},{11,12},{13,14},{2,1},{4,3},{6,5},{10,9},... | collective-permute-start | bytes 983048 | tf_op jit(solution)/shard_map/ppermute | solution.py:31
  158.8 16.5 %collective-permute-start.24 = (f32[128,896]{1,0:T(8,128)S(1)}, f32[128,896]{1,0:T(8,128)S(1)}, u32[]{:S(2)}, u32[]{:S(2)}) collective-permute-start(f32[128,896]{1,0:T(8,128)S(1)} %get-tuple-element.82), channel_id=1, source_target_pairs={{1,2},{3,4},{5,6},{9,10},{11,12},{13,14},{2,1},{4,3},{6,5},{10,9},... | collective-permute-start | bytes 1376264 | tf_op jit(solution)/shard_map/ppermute | solution.py:32
  165.2 15.3 %collective-permute-start.26 = (f32[128,640]{1,0:T(8,128)S(1)}, f32[128,640]{1,0:T(8,128)S(1)}, u32[]{:S(2)}, u32[]{:S(2)}) collective-permute-start(f32[128,640]{1,0:T(8,128)S(1)} %collective-permute-done.25.detour), channel_id=1, source_target_pairs={{0,8},{15,7},{16,24},{31,23},{32,40},{47,39},{48,56},{63,55},{64,7... | collective-permute-start | bytes 983048 | tf_op jit(solution)/shard_map/ppermute | solution.py:33
  166.5 33.6 %collective-permute-start.28 = (f32[2,256,128]{2,1,0:T(8,128)S(1)}, f32[2,256,128]{2,1,0:T(8,128)S(1)}, u32[]{:S(2)}, u32[]{:S(2)}) collective-permute-start(f32[2,256,128]{2,1,0:T(8,128)S(1)} %get-tuple-element.86), channel_id=1, source_target_pairs={{16,32},{48,64},{80,96},{112,128},{144,160},{176,192},{208,224},{3... | collective-permute-start | bytes 786440 | tf_op jit(solution)/shard_map/ppermute | solution.py:47
  168.8 31.3 %collective-permute-start.29 = (f32[2,256,128]{2,1,0:T(8,128)S(1)}, f32[2,256,128]{2,1,0:T(8,128)S(1)}, u32[]{:S(2)}, u32[]{:S(2)}) collective-permute-start(f32[2,256,128]{2,1,0:T(8,128)S(1)} %get-tuple-element.87), channel_id=1, source_target_pairs={{0,16},{32,48},{64,80},{96,112},{128,144},{160,176},{192,208},{224... | collective-permute-start | bytes 786440 | tf_op jit(solution)/shard_map/ppermute | solution.py:48
  181.3 21.5 %collective-permute-start.30 = (f32[2,256,128]{2,1,0:T(8,128)S(1)}, f32[2,256,128]{2,1,0:T(8,128)S(1)}, u32[]{:S(2)}, u32[]{:S(2)}) collective-permute-start(f32[2,256,128]{2,1,0:T(8,128)S(1)} %get-tuple-element.91), channel_id=1, source_target_pairs={{16,32},{48,64},{80,96},{112,128},{144,160},{176,192},{208,224},{3... | collective-permute-start | bytes 786440 | tf_op jit(solution)/shard_map/ppermute | solution.py:47
  183.2 20.7 %collective-permute-start.31 = (f32[2,256,128]{2,1,0:T(8,128)S(1)}, f32[2,256,128]{2,1,0:T(8,128)S(1)}, u32[]{:S(2)}, u32[]{:S(2)}) collective-permute-start(f32[2,256,128]{2,1,0:T(8,128)S(1)} %get-tuple-element.92), channel_id=1, source_target_pairs={{0,16},{32,48},{64,80},{96,112},{128,144},{160,176},{192,208},{224... | collective-permute-start | bytes 786440 | tf_op jit(solution)/shard_map/ppermute | solution.py:48
  (6 other events, 60.3 us)

commit v8 on v7

--- a/solution.py
+++ b/solution.py
@@ -414,18 +414,12 @@
     out_even[...] = lines[:, even_rows, :]
 
 
-def update_centre_kernel(
-    meta, field, total, lines, upper_odd, upper_even, lower_odd, lower_even, fresh, zeros
-):
+def update_centre_kernel(meta, field, total, lines, mid_odd, mid_even, fresh, zeros):
     wide, half = total.shape[2], lines.shape[1] // 2
     first, last, mid = inner_rows(half, wide - 2 * half)
     fresh[:, mid, :] = field[:, mid, :] - step_size * total[:, mid, :]
-    start = mid.start
-    for odd, even in ((upper_odd, upper_even), (lower_odd, lower_even)):
-        rows = slice(start, start + odd.shape[1])
-        for band, cols in ((odd, odd_side(meta, odd, wide)), (even, even_side(meta, even, wide))):
-            fresh[:, rows, cols] = fresh[:, rows, cols] - step_size * band[...]
-        start += odd.shape[1]
+    for band, cols in both_sides(meta, mid_odd, mid_even, wide):
+        fresh[:, mid, cols] = fresh[:, mid, cols] - step_size * band[...]
     clear_outside(meta, fresh.at[:, mid, :], half)
     for rows, outer in (first, last):
         fresh[:, rows, :] = lines[:, outer, :]
@@ -514,7 +508,7 @@
     meta = jnp.concatenate([places, counts[0], offsets[0, 0].reshape(-1)]).astype(jnp.int32)
 
     column, band = (2, 2 * half, half), (2, 2 * half, side)
-    mid_column, mid_band = (2, tile - 2 * half, half), (2, tile // 2 - half, side)
+    mid_column, mid_band = (2, tile - 2 * half, half), (2, tile - 2 * half, side)
     whole, lines = (2, wide, wide), (2, 2 * half, wide)
     line = (2, half, wide)
     sends = ((half, wide + CUT), (half, wide - CUT), line)
@@ -564,7 +558,7 @@
             functools.partial(gradient_kernel, side, windows),
             meta,
             (field, total, *halos, probes, tables, amps),
-            (whole, whole, *sends, *((mid_column,) * 2 if last else (mid_band,) * 4)),
+            (whole, whole, *sends, *(mid_column if last else mid_band,) * 2),
             scratch=(pltpu.VMEM((2, side, side), bf), pltpu.VMEM((2, side, side), jnp.float32)),
             aliases={1: 0, 2: 1},
             flops=windows * 16 * side**3,
@@ -577,7 +571,6 @@
         mids = swap_columns(*rest[3:5])
         if last:
             break
-        mids += swap_columns(*rest[5:])
         *edges, rows = call(
             update_edges_kernel,
             meta,

time: 206 us -> 204 us (level)
    ppermute x8 -> x7, waiting for transfers between devices: 24.3 us -> 13.2 us  [swap_columns(): from_odd = lax.ppermute(odd_cells, 'gx', pairs(count, 1))]
    ppermute x8 -> x7, starting transfers between devices: 34.9 us -> 26.7 us  [swap_columns(): from_even = lax.ppermute(even_cells, 'gx', pairs(count, 0))]
    ppermute x8 -> x7, starting transfers between devices: 22.8 us -> 30.4 us  [swap_columns(): from_odd = lax.ppermute(odd_cells, 'gx', pairs(count, 1))]
    ppermute x8 -> x7, waiting for transfers between devices: 15 us -> 21.1 us  [swap_columns(): from_even = lax.ppermute(even_cells, 'gx', pairs(count, 0))]
  transfers between devices with their start and end apart: 32 -> 30, of which waited for: 13 -> 12; matrix products, arithmetic and copies ran while one was open for 1% -> 1% of each run, Pallas kernels for 6% -> 6%
where the time goes in v8:
time: 204 us; the launch traced here: 203 us
  starting transfers between devices  107 us (52%)
  waiting for transfers between devices  59.4 us (29%)
  Pallas kernels  26 us (13%)
  local copies, waits for them, and re-layouts  7.09 us (3%)
    ppermute x7, starting transfers between devices, swap_columns(): from_odd = lax.ppermute(odd_cells, 'gx', pairs(count, 1))  30.4 us
    ppermute x4, starting transfers between devices, swap_odd(): straight = lax.ppermute(direct, 'gy', near + far)  28.3 us
    ppermute x7, starting transfers between devices, swap_columns(): from_even = lax.ppermute(even_cells, 'gx', pairs(count, 0))  26.7 us
    pallas_call x13, Pallas kernels, call(): pl.pallas_call(kernel, out_shape=shapes, in_specs=[smem, anywhere if far...  26 us
    ppermute x7, waiting for transfers between devices, swap_columns(): from_even = lax.ppermute(even_cells, 'gx', pairs(count, 0))  21.1 us
    ppermute x4, starting transfers between devices, swap_odd(): first = lax.ppermute(detour, 'gy', near + [(low, 0), (low + 1, count - 1)])  14.9 us
    ppermute x7, waiting for transfers between devices, swap_columns(): from_odd = lax.ppermute(odd_cells, 'gx', pairs(count, 1))  13.2 us
    ppermute x4, waiting for transfers between devices, swap_odd(): straight = lax.ppermute(direct, 'gy', near + far)  13.1 us
  transfers between devices with their start and end apart: 30, of which 12 were waited for; matrix products, arithmetic and copies ran while one was open for 1% of the time, Pallas kernels for 6%

profile of v8, /device:TPU:15, one launch (start us, length us, event | category | flops | bytes accessed | tf_op | source)
XLA Modules:
  0.0 203.0 jit_solution(679211489688214034)
XLA Ops:
  3.7 6.1 %collective-permute-start.2 = (f32[2,128,128]{2,1,0:T(8,128)}, f32[2,128,128]{2,1,0:T(8,128)S(1)}, u32[]{:S(2)}, u32[]{:S(2)}) collective-permute-start(f32[2,128,128]{2,1,0:T(8,128)} %get-tuple-element.49), channel_id=1, source_target_pairs={{16,32},{48,64},{80,96},{112,128},{144,160},{176,192},{208,224},{3... | collective-permute-start | bytes 393224 | tf_op jit(solution)/shard_map/ppermute | solution.py:47
  9.9 1.8 broadcast_select_fusion
  13.2 1.9 collective-permute-start
  19.0 1.8 collective-permute-start.9
  22.5 4.7 %collective-permute-start.7 = (f32[128,640]{1,0:T(8,128)S(1)}, f32[128,640]{1,0:T(8,128)S(1)}, u32[]{:S(2)}, u32[]{:S(2)}) collective-permute-start(f32[128,640]{1,0:T(8,128)S(1)} %get-tuple-element.56), channel_id=1, source_target_pairs={{1,2},{3,4},{5,6},{9,10},{11,12},{13,14},{2,1},{4,3},{6,5},{10,9},... | collective-permute-start | bytes 983048 | tf_op jit(solution)/shard_map/ppermute | solution.py:31
  27.1 8.3 %collective-permute-start.6 = (f32[128,896]{1,0:T(8,128)S(1)}, f32[128,896]{1,0:T(8,128)S(1)}, u32[]{:S(2)}, u32[]{:S(2)}) collective-permute-start(f32[128,896]{1,0:T(8,128)S(1)} %get-tuple-element.55), channel_id=1, source_target_pairs={{1,2},{3,4},{5,6},{9,10},{11,12},{13,14},{2,1},{4,3},{6,5},{10,9},... | collective-permute-start | bytes 1376264 | tf_op jit(solution)/shard_map/ppermute | solution.py:32
  36.8 2.9 %collective-permute-start.4 = (f32[2,256,128]{2,1,0:T(8,128)}, f32[2,256,128]{2,1,0:T(8,128)S(1)}, u32[]{:S(2)}, u32[]{:S(2)}) collective-permute-start(f32[2,256,128]{2,1,0:T(8,128)} %copy-done.5), channel_id=1, source_target_pairs={{16,32},{48,64},{80,96},{112,128},{144,160},{176,192},{208,224},{3... | collective-permute-start | bytes 786440 | tf_op jit(solution)/shard_map/ppermute | solution.py:47
  42.1 4.7 %shard_map.59 = (f32[4,2,256,256]{3,2,1,0:T(8,128)S(1)}, bf16[4,8,256,256]{3,2,1,0:T(8,128)(2,1)S(1)}, f32[4,256,256]{2,1,0:T(8,128)S(1)}) custom-call(s32[13]{0:T(128)S(1)} %concatenate.4.meta, f32[2,256,256]{2,1,0:T(8,128)S(1)} %copy-done.4, f32[4,256,256]{2,1,0:T(8,128)S(1)} %bitcast.7), custom_call_target="tpu_custom_call" | custom-call | flops 1000000000 | bytes 8912896 | tf_op jit(solution)/shard_map/pallas_call | solution.py:482
  46.8 4.1 %collective-permute-done.4.side_odd = f32[2,256,128]{2,1,0:T(8,128)S(1)} collective-permute-done((f32[2,256,128]{2,1,0:T(8,128)}, f32[2,256,128]{2,1,0:T(8,128)S(1)}, u32[]{:S(2)}, u32[]{:S(2)}) %collective-permute-start.4) | collective-permute-done | bytes 262176 | tf_op jit(solution)/shard_map/ppermute | solution.py:47
  50.9 4.9 %collective-permute-done.5.side_even = f32[2,256,128]{2,1,0:T(8,128)S(1)} collective-permute-done((f32[2,256,128]{2,1,0:T(8,128)S(1)}, f32[2,256,128]{2,1,0:T(8,128)S(1)}, u32[]{:S(2)}, u32[]{:S(2)}) %collective-permute-start.5) | collective-permute-done | bytes 262176 | tf_op jit(solution)/shard_map/ppermute | solution.py:48
  56.9 4.8 %shard_map.60 = (f32[2,768,768]{2,1,0:T(8,128)S(1)}, f32[2,768,768]{2,1,0:T(8,128)S(1)}, f32[128,896]{1,0:T(8,128)S(1)}, f32[128,640]{1,0:T(8,128)S(1)}, f32[2,1...) custom-call(s32[13]{0:T(128)S(1)} %concatenate.4.meta, ...), custom_call_target="tpu_custom_call", output_to_operand_aliasing={{0}: (1, {}), {1}: (2, {})} | custom-call | flops 1073741824 | bytes 30736384 | tf_op jit(solution)/shard_map/pallas_call | solution.py:482
  61.8 5.1 %collective-permute-start.11 = (f32[128,640]{1,0:T(8,128)S(1)}, f32[128,640]{1,0:T(8,128)S(1)}, u32[]{:S(2)}, u32[]{:S(2)}) collective-permute-start(f32[128,640]{1,0:T(8,128)S(1)} %get-tuple-element.63), channel_id=1, source_target_pairs={{1,2},{3,4},{5,6},{9,10},{11,12},{13,14},{2,1},{4,3},{6,5},{10,9},... | collective-permute-start | bytes 983048 | tf_op jit(solution)/shard_map/ppermute | solution.py:31
  66.9 6.1 %collective-permute-start.10 = (f32[128,896]{1,0:T(8,128)S(1)}, f32[128,896]{1,0:T(8,128)S(1)}, u32[]{:S(2)}, u32[]{:S(2)}) collective-permute-start(f32[128,896]{1,0:T(8,128)S(1)} %get-tuple-element.62), channel_id=1, source_target_pairs={{1,2},{3,4},{5,6},{9,10},{11,12},{13,14},{2,1},{4,3},{6,5},{10,9},... | collective-permute-start | bytes 1376264 | tf_op jit(solution)/shard_map/ppermute | solution.py:32
  74.3 8.5 %collective-permute-done.10.direct = f32[128,896]{1,0:T(8,128)S(1)} collective-permute-done((f32[128,896]{1,0:T(8,128)S(1)}, f32[128,896]{1,0:T(8,128)S(1)}, u32[]{:S(2)}, u32[]{:S(2)}) %collective-permute-start.10) | collective-permute-done | bytes 458784 | tf_op jit(solution)/shard_map/ppermute | solution.py:32
  82.8 4.9 %collective-permute-done.12.relayed = f32[128,640]{1,0:T(8,128)S(1)} collective-permute-done((f32[128,640]{1,0:T(8,128)S(1)}, f32[128,640]{1,0:T(8,128)S(1)}, u32[]{:S(2)}, u32[]{:S(2)}) %collective-permute-start.12) | collective-permute-done | bytes 327712 | tf_op jit(solution)/shard_map/ppermute | solution.py:33
  88.5 2.6 %collective-permute-start.14 = (f32[2,256,256]{2,1,0:T(8,128)S(1)}, f32[2,256,256]{2,1,0:T(8,128)S(1)}, u32[]{:S(2)}, u32[]{:S(2)}) collective-permute-start(f32[2,256,256]{2,1,0:T(8,128)S(1)} %get-tuple-element.66), channel_id=1, source_target_pairs={{16,32},{48,64},{80,96},{112,128},{144,160},{176,192},{208,224},{3... | collective-permute-start | bytes 1572872 | tf_op jit(solution)/shard_map/ppermute | solution.py:47
  91.1 9.5 %collective-permute-start.15 = (f32[2,256,256]{2,1,0:T(8,128)S(1)}, f32[2,256,256]{2,1,0:T(8,128)S(1)}, u32[]{:S(2)}, u32[]{:S(2)}) collective-permute-start(f32[2,256,256]{2,1,0:T(8,128)S(1)} %get-tuple-element.67), channel_id=1, source_target_pairs={{0,16},{32,48},{64,80},{96,112},{128,144},{160,176},{192,208},{224... | collective-permute-start | bytes 1572872 | tf_op jit(solution)/shard_map/ppermute | solution.py:48
  102.2 7.2 %collective-permute-done.15.band_even = f32[2,256,256]{2,1,0:T(8,128)S(1)} collective-permute-done((f32[2,256,256]{2,1,0:T(8,128)S(1)}, f32[2,256,256]{2,1,0:T(8,128)S(1)}, u32[]{:S(2)}, u32[]{:S(2)}) %collective-permute-start.15) | collective-permute-done | bytes 524320 | tf_op jit(solution)/shard_map/ppermute | solution.py:48
  110.7 3.8 %collective-permute-start.19 = (f32[128,640]{1,0:T(8,128)S(1)}, f32[128,640]{1,0:T(8,128)S(1)}, u32[]{:S(2)}, u32[]{:S(2)}) collective-permute-start(f32[128,640]{1,0:T(8,128)S(1)} %get-tuple-element.74), channel_id=1, source_target_pairs={{1,2},{3,4},{5,6},{9,10},{11,12},{13,14},{2,1},{4,3},{6,5},{10,9},... | collective-permute-start | bytes 983048 | tf_op jit(solution)/shard_map/ppermute | solution.py:31
  114.5 1.9 collective-permute-start.16
  116.5 1.9 collective-permute-start.17
  118.3 6.8 %collective-permute-start.18 = (f32[128,896]{1,0:T(8,128)S(1)}, f32[128,896]{1,0:T(8,128)S(1)}, u32[]{:S(2)}, u32[]{:S(2)}) collective-permute-start(f32[128,896]{1,0:T(8,128)S(1)} %get-tuple-element.73), channel_id=1, source_target_pairs={{1,2},{3,4},{5,6},{9,10},{11,12},{13,14},{2,1},{4,3},{6,5},{10,9},... | collective-permute-start | bytes 1376264 | tf_op jit(solution)/shard_map/ppermute | solution.py:32
  126.5 6.4 %collective-permute-done.16.mid_odd = f32[2,256,256]{2,1,0:T(8,128)S(1)} collective-permute-done((f32[2,256,256]{2,1,0:T(8,128)S(1)}, f32[2,256,256]{2,1,0:T(8,128)S(1)}, u32[]{:S(2)}, u32[]{:S(2)}) %collective-permute-start.16) | collective-permute-done | bytes 524320 | tf_op jit(solution)/shard_map/ppermute | solution.py:47
  132.8 7.9 %collective-permute-done.17.mid_even = f32[2,256,256]{2,1,0:T(8,128)S(1)} collective-permute-done((f32[2,256,256]{2,1,0:T(8,128)S(1)}, f32[2,256,256]{2,1,0:T(8,128)S(1)}, u32[]{:S(2)}, u32[]{:S(2)}) %collective-permute-start.17) | collective-permute-done | bytes 524320 | tf_op jit(solution)/shard_map/ppermute | solution.py:48
  142.1 4.6 %collective-permute-done.18.halo_direct = f32[128,896]{1,0:T(8,128)S(1)} collective-permute-done((f32[128,896]{1,0:T(8,128)S(1)}, f32[128,896]{1,0:T(8,128)S(1)}, u32[]{:S(2)}, u32[]{:S(2)}) %collective-permute-start.18) | collective-permute-done | bytes 458784 | tf_op jit(solution)/shard_map/ppermute | solution.py:32
  146.7 4.8 %shard_map.64 = (f32[2,768,768]{2,1,0:T(8,128)S(1)}, f32[2,768,768]{2,1,0:T(8,128)S(1)}, f32[128,896]{1,0:T(8,128)S(1)}, f32[128,640]{1,0:T(8,128)S(1)}, f32[2,1...) custom-call(s32[13]{0:T(128)S(1)} %concatenate.4.meta, ...), custom_call_target="tpu_custom_call", output_to_operand_aliasing={{0}: (1, {}), {1}: (2, {})} | custom-call | flops 1073741824 | bytes 30212096 | tf_op jit(solution)/shard_map/pallas_call | solution.py:482
  152.9 7.1 %collective-permute-start.22 = (f32[128,896]{1,0:T(8,128)S(1)}, f32[128,896]{1,0:T(8,128)S(1)}, u32[]{:S(2)}, u32[]{:S(2)}) collective-permute-start(f32[128,896]{1,0:T(8,128)S(1)} %get-tuple-element.78), channel_id=1, source_target_pairs={{1,2},{3,4},{5,6},{9,10},{11,12},{13,14},{2,1},{4,3},{6,5},{10,9},... | collective-permute-start | bytes 1376264 | tf_op jit(solution)/shard_map/ppermute | solution.py:32
  161.3 9.7 %collective-permute-start.26 = (f32[2,256,128]{2,1,0:T(8,128)S(1)}, f32[2,256,128]{2,1,0:T(8,128)S(1)}, u32[]{:S(2)}, u32[]{:S(2)}) collective-permute-start(f32[2,256,128]{2,1,0:T(8,128)S(1)} %get-tuple-element.82), channel_id=1, source_target_pairs={{16,32},{48,64},{80,96},{112,128},{144,160},{176,192},{208,224},{3... | collective-permute-start | bytes 786440 | tf_op jit(solution)/shard_map/ppermute | solution.py:47
  171.1 7.0 %collective-permute-done.24.relayed = f32[128,640]{1,0:T(8,128)S(1)} collective-permute-done((f32[128,640]{1,0:T(8,128)S(1)}, f32[128,640]{1,0:T(8,128)S(1)}, u32[]{:S(2)}, u32[]{:S(2)}) %collective-permute-start.24) | collective-permute-done | bytes 327712 | tf_op jit(solution)/shard_map/ppermute | solution.py:33
  178.8 5.2 %collective-permute-start.28 = (f32[2,256,128]{2,1,0:T(8,128)S(1)}, f32[2,256,128]{2,1,0:T(8,128)S(1)}, u32[]{:S(2)}, u32[]{:S(2)}) collective-permute-start(f32[2,256,128]{2,1,0:T(8,128)S(1)} %get-tuple-element.87), channel_id=1, source_target_pairs={{16,32},{48,64},{80,96},{112,128},{144,160},{176,192},{208,224},{3... | collective-permute-start | bytes 786440 | tf_op jit(solution)/shard_map/ppermute | solution.py:47
  184.0 13.6 %collective-permute-start.29 = (f32[2,256,128]{2,1,0:T(8,128)S(1)}, f32[2,256,128]{2,1,0:T(8,128)S(1)}, u32[]{:S(2)}, u32[]{:S(2)}) collective-permute-start(f32[2,256,128]{2,1,0:T(8,128)S(1)} %get-tuple-element.88), channel_id=1, source_target_pairs={{0,16},{32,48},{64,80},{96,112},{128,144},{160,176},{192,208},{224... | collective-permute-start | bytes 786440 | tf_op jit(solution)/shard_map/ppermute | solution.py:48
  197.7 2.6 %shard_map.66 = (f32[2,512,512]{2,1,0:T(8,128)}, f32[2,256,128]{2,1,0:T(8,128)S(1)}, f32[2,256,128]{2,1,0:T(8,128)S(1)}) custom-call(s32[13]{0:T(128)S(1)} %concatenate.4.meta, f32[2,768,768]{2,1,0:T(8,128)S(1)} %get-tuple-element.76.field, f32[2,768,768]{2,1,0:T(8,128)S(1)} %get-tuple-element.77.total, f32[2,128,768]{2,1,0:T(8,128)S(1)} %get-tuple-element.81.line, ...), custom_call_target="tpu_custom_call" | custom-call | bytes 14155776 | tf_op jit(solution)/shard_map/pallas_call | solution.py:482
  (58 shorter events, 28.7 us)
Async XLA Ops:
  0.1 1.6 copy-start
  1.7 54.1 %copy-start.2 = (f32[2,512,512]{2,1,0:T(8,128)S(1)}, f32[2,512,512]{2,1,0:T(8,128)}, u32[]{:S(2)}) copy-start(f32[2,512,512]{2,1,0:T(8,128)} %own.5) | copy-start | bytes 6291460
  3.7 13.0 %collective-permute-start.2 = (f32[2,128,128]{2,1,0:T(8,128)}, f32[2,128,128]{2,1,0:T(8,128)S(1)}, u32[]{:S(2)}, u32[]{:S(2)}) collective-permute-start(f32[2,128,128]{2,1,0:T(8,128)} %get-tuple-element.49), channel_id=1, source_target_pairs={{16,32},{48,64},{80,96},{112,128},{144,160},{176,192},{208,224},{3... | collective-permute-start | bytes 393224 | tf_op jit(solution)/shard_map/ppermute | solution.py:47
  9.8 6.9 %collective-permute-start.3 = (f32[2,128,128]{2,1,0:T(8,128)S(1)}, f32[2,128,128]{2,1,0:T(8,128)S(1)}, u32[]{:S(2)}, u32[]{:S(2)}) collective-permute-start(f32[2,128,128]{2,1,0:T(8,128)S(1)} %get-tuple-element.50), channel_id=1, source_target_pairs={{0,16},{32,48},{64,80},{96,112},{128,144},{160,176},{192,208},{224... | collective-permute-start | bytes 393224 | tf_op jit(solution)/shard_map/ppermute | solution.py:48
  11.8 9.0 %collective-permute-start.1 = (f32[2,128,128]{2,1,0:T(8,128)}, f32[2,128,128]{2,1,0:T(8,128)S(1)}, u32[]{:S(2)}, u32[]{:S(2)}) collective-permute-start(f32[2,128,128]{2,1,0:T(8,128)} %get-tuple-element.89), channel_id=1, source_target_pairs={{0,16},{32,48},{64,80},{96,112},{128,144},{160,176},{192,208},{224... | collective-permute-start | bytes 393224 | tf_op jit(solution)/shard_map/ppermute | solution.py:48
  13.2 8.6 %collective-permute-start = (f32[2,128,128]{2,1,0:T(8,128)}, f32[2,128,128]{2,1,0:T(8,128)S(1)}, u32[]{:S(2)}, u32[]{:S(2)}) collective-permute-start(f32[2,128,128]{2,1,0:T(8,128)} %get-tuple-element.90), channel_id=1, source_target_pairs={{16,32},{48,64},{80,96},{112,128},{144,160},{176,192},{208,224},{3... | collective-permute-start | bytes 393224 | tf_op jit(solution)/shard_map/ppermute | solution.py:47
  19.0 37.9 %collective-permute-start.9 = (f32[2,128,768]{2,1,0:T(8,128)S(1)}, f32[2,128,768]{2,1,0:T(8,128)S(1)}, u32[]{:S(2)}, u32[]{:S(2)}) collective-permute-start(f32[2,128,768]{2,1,0:T(8,128)S(1)} %shard_map.57.even_line), channel_id=1, source_target_pairs={{0,1},{2,3},{4,5},{6,7},{8,9},{10,11},{12,13},{14,15},{1,0},{3,2},... | collective-permute-start | bytes 2359304 | tf_op jit(solution)/shard_map/ppermute | solution.py:38
  22.5 13.0 %collective-permute-start.7 = (f32[128,640]{1,0:T(8,128)S(1)}, f32[128,640]{1,0:T(8,128)S(1)}, u32[]{:S(2)}, u32[]{:S(2)}) collective-permute-start(f32[128,640]{1,0:T(8,128)S(1)} %get-tuple-element.56), channel_id=1, source_target_pairs={{1,2},{3,4},{5,6},{9,10},{11,12},{13,14},{2,1},{4,3},{6,5},{10,9},... | collective-permute-start | bytes 983048 | tf_op jit(solution)/shard_map/ppermute | solution.py:31
  27.1 29.7 %collective-permute-start.6 = (f32[128,896]{1,0:T(8,128)S(1)}, f32[128,896]{1,0:T(8,128)S(1)}, u32[]{:S(2)}, u32[]{:S(2)}) collective-permute-start(f32[128,896]{1,0:T(8,128)S(1)} %get-tuple-element.55), channel_id=1, source_target_pairs={{1,2},{3,4},{5,6},{9,10},{11,12},{13,14},{2,1},{4,3},{6,5},{10,9},... | collective-permute-start | bytes 1376264 | tf_op jit(solution)/shard_map/ppermute | solution.py:32
  35.5 21.4 %collective-permute-start.8 = (f32[128,640]{1,0:T(8,128)S(1)}, f32[128,640]{1,0:T(8,128)S(1)}, u32[]{:S(2)}, u32[]{:S(2)}) collective-permute-start(f32[128,640]{1,0:T(8,128)S(1)} %collective-permute-done.7.halo_detour), channel_id=1, source_target_pairs={{0,8},{15,7},{16,24},{31,23},{32,40},{47,39},{48,56},{63,55},{64,7... | collective-permute-start | bytes 983048 | tf_op jit(solution)/shard_map/ppermute | solution.py:33
  36.8 14.1 %collective-permute-start.4 = (f32[2,256,128]{2,1,0:T(8,128)}, f32[2,256,128]{2,1,0:T(8,128)S(1)}, u32[]{:S(2)}, u32[]{:S(2)}) collective-permute-start(f32[2,256,128]{2,1,0:T(8,128)} %copy-done.5), channel_id=1, source_target_pairs={{16,32},{48,64},{80,96},{112,128},{144,160},{176,192},{208,224},{3... | collective-permute-start | bytes 786440 | tf_op jit(solution)/shard_map/ppermute | solution.py:47
  39.7 16.1 %collective-permute-start.5 = (f32[2,256,128]{2,1,0:T(8,128)S(1)}, f32[2,256,128]{2,1,0:T(8,128)S(1)}, u32[]{:S(2)}, u32[]{:S(2)}) collective-permute-start(f32[2,256,128]{2,1,0:T(8,128)S(1)} %get-tuple-element.52), channel_id=1, source_target_pairs={{0,16},{32,48},{64,80},{96,112},{128,144},{160,176},{192,208},{224... | collective-permute-start | bytes 786440 | tf_op jit(solution)/shard_map/ppermute | solution.py:48
  61.7 26.0 %collective-permute-start.13 = (f32[2,128,768]{2,1,0:T(8,128)S(1)}, f32[2,128,768]{2,1,0:T(8,128)S(1)}, u32[]{:S(2)}, u32[]{:S(2)}) collective-permute-start(f32[2,128,768]{2,1,0:T(8,128)S(1)} %get-tuple-element.64), channel_id=1, source_target_pairs={{0,1},{2,3},{4,5},{6,7},{8,9},{10,11},{12,13},{14,15},{1,0},{3,2},... | collective-permute-start | bytes 2359304 | tf_op jit(solution)/shard_map/ppermute | solution.py:38
  61.8 11.2 %collective-permute-start.11 = (f32[128,640]{1,0:T(8,128)S(1)}, f32[128,640]{1,0:T(8,128)S(1)}, u32[]{:S(2)}, u32[]{:S(2)}) collective-permute-start(f32[128,640]{1,0:T(8,128)S(1)} %get-tuple-element.63), channel_id=1, source_target_pairs={{1,2},{3,4},{5,6},{9,10},{11,12},{13,14},{2,1},{4,3},{6,5},{10,9},... | collective-permute-start | bytes 983048 | tf_op jit(solution)/shard_map/ppermute | solution.py:31
  66.9 15.9 %collective-permute-start.10 = (f32[128,896]{1,0:T(8,128)S(1)}, f32[128,896]{1,0:T(8,128)S(1)}, u32[]{:S(2)}, u32[]{:S(2)}) collective-permute-start(f32[128,896]{1,0:T(8,128)S(1)} %get-tuple-element.62), channel_id=1, source_target_pairs={{1,2},{3,4},{5,6},{9,10},{11,12},{13,14},{2,1},{4,3},{6,5},{10,9},... | collective-permute-start | bytes 1376264 | tf_op jit(solution)/shard_map/ppermute | solution.py:32
  73.0 14.7 %collective-permute-start.12 = (f32[128,640]{1,0:T(8,128)S(1)}, f32[128,640]{1,0:T(8,128)S(1)}, u32[]{:S(2)}, u32[]{:S(2)}) collective-permute-start(f32[128,640]{1,0:T(8,128)S(1)} %collective-permute-done.11.detour), channel_id=1, source_target_pairs={{0,8},{15,7},{16,24},{31,23},{32,40},{47,39},{48,56},{63,55},{64,7... | collective-permute-start | bytes 983048 | tf_op jit(solution)/shard_map/ppermute | solution.py:33
  88.5 13.7 %collective-permute-start.14 = (f32[2,256,256]{2,1,0:T(8,128)S(1)}, f32[2,256,256]{2,1,0:T(8,128)S(1)}, u32[]{:S(2)}, u32[]{:S(2)}) collective-permute-start(f32[2,256,256]{2,1,0:T(8,128)S(1)} %get-tuple-element.66), channel_id=1, source_target_pairs={{16,32},{48,64},{80,96},{112,128},{144,160},{176,192},{208,224},{3... | collective-permute-start | bytes 1572872 | tf_op jit(solution)/shard_map/ppermute | solution.py:47
  91.1 18.3 %collective-permute-start.15 = (f32[2,256,256]{2,1,0:T(8,128)S(1)}, f32[2,256,256]{2,1,0:T(8,128)S(1)}, u32[]{:S(2)}, u32[]{:S(2)}) collective-permute-start(f32[2,256,256]{2,1,0:T(8,128)S(1)} %get-tuple-element.67), channel_id=1, source_target_pairs={{0,16},{32,48},{64,80},{96,112},{128,144},{160,176},{192,208},{224... | collective-permute-start | bytes 1572872 | tf_op jit(solution)/shard_map/ppermute | solution.py:48
  110.6 36.0 %collective-permute-start.21 = (f32[2,128,768]{2,1,0:T(8,128)S(1)}, f32[2,128,768]{2,1,0:T(8,128)S(1)}, u32[]{:S(2)}, u32[]{:S(2)}) collective-permute-start(f32[2,128,768]{2,1,0:T(8,128)S(1)} %get-tuple-element.75), channel_id=1, source_target_pairs={{0,1},{2,3},{4,5},{6,7},{8,9},{10,11},{12,13},{14,15},{1,0},{3,2},... | collective-permute-start | bytes 2359304 | tf_op jit(solution)/shard_map/ppermute | solution.py:38
  110.7 14.4 %collective-permute-start.19 = (f32[128,640]{1,0:T(8,128)S(1)}, f32[128,640]{1,0:T(8,128)S(1)}, u32[]{:S(2)}, u32[]{:S(2)}) collective-permute-start(f32[128,640]{1,0:T(8,128)S(1)} %get-tuple-element.74), channel_id=1, source_target_pairs={{1,2},{3,4},{5,6},{9,10},{11,12},{13,14},{2,1},{4,3},{6,5},{10,9},... | collective-permute-start | bytes 983048 | tf_op jit(solution)/shard_map/ppermute | solution.py:31
  114.5 18.3 %collective-permute-start.16 = (f32[2,256,256]{2,1,0:T(8,128)S(1)}, f32[2,256,256]{2,1,0:T(8,128)S(1)}, u32[]{:S(2)}, u32[]{:S(2)}) collective-permute-start(f32[2,256,256]{2,1,0:T(8,128)S(1)} %get-tuple-element.69), channel_id=1, source_target_pairs={{16,32},{48,64},{80,96},{112,128},{144,160},{176,192},{208,224},{3... | collective-permute-start | bytes 1572872 | tf_op jit(solution)/shard_map/ppermute | solution.py:47
  116.5 24.2 %collective-permute-start.17 = (f32[2,256,256]{2,1,0:T(8,128)S(1)}, f32[2,256,256]{2,1,0:T(8,128)S(1)}, u32[]{:S(2)}, u32[]{:S(2)}) collective-permute-start(f32[2,256,256]{2,1,0:T(8,128)S(1)} %get-tuple-element.70), channel_id=1, source_target_pairs={{0,16},{32,48},{64,80},{96,112},{128,144},{160,176},{192,208},{224... | collective-permute-start | bytes 1572872 | tf_op jit(solution)/shard_map/ppermute | solution.py:48
  118.3 28.4 %collective-permute-start.18 = (f32[128,896]{1,0:T(8,128)S(1)}, f32[128,896]{1,0:T(8,128)S(1)}, u32[]{:S(2)}, u32[]{:S(2)}) collective-permute-start(f32[128,896]{1,0:T(8,128)S(1)} %get-tuple-element.73), channel_id=1, source_target_pairs={{1,2},{3,4},{5,6},{9,10},{11,12},{13,14},{2,1},{4,3},{6,5},{10,9},... | collective-permute-start | bytes 1376264 | tf_op jit(solution)/shard_map/ppermute | solution.py:32
  125.2 21.5 %collective-permute-start.20 = (f32[128,640]{1,0:T(8,128)S(1)}, f32[128,640]{1,0:T(8,128)S(1)}, u32[]{:S(2)}, u32[]{:S(2)}) collective-permute-start(f32[128,640]{1,0:T(8,128)S(1)} %collective-permute-done.19.halo_detour), channel_id=1, source_target_pairs={{0,8},{15,7},{16,24},{31,23},{32,40},{47,39},{48,56},{63,55},{64,7... | collective-permute-start | bytes 983048 | tf_op jit(solution)/shard_map/ppermute | solution.py:33
  151.5 26.6 %collective-permute-start.25 = (f32[2,128,768]{2,1,0:T(8,128)S(1)}, f32[2,128,768]{2,1,0:T(8,128)S(1)}, u32[]{:S(2)}, u32[]{:S(2)}) collective-permute-start(f32[2,128,768]{2,1,0:T(8,128)S(1)} %get-tuple-element.80), channel_id=1, source_target_pairs={{0,1},{2,3},{4,5},{6,7},{8,9},{10,11},{12,13},{14,15},{1,0},{3,2},... | collective-permute-start | bytes 2359304 | tf_op jit(solution)/shard_map/ppermute | solution.py:38
  151.6 8.4 %collective-permute-start.23 = (f32[128,640]{1,0:T(8,128)S(1)}, f32[128,640]{1,0:T(8,128)S(1)}, u32[]{:S(2)}, u32[]{:S(2)}) collective-permute-start(f32[128,640]{1,0:T(8,128)S(1)} %get-tuple-element.79), channel_id=1, source_target_pairs={{1,2},{3,4},{5,6},{9,10},{11,12},{13,14},{2,1},{4,3},{6,5},{10,9},... | collective-permute-start | bytes 983048 | tf_op jit(solution)/shard_map/ppermute | solution.py:31
  152.9 18.2 %collective-permute-start.22 = (f32[128,896]{1,0:T(8,128)S(1)}, f32[128,896]{1,0:T(8,128)S(1)}, u32[]{:S(2)}, u32[]{:S(2)}) collective-permute-start(f32[128,896]{1,0:T(8,128)S(1)} %get-tuple-element.78), channel_id=1, source_target_pairs={{1,2},{3,4},{5,6},{9,10},{11,12},{13,14},{2,1},{4,3},{6,5},{10,9},... | collective-permute-start | bytes 1376264 | tf_op jit(solution)/shard_map/ppermute | solution.py:32
  160.0 18.1 %collective-permute-start.24 = (f32[128,640]{1,0:T(8,128)S(1)}, f32[128,640]{1,0:T(8,128)S(1)}, u32[]{:S(2)}, u32[]{:S(2)}) collective-permute-start(f32[128,640]{1,0:T(8,128)S(1)} %collective-permute-done.23.detour), channel_id=1, source_target_pairs={{0,8},{15,7},{16,24},{31,23},{32,40},{47,39},{48,56},{63,55},{64,7... | collective-permute-start | bytes 983048 | tf_op jit(solution)/shard_map/ppermute | solution.py:33
  161.3 36.4 %collective-permute-start.26 = (f32[2,256,128]{2,1,0:T(8,128)S(1)}, f32[2,256,128]{2,1,0:T(8,128)S(1)}, u32[]{:S(2)}, u32[]{:S(2)}) collective-permute-start(f32[2,256,128]{2,1,0:T(8,128)S(1)} %get-tuple-element.82), channel_id=1, source_target_pairs={{16,32},{48,64},{80,96},{112,128},{144,160},{176,192},{208,224},{3... | collective-permute-start | bytes 786440 | tf_op jit(solution)/shard_map/ppermute | solution.py:47
  171.0 26.7 %collective-permute-start.27 = (f32[2,256,128]{2,1,0:T(8,128)S(1)}, f32[2,256,128]{2,1,0:T(8,128)S(1)}, u32[]{:S(2)}, u32[]{:S(2)}) collective-permute-start(f32[2,256,128]{2,1,0:T(8,128)S(1)} %get-tuple-element.83), channel_id=1, source_target_pairs={{0,16},{32,48},{64,80},{96,112},{128,144},{160,176},{192,208},{224... | collective-permute-start | bytes 786440 | tf_op jit(solution)/shard_map/ppermute | solution.py:48
  178.8 21.5 %collective-permute-start.28 = (f32[2,256,128]{2,1,0:T(8,128)S(1)}, f32[2,256,128]{2,1,0:T(8,128)S(1)}, u32[]{:S(2)}, u32[]{:S(2)}) collective-permute-start(f32[2,256,128]{2,1,0:T(8,128)S(1)} %get-tuple-element.87), channel_id=1, source_target_pairs={{16,32},{48,64},{80,96},{112,128},{144,160},{176,192},{208,224},{3... | collective-permute-start | bytes 786440 | tf_op jit(solution)/shard_map/ppermute | solution.py:47
  184.0 17.4 %collective-permute-start.29 = (f32[2,256,128]{2,1,0:T(8,128)S(1)}, f32[2,256,128]{2,1,0:T(8,128)S(1)}, u32[]{:S(2)}, u32[]{:S(2)}) collective-permute-start(f32[2,256,128]{2,1,0:T(8,128)S(1)} %get-tuple-element.88), channel_id=1, source_target_pairs={{0,16},{32,48},{64,80},{96,112},{128,144},{160,176},{192,208},{224... | collective-permute-start | bytes 786440 | tf_op jit(solution)/shard_map/ppermute | solution.py:48
  (4 other events, 4.6 us)

commit v9 on v7

--- a/solution.py
+++ b/solution.py
@@ -325,14 +325,12 @@
     return pl.ds(pl.multiple_of(margin + low * (tile - half), half), half)
 
 
-def sides_kernel(meta, own, even_a, even_b, mid_a, mid_b, odd_own):
-    tile, half = own.shape[1], even_a.shape[1]
-    for rows, pair in (
-        (strip(meta, False, half, tile, 0), (even_a, even_b)),
-        (slice(half, tile - half), (mid_a, mid_b)),
-    ):
-        for out, cols in both_sides(meta, *pair, tile):
-            out[...] = own[:, rows, cols]
+def sides_kernel(meta, own, rest_odd, rest_even, odd_own):
+    tile, half = own.shape[1], rest_odd.shape[2]
+    even_rows = strip(meta, False, half, tile, 0)
+    for out, cols in both_sides(meta, rest_odd, rest_even, tile):
+        out[:, :half, :] = own[:, even_rows, cols]
+        out[:, half:, :] = own[:, half : tile - half, cols]
     odd_own[...] = own[:, strip(meta, True, half, tile, 0), :]
 
 
@@ -345,7 +343,7 @@
     else:
         line[:, :, half : half + tile] = own[:, strip(meta, False, half, tile, 0), :]
     for side, cols in both_sides(meta, side_odd, side_even, wide):
-        line[:, :, cols] = side[...]
+        line[:, :, cols] = side[:, :half, :]
     if odd:
         pack(line[0], line[1], *sends)
 
@@ -366,7 +364,7 @@
     field[:, strip(meta, False, half, tile, half), :] = even_line[...]
     field[:, mid, half : half + tile] = own[:, half : tile - half, :]
     for side, cols in both_sides(meta, side_odd, side_even, wide):
-        field[:, mid, cols] = side[...]
+        field[:, mid, cols] = side[:, half:, :]
     total[...] = jnp.zeros_like(total)
 
 
@@ -519,7 +517,7 @@
     line = (2, half, wide)
     sends = ((half, wide + CUT), (half, wide - CUT), line)
 
-    block = (2, half, half)
+    rest = (2, tile - half, half)
 
     def corner(low, right):
         return object_field[:, low * (tile - half) :, right * (tile - half) :][:, :half, :half]
@@ -532,10 +530,9 @@
         sides_kernel,
         places,
         (object_field,),
-        (block, block, mid_column, mid_column, (2, half, tile)),
-    )
-    even_sides = swap_columns(*sides[:2])
-    mids = swap_columns(*sides[2:])
+        (rest, rest, (2, half, tile)),
+    )
+    sides = swap_columns(*sides)
     *parts, odd_line = call(
         functools.partial(edge_kernel, True),
         meta,
@@ -544,7 +541,7 @@
     )
     odd_halo = swap_odd(*parts)
     (even_line,) = call(
-        functools.partial(edge_kernel, False), meta, (object_field, *even_sides), (line,)
+        functools.partial(edge_kernel, False), meta, (object_field, *sides), (line,)
     )
     halos = (*odd_halo, swap_even(even_line))
     probes, tables, amps = call(
@@ -556,7 +553,7 @@
         room=12 * MIB,
     )
     field, total = call(
-        centre_kernel, meta, (object_field, odd_line, even_line, *mids), (whole, whole)
+        centre_kernel, meta, (object_field, odd_line, even_line, *sides), (whole, whole)
     )
     for iteration in range(ITERS):
         last = iteration + 1 == ITERS

time: 206 us -> 204 us (level)
  starting transfers between devices: 108 us -> 91.3 us
  waiting for transfers between devices: 61.2 us -> 76.6 us
    ppermute x8 -> x7, starting transfers between devices: 34.9 us -> 27.8 us  [swap_columns(): from_even = lax.ppermute(even_cells, 'gx', pairs(count, 0))]
    ppermute x8 -> x7, waiting for transfers between devices: 24.3 us -> 30.6 us  [swap_columns(): from_odd = lax.ppermute(odd_cells, 'gx', pairs(count, 1))]
    ppermute x4, starting transfers between devices: 15.5 us -> 9.92 us  [swap_odd(): first = lax.ppermute(detour, 'gy', near + [(low, 0), (low + 1, count - 1)])]
    ppermute x8 -> x7, waiting for transfers between devices: 15 us -> 19 us  [swap_columns(): from_even = lax.ppermute(even_cells, 'gx', pairs(count, 0))]
    ppermute x8 -> x7, starting transfers between devices: 22.8 us -> 19.2 us  [swap_columns(): from_odd = lax.ppermute(odd_cells, 'gx', pairs(count, 1))]
    ppermute x4, waiting for transfers between devices: 10.2 us -> 13.4 us  [swap_odd(): second = lax.ppermute(first, 'gy', [(0, low + 1), (count - 1, low)])]
    unnamed x13 -> x11, local copies, waits for them, and re-layouts: 6.92 us -> 6.22 us
  transfers between devices with their start and end apart: 32 -> 30, of which waited for: 13 -> 16; matrix products, arithmetic and copies ran while one was open for 1% -> 1% of each run, Pallas kernels for 6% -> 6%
where the time goes in v9:
time: 204 us; the launch traced here: 203 us
  starting transfers between devices  91.3 us (45%)
  waiting for transfers between devices  76.6 us (38%)
  Pallas kernels  26 us (13%)
  local copies, waits for them, and re-layouts  6.39 us (3%)
    ppermute x7, waiting for transfers between devices, swap_columns(): from_odd = lax.ppermute(odd_cells, 'gx', pairs(count, 1))  30.6 us
    ppermute x4, starting transfers between devices, swap_odd(): straight = lax.ppermute(direct, 'gy', near + far)  28.1 us
    ppermute x7, starting transfers between devices, swap_columns(): from_even = lax.ppermute(even_cells, 'gx', pairs(count, 0))  27.8 us
    pallas_call x13, Pallas kernels, call(): pl.pallas_call(kernel, out_shape=shapes, in_specs=[smem, anywhere if far...  26 us
    ppermute x7, starting transfers between devices, swap_columns(): from_odd = lax.ppermute(odd_cells, 'gx', pairs(count, 1))  19.2 us
    ppermute x7, waiting for transfers between devices, swap_columns(): from_even = lax.ppermute(even_cells, 'gx', pairs(count, 0))  19 us
    ppermute x4, waiting for transfers between devices, swap_odd(): straight = lax.ppermute(direct, 'gy', near + far)  13.5 us
    ppermute x4, waiting for transfers between devices, swap_odd(): second = lax.ppermute(first, 'gy', [(0, low + 1), (count - 1, low)])  13.4 us
  transfers between devices with their start and end apart: 30, of which 16 were waited for; matrix products, arithmetic and copies ran while one was open for 1% of the time, Pallas kernels for 6%

profile of v9, /device:TPU:15, one launch (start us, length us, event | category | flops | bytes accessed | tf_op | source)
XLA Modules:
  0.0 203.4 jit_solution(3875901988796835775)
XLA Ops:
  3.2 6.1 %collective-permute-start.2 = (f32[2,384,128]{2,1,0:T(8,128)}, f32[2,384,128]{2,1,0:T(8,128)S(1)}, u32[]{:S(2)}, u32[]{:S(2)}) collective-permute-start(f32[2,384,128]{2,1,0:T(8,128)} %get-tuple-element.49), channel_id=1, source_target_pairs={{16,32},{48,64},{80,96},{112,128},{144,160},{176,192},{208,224},{3... | collective-permute-start | bytes 1179656 | tf_op jit(solution)/shard_map/ppermute | solution.py:47
  12.8 1.9 collective-permute-start
  16.3 2.0 collective-permute-done.2.side_odd
  18.2 9.5 %collective-permute-done.3.side_even = f32[2,384,128]{2,1,0:T(8,128)S(1)} collective-permute-done((f32[2,384,128]{2,1,0:T(8,128)}, f32[2,384,128]{2,1,0:T(8,128)S(1)}, u32[]{:S(2)}, u32[]{:S(2)}) %collective-permute-start.3) | collective-permute-done | bytes 393248 | tf_op jit(solution)/shard_map/ppermute | solution.py:48
  33.4 3.4 %collective-permute-start.5 = (f32[128,640]{1,0:T(8,128)S(1)}, f32[128,640]{1,0:T(8,128)S(1)}, u32[]{:S(2)}, u32[]{:S(2)}) collective-permute-start(f32[128,640]{1,0:T(8,128)S(1)} %get-tuple-element.54), channel_id=1, source_target_pairs={{1,2},{3,4},{5,6},{9,10},{11,12},{13,14},{2,1},{4,3},{6,5},{10,9},... | collective-permute-start | bytes 983048 | tf_op jit(solution)/shard_map/ppermute | solution.py:31
  36.9 9.9 %collective-permute-start.4 = (f32[128,896]{1,0:T(8,128)S(1)}, f32[128,896]{1,0:T(8,128)S(1)}, u32[]{:S(2)}, u32[]{:S(2)}) collective-permute-start(f32[128,896]{1,0:T(8,128)S(1)} %get-tuple-element.53), channel_id=1, source_target_pairs={{1,2},{3,4},{5,6},{9,10},{11,12},{13,14},{2,1},{4,3},{6,5},{10,9},... | collective-permute-start | bytes 1376264 | tf_op jit(solution)/shard_map/ppermute | solution.py:32
  50.3 4.7 %shard_map.59 = (f32[4,2,256,256]{3,2,1,0:T(8,128)S(1)}, bf16[4,8,256,256]{3,2,1,0:T(8,128)(2,1)S(1)}, f32[4,256,256]{2,1,0:T(8,128)S(1)}) custom-call(s32[13]{0:T(128)S(1)} %concatenate.4.meta, f32[2,256,256]{2,1,0:T(8,128)S(1)} %copy-done.4, f32[4,256,256]{2,1,0:T(8,128)S(1)} %bitcast.7), custom_call_target="tpu_custom_call" | custom-call | flops 1000000000 | bytes 8912896 | tf_op jit(solution)/shard_map/pallas_call | solution.py:486
  56.0 4.7 %collective-permute-done.6.halo_relayed = f32[128,640]{1,0:T(8,128)S(1)} collective-permute-done((f32[128,640]{1,0:T(8,128)S(1)}, f32[128,640]{1,0:T(8,128)S(1)}, u32[]{:S(2)}, u32[]{:S(2)}) %collective-permute-start.6) | collective-permute-done | bytes 327712 | tf_op jit(solution)/shard_map/ppermute | solution.py:33
  60.8 4.6 %shard_map.60 = (f32[2,768,768]{2,1,0:T(8,128)S(1)}, f32[2,768,768]{2,1,0:T(8,128)S(1)}, f32[128,896]{1,0:T(8,128)S(1)}, f32[128,640]{1,0:T(8,128)S(1)}, f32[2,1...) custom-call(s32[13]{0:T(128)S(1)} %concatenate.4.meta, ...), custom_call_target="tpu_custom_call", output_to_operand_aliasing={{0}: (1, {}), {1}: (2, {})} | custom-call | flops 1073741824 | bytes 30736384 | tf_op jit(solution)/shard_map/pallas_call | solution.py:486
  66.8 6.5 %collective-permute-start.8 = (f32[128,896]{1,0:T(8,128)S(1)}, f32[128,896]{1,0:T(8,128)S(1)}, u32[]{:S(2)}, u32[]{:S(2)}) collective-permute-start(f32[128,896]{1,0:T(8,128)S(1)} %get-tuple-element.60), channel_id=1, source_target_pairs={{1,2},{3,4},{5,6},{9,10},{11,12},{13,14},{2,1},{4,3},{6,5},{10,9},... | collective-permute-start | bytes 1376264 | tf_op jit(solution)/shard_map/ppermute | solution.py:32
  74.6 8.1 %collective-permute-done.8.direct = f32[128,896]{1,0:T(8,128)S(1)} collective-permute-done((f32[128,896]{1,0:T(8,128)S(1)}, f32[128,896]{1,0:T(8,128)S(1)}, u32[]{:S(2)}, u32[]{:S(2)}) %collective-permute-start.8) | collective-permute-done | bytes 458784 | tf_op jit(solution)/shard_map/ppermute | solution.py:32
  82.7 5.6 %collective-permute-done.10.relayed = f32[128,640]{1,0:T(8,128)S(1)} collective-permute-done((f32[128,640]{1,0:T(8,128)S(1)}, f32[128,640]{1,0:T(8,128)S(1)}, u32[]{:S(2)}, u32[]{:S(2)}) %collective-permute-start.10) | collective-permute-done | bytes 327712 | tf_op jit(solution)/shard_map/ppermute | solution.py:33
  89.2 1.9 collective-permute-start.12
  91.2 13.4 %collective-permute-done.12.band_odd = f32[2,256,256]{2,1,0:T(8,128)S(1)} collective-permute-done((f32[2,256,256]{2,1,0:T(8,128)S(1)}, f32[2,256,256]{2,1,0:T(8,128)S(1)}, u32[]{:S(2)}, u32[]{:S(2)}) %collective-permute-start.12) | collective-permute-done | bytes 524320 | tf_op jit(solution)/shard_map/ppermute | solution.py:47
  104.6 2.9 %collective-permute-done.13.band_even = f32[2,256,256]{2,1,0:T(8,128)S(1)} collective-permute-done((f32[2,256,256]{2,1,0:T(8,128)S(1)}, f32[2,256,256]{2,1,0:T(8,128)S(1)}, u32[]{:S(2)}, u32[]{:S(2)}) %collective-permute-start.13) | collective-permute-done | bytes 524320 | tf_op jit(solution)/shard_map/ppermute | solution.py:48
  108.8 3.9 %collective-permute-start.19 = (f32[128,640]{1,0:T(8,128)S(1)}, f32[128,640]{1,0:T(8,128)S(1)}, u32[]{:S(2)}, u32[]{:S(2)}) collective-permute-start(f32[128,640]{1,0:T(8,128)S(1)} %get-tuple-element.74), channel_id=1, source_target_pairs={{1,2},{3,4},{5,6},{9,10},{11,12},{13,14},{2,1},{4,3},{6,5},{10,9},... | collective-permute-start | bytes 983048 | tf_op jit(solution)/shard_map/ppermute | solution.py:31
  112.7 1.9 collective-permute-start.14
  114.6 2.6 %collective-permute-start.15 = (f32[2,128,256]{2,1,0:T(8,128)S(1)}, f32[2,128,256]{2,1,0:T(8,128)S(1)}, u32[]{:S(2)}, u32[]{:S(2)}) collective-permute-start(f32[2,128,256]{2,1,0:T(8,128)S(1)} %get-tuple-element.68), channel_id=1, source_target_pairs={{0,16},{32,48},{64,80},{96,112},{128,144},{160,176},{192,208},{224... | collective-permute-start | bytes 786440 | tf_op jit(solution)/shard_map/ppermute | solution.py:48
  117.2 6.2 %collective-permute-start.18 = (f32[128,896]{1,0:T(8,128)S(1)}, f32[128,896]{1,0:T(8,128)S(1)}, u32[]{:S(2)}, u32[]{:S(2)}) collective-permute-start(f32[128,896]{1,0:T(8,128)S(1)} %get-tuple-element.73), channel_id=1, source_target_pairs={{1,2},{3,4},{5,6},{9,10},{11,12},{13,14},{2,1},{4,3},{6,5},{10,9},... | collective-permute-start | bytes 1376264 | tf_op jit(solution)/shard_map/ppermute | solution.py:32
  125.3 3.0 %collective-permute-start.16 = (f32[2,128,256]{2,1,0:T(8,128)S(1)}, f32[2,128,256]{2,1,0:T(8,128)S(1)}, u32[]{:S(2)}, u32[]{:S(2)}) collective-permute-start(f32[2,128,256]{2,1,0:T(8,128)S(1)} %get-tuple-element.69), channel_id=1, source_target_pairs={{16,32},{48,64},{80,96},{112,128},{144,160},{176,192},{208,224},{3... | collective-permute-start | bytes 786440 | tf_op jit(solution)/shard_map/ppermute | solution.py:47
  129.3 3.7 %collective-permute-start.17 = (f32[2,128,256]{2,1,0:T(8,128)S(1)}, f32[2,128,256]{2,1,0:T(8,128)S(1)}, u32[]{:S(2)}, u32[]{:S(2)}) collective-permute-start(f32[2,128,256]{2,1,0:T(8,128)S(1)} %get-tuple-element.70), channel_id=1, source_target_pairs={{0,16},{32,48},{64,80},{96,112},{128,144},{160,176},{192,208},{224... | collective-permute-start | bytes 786440 | tf_op jit(solution)/shard_map/ppermute | solution.py:48
  133.0 13.8 %collective-permute-done.16.lower_odd = f32[2,128,256]{2,1,0:T(8,128)S(1)} collective-permute-done((f32[2,128,256]{2,1,0:T(8,128)S(1)}, f32[2,128,256]{2,1,0:T(8,128)S(1)}, u32[]{:S(2)}, u32[]{:S(2)}) %collective-permute-start.16) | collective-permute-done | bytes 262176 | tf_op jit(solution)/shard_map/ppermute | solution.py:47
  146.8 3.7 %collective-permute-done.17.lower_even = f32[2,128,256]{2,1,0:T(8,128)S(1)} collective-permute-done((f32[2,128,256]{2,1,0:T(8,128)S(1)}, f32[2,128,256]{2,1,0:T(8,128)S(1)}, u32[]{:S(2)}, u32[]{:S(2)}) %collective-permute-start.17) | collective-permute-done | bytes 262176 | tf_op jit(solution)/shard_map/ppermute | solution.py:48
  151.8 4.6 %shard_map.64 = (f32[2,768,768]{2,1,0:T(8,128)S(1)}, f32[2,768,768]{2,1,0:T(8,128)S(1)}, f32[128,896]{1,0:T(8,128)S(1)}, f32[128,640]{1,0:T(8,128)S(1)}, f32[2,1...) custom-call(s32[13]{0:T(128)S(1)} %concatenate.4.meta, ...), custom_call_target="tpu_custom_call", output_to_operand_aliasing={{0}: (1, {}), {1}: (2, {})} | custom-call | flops 1073741824 | bytes 30212096 | tf_op jit(solution)/shard_map/pallas_call | solution.py:486
  157.9 5.6 %collective-permute-start.22 = (f32[128,896]{1,0:T(8,128)S(1)}, f32[128,896]{1,0:T(8,128)S(1)}, u32[]{:S(2)}, u32[]{:S(2)}) collective-permute-start(f32[128,896]{1,0:T(8,128)S(1)} %get-tuple-element.78), channel_id=1, source_target_pairs={{1,2},{3,4},{5,6},{9,10},{11,12},{13,14},{2,1},{4,3},{6,5},{10,9},... | collective-permute-start | bytes 1376264 | tf_op jit(solution)/shard_map/ppermute | solution.py:32
  164.8 2.4 %collective-permute-start.26 = (f32[2,256,128]{2,1,0:T(8,128)S(1)}, f32[2,256,128]{2,1,0:T(8,128)S(1)}, u32[]{:S(2)}, u32[]{:S(2)}) collective-permute-start(f32[2,256,128]{2,1,0:T(8,128)S(1)} %get-tuple-element.82), channel_id=1, source_target_pairs={{16,32},{48,64},{80,96},{112,128},{144,160},{176,192},{208,224},{3... | collective-permute-start | bytes 786440 | tf_op jit(solution)/shard_map/ppermute | solution.py:47
  167.2 3.2 %collective-permute-start.27 = (f32[2,256,128]{2,1,0:T(8,128)S(1)}, f32[2,256,128]{2,1,0:T(8,128)S(1)}, u32[]{:S(2)}, u32[]{:S(2)}) collective-permute-start(f32[2,256,128]{2,1,0:T(8,128)S(1)} %get-tuple-element.83), channel_id=1, source_target_pairs={{0,16},{32,48},{64,80},{96,112},{128,144},{160,176},{192,208},{224... | collective-permute-start | bytes 786440 | tf_op jit(solution)/shard_map/ppermute | solution.py:48
  170.4 5.4 %collective-permute-done.22.direct = f32[128,896]{1,0:T(8,128)S(1)} collective-permute-done((f32[128,896]{1,0:T(8,128)S(1)}, f32[128,896]{1,0:T(8,128)S(1)}, u32[]{:S(2)}, u32[]{:S(2)}) %collective-permute-start.22) | collective-permute-done | bytes 458784 | tf_op jit(solution)/shard_map/ppermute | solution.py:32
  175.8 3.1 %collective-permute-done.24.relayed = f32[128,640]{1,0:T(8,128)S(1)} collective-permute-done((f32[128,640]{1,0:T(8,128)S(1)}, f32[128,640]{1,0:T(8,128)S(1)}, u32[]{:S(2)}, u32[]{:S(2)}) %collective-permute-start.24) | collective-permute-done | bytes 327712 | tf_op jit(solution)/shard_map/ppermute | solution.py:33
  179.6 1.9 collective-permute-start.28
  181.5 16.6 %collective-permute-start.29 = (f32[2,256,128]{2,1,0:T(8,128)S(1)}, f32[2,256,128]{2,1,0:T(8,128)S(1)}, u32[]{:S(2)}, u32[]{:S(2)}) collective-permute-start(f32[2,256,128]{2,1,0:T(8,128)S(1)} %get-tuple-element.88), channel_id=1, source_target_pairs={{0,16},{32,48},{64,80},{96,112},{128,144},{160,176},{192,208},{224... | collective-permute-start | bytes 786440 | tf_op jit(solution)/shard_map/ppermute | solution.py:48
  198.1 2.5 %shard_map.66 = (f32[2,512,512]{2,1,0:T(8,128)}, f32[2,256,128]{2,1,0:T(8,128)S(1)}, f32[2,256,128]{2,1,0:T(8,128)S(1)}) custom-call(s32[13]{0:T(128)S(1)} %concatenate.4.meta, f32[2,768,768]{2,1,0:T(8,128)S(1)} %get-tuple-element.76.field, f32[2,768,768]{2,1,0:T(8,128)S(1)} %get-tuple-element.77.total, f32[2,128,768]{2,1,0:T(8,128)S(1)} %get-tuple-element.81.line, ...), custom_call_target="tpu_custom_call" | custom-call | bytes 14155776 | tf_op jit(solution)/shard_map/pallas_call | solution.py:486
  (56 shorter events, 32.9 us)
Async XLA Ops:
  0.1 1.6 copy-start
  1.7 53.3 %copy-start.2 = (f32[2,512,512]{2,1,0:T(8,128)S(1)}, f32[2,512,512]{2,1,0:T(8,128)}, u32[]{:S(2)}) copy-start(f32[2,512,512]{2,1,0:T(8,128)} %own.5) | copy-start | bytes 6291460
  3.2 15.0 %collective-permute-start.2 = (f32[2,384,128]{2,1,0:T(8,128)}, f32[2,384,128]{2,1,0:T(8,128)S(1)}, u32[]{:S(2)}, u32[]{:S(2)}) collective-permute-start(f32[2,384,128]{2,1,0:T(8,128)} %get-tuple-element.49), channel_id=1, source_target_pairs={{16,32},{48,64},{80,96},{112,128},{144,160},{176,192},{208,224},{3... | collective-permute-start | bytes 1179656 | tf_op jit(solution)/shard_map/ppermute | solution.py:47
  9.4 18.4 %collective-permute-start.3 = (f32[2,384,128]{2,1,0:T(8,128)}, f32[2,384,128]{2,1,0:T(8,128)S(1)}, u32[]{:S(2)}, u32[]{:S(2)}) collective-permute-start(f32[2,384,128]{2,1,0:T(8,128)} %get-tuple-element.50), channel_id=1, source_target_pairs={{0,16},{32,48},{64,80},{96,112},{128,144},{160,176},{192,208},{224... | collective-permute-start | bytes 1179656 | tf_op jit(solution)/shard_map/ppermute | solution.py:48
  11.3 20.2 %collective-permute-start.1 = (f32[2,128,128]{2,1,0:T(8,128)}, f32[2,128,128]{2,1,0:T(8,128)S(1)}, u32[]{:S(2)}, u32[]{:S(2)}) collective-permute-start(f32[2,128,128]{2,1,0:T(8,128)} %get-tuple-element.89), channel_id=1, source_target_pairs={{0,16},{32,48},{64,80},{96,112},{128,144},{160,176},{192,208},{224... | collective-permute-start | bytes 393224 | tf_op jit(solution)/shard_map/ppermute | solution.py:48
  12.8 19.6 %collective-permute-start = (f32[2,128,128]{2,1,0:T(8,128)}, f32[2,128,128]{2,1,0:T(8,128)}, u32[]{:S(2)}, u32[]{:S(2)}) collective-permute-start(f32[2,128,128]{2,1,0:T(8,128)} %get-tuple-element.90), channel_id=1, source_target_pairs={{16,32},{48,64},{80,96},{112,128},{144,160},{176,192},{208,224},{3... | collective-permute-start | bytes 393224 | tf_op jit(solution)/shard_map/ppermute | solution.py:47
  30.0 30.8 %collective-permute-start.7 = (f32[2,128,768]{2,1,0:T(8,128)S(1)}, f32[2,128,768]{2,1,0:T(8,128)S(1)}, u32[]{:S(2)}, u32[]{:S(2)}) collective-permute-start(f32[2,128,768]{2,1,0:T(8,128)S(1)} %shard_map.57.even_line), channel_id=1, source_target_pairs={{0,1},{2,3},{4,5},{6,7},{8,9},{10,11},{12,13},{14,15},{1,0},{3,2},... | collective-permute-start | bytes 2359304 | tf_op jit(solution)/shard_map/ppermute | solution.py:38
  33.4 13.3 %collective-permute-start.5 = (f32[128,640]{1,0:T(8,128)S(1)}, f32[128,640]{1,0:T(8,128)S(1)}, u32[]{:S(2)}, u32[]{:S(2)}) collective-permute-start(f32[128,640]{1,0:T(8,128)S(1)} %get-tuple-element.54), channel_id=1, source_target_pairs={{1,2},{3,4},{5,6},{9,10},{11,12},{13,14},{2,1},{4,3},{6,5},{10,9},... | collective-permute-start | bytes 983048 | tf_op jit(solution)/shard_map/ppermute | solution.py:31
  36.9 19.2 %collective-permute-start.4 = (f32[128,896]{1,0:T(8,128)S(1)}, f32[128,896]{1,0:T(8,128)S(1)}, u32[]{:S(2)}, u32[]{:S(2)}) collective-permute-start(f32[128,896]{1,0:T(8,128)S(1)} %get-tuple-element.53), channel_id=1, source_target_pairs={{1,2},{3,4},{5,6},{9,10},{11,12},{13,14},{2,1},{4,3},{6,5},{10,9},... | collective-permute-start | bytes 1376264 | tf_op jit(solution)/shard_map/ppermute | solution.py:32
  46.7 14.0 %collective-permute-start.6 = (f32[128,640]{1,0:T(8,128)S(1)}, f32[128,640]{1,0:T(8,128)S(1)}, u32[]{:S(2)}, u32[]{:S(2)}) collective-permute-start(f32[128,640]{1,0:T(8,128)S(1)} %collective-permute-done.5.halo_detour), channel_id=1, source_target_pairs={{0,8},{15,7},{16,24},{31,23},{32,40},{47,39},{48,56},{63,55},{64,7... | collective-permute-start | bytes 983048 | tf_op jit(solution)/shard_map/ppermute | solution.py:33
  65.4 22.9 %collective-permute-start.11 = (f32[2,128,768]{2,1,0:T(8,128)S(1)}, f32[2,128,768]{2,1,0:T(8,128)S(1)}, u32[]{:S(2)}, u32[]{:S(2)}) collective-permute-start(f32[2,128,768]{2,1,0:T(8,128)S(1)} %get-tuple-element.62), channel_id=1, source_target_pairs={{0,1},{2,3},{4,5},{6,7},{8,9},{10,11},{12,13},{14,15},{1,0},{3,2},... | collective-permute-start | bytes 2359304 | tf_op jit(solution)/shard_map/ppermute | solution.py:38
  65.5 7.8 %collective-permute-start.9 = (f32[128,640]{1,0:T(8,128)S(1)}, f32[128,640]{1,0:T(8,128)S(1)}, u32[]{:S(2)}, u32[]{:S(2)}) collective-permute-start(f32[128,640]{1,0:T(8,128)S(1)} %get-tuple-element.61), channel_id=1, source_target_pairs={{1,2},{3,4},{5,6},{9,10},{11,12},{13,14},{2,1},{4,3},{6,5},{10,9},... | collective-permute-start | bytes 983048 | tf_op jit(solution)/shard_map/ppermute | solution.py:31
  66.8 15.9 %collective-permute-start.8 = (f32[128,896]{1,0:T(8,128)S(1)}, f32[128,896]{1,0:T(8,128)S(1)}, u32[]{:S(2)}, u32[]{:S(2)}) collective-permute-start(f32[128,896]{1,0:T(8,128)S(1)} %get-tuple-element.60), channel_id=1, source_target_pairs={{1,2},{3,4},{5,6},{9,10},{11,12},{13,14},{2,1},{4,3},{6,5},{10,9},... | collective-permute-start | bytes 1376264 | tf_op jit(solution)/shard_map/ppermute | solution.py:32
  73.3 15.0 %collective-permute-start.10 = (f32[128,640]{1,0:T(8,128)S(1)}, f32[128,640]{1,0:T(8,128)S(1)}, u32[]{:S(2)}, u32[]{:S(2)}) collective-permute-start(f32[128,640]{1,0:T(8,128)S(1)} %collective-permute-done.9.detour), channel_id=1, source_target_pairs={{0,8},{15,7},{16,24},{31,23},{32,40},{47,39},{48,56},{63,55},{64,7... | collective-permute-start | bytes 983048 | tf_op jit(solution)/shard_map/ppermute | solution.py:33
  89.2 15.4 %collective-permute-start.12 = (f32[2,256,256]{2,1,0:T(8,128)S(1)}, f32[2,256,256]{2,1,0:T(8,128)S(1)}, u32[]{:S(2)}, u32[]{:S(2)}) collective-permute-start(f32[2,256,256]{2,1,0:T(8,128)S(1)} %get-tuple-element.64), channel_id=1, source_target_pairs={{16,32},{48,64},{80,96},{112,128},{144,160},{176,192},{208,224},{3... | collective-permute-start | bytes 1572872 | tf_op jit(solution)/shard_map/ppermute | solution.py:47
  91.1 16.4 %collective-permute-start.13 = (f32[2,256,256]{2,1,0:T(8,128)S(1)}, f32[2,256,256]{2,1,0:T(8,128)S(1)}, u32[]{:S(2)}, u32[]{:S(2)}) collective-permute-start(f32[2,256,256]{2,1,0:T(8,128)S(1)} %get-tuple-element.65), channel_id=1, source_target_pairs={{0,16},{32,48},{64,80},{96,112},{128,144},{160,176},{192,208},{224... | collective-permute-start | bytes 1572872 | tf_op jit(solution)/shard_map/ppermute | solution.py:48
  108.7 43.2 %collective-permute-start.21 = (f32[2,128,768]{2,1,0:T(8,128)S(1)}, f32[2,128,768]{2,1,0:T(8,128)S(1)}, u32[]{:S(2)}, u32[]{:S(2)}) collective-permute-start(f32[2,128,768]{2,1,0:T(8,128)S(1)} %get-tuple-element.75), channel_id=1, source_target_pairs={{0,1},{2,3},{4,5},{6,7},{8,9},{10,11},{12,13},{14,15},{1,0},{3,2},... | collective-permute-start | bytes 2359304 | tf_op jit(solution)/shard_map/ppermute | solution.py:38
  108.8 14.6 %collective-permute-start.19 = (f32[128,640]{1,0:T(8,128)S(1)}, f32[128,640]{1,0:T(8,128)S(1)}, u32[]{:S(2)}, u32[]{:S(2)}) collective-permute-start(f32[128,640]{1,0:T(8,128)S(1)} %get-tuple-element.74), channel_id=1, source_target_pairs={{1,2},{3,4},{5,6},{9,10},{11,12},{13,14},{2,1},{4,3},{6,5},{10,9},... | collective-permute-start | bytes 983048 | tf_op jit(solution)/shard_map/ppermute | solution.py:31
  112.7 12.6 %collective-permute-start.14 = (f32[2,128,256]{2,1,0:T(8,128)S(1)}, f32[2,128,256]{2,1,0:T(8,128)S(1)}, u32[]{:S(2)}, u32[]{:S(2)}) collective-permute-start(f32[2,128,256]{2,1,0:T(8,128)S(1)} %get-tuple-element.67), channel_id=1, source_target_pairs={{16,32},{48,64},{80,96},{112,128},{144,160},{176,192},{208,224},{3... | collective-permute-start | bytes 786440 | tf_op jit(solution)/shard_map/ppermute | solution.py:47
  114.6 14.7 %collective-permute-start.15 = (f32[2,128,256]{2,1,0:T(8,128)S(1)}, f32[2,128,256]{2,1,0:T(8,128)S(1)}, u32[]{:S(2)}, u32[]{:S(2)}) collective-permute-start(f32[2,128,256]{2,1,0:T(8,128)S(1)} %get-tuple-element.68), channel_id=1, source_target_pairs={{0,16},{32,48},{64,80},{96,112},{128,144},{160,176},{192,208},{224... | collective-permute-start | bytes 786440 | tf_op jit(solution)/shard_map/ppermute | solution.py:48
  117.2 34.6 %collective-permute-start.18 = (f32[128,896]{1,0:T(8,128)S(1)}, f32[128,896]{1,0:T(8,128)S(1)}, u32[]{:S(2)}, u32[]{:S(2)}) collective-permute-start(f32[128,896]{1,0:T(8,128)S(1)} %get-tuple-element.73), channel_id=1, source_target_pairs={{1,2},{3,4},{5,6},{9,10},{11,12},{13,14},{2,1},{4,3},{6,5},{10,9},... | collective-permute-start | bytes 1376264 | tf_op jit(solution)/shard_map/ppermute | solution.py:32
  123.4 28.4 %collective-permute-start.20 = (f32[128,640]{1,0:T(8,128)S(1)}, f32[128,640]{1,0:T(8,128)S(1)}, u32[]{:S(2)}, u32[]{:S(2)}) collective-permute-start(f32[128,640]{1,0:T(8,128)S(1)} %collective-permute-done.19.halo_detour), channel_id=1, source_target_pairs={{0,8},{15,7},{16,24},{31,23},{32,40},{47,39},{48,56},{63,55},{64,7... | collective-permute-start | bytes 983048 | tf_op jit(solution)/shard_map/ppermute | solution.py:33
  125.3 21.6 %collective-permute-start.16 = (f32[2,128,256]{2,1,0:T(8,128)S(1)}, f32[2,128,256]{2,1,0:T(8,128)S(1)}, u32[]{:S(2)}, u32[]{:S(2)}) collective-permute-start(f32[2,128,256]{2,1,0:T(8,128)S(1)} %get-tuple-element.69), channel_id=1, source_target_pairs={{16,32},{48,64},{80,96},{112,128},{144,160},{176,192},{208,224},{3... | collective-permute-start | bytes 786440 | tf_op jit(solution)/shard_map/ppermute | solution.py:47
  129.3 21.2 %collective-permute-start.17 = (f32[2,128,256]{2,1,0:T(8,128)S(1)}, f32[2,128,256]{2,1,0:T(8,128)S(1)}, u32[]{:S(2)}, u32[]{:S(2)}) collective-permute-start(f32[2,128,256]{2,1,0:T(8,128)S(1)} %get-tuple-element.70), channel_id=1, source_target_pairs={{0,16},{32,48},{64,80},{96,112},{128,144},{160,176},{192,208},{224... | collective-permute-start | bytes 786440 | tf_op jit(solution)/shard_map/ppermute | solution.py:48
  156.5 22.4 %collective-permute-start.25 = (f32[2,128,768]{2,1,0:T(8,128)S(1)}, f32[2,128,768]{2,1,0:T(8,128)S(1)}, u32[]{:S(2)}, u32[]{:S(2)}) collective-permute-start(f32[2,128,768]{2,1,0:T(8,128)S(1)} %get-tuple-element.80), channel_id=1, source_target_pairs={{0,1},{2,3},{4,5},{6,7},{8,9},{10,11},{12,13},{14,15},{1,0},{3,2},... | collective-permute-start | bytes 2359304 | tf_op jit(solution)/shard_map/ppermute | solution.py:38
  156.6 6.9 %collective-permute-start.23 = (f32[128,640]{1,0:T(8,128)S(1)}, f32[128,640]{1,0:T(8,128)S(1)}, u32[]{:S(2)}, u32[]{:S(2)}) collective-permute-start(f32[128,640]{1,0:T(8,128)S(1)} %get-tuple-element.79), channel_id=1, source_target_pairs={{1,2},{3,4},{5,6},{9,10},{11,12},{13,14},{2,1},{4,3},{6,5},{10,9},... | collective-permute-start | bytes 983048 | tf_op jit(solution)/shard_map/ppermute | solution.py:31
  157.9 17.9 %collective-permute-start.22 = (f32[128,896]{1,0:T(8,128)S(1)}, f32[128,896]{1,0:T(8,128)S(1)}, u32[]{:S(2)}, u32[]{:S(2)}) collective-permute-start(f32[128,896]{1,0:T(8,128)S(1)} %get-tuple-element.78), channel_id=1, source_target_pairs={{1,2},{3,4},{5,6},{9,10},{11,12},{13,14},{2,1},{4,3},{6,5},{10,9},... | collective-permute-start | bytes 1376264 | tf_op jit(solution)/shard_map/ppermute | solution.py:32
  163.5 15.4 %collective-permute-start.24 = (f32[128,640]{1,0:T(8,128)S(1)}, f32[128,640]{1,0:T(8,128)S(1)}, u32[]{:S(2)}, u32[]{:S(2)}) collective-permute-start(f32[128,640]{1,0:T(8,128)S(1)} %collective-permute-done.23.detour), channel_id=1, source_target_pairs={{0,8},{15,7},{16,24},{31,23},{32,40},{47,39},{48,56},{63,55},{64,7... | collective-permute-start | bytes 983048 | tf_op jit(solution)/shard_map/ppermute | solution.py:33
  164.8 33.3 %collective-permute-start.26 = (f32[2,256,128]{2,1,0:T(8,128)S(1)}, f32[2,256,128]{2,1,0:T(8,128)S(1)}, u32[]{:S(2)}, u32[]{:S(2)}) collective-permute-start(f32[2,256,128]{2,1,0:T(8,128)S(1)} %get-tuple-element.82), channel_id=1, source_target_pairs={{16,32},{48,64},{80,96},{112,128},{144,160},{176,192},{208,224},{3... | collective-permute-start | bytes 786440 | tf_op jit(solution)/shard_map/ppermute | solution.py:47
  167.2 30.9 %collective-permute-start.27 = (f32[2,256,128]{2,1,0:T(8,128)S(1)}, f32[2,256,128]{2,1,0:T(8,128)S(1)}, u32[]{:S(2)}, u32[]{:S(2)}) collective-permute-start(f32[2,256,128]{2,1,0:T(8,128)S(1)} %get-tuple-element.83), channel_id=1, source_target_pairs={{0,16},{32,48},{64,80},{96,112},{128,144},{160,176},{192,208},{224... | collective-permute-start | bytes 786440 | tf_op jit(solution)/shard_map/ppermute | solution.py:48
  179.6 21.1 %collective-permute-start.28 = (f32[2,256,128]{2,1,0:T(8,128)S(1)}, f32[2,256,128]{2,1,0:T(8,128)S(1)}, u32[]{:S(2)}, u32[]{:S(2)}) collective-permute-start(f32[2,256,128]{2,1,0:T(8,128)S(1)} %get-tuple-element.87), channel_id=1, source_target_pairs={{16,32},{48,64},{80,96},{112,128},{144,160},{176,192},{208,224},{3... | collective-permute-start | bytes 786440 | tf_op jit(solution)/shard_map/ppermute | solution.py:47
  181.5 20.4 %collective-permute-start.29 = (f32[2,256,128]{2,1,0:T(8,128)S(1)}, f32[2,256,128]{2,1,0:T(8,128)S(1)}, u32[]{:S(2)}, u32[]{:S(2)}) collective-permute-start(f32[2,256,128]{2,1,0:T(8,128)S(1)} %get-tuple-element.88), channel_id=1, source_target_pairs={{0,16},{32,48},{64,80},{96,112},{128,144},{160,176},{192,208},{224... | collective-permute-start | bytes 786440 | tf_op jit(solution)/shard_map/ppermute | solution.py:48
  (3 other events, 3.9 us)
